TPU v7x, 32 devices: a whole 2x2x4 slice. The times are simulated.
32 devices in a mesh: dp: 8 (over z, y), tensor: 4 (over x, core).
Axes of the slice: x: 2, y: 2, z: 4, core: 2. Of those that a mesh axis runs over, the one named last changes fastest.
Arguments:
- hidden_in: bfloat16 [1024, 24, 768], P('tensor', 'dp'), may hold values from -6 to 6
- doc_ids: int32 [1024, 24], P(None, 'dp'), may hold values from -1 to 7, as said below
- first_gain: bfloat16 [768], replicated, may hold values from 0.5 to 1.5
- first_shift: bfloat16 [768], replicated, may hold values from -1 to 1
- qkv_weight: bfloat16 [768, 3, 768], P(None, None, 'tensor'), may hold values from -0.3125 to 0.3125
- qv_bias: bfloat16 [2, 768], P(None, 'tensor'), may hold values from -1 to 1
- proj_weight: bfloat16 [768, 768], P('tensor'), may hold values from -0.75 to 0.75
- proj_bias: bfloat16 [768], replicated, may hold values from -1 to 1
- second_gain: bfloat16 [768], replicated, may hold values from 0.5 to 1.5
- second_shift: bfloat16 [768], replicated, may hold values from -1 to 1
- up_weight: bfloat16 [768, 3072], P(None, 'tensor'), may hold values from -0.21875 to 0.21875
- up_bias: bfloat16 [3072], P('tensor'), may hold values from -1 to 1
- down_weight: bfloat16 [3072, 768], P('tensor'), may hold values from -0.15625 to 0.15625
- down_bias: bfloat16 [768], replicated, may hold values from -1 to 1
- out_grad: bfloat16 [1024, 24, 768], P('tensor', 'dp'), may hold values from -6 to 6
Outputs:
- block_out: bfloat16 [1024, 24, 768], P('tensor', 'dp')
- in_grad: bfloat16 [1024, 24, 768], P('tensor', 'dp')
- first_gain_grad: float32 [768], replicated
- first_shift_grad: float32 [768], replicated
- qkv_weight_grad: float32 [768, 3, 768], P(None, None, 'tensor')
- qv_bias_grad: float32 [2, 768], P(None, 'tensor')
- proj_weight_grad: float32 [768, 768], P('tensor')
- proj_bias_grad: float32 [768], replicated
- second_gain_grad: float32 [768], replicated
- second_shift_grad: float32 [768], replicated
- up_weight_grad: float32 [768, 3072], P(None, 'tensor')
- up_bias_grad: float32 [3072], P('tensor')
- down_weight_grad: float32 [3072, 768], P('tensor')
- down_bias_grad: float32 [768], replicated
Inputs may be any that keep to these rules, and one draw needn't show every extreme that they name: `doc_ids`: each sequence's 1024 positions hold exactly 8 documents with ids 0 to 7 in rising order, each id on a run of consecutive positions, followed by a tail of one to 128 positions that holds -1 (padding).
All inputs are finite; a program needn't handle non-finite values.
Results may differ from a plain program's by a relative error of at most 0.019.
Values may be sent and summed in bfloat16 or wider, within the bound.
No kernel may reach another device: no remote copies, remote signals or barrier semaphores. Data moves between devices by JAX's collectives and lax.ppermute only.
A program may use at most 128 MiB of HBM per device.

v0:
```python
import functools

import jax
import jax.numpy as jnp
from jax import lax
from jax.experimental import pallas as pl
from jax.experimental.pallas import tpu as pltpu
from jax.sharding import PartitionSpec as P

HEAD_DIM = 64
NORM_EPS = 1e-05
MASKED = -1e30
BF = jnp.bfloat16
F32 = jnp.float32
VMEM_LIMIT = 56 * 1024 * 1024

SLOT = ((0, 2, 4, 5), (1, 3, 6, 7))
SLOT_ROW = (0, 1, 0, 1, 0, 0)
SLOT_K = (0, 0, 1, 1, 2, 3)
X_SWAP = ((0, 2), (1, 3), (2, 0), (3, 1))
CORE_SWAP = ((0, 1), (1, 0), (2, 3), (3, 2))


def x_swap(value):
    return lax.ppermute(value, "tensor", X_SWAP)


def core_swap(value):
    return lax.ppermute(value, "tensor", CORE_SWAP)


def params(semantics=None):
    return pltpu.CompilerParams(vmem_limit_bytes=VMEM_LIMIT)


def fixed(shape):
    return pl.BlockSpec(shape, lambda *ids: (0,) * len(shape), pipeline_mode=pl.Buffered(1))


def nt(left, right):
    return lax.dot_general(left, right, (((1,), (1,)), ((), ())), preferred_element_type=F32)


def nn(left, right):
    return lax.dot_general(left, right, (((1,), (0,)), ((), ())), preferred_element_type=F32)


def tn(left, right):
    return lax.dot_general(left, right, (((0,), (0,)), ((), ())), preferred_element_type=F32)


SMALL_COST = pl.CostEstimate(flops=1, bytes_accessed=1, transcendentals=0)


def swapped_slot(slot):
    return jnp.where(slot < 4, slot ^ 2, slot ^ 1)


def own_first(step):
    return jnp.where(step == 2, 4, jnp.where((step == 3) | (step == 4), step - 1, step))


def key_mask(start_row, key_first, size, diagonal):
    keys = lax.broadcasted_iota(jnp.int32, (size, size), 0)
    mask = keys >= start_row - key_first
    if diagonal:
        mask = mask & (keys <= lax.broadcasted_iota(jnp.int32, (size, size), 1))
    return mask


def head_rows(size):
    lane = lax.broadcasted_iota(jnp.int32, (size, 2 * HEAD_DIM), 1)

    def select(value):
        zero = jnp.zeros((size, 2 * HEAD_DIM), value.dtype)
        pair = value[:, : 2 * HEAD_DIM]
        return (
            jnp.where(lane < HEAD_DIM, pair, zero),
            jnp.where(lane < HEAD_DIM, zero, pair),
            value[:, 2 * HEAD_DIM :],
        )

    return select


def pair_lanes(value, head):
    first = 2 * HEAD_DIM * (head // 2)
    return value[:, first : first + 2 * HEAD_DIM]


def attend_forward_kernel(size, table, start_ref, q_ref, k_ref, v_ref, out_ref, lse_ref):
    slot = pl.program_id(1)
    row, block, low = table[0, slot], table[1, slot], table[2, slot]
    start_row = start_ref[0:1, :]
    select = head_rows(size)
    heads = select(q_ref[...] * jnp.asarray(HEAD_DIM**-0.5, BF))

    def load(key_block):
        at = pl.multiple_of(table[3 + row, key_block] * size, size)
        return k_ref[pl.ds(at, size), :], jnp.transpose(v_ref[pl.ds(at, size), :])

    key, value_t = load(block)
    mask = key_mask(start_row, block * size, size, True)
    all_scores = [nt(pair_lanes(key, head), heads[head]) for head in range(3)]
    carry = []
    for head in range(3):
        scores = jnp.where(mask, all_scores[head], MASKED)
        top = jnp.max(scores, axis=0, keepdims=True)
        weight = jnp.exp(scores - top)
        total = jnp.sum(weight, axis=0, keepdims=True)
        acc = nn(value_t[head * HEAD_DIM : (head + 1) * HEAD_DIM], weight.astype(BF))
        carry += [top, total, acc]

    def earlier(step, carry):
        key_block = block - 1 - step
        key, value_t = load(key_block)
        mask = key_mask(start_row, key_block * size, size, False)
        all_scores = [nt(pair_lanes(key, head), heads[head]) for head in range(3)]
        new = []
        for head in range(3):
            top, total, acc = carry[3 * head : 3 * head + 3]
            scores = jnp.where(mask, all_scores[head], MASKED)
            higher = jnp.maximum(top, jnp.max(scores, axis=0, keepdims=True))
            shrink = jnp.exp(top - higher)
            weight = jnp.exp(scores - higher)
            total = total * shrink + jnp.sum(weight, axis=0, keepdims=True)
            acc = acc * shrink + nn(
                value_t[head * HEAD_DIM : (head + 1) * HEAD_DIM], weight.astype(BF)
            )
            new += [higher, total, acc]
        return tuple(new)

    carry = lax.fori_loop(0, block - low, earlier, tuple(carry))
    parts = [carry[3 * head + 2] / carry[3 * head + 1] for head in range(3)]
    parts.append(jnp.zeros_like(parts[0]))
    out_ref[...] = jnp.transpose(jnp.concatenate(parts, axis=0)).astype(BF)
    for head in range(3):
        lse_ref[0, head : head + 1, :] = carry[3 * head] + jnp.log(carry[3 * head + 1])


def attend_forward(qkv, table, starts, size):
    width = 4 * HEAD_DIM
    shards = qkv.shape[1] // (3 * width)
    tokens = qkv.shape[0]
    return pl.pallas_call(
        functools.partial(attend_forward_kernel, size),
        grid_spec=pltpu.PrefetchScalarGridSpec(
            num_scalar_prefetch=1,
            grid=(shards, 6),
            in_specs=[
                pl.BlockSpec((8, size), lambda p, s, *_: (0, s)),
                pl.BlockSpec((size, width), lambda p, s, *_: (s, 3 * p)),
                pl.BlockSpec((tokens, width), lambda p, s, *_: (0, 3 * p + 1)),
                pl.BlockSpec((tokens, width), lambda p, s, *_: (0, 3 * p + 2)),
            ],
            out_specs=[
                pl.BlockSpec((size, width), lambda p, s, *_: (s, p)),
                pl.BlockSpec((1, 8, size), lambda p, s, *_: (p, 0, s)),
            ],
        ),
        out_shape=[
            jax.ShapeDtypeStruct((6 * size, shards * width), BF),
            jax.ShapeDtypeStruct((shards, 8, 6 * size), F32),
        ],
        compiler_params=params(),
        cost_estimate=SMALL_COST,
        name="attend_forward",
    )(table, starts, qkv, qkv, qkv)


def attend_backward_kernel(
    size, table, start_ref, q_ref, k_ref, v_ref, out_ref, grad_ref, lse_ref,
    d_ref, sum_ref, dk_acc, dv_acc,
):
    slot = pl.program_id(0)
    width = 4 * HEAD_DIM
    row, block, low = table[0, slot], table[1, slot], table[2, slot]
    start_row = start_ref[0:1, :]
    select = head_rows(size)
    q_heads = select(q_ref[...] * jnp.asarray(HEAD_DIM**-0.5, BF))
    grad = grad_ref[...]
    g_heads = select(grad)
    products = jnp.transpose(grad.astype(F32) * out_ref[...].astype(F32))
    deltas = [
        jnp.sum(products[head * HEAD_DIM : (head + 1) * HEAD_DIM], axis=0, keepdims=True)
        for head in range(3)
    ]

    @pl.when(slot == 0)
    def _():
        dk_acc[...] = jnp.zeros_like(dk_acc)
        dv_acc[...] = jnp.zeros_like(dv_acc)
        sum_ref[...] = jnp.zeros_like(sum_ref)

    def one_block(key_block, diagonal):
        at = pl.multiple_of(table[3 + row, key_block] * size, size)
        key, value = k_ref[pl.ds(at, size), :], v_ref[pl.ds(at, size), :]
        key_t = jnp.transpose(key)
        mask = key_mask(start_row, key_block * size, size, diagonal)
        all_scores = [nt(pair_lanes(key, head), q_heads[head]) for head in range(3)]
        all_grads = [nt(pair_lanes(value, head), g_heads[head]) for head in range(3)]
        dq_parts, dk_parts, dv_parts = [], [], []
        for head in range(3):
            scores = jnp.where(mask, all_scores[head], MASKED)
            prob = jnp.exp(scores - lse_ref[0, head : head + 1, :])
            score_grad = (prob * (all_grads[head] - deltas[head])).astype(BF)
            dk_parts.append(nn(score_grad, q_heads[head]))
            dv_parts.append(nn(prob.astype(BF), g_heads[head]))
            dq_parts.append(nn(key_t[head * HEAD_DIM : (head + 1) * HEAD_DIM], score_grad))
        dk_acc[pl.ds(at, size), : width // 2] += dk_parts[0] + dk_parts[1]
        dk_acc[pl.ds(at, size), width // 2 :] += dk_parts[2]
        dv_acc[pl.ds(at, size), : width // 2] += dv_parts[0] + dv_parts[1]
        dv_acc[pl.ds(at, size), width // 2 :] += dv_parts[2]
        return jnp.concatenate(dq_parts, axis=0)

    dq_t = one_block(block, True)
    dq_t = lax.fori_loop(
        0, block - low, lambda step, acc: acc + one_block(block - 1 - step, False), dq_t
    )
    dq_t = jnp.concatenate([dq_t, jnp.zeros((HEAD_DIM, size), F32)], axis=0)
    dq = (jnp.transpose(dq_t) * HEAD_DIM**-0.5).astype(BF)
    d_ref[pl.ds(pl.multiple_of(slot * size, size), size), :width] = dq
    sum_ref[0:1, :] += jnp.sum(dq.astype(F32), axis=0, keepdims=True)

    @pl.when(slot == pl.num_programs(0) - 1)
    def _():
        d_ref[6 * size :, :width] = jnp.zeros((2 * size, width), BF)
        d_ref[:, width : 2 * width] = dk_acc[...].astype(BF)
        dv = dv_acc[...].astype(BF)
        d_ref[:, 2 * width :] = dv
        sum_ref[1:2, :] = jnp.sum(dv.astype(F32), axis=0, keepdims=True)


def attend_backward(qkv, attended, grad, lse, table, starts, size, shard):
    tokens = qkv.shape[0]
    width = 4 * HEAD_DIM
    block = pl.BlockSpec((size, width), lambda s, *_: (s, shard))
    return pl.pallas_call(
        functools.partial(attend_backward_kernel, size),
        grid_spec=pltpu.PrefetchScalarGridSpec(
            num_scalar_prefetch=1,
            grid=(6,),
            in_specs=[
                pl.BlockSpec((8, size), lambda s, *_: (0, s)),
                pl.BlockSpec((size, width), lambda s, *_: (s, 3 * shard)),
                pl.BlockSpec((tokens, width), lambda s, *_: (0, 3 * shard + 1)),
                pl.BlockSpec((tokens, width), lambda s, *_: (0, 3 * shard + 2)),
                block,
                block,
                pl.BlockSpec((1, 8, size), lambda s, *_: (shard, 0, s)),
            ],
            out_specs=[
                pl.BlockSpec((tokens, 3 * width), lambda s, *_: (0, 0)),
                pl.BlockSpec((8, width), lambda s, *_: (0, 0)),
            ],
            scratch_shapes=[pltpu.VMEM((tokens, width), F32), pltpu.VMEM((tokens, width), F32)],
        ),
        out_shape=[
            jax.ShapeDtypeStruct((tokens, 3 * width), BF),
            jax.ShapeDtypeStruct((8, width), F32),
        ],
        compiler_params=params(),
        cost_estimate=SMALL_COST,
        name="attend_backward",
    )(table, starts, qkv, qkv, qkv, attended, grad, lse)


GELU_C = 0.7978845608028654
GELU_A = 0.044715


def mlp_kernel(
    x_ref, own_ref, other_ref, bg_ref, vec_ref, upb_ref, up_own, up_far, dn_own, dn_far,
    res_ref, mid_ref, act_ref, hg_ref, out_ref, give_ref, midin_ref, upbg_ref,
):
    step = pl.program_id(0)
    proj_bias, gain, shift = vec_ref[0:1, :], vec_ref[1:2, :], vec_ref[2:3, :]
    residual = (
        x_ref[...].astype(F32) + own_ref[...].astype(F32) + other_ref[...].astype(F32) + proj_bias
    )
    res_ref[...] = residual
    centered = residual - jnp.mean(residual, axis=-1, keepdims=True)
    variance = jnp.mean(centered * centered, axis=-1, keepdims=True)
    mid = (centered * lax.rsqrt(variance + NORM_EPS) * gain + shift).astype(BF)
    mid_ref[...] = mid
    bg = bg_ref[...]

    @pl.when(step == 0)
    def _():
        upbg_ref[...] = jnp.zeros_like(upbg_ref)

    out = None
    midin = None
    for part, (up_w, dn_w) in enumerate(((up_own[...], dn_own[...]), (up_far[0], dn_far[0]))):
        hidden = nn(mid, up_w) + upb_ref[part : part + 1, :]
        act_grad = nt(bg, dn_w)
        square = hidden * hidden
        bent = jnp.tanh(GELU_C * (hidden + GELU_A * hidden * square))
        half = 0.5 * (1.0 + bent)
        act = (hidden * half).astype(BF)
        slope = half + 0.5 * hidden * (1.0 - bent * bent) * (GELU_C + 3.0 * GELU_C * GELU_A * square)
        grad = (act_grad * slope).astype(BF)
        act_ref[part] = act
        hg_ref[part] = grad
        upbg_ref[part : part + 1, :] += jnp.sum(grad.astype(F32), axis=0, keepdims=True)
        out_part = nn(act, dn_w)
        midin_part = nt(grad, up_w)
        out = out_part if out is None else out + out_part
        midin = midin_part if midin is None else midin + midin_part
    midin_ref[...] = midin.astype(BF)

    @pl.when(step < 3)
    def _():
        out_ref[...] = out + residual + vec_ref[3:4, :]

    @pl.when(step >= 3)
    def _():
        give_ref[...] = out.astype(BF)


def mlp(tokens, own, other, bg, vectors, up_bias, up_own, down_own, far, size):
    rows, width = own.shape
    inner = up_own.shape[1]
    block = pl.BlockSpec((size, width), lambda i: (own_first(i), 0))
    wide = pl.BlockSpec((2, size, inner), lambda i: (0, own_first(i), 0))
    return pl.pallas_call(
        mlp_kernel,
        grid=(rows // size,),
        in_specs=[
            block,
            block,
            pl.BlockSpec((size, width), lambda i: (swapped_slot(own_first(i)), 0)),
            block,
            fixed((8, width)),
            fixed((8, inner)),
            fixed((width, inner)),
            pl.BlockSpec((1, width, inner), lambda i: (0, 0, 0), pipeline_mode=pl.Buffered(1)),
            fixed((inner, width)),
            pl.BlockSpec((1, inner, width), lambda i: (1, 0, 0), pipeline_mode=pl.Buffered(1)),
        ],
        out_specs=[
            block, block, wide, wide,
            pl.BlockSpec((size, width), lambda i: (jnp.minimum(i, 2), 0)),
            pl.BlockSpec((size, width), lambda i: (jnp.maximum(i - 3, 0), 0)),
            block,
            pl.BlockSpec((8, inner), lambda i: (0, 0)),
        ],
        out_shape=[
            jax.ShapeDtypeStruct((rows, width), F32),
            jax.ShapeDtypeStruct((rows, width), BF),
            jax.ShapeDtypeStruct((2, rows, inner), BF),
            jax.ShapeDtypeStruct((2, rows, inner), BF),
            jax.ShapeDtypeStruct((rows // 2, width), F32),
            jax.ShapeDtypeStruct((rows // 2, width), BF),
            jax.ShapeDtypeStruct((rows, width), BF),
            jax.ShapeDtypeStruct((8, inner), F32),
        ],
        compiler_params=params(),
        cost_estimate=SMALL_COST,
        name="mlp",
    )(tokens, own, other, bg, vectors, up_bias, up_own, far, down_own, far)


def mid_backward_kernel(
    res_ref, own_ref, other_ref, bg_ref, vec_ref, proj_ref, rg_ref, ag_ref, atg_ref, sum_ref
):
    step = pl.program_id(0)
    gain = vec_ref[1:2, :]
    residual = res_ref[...]
    centered = residual - jnp.mean(residual, axis=-1, keepdims=True)
    rstd = lax.rsqrt(jnp.mean(centered * centered, axis=-1, keepdims=True) + NORM_EPS)
    xhat = centered * rstd
    mid_in = own_ref[...].astype(F32) + other_ref[...].astype(F32)
    gy = mid_in * gain
    through = rstd * (
        gy
        - jnp.mean(gy, axis=-1, keepdims=True)
        - xhat * jnp.mean(gy * xhat, axis=-1, keepdims=True)
    )
    total = bg_ref[...].astype(F32) + through
    low = total.astype(BF)
    ag_ref[...] = low
    atg_ref[...] = nt(low, proj_ref[...]).astype(BF)

    @pl.when(step < 3)
    def _():
        rg_ref[...] = total

    @pl.when(step == 0)
    def _():
        sum_ref[...] = jnp.zeros_like(sum_ref)

    sum_ref[0:1, :] += jnp.sum(mid_in * xhat, axis=0, keepdims=True)
    sum_ref[1:2, :] += jnp.sum(mid_in, axis=0, keepdims=True)
    sum_ref[2:3, :] += jnp.sum(low.astype(F32), axis=0, keepdims=True)
    sum_ref[3:4, :] += jnp.sum(bg_ref[...].astype(F32), axis=0, keepdims=True)


def mid_backward(residual, own, other, bg, vectors, proj, size):
    rows, width = own.shape
    inner = proj.shape[0]
    block = pl.BlockSpec((size, width), lambda i: (own_first(i), 0))
    return pl.pallas_call(
        mid_backward_kernel,
        grid=(rows // size,),
        in_specs=[
            block,
            block,
            pl.BlockSpec((size, width), lambda i: (swapped_slot(own_first(i)), 0)),
            block,
            fixed((8, width)),
            fixed((inner, width)),
        ],
        out_specs=[
            pl.BlockSpec((size, width), lambda i: (jnp.minimum(i, 2), 0)),
            block,
            pl.BlockSpec((size, inner), lambda i: (own_first(i), 0)),
            pl.BlockSpec((8, width), lambda i: (0, 0)),
        ],
        out_shape=[
            jax.ShapeDtypeStruct((rows // 2, width), F32),
            jax.ShapeDtypeStruct((rows, width), BF),
            jax.ShapeDtypeStruct((rows, inner), BF),
            jax.ShapeDtypeStruct((8, width), F32),
        ],
        compiler_params=params(),
        cost_estimate=SMALL_COST,
        name="mid_backward",
    )(residual, own, other, bg, vectors, proj)


def first_kernel(x_ref, vec_ref, far_ref, own_ref, bias_ref, normed_ref, qkv_ref):
    stream = x_ref[...].astype(F32)
    centered = stream - jnp.mean(stream, axis=-1, keepdims=True)
    variance = jnp.mean(centered * centered, axis=-1, keepdims=True)
    normed = (
        centered * lax.rsqrt(variance + NORM_EPS) * vec_ref[4:5, :] + vec_ref[5:6, :]
    ).astype(BF)
    normed_ref[...] = normed
    lanes = 4 * HEAD_DIM
    feats = far_ref.shape[0] // 3
    for shard, w_ref in enumerate((far_ref, own_ref)):
        for i in range(3):
            at = (3 * shard + i) * lanes
            part = nt(normed, w_ref[i * feats : (i + 1) * feats]) + bias_ref[
                3 * shard + i : 3 * shard + i + 1, :feats
            ]
            qkv_ref[:, at : at + feats] = part.astype(BF)
            qkv_ref[:, at + feats : at + lanes] = jnp.zeros((part.shape[0], lanes - feats), BF)


def first(tokens, vectors, far, own, bias, size):
    rows, width = tokens.shape
    outs = 6 * 4 * HEAD_DIM
    block = pl.BlockSpec((size, width), lambda i: (i, 0))
    return pl.pallas_call(
        first_kernel,
        grid=(rows // size,),
        in_specs=[block, fixed((8, width)), fixed(far.shape), fixed(own.shape), fixed(bias.shape)],
        out_specs=[block, pl.BlockSpec((size, outs), lambda i: (i, 0))],
        out_shape=[
            jax.ShapeDtypeStruct((rows, width), BF),
            jax.ShapeDtypeStruct((rows, outs), BF),
        ],
        compiler_params=params(),
        cost_estimate=SMALL_COST,
        name="first_norm_qkv",
    )(tokens, vectors, far, own, bias)


def first_in_kernel(far_d, own_d, far_w, own_w, own_ref, give_ref):
    step = pl.program_id(0)
    half = far_d.shape[0] // 2
    lanes = 4 * HEAD_DIM
    feats = far_w.shape[0] // 3
    total = None
    for d_ref, w_ref in ((far_d, far_w), (own_d, own_w)):
        for i in range(3):
            part = nn(d_ref[:, i * lanes : i * lanes + feats], w_ref[i * feats : (i + 1) * feats])
            total = part if total is None else total + part
    total = total.astype(BF)

    @pl.when(step == 0)
    def _():
        own_ref[: 2 * half] = total

    @pl.when(step == 1)
    def _():
        give_ref[: 2 * half] = total

    @pl.when(step == 2)
    def _():
        own_ref[2 * half : 3 * half] = total[:half]
        give_ref[2 * half : 3 * half] = total[half:]

    @pl.when(step == 3)
    def _():
        own_ref[3 * half :] = total[:half]
        give_ref[3 * half :] = total[half:]


def first_in(far_grad, own_grad, far, own, size):
    rows, lanes = far_grad.shape
    width = far.shape[1]
    block = pl.BlockSpec((2 * size, lanes), lambda i: (i, 0))
    whole = pl.BlockSpec((rows // 2, width), lambda i: (0, 0))
    return pl.pallas_call(
        first_in_kernel,
        grid=(4,),
        in_specs=[block, block, fixed(far.shape), fixed(own.shape)],
        out_specs=[whole, whole],
        out_shape=[jax.ShapeDtypeStruct((rows // 2, width), BF)] * 2,
        compiler_params=params(),
        cost_estimate=SMALL_COST,
        name="first_in",
    )(far_grad, own_grad, far, own)


def first_backward_kernel(x_ref, own_ref, got_ref, rg_ref, vec_ref, *refs):
    extra_ref, (in_ref, sum_ref) = (refs[0] if len(refs) == 3 else None), refs[-2:]
    stream = x_ref[...].astype(F32)
    centered = stream - jnp.mean(stream, axis=-1, keepdims=True)
    rstd = lax.rsqrt(jnp.mean(centered * centered, axis=-1, keepdims=True) + NORM_EPS)
    xhat = centered * rstd
    grad = own_ref[...].astype(F32) + got_ref[...].astype(F32)
    if extra_ref is not None:
        grad = grad + extra_ref[...].astype(F32)
    gy = grad * vec_ref[4:5, :]
    through = rstd * (
        gy
        - jnp.mean(gy, axis=-1, keepdims=True)
        - xhat * jnp.mean(gy * xhat, axis=-1, keepdims=True)
    )
    in_ref[...] = (rg_ref[...] + through).astype(BF)

    @pl.when(pl.program_id(0) == 0)
    def _():
        sum_ref[...] = jnp.zeros_like(sum_ref)

    sum_ref[0:1, :] += jnp.sum(grad * xhat, axis=0, keepdims=True)
    sum_ref[1:2, :] += jnp.sum(grad, axis=0, keepdims=True)


def first_backward(tokens, own, got, residual_grad, vectors, extra, size, owned):
    width = tokens.shape[1]
    stride = owned[1] - owned[0] if len(owned) > 1 else 1
    block = pl.BlockSpec((size, width), lambda i: (owned[0] + stride * i, 0))
    slot = pl.BlockSpec((size, width), lambda i: (owned[0] + 2 * stride * i, 0))
    more = () if extra is None else (extra,)
    return pl.pallas_call(
        first_backward_kernel,
        grid=(len(owned),),
        in_specs=[slot, block, block, block, fixed((8, width))]
        + [pl.BlockSpec((size, width), lambda i: (0, 0))] * len(more),
        out_specs=[
            pl.BlockSpec((size, width), lambda i: (i, 0)),
            pl.BlockSpec((8, width), lambda i: (0, 0)),
        ],
        out_shape=[
            jax.ShapeDtypeStruct((len(owned) * size, width), BF),
            jax.ShapeDtypeStruct((8, width), F32),
        ],
        compiler_params=params(),
        cost_estimate=SMALL_COST,
        name="first_backward",
    )(tokens, own, got, residual_grad, vectors, *more)


def dp_partners(count, bit):
    return [(d, d ^ bit) for d in range(count)]


def dp_bits():
    return [1 << i for i in range(lax.axis_size("dp").bit_length() - 1)]


def dp_swap(value, bit):
    return lax.ppermute(value, "dp", dp_partners(lax.axis_size("dp"), bit))


def upper(bit):
    return (lax.axis_index("dp") & bit) != 0


def keep_and_give(value, side, rows):
    keep = lax.dynamic_slice_in_dim(value, side * rows, rows, 0)
    give = lax.dynamic_slice_in_dim(value, (1 - side) * rows, rows, 0)
    return keep, give


def halve(value, bit):
    keep, give = keep_and_give(value, jnp.where(upper(bit), 1, 0), value.shape[0] // 2)
    return keep.astype(F32) + dp_swap(give.astype(BF), bit).astype(F32)


def double(value, bit, axis=0):
    got = dp_swap(value, bit)
    return jnp.where(
        upper(bit),
        jnp.concatenate([got, value], axis=axis),
        jnp.concatenate([value, got], axis=axis),
    )


def dp_part(value, axis):
    bits = dp_bits()
    place = sum(jnp.where(upper(bit), value.shape[axis] // (2 * bit), 0) for bit in bits)
    return lax.dynamic_slice_in_dim(value, place, value.shape[axis] // (2 * bits[-1]), axis)


def sum_everywhere(value):
    value = value + core_swap(value)
    value = value + x_swap(value)
    for bit in dp_bits():
        value = value + dp_swap(value, bit)
    return value


def after(value, *earlier):
    return lax.optimization_barrier((value,) + earlier)[0]


def body(
    hidden_in,
    doc_ids,
    first_gain,
    first_shift,
    qkv_weight,
    qv_bias,
    proj_weight,
    proj_bias,
    second_gain,
    second_shift,
    up_weight,
    up_bias,
    down_weight,
    down_bias,
    out_grad,
):
    size, rows_dev, width = hidden_in.shape
    length = doc_ids.shape[0]
    place = lax.axis_index("tensor")
    right = place >= 2
    feats = qkv_weight.shape[2]
    inner = up_weight.shape[1]

    def split_rows(value):
        first, mid, last = value[:, 0], value[:, 1], value[:, 2]
        return jnp.where(right, last, first), mid, jnp.where(right, first, last)

    def join_rows(main, mid, other):
        return jnp.stack(
            [jnp.where(right, other, main), mid, jnp.where(right, main, other)], axis=1
        )

    pieces = jnp.stack([dp_part(up_weight, 0), dp_part(down_weight, 0)])
    with jax.named_scope("mlp_weights_x"):
        far_mlp = x_swap(pieces)

    main, mid, away = split_rows(hidden_in)
    home = jnp.concatenate([main, mid], axis=0)
    with jax.named_scope("tokens"):
        far = x_swap(jnp.concatenate([away, mid], axis=0))
        near = core_swap(home)
        far_near = core_swap(far)
    tokens = jnp.concatenate(
        [home, near, far[:size], far_near[:size], far[size:], far_near[size:]], axis=0
    )

    qkv_own = jnp.transpose(qkv_weight, (1, 2, 0)).reshape(3 * feats, width)
    biases = jnp.concatenate([qv_bias, up_bias.reshape(-1, feats)], axis=0)
    with jax.named_scope("qkv_weights_x"):
        qkv_far = x_swap(qkv_own)
        biases_far = x_swap(biases)
    with jax.named_scope("proj_weight_x"):
        proj_far = x_swap(proj_weight)
    with jax.named_scope("mlp_weights_dp"):
        for bit in reversed(dp_bits()[1:]):
            far_mlp = double(far_mlp, bit, 1)
        part_mlp = far_mlp
        far_mlp = double(far_mlp, dp_bits()[0], 1)

    local_ids = lax.dynamic_slice_in_dim(doc_ids, place * size, size, 0)
    cot = jnp.where((local_ids >= 0)[:, :, None], out_grad, jnp.zeros_like(out_grad))
    g_main, g_mid, g_away = split_rows(cot)
    g_home = jnp.concatenate([g_main, g_mid], axis=0)
    with jax.named_scope("cotangent"):
        g_near = core_swap(g_home)
        g_far = x_swap(g_away)
        g_far_near = core_swap(g_far)
    branch_grad = jnp.concatenate([g_home, g_near, g_far, g_far_near], axis=0)

    ids = jnp.stack([jnp.where(right, doc_ids[:, 2], doc_ids[:, 0]), doc_ids[:, 1]])
    position = lax.broadcasted_iota(jnp.int32, ids.shape, 1)
    count_below = jnp.stack(
        [jnp.sum(((ids >= 0) & (ids < d)).astype(jnp.int32), axis=1) for d in range(8)], axis=1
    )
    which = ids[:, :, None] == jnp.arange(8, dtype=jnp.int32)[None, None, :]
    starts = jnp.sum(jnp.where(which, count_below[:, None, :], 0), axis=2)
    starts = jnp.where(ids >= 0, starts, position).reshape(2, length // size, size)
    slot_row = jnp.array(SLOT_ROW, jnp.int32)
    slot_block = jnp.array(SLOT_K, jnp.int32) ^ place
    slot_start = starts.reshape(-1, size)[slot_row * (length // size) + slot_block]
    low_block = slot_start[:, 0] // size
    where_key = jnp.array(SLOT, jnp.int32)[:, jnp.arange(4, dtype=jnp.int32) ^ place]
    table = jnp.concatenate(
        [
            jnp.pad(jnp.stack([slot_row, slot_block, low_block]), ((0, 0), (0, 2))),
            jnp.pad(where_key, ((0, 0), (0, 4))),
        ]
    )
    start_rows = jnp.broadcast_to(slot_start.reshape(1, -1), (8, 6 * size))

    vectors = jnp.stack(
        [proj_bias, second_gain, second_shift, down_bias, first_gain, first_shift]
        + [jnp.zeros_like(proj_bias)] * 2
    ).astype(F32)
    up_biases = jnp.stack(
        [up_bias, biases_far[2:].reshape(-1)] + [jnp.zeros_like(up_bias)] * 6
    ).astype(F32)

    none = jnp.zeros((1, feats), qv_bias.dtype)
    qkv_bias = jnp.concatenate(
        [biases_far[:1], none, biases_far[1:2], qv_bias[:1], none, qv_bias[1:], none, none]
    ).astype(F32)
    normed, qkv = first(tokens, vectors, qkv_far, qkv_own, qkv_bias, 2 * size)

    attended, lse = attend_forward(after(qkv, part_mlp), table, start_rows, size)
    gap = jnp.zeros((4 * HEAD_DIM - feats, width), BF)
    proj_both = jnp.concatenate([proj_far, gap, proj_weight, gap], axis=0)
    attn_part = nn(after(attended, g_far, far_mlp), proj_both).astype(BF)
    with jax.named_scope("attn_core"):
        attn_other = core_swap(attn_part)

    residual, normed_mid, act, hidden_grad, out_own, out_give, mid_part, up_sums = mlp(
        tokens, attn_part, attn_other, branch_grad, vectors, up_biases,
        up_weight, down_weight, far_mlp, size,
    )

    lanes = 4 * HEAD_DIM
    bit_y, bits_z = dp_bits()[0], dp_bits()[1:]

    def shard_rows(value):
        return jnp.concatenate([value[i * lanes : i * lanes + feats] for i in range(3)], axis=0)

    with jax.named_scope("mid_core"):
        mid_other = core_swap(mid_part)
    down_away = tn(act[1], branch_grad).astype(BF)
    with jax.named_scope("down_grad_x"):
        down_got = x_swap(down_away)
    residual_grad, attn_grad, attended_grad, mid_sums = mid_backward(
        after(residual, down_away), mid_part, mid_other, branch_grad, vectors, proj_both, size
    )

    act, hidden_grad, out_own, out_give, attended_grad = lax.optimization_barrier(
        (act, hidden_grad, out_own, out_give, attended_grad)
    )
    up_away = tn(normed_mid, hidden_grad[1]).astype(BF)
    with jax.named_scope("up_grad_x"):
        up_got = x_swap(up_away)
    d_far, sums_far = attend_backward(
        qkv, attended, after(attended_grad, up_away), lse, table, start_rows, size, 0
    )
    qkv_away = shard_rows(tn(d_far, normed)).astype(BF)
    with jax.named_scope("down_grad_dp"):
        down = tn(act[0], after(branch_grad, qkv_away)) + down_got.astype(F32)
    with jax.named_scope("qkv_grad_x"):
        qkv_got = x_swap(qkv_away)
    d_own, sums_own = attend_backward(
        qkv, attended, after(attended_grad, down), lse, table, start_rows, size, 1
    )
    with jax.named_scope("down_grad_dp"):
        down = halve(down, bit_y)
    act, hidden_grad, attended, attn_grad, d_own, down, out_give = lax.optimization_barrier(
        (act, hidden_grad, attended, attn_grad, d_own, down, out_give)
    )

    own_in, give_in = first_in(d_far, d_own, qkv_far, qkv_own, size)
    with jax.named_scope("first_core"):
        got_in = core_swap(give_in)
    with jax.named_scope("block_out"):
        out_got = core_swap(out_give)
    proj_pair = tn(attended, attn_grad)
    with jax.named_scope("proj_grad_x"):
        proj_got = x_swap(proj_pair[:feats].astype(BF))
    with jax.named_scope("up_grad_dp"):
        up = tn(normed_mid, hidden_grad[0]) + up_got.astype(F32)
    with jax.named_scope("qkv_grad_dp"):
        qkv_sum = shard_rows(tn(d_own, normed)) + qkv_got.astype(F32)
        tail = jnp.concatenate(
            [qkv_sum, proj_pair[lanes : lanes + feats] + proj_got.astype(F32)], axis=0
        )
    with jax.named_scope("first_mid_x"):
        extra = x_swap(
            (own_in[3 * size :].astype(F32) + got_in[3 * size :].astype(F32)).astype(BF)
        )
    in_main, sums_main = first_backward(
        tokens, own_in, got_in, residual_grad, vectors, None, size, (0, 2)
    )
    in_mid, sums_mid = first_backward(
        tokens, own_in, got_in, residual_grad, vectors, extra, size, (1,)
    )
    with jax.named_scope("in_grad_x"):
        in_away = x_swap(in_main[size:])
    with jax.named_scope("block_out"):
        out_full = (out_own + out_got.astype(F32)).astype(BF)
        out_away = x_swap(out_full[2 * size :])

    sums = [down, up, tail]
    stages = [1, 0, 0]
    steps = [functools.partial(halve, bit=bit) for bit in dp_bits()]
    steps += [functools.partial(double, bit=bit) for bit in reversed(dp_bits())]
    names = ("down_grad_dp", "up_grad_dp", "tail_grad_dp")
    started = 1
    while min(stages) < len(steps):
        started = min(started + 1, 3)
        for i in range(started):
            if stages[i] < len(steps):
                value = sums[i]
                if stages[i] == len(steps) // 2:
                    value = value.astype(BF)
                with jax.named_scope(names[i]):
                    sums[i] = steps[stages[i]](value)
                stages[i] += 1
        sums = list(lax.optimization_barrier(tuple(sums)))
    down_sum, up_sum, tail_sum = sums

    block_out = join_rows(out_full[:size], out_full[size : 2 * size], out_away)
    in_grad = join_rows(in_main[:size], in_mid, in_away)

    up_slots = jnp.zeros((4, inner), F32)
    up_slots = lax.dynamic_update_slice_in_dim(up_slots, up_sums[0:1], place, 0)
    up_slots = lax.dynamic_update_slice_in_dim(up_slots, up_sums[1:2], place ^ 2, 0)
    qv_own = sums_own[:2, :feats].reshape(1, -1)
    qv_far = sums_far[:2, :feats].reshape(1, -1)
    qv_slots = jnp.zeros((4, 2 * feats), F32)
    qv_slots = lax.dynamic_update_slice_in_dim(qv_slots, qv_own, place, 0)
    qv_slots = lax.dynamic_update_slice_in_dim(qv_slots, qv_far, place ^ 2, 0)
    small = jnp.concatenate(
        [
            (sums_main + sums_mid)[:2],
            0.5 * mid_sums[:4],
            up_slots,
            qv_slots.reshape(-1, width),
        ],
        axis=0,
    )
    with jax.named_scope("small_sums"):
        small = sum_everywhere(small)
    up_bias_grad = lax.dynamic_slice_in_dim(small, 6 + place, 1, 0)[0]
    qv_all = small[10:].reshape(4, 2, feats)
    qv_bias_grad = lax.dynamic_slice_in_dim(qv_all, place, 1, 0)[0]

    qkv_weight_grad = jnp.transpose(
        tail_sum[: 3 * feats].reshape(3, feats, width), (2, 0, 1)
    ).astype(F32)
    return (
        block_out,
        in_grad,
        small[0],
        small[1],
        qkv_weight_grad,
        qv_bias_grad,
        tail_sum[3 * feats :].astype(F32),
        small[4],
        small[2],
        small[3],
        up_sum.astype(F32),
        up_bias_grad,
        down_sum.astype(F32),
        small[5],
    )


def solution(mesh):
    in_specs = (
        P("tensor", "dp", None),
        P(None, "dp"),
        P(),
        P(),
        P(None, None, "tensor"),
        P(None, "tensor"),
        P("tensor", None),
        P(),
        P(),
        P(),
        P(None, "tensor"),
        P("tensor"),
        P("tensor", None),
        P(),
        P("tensor", "dp", None),
    )
    out_specs = (
        P("tensor", "dp", None),
        P("tensor", "dp", None),
        P(),
        P(),
        P(None, None, "tensor"),
        P(None, "tensor"),
        P("tensor", None),
        P(),
        P(),
        P(),
        P(None, "tensor"),
        P("tensor"),
        P("tensor", None),
        P(),
    )
    return jax.shard_map(body, mesh=mesh, in_specs=in_specs, out_specs=out_specs, check_vma=False)
```

profile of v0, /device:TPU:8, one launch (start us, length us, event | category | flops | bytes accessed | tf_op | source)
XLA Modules:
  0.0 381.7 jit_solution(12758723369171913791)
XLA Ops:
  2.9 1.5 collective-permute-start.4
  6.0 1.5 collective-permute-start.10
  16.2 2.7 collective-permute-start.6
  18.8 13.4 %collective-permute-done.6 = bf16[2,96,768]{2,1,0:T(8,128)(2,1)S(1)} collective-permute-done((bf16[2,96,768]{2,1,0:T(8,128)(2,1)}, bf16[2,96,768]{2,1,0:T(8,128)(2,1)S(1)}, u32[]{:S(2)}, u32[]{:S(2)}) %collective-permute-start.6) | collective-permute-done | bytes 294944 | tf_op jit(solution)/shard_map/mlp_weights_dp/ppermute | solution.py:578
  32.3 2.1 maximum_select_fusion.5
  36.2 2.0 slice_bitcast_fusion.1
  48.5 1.5 collective-permute-done.7
  50.0 1.5 collective-permute-start.3
  51.5 2.9 maximum_select_fusion.1
  54.4 1.5 collective-permute-start.9
  65.0 7.8 %collective-permute-done.3.far_ref.far_w = bf16[576,768]{1,0:T(8,128)(2,1)} collective-permute-done((bf16[576,768]{1,0:T(8,128)(2,1)}, bf16[576,768]{1,0:T(8,128)(2,1)}, u32[]{:S(2)}, u32[]{:S(2)}) %collective-permute-start.3) | collective-permute-done | bytes 884768 | tf_op jit(solution)/shard_map/qkv_weights_x/ppermute | solution.py:25
  72.9 10.1 %first_norm_qkv.1 = (bf16[2048,768]{1,0:T(8,128)(2,1)}, bf16[2048,1536]{1,0:T(8,128)(2,1)}) custom-call(bf16[2048,768]{1,0:T(8,128)(2,1)} %copy-done, f32[8,768]{1,0:T(8,128)} %convert_element_type.160.vec_ref, bf16[576,768]{1,0:T(8,128)(2,1)} %collective-permute-done.3.far_ref.far_w, bf16[576,768]{1,0:T(8,128)(2,1)} %bitcast.100, ...), custom_call_target="tpu_custom_call" | custom-call | flops 1 | bytes 1 | tf_op jit(solution)/shard_map/first_norm_qkv/pallas_call | solution.py:456
  83.6 17.0 %attend_forward.1 = (bf16[1536,512]{1,0:T(8,128)(2,1)}, f32[2,8,1536]{2,1,0:T(8,128)}) custom-call(s32[5,8]{1,0:T(8,128)} %pad_add_fusion.1.table, s32[8,1536]{1,0:T(8,128)} %broadcast_in_dim.54.start_ref, bf16[2048,1536]{1,0:T(8,128)(2,1)} %get-tuple-element.79.q_ref.k_ref.v_ref, bf16[2048,1536]{1,0:T(8,128)(2,1)} %get-tuple-element.79.q_ref.k_ref.v_ref, ...), custom_call_target="tpu_custom_call" | custom-call | flops 1 | bytes 1 | tf_op jit(solution)/shard_map/attend_forward/pallas_call | solution.py:145
  100.6 4.0 %maximum_select_fusion.up_far.dn_far = bf16[2,768,768]{2,1,0:T(8,128)(2,1)} fusion(bf16[2,384,768]{2,1,0:T(8,128)(2,1)} %maximum_select_fusion.1, bf16[2,384,768]{2,1,0:T(8,128)(2,1)} %collective-permute-done.9, pred[]{:T(512)S(6)} %ne.64), kind=kLoop, calls=%fused_computation.3 | loop fusion | flops 10616832 | bytes 4718593 | tf_op jit(solution)/shard_map/mlp_weights_dp/jit(_where)/select_n | solution.py:598
  104.6 2.5 convolution_convert_fusion.own_ref
  109.3 1.8 constant_dynamic-update-slice_fusion.6
  115.8 25.4 %mlp.1 = (f32[1536,768]{1,0:T(8,128)}, bf16[1536,768]{1,0:T(8,128)(2,1)}, bf16[2,1536,768]{2,1,0:T(8,128)(2,1)}, bf16[2,1536,768]{2,1,0:T(8,128)(2,1)}, f32[768,...) custom-call(bf16[2048,768]{1,0:T(8,128)(2,1)} %copy-done, ...), custom_call_target="tpu_custom_call" | custom-call | flops 1 | bytes 1 | tf_op jit(solution)/shard_map/mlp/pallas_call | solution.py:326
  141.6 1.9 pad_maximum_fusion.6.proj_ref
  143.5 4.4 %fusion.16 = bf16[768,768]{1,0:T(8,128)(2,1)S(1)} fusion(bf16[1536,768]{1,0:T(8,128)(2,1)} %constant_dynamic-update-slice_fusion.3.bg_ref, bf16[2,1536,768]{2,1,0:T(8,128)(2,1)} %get-tuple-element.91), kind=kOutput, calls=%fused_computation.23 | convolution fusion | flops 1812529152 | bytes 5898240 | tf_op jit(solution)/shard_map/dot_general | solution.py:49
  147.9 3.7 collective-permute-start.15
  153.0 11.7 %mid_backward.1 = (f32[768,768]{1,0:T(8,128)}, bf16[1536,768]{1,0:T(8,128)(2,1)}, bf16[1536,512]{1,0:T(8,128)(2,1)}, f32[8,768]{1,0:T(8,128)}) custom-call(f32[1536,768]{1,0:T(8,128)} %get-tuple-element.87.res_ref, bf16[1536,768]{1,0:T(8,128)(2,1)} %get-tuple-element.88.own_ref, bf16[1536,768]{1,0:T(8,128)(2,1)} %copy-done.13, ...), custom_call_target="tpu_custom_call" | custom-call | flops 1 | bytes 1 | tf_op jit(solution)/shard_map/mid_backward/pallas_call | solution.py:403
  164.8 4.7 %fusion.19 = bf16[768,768]{1,0:T(8,128)(2,1)} fusion(bf16[1536,768]{1,0:T(8,128)(2,1)} %get-tuple-element.95, bf16[2,1536,768]{2,1,0:T(8,128)(2,1)S(1)} %bitcast.113), kind=kOutput, calls=%fused_computation.24 | convolution fusion | flops 1812529152 | bytes 5898240 | tf_op jit(solution)/shard_map/dot_general | solution.py:49
  169.5 14.2 %attend_backward.2 = (bf16[2048,768]{1,0:T(8,128)(2,1)}, f32[8,256]{1,0:T(8,128)}) custom-call(s32[5,8]{1,0:T(8,128)} %pad_add_fusion.1.table, s32[8,1536]{1,0:T(8,128)} %broadcast_in_dim.54.start_ref, bf16[2048,1536]{1,0:T(8,128)(2,1)} %get-tuple-element.79.q_ref.k_ref.v_ref, bf16[2048,1536]{1,0:T(8,128)(2,1)} %get-tuple-element.79.q_ref.k_ref.v_ref, ...), custom_call_target="tpu_custom_call" | custom-call | flops 1 | bytes 1 | tf_op jit(solution)/shard_map/attend_backward/pallas_call | solution.py:238
  183.7 4.7 %convolution_convert_fusion.1 = bf16[768,768]{1,0:T(8,128)(2,1)S(1)} fusion(bf16[2048,768]{1,0:T(8,128)(2,1)} %get-tuple-element.98.far_d, bf16[2048,768]{1,0:T(8,128)(2,1)S(1)} %copy-done.35), kind=kOutput, calls=%fused_computation.22 | convolution fusion | flops 2416508928 | bytes 7471104 | tf_op jit(solution)/shard_map/dot_general | solution.py:49
  188.6 4.1 %convert_add_fusion.1 = f32[768,768]{1,0:T(8,128)S(1)} fusion(bf16[768,768]{1,0:T(8,128)(2,1)} %collective-permute-done.15, bf16[1536,768]{1,0:T(8,128)(2,1)} %constant_dynamic-update-slice_fusion.3.bg_ref, bf16[2,1536,768]{2,1,0:T(8,128)(2,1)S(1)} %bitcast.117), kind=kOutput, calls=%fused_computation.16 | convolution fusion | flops 1813118976 | bytes 8257536 | tf_op jit(solution)/shard_map/down_grad_dp/dot_general | solution.py:49
  193.5 1.5 collective-permute-start.16
  195.0 1.4 collective-permute-start.28
  197.1 14.5 %attend_backward.3 = (bf16[2048,768]{1,0:T(8,128)(2,1)}, f32[8,256]{1,0:T(8,128)}) custom-call(s32[5,8]{1,0:T(8,128)} %pad_add_fusion.1.table, s32[8,1536]{1,0:T(8,128)} %broadcast_in_dim.54.start_ref, bf16[2048,1536]{1,0:T(8,128)(2,1)} %get-tuple-element.79.q_ref.k_ref.v_ref, bf16[2048,1536]{1,0:T(8,128)(2,1)} %get-tuple-element.79.q_ref.k_ref.v_ref, ...), custom_call_target="tpu_custom_call" | custom-call | flops 1 | bytes 1 | tf_op jit(solution)/shard_map/attend_backward/pallas_call | solution.py:238
  214.7 2.9 collective-permute-start.31
  217.6 2.7 fusion.41
  220.5 22.6 %collective-permute-done.30 = bf16[576,768]{1,0:T(8,128)(2,1)S(1)} collective-permute-done((bf16[576,768]{1,0:T(8,128)(2,1)S(1)}, bf16[576,768]{1,0:T(8,128)(2,1)S(1)}, u32[]{:S(2)}, u32[]{:S(2)}) %collective-permute-start.30) | collective-permute-done | bytes 884768 | tf_op jit(solution)/shard_map/qkv_grad_x/ppermute | solution.py:25
  243.3 1.5 copy-done.37
  244.8 3.4 convert_add_fusion
  249.1 11.8 %collective-permute-done.29 = bf16[384,768]{1,0:T(8,128)(2,1)S(1)} collective-permute-done((bf16[384,768]{1,0:T(8,128)(2,1)S(1)}, bf16[384,768]{1,0:T(8,128)(2,1)S(1)}, u32[]{:S(2)}, u32[]{:S(2)}) %collective-permute-start.29) | collective-permute-done | bytes 589856 | tf_op jit(solution)/shard_map/up_grad_dp/ppermute | solution.py:578
  261.0 3.3 collective-permute-start.32
  267.5 9.6 %first_in.1 = (bf16[1024,768]{1,0:T(8,128)(2,1)}, bf16[1024,768]{1,0:T(8,128)(2,1)}) custom-call(bf16[2048,768]{1,0:T(8,128)(2,1)} %get-tuple-element.98.far_d, bf16[2048,768]{1,0:T(8,128)(2,1)} %get-tuple-element.105.own_d, bf16[576,768]{1,0:T(8,128)(2,1)} %collective-permute-done.3.far_ref.far_w, bf16[576,768]{1,0:T(8,128)(2,1)} %bitcast.101), custom_call_target="tpu_custom_call" | custom-call | flops 1 | bytes 1 | tf_op jit(solution)/shard_map/first_in/pallas_call | solution.py:507
  283.3 2.6 collective-permute-start.35
  285.9 2.1 collective-permute-start.37
  288.0 3.6 collective-permute-done.36
  292.6 2.2 collective-permute-done.35
  294.9 5.8 %collective-permute-done.37 = bf16[192,768]{1,0:T(8,128)(2,1)S(1)} collective-permute-done((bf16[192,768]{1,0:T(8,128)(2,1)S(1)}, bf16[192,768]{1,0:T(8,128)(2,1)S(1)}, u32[]{:S(2)}, u32[]{:S(2)}) %collective-permute-start.37) | collective-permute-done | bytes 294944 | tf_op jit(solution)/shard_map/tail_grad_dp/ppermute | solution.py:578
  300.9 2.9 collective-permute-start.39
  303.8 1.5 add_convert_fusion.1
  305.3 2.1 collective-permute-start.21
  307.4 2.5 collective-permute-start.38
  309.9 3.2 collective-permute-done.39
  313.2 7.7 %collective-permute-done.38 = bf16[192,768]{1,0:T(8,128)(2,1)S(1)} collective-permute-done((bf16[192,768]{1,0:T(8,128)(2,1)S(1)}, bf16[192,768]{1,0:T(8,128)(2,1)S(1)}, u32[]{:S(2)}, u32[]{:S(2)}) %collective-permute-start.38) | collective-permute-done | bytes 294944 | tf_op jit(solution)/shard_map/down_grad_dp/ppermute | solution.py:578
  321.1 1.5 collective-permute-start.41
  323.4 3.7 first_backward.2
  328.2 1.7 collective-permute-start.20
  330.6 3.0 first_backward.3
  333.7 2.5 collective-permute-start.42
  337.0 4.4 %collective-permute-done.43 = bf16[96,768]{1,0:T(8,128)(2,1)S(1)} collective-permute-done((bf16[96,768]{1,0:T(8,128)(2,1)S(1)}, bf16[96,768]{1,0:T(8,128)(2,1)S(1)}, u32[]{:S(2)}, u32[]{:S(2)}) %collective-permute-start.43) | collective-permute-done | bytes 147488 | tf_op jit(solution)/shard_map/tail_grad_dp/ppermute | solution.py:578
  341.4 3.7 collective-permute-done.42
  346.8 1.7 collective-permute-start.45
  348.6 1.9 collective-permute-done.23
  350.6 1.5 collective-permute-start.24
  353.2 6.8 %collective-permute-done.24 = f32[12,768]{1,0:T(8,128)S(1)} collective-permute-done((f32[12,768]{1,0:T(8,128)S(1)}, f32[12,768]{1,0:T(8,128)S(1)}, u32[]{:S(2)}, u32[]{:S(2)}) %collective-permute-start.24) | collective-permute-done | bytes 36896 | tf_op jit(solution)/shard_map/small_sums/ppermute | solution.py:578
  360.0 2.4 collective-permute-start.25
  367.0 2.9 collective-permute-done.26
  371.2 1.7 slice_reduce_fusion.1
  372.8 2.8 collective-permute-done.46
  378.3 1.6 convert_element_type.200
  379.9 1.6 convert_element_type.201
  (288 shorter events, 74.5 us)
Async XLA Ops:
  0.7 7.6 %copy-start.15 = (bf16[256,3,768]{2,0,1:T(8,128)(2,1)S(1)}, bf16[256,3,768]{2,0,1:T(8,128)(2,1)}, u32[]{:S(2)}) copy-start(bf16[256,3,768]{2,0,1:T(8,128)(2,1)} %param.32) | copy-start | bytes 3538948
  2.9 51.5 %collective-permute-start.4 = (bf16[6,192]{1,0:T(8,128)(2,1)}, bf16[6,192]{1,0:T(8,128)(2,1)}, u32[]{:S(2)}, u32[]{:S(2)}) collective-permute-start(bf16[6,192]{1,0:T(8,128)(2,1)} %pad_maximum_fusion.10), channel_id=1, source_target_pairs={{0,2},{1,3},{2,0},{3,1},{4,6},{5,7},{6,4},{7,5},{8,10},{9,11},{10,... | collective-permute-start | bytes 6920 | tf_op jit(solution)/shard_map/qkv_weights_x/ppermute | solution.py:25
  5.4 10.8 %collective-permute-start.5 = (bf16[2,96,768]{2,1,0:T(8,128)(2,1)S(1)}, bf16[2,96,768]{2,1,0:T(8,128)(2,1)}, u32[]{:S(2)}, u32[]{:S(2)}) collective-permute-start(bf16[2,96,768]{2,1,0:T(8,128)(2,1)S(1)} %pad_maximum_fusion.8), channel_id=1, source_target_pairs={{0,2},{1,3},{2,0},{3,1},{4,6},{5,7},{6,4},{7,5},{8,10},{9,11},{10,... | collective-permute-start | bytes 884744 | tf_op jit(solution)/shard_map/mlp_weights_x/ppermute | solution.py:25
  6.0 98.6 %collective-permute-start.10 = (bf16[192,768]{1,0:T(8,128)(2,1)}, bf16[192,768]{1,0:T(8,128)(2,1)}, u32[]{:S(2)}, u32[]{:S(2)}) collective-permute-start(bf16[192,768]{1,0:T(8,128)(2,1)} %param.24), channel_id=1, source_target_pairs={{0,2},{1,3},{2,0},{3,1},{4,6},{5,7},{6,4},{7,5},{8,10},{9,11},{10,... | collective-permute-start | bytes 884744 | tf_op jit(solution)/shard_map/proj_weight_x/ppermute | solution.py:25
  12.0 23.6 %copy-start.32 = (s32[1,6]{1,0:T(1,128)S(1)}, s32[1,6]{1,0:T(1,128)}, u32[]{:S(2)}) copy-start(s32[1,6]{1,0:T(1,128)} %constant.93) | copy-start | bytes 76
  12.0 23.6 %copy-start.27 = (s32[2,4]{0,1:T(4,128)S(1)}, s32[2,4]{0,1:T(4,128)}, u32[]{:S(2)}) copy-start(s32[2,4]{0,1:T(4,128)} %constant.26.clone) | copy-start | bytes 100
  12.0 26.3 %collective-permute-start.1 = (bf16[512,768]{1,0:T(8,128)(2,1)}, bf16[512,768]{1,0:T(8,128)(2,1)}, u32[]{:S(2)}, u32[]{:S(2)}) collective-permute-start(bf16[512,768]{1,0:T(8,128)(2,1)} %get-tuple-element.176), channel_id=1, source_target_pairs={{0,2},{1,3},{2,0},{3,1},{4,6},{5,7},{6,4},{7,5},{8,10},{9,11},{10,... | collective-permute-start | bytes 2359304 | tf_op jit(solution)/shard_map/tokens/ppermute | solution.py:25
  12.5 46.7 %collective-permute-start = (bf16[512,768]{1,0:T(8,128)(2,1)}, bf16[512,768]{1,0:T(8,128)(2,1)}, u32[]{:S(2)}, u32[]{:S(2)}) collective-permute-start(bf16[512,768]{1,0:T(8,128)(2,1)} %get-tuple-element.177), channel_id=1, source_target_pairs={{0,1},{1,0},{2,3},{3,2},{4,5},{5,4},{6,7},{7,6},{8,9},{9,8},{10,11... | collective-permute-start | bytes 2359304 | tf_op jit(solution)/shard_map/tokens/ppermute | solution.py:29
  16.2 16.1 %collective-permute-start.6 = (bf16[2,96,768]{2,1,0:T(8,128)(2,1)}, bf16[2,96,768]{2,1,0:T(8,128)(2,1)S(1)}, u32[]{:S(2)}, u32[]{:S(2)}) collective-permute-start(bf16[2,96,768]{2,1,0:T(8,128)(2,1)} %collective-permute-done.5), channel_id=1, source_target_pairs={{0,16},{4,20},{8,24},{12,28},{16,0},{20,4},{24,8},{28,12},{1,17},{... | collective-permute-start | bytes 884744 | tf_op jit(solution)/shard_map/mlp_weights_dp/ppermute | solution.py:578
  34.3 15.6 %collective-permute-start.7 = (bf16[2,192,768]{2,1,0:T(8,128)(2,1)}, bf16[2,192,768]{2,1,0:T(8,128)(2,1)}, u32[]{:S(2)}, u32[]{:S(2)}) collective-permute-start(bf16[2,192,768]{2,1,0:T(8,128)(2,1)} %maximum_select_fusion.5), channel_id=1, source_target_pairs={{0,8},{4,12},{8,0},{12,4},{16,24},{20,28},{24,16},{28,20},{1,9},{5... | collective-permute-start | bytes 1769480 | tf_op jit(solution)/shard_map/mlp_weights_dp/ppermute | solution.py:578
  38.3 23.7 %collective-permute-start.2 = (bf16[512,768]{1,0:T(8,128)(2,1)}, bf16[512,768]{1,0:T(8,128)(2,1)}, u32[]{:S(2)}, u32[]{:S(2)}) collective-permute-start(bf16[512,768]{1,0:T(8,128)(2,1)} %collective-permute-done.1), channel_id=1, source_target_pairs={{0,1},{1,0},{2,3},{3,2},{4,5},{5,4},{6,7},{7,6},{8,9},{9,8},{10,11... | collective-permute-start | bytes 2359304 | tf_op jit(solution)/shard_map/tokens/ppermute | solution.py:29
  50.0 22.9 %collective-permute-start.3 = (bf16[576,768]{1,0:T(8,128)(2,1)}, bf16[576,768]{1,0:T(8,128)(2,1)}, u32[]{:S(2)}, u32[]{:S(2)}) collective-permute-start(bf16[576,768]{1,0:T(8,128)(2,1)} %bitcast.99), channel_id=1, source_target_pairs={{0,2},{1,3},{2,0},{3,1},{4,6},{5,7},{6,4},{7,5},{8,10},{9,11},{10,... | collective-permute-start | bytes 2654216 | tf_op jit(solution)/shard_map/qkv_weights_x/ppermute | solution.py:25
  54.4 46.2 %collective-permute-start.9 = (bf16[2,384,768]{2,1,0:T(8,128)(2,1)}, bf16[2,384,768]{2,1,0:T(8,128)(2,1)}, u32[]{:S(2)}, u32[]{:S(2)}) collective-permute-start(bf16[2,384,768]{2,1,0:T(8,128)(2,1)} %maximum_select_fusion.1), channel_id=1, source_target_pairs={{0,4},{4,0},{8,12},{12,8},{16,20},{20,16},{24,28},{28,24},{1,5},{5... | collective-permute-start | bytes 3538952 | tf_op jit(solution)/shard_map/mlp_weights_dp/ppermute | solution.py:578
  59.2 45.4 %collective-permute-start.8 = (bf16[256,768]{1,0:T(8,128)(2,1)}, bf16[256,768]{1,0:T(8,128)(2,1)S(1)}, u32[]{:S(2)}, u32[]{:S(2)}) collective-permute-start(bf16[256,768]{1,0:T(8,128)(2,1)} %get-tuple-element.173), channel_id=1, source_target_pairs={{0,2},{1,3},{2,0},{3,1},{4,6},{5,7},{6,4},{7,5},{8,10},{9,11},{10,... | collective-permute-start | bytes 1179656 | tf_op jit(solution)/shard_map/cotangent/ppermute | solution.py:25
  65.0 7.8 %copy-start = (bf16[2048,768]{1,0:T(8,128)(2,1)}, bf16[2048,768]{1,0:T(8,128)(2,1)S(1)}, u32[]{:S(2)}) copy-start(bf16[2048,768]{1,0:T(8,128)(2,1)S(1)} %slice_dynamic-update-slice_fusion.x_ref) | copy-start | bytes 9437188
  65.0 17.9 %copy-start.26 = (s32[1536]{0:T(1024)S(1)}, s32[1536]{0:T(1024)}, u32[]{:S(2)}) copy-start(s32[1536]{0:T(1024)} %broadcast_in_dim.53) | copy-start | bytes 18436
  107.2 8.6 %collective-permute-start.11 = (bf16[1536,768]{1,0:T(8,128)(2,1)S(1)}, bf16[1536,768]{1,0:T(8,128)(2,1)}, u32[]{:S(2)}, u32[]{:S(2)}) collective-permute-start(bf16[1536,768]{1,0:T(8,128)(2,1)S(1)} %convolution_convert_fusion.own_ref), channel_id=1, source_target_pairs={{0,1},{1,0},{2,3},{3,2},{4,5},{5,4},{6,7},{7,6},{8,9},{9,8},{10,11... | collective-permute-start | bytes 7077896 | tf_op jit(solution)/shard_map/attn_core/ppermute | solution.py:29
  108.3 5.0 %collective-permute-start.12 = (bf16[512,768]{1,0:T(8,128)(2,1)}, bf16[512,768]{1,0:T(8,128)(2,1)S(1)}, u32[]{:S(2)}, u32[]{:S(2)}) collective-permute-start(bf16[512,768]{1,0:T(8,128)(2,1)} %pad_maximum_fusion.7), channel_id=1, source_target_pairs={{0,1},{1,0},{2,3},{3,2},{4,5},{5,4},{6,7},{7,6},{8,9},{9,8},{10,11... | collective-permute-start | bytes 2359304 | tf_op jit(solution)/shard_map/cotangent/ppermute | solution.py:29
  111.8 3.2 collective-permute-start.13
  115.8 25.8 %copy-start.22 = (bf16[64,768]{1,0:T(8,128)(2,1)S(1)}, bf16[64,768]{1,0:T(8,128)(2,1)}, u32[]{:S(2)}) copy-start(bf16[64,768]{1,0:T(8,128)(2,1)} %copy-done.21) | copy-start | bytes 294916
  115.8 25.8 %copy-start.24 = (bf16[192,768]{1,0:T(8,128)(2,1)S(1)}, bf16[192,768]{1,0:T(8,128)(2,1)}, u32[]{:S(2)}) copy-start(bf16[192,768]{1,0:T(8,128)(2,1)} %param.24) | copy-start | bytes 884740
  141.2 10.4 %collective-permute-start.14 = (bf16[1536,768]{1,0:T(8,128)(2,1)}, bf16[1536,768]{1,0:T(8,128)(2,1)S(1)}, u32[]{:S(2)}, u32[]{:S(2)}) collective-permute-start(bf16[1536,768]{1,0:T(8,128)(2,1)} %get-tuple-element.88.own_ref), channel_id=1, source_target_pairs={{0,1},{1,0},{2,3},{3,2},{4,5},{5,4},{6,7},{7,6},{8,9},{9,8},{10,11... | collective-permute-start | bytes 7077896 | tf_op jit(solution)/shard_map/mid_core/ppermute | solution.py:29
  147.9 40.6 %collective-permute-start.15 = (bf16[768,768]{1,0:T(8,128)(2,1)S(1)}, bf16[768,768]{1,0:T(8,128)(2,1)}, u32[]{:S(2)}, u32[]{:S(2)}) collective-permute-start(bf16[768,768]{1,0:T(8,128)(2,1)S(1)} %fusion.16), channel_id=1, source_target_pairs={{0,2},{1,3},{2,0},{3,1},{4,6},{5,7},{6,4},{7,5},{8,10},{9,11},{10,... | collective-permute-start | bytes 3538952 | tf_op jit(solution)/shard_map/down_grad_x/ppermute | solution.py:25
  151.6 13.2 %slice-start = ((s8[4718592]{0:T(1024)(128)(4,1)}), s8[4194304]{0:T(1024)(128)(4,1)S(1)}, s32[]{:S(2)}) async-start(s8[4718592]{0:T(1024)(128)(4,1)} %bitcast.112), calls=%async_computation | async-start | bytes 8388608
  151.6 13.2 %slice-start.1 = ((s8[4718592]{0:T(1024)(128)(4,1)}), s8[524288]{0:T(1024)(128)(4,1)S(1)}, s32[]{:S(2)}) async-start(s8[4718592]{0:T(1024)(128)(4,1)} %bitcast.112), calls=%async_computation.1 | async-start | bytes 1048576
  169.5 14.2 %copy-start.35 = (bf16[2048,768]{1,0:T(8,128)(2,1)S(1)}, bf16[2048,768]{1,0:T(8,128)(2,1)}, u32[]{:S(2)}) copy-start(bf16[2048,768]{1,0:T(8,128)(2,1)} %get-tuple-element.99) | copy-start | bytes 9437188
  193.5 18.1 %collective-permute-start.16 = (bf16[384,768]{1,0:T(8,128)(2,1)}, bf16[384,768]{1,0:T(8,128)(2,1)}, u32[]{:S(2)}, u32[]{:S(2)}) collective-permute-start(bf16[384,768]{1,0:T(8,128)(2,1)} %dynamic-slice_convert_fusion.2), channel_id=1, source_target_pairs={{0,4},{4,0},{8,12},{12,8},{16,20},{20,16},{24,28},{28,24},{1,5},{5... | collective-permute-start | bytes 1769480 | tf_op jit(solution)/shard_map/down_grad_dp/ppermute | solution.py:578
  195.0 48.2 %collective-permute-start.28 = (bf16[768,768]{1,0:T(8,128)(2,1)}, bf16[768,768]{1,0:T(8,128)(2,1)}, u32[]{:S(2)}, u32[]{:S(2)}) collective-permute-start(bf16[768,768]{1,0:T(8,128)(2,1)} %fusion.19), channel_id=1, source_target_pairs={{0,2},{1,3},{2,0},{3,1},{4,6},{5,7},{6,4},{7,5},{8,10},{9,11},{10,... | collective-permute-start | bytes 3538952 | tf_op jit(solution)/shard_map/up_grad_x/ppermute | solution.py:25
  196.5 46.6 %collective-permute-start.30 = (bf16[576,768]{1,0:T(8,128)(2,1)S(1)}, bf16[576,768]{1,0:T(8,128)(2,1)S(1)}, u32[]{:S(2)}, u32[]{:S(2)}) collective-permute-start(bf16[576,768]{1,0:T(8,128)(2,1)S(1)} %pad_maximum_fusion.5), channel_id=1, source_target_pairs={{0,2},{1,3},{2,0},{3,1},{4,6},{5,7},{6,4},{7,5},{8,10},{9,11},{10,... | collective-permute-start | bytes 2654216 | tf_op jit(solution)/shard_map/qkv_grad_x/ppermute | solution.py:25
  197.1 16.0 %copy-start.12 = (bf16[1536,768]{1,0:T(8,128)(2,1)S(1)}, bf16[1536,768]{1,0:T(8,128)(2,1)}, u32[]{:S(2)}) copy-start(bf16[1536,768]{1,0:T(8,128)(2,1)} %get-tuple-element.120) | copy-start | bytes 7077892
  213.0 36.1 %collective-permute-start.27 = (bf16[192,768]{1,0:T(8,128)(2,1)S(1)}, bf16[192,768]{1,0:T(8,128)(2,1)S(1)}, u32[]{:S(2)}, u32[]{:S(2)}) collective-permute-start(bf16[192,768]{1,0:T(8,128)(2,1)S(1)} %dynamic-slice_convert_fusion.5), channel_id=1, source_target_pairs={{0,8},{4,12},{8,0},{12,4},{16,24},{20,28},{24,16},{28,20},{1,9},{5... | collective-permute-start | bytes 884744 | tf_op jit(solution)/shard_map/down_grad_dp/ppermute | solution.py:578
  213.2 30.1 %slice-start.2 = ((s8[4718592]{0:T(1024)(128)(4,1)}), s8[4194304]{0:T(1024)(128)(4,1)S(1)}, s32[]{:S(2)}) async-start(s8[4718592]{0:T(1024)(128)(4,1)} %bitcast.114), calls=%async_computation.2 | async-start | bytes 8388608
  214.7 28.6 %slice-start.3 = ((s8[4718592]{0:T(1024)(128)(4,1)}), s8[524288]{0:T(1024)(128)(4,1)S(1)}, s32[]{:S(2)}) async-start(s8[4718592]{0:T(1024)(128)(4,1)} %bitcast.114), calls=%async_computation.3 | async-start | bytes 1048576
  214.7 34.1 %collective-permute-start.31 = (bf16[192,768]{1,0:T(8,128)(2,1)S(1)}, bf16[192,768]{1,0:T(8,128)(2,1)S(1)}, u32[]{:S(2)}, u32[]{:S(2)}) collective-permute-start(bf16[192,768]{1,0:T(8,128)(2,1)S(1)} %slice.317), channel_id=1, source_target_pairs={{0,2},{1,3},{2,0},{3,1},{4,6},{5,7},{6,4},{7,5},{8,10},{9,11},{10,... | collective-permute-start | bytes 884744 | tf_op jit(solution)/shard_map/proj_grad_x/ppermute | solution.py:25
  248.2 12.6 %collective-permute-start.29 = (bf16[384,768]{1,0:T(8,128)(2,1)S(1)}, bf16[384,768]{1,0:T(8,128)(2,1)S(1)}, u32[]{:S(2)}, u32[]{:S(2)}) collective-permute-start(bf16[384,768]{1,0:T(8,128)(2,1)S(1)} %dynamic-slice_convert_fusion.1), channel_id=1, source_target_pairs={{0,4},{4,0},{8,12},{12,8},{16,20},{20,16},{24,28},{28,24},{1,5},{5... | collective-permute-start | bytes 1769480 | tf_op jit(solution)/shard_map/up_grad_dp/ppermute | solution.py:578
  249.0 16.1 %copy-start.5 = (f32[768,768]{1,0:T(8,128)}, f32[768,768]{1,0:T(8,128)S(1)}, u32[]{:S(2)}) copy-start(f32[768,768]{1,0:T(8,128)S(1)} %pad_maximum_fusion) | copy-start | bytes 7077892
  261.0 16.2 %collective-permute-start.32 = (bf16[96,768]{1,0:T(8,128)(2,1)S(1)}, bf16[96,768]{1,0:T(8,128)(2,1)}, u32[]{:S(2)}, u32[]{:S(2)}) collective-permute-start(bf16[96,768]{1,0:T(8,128)(2,1)S(1)} %dynamic-slice_convert_fusion.8), channel_id=1, source_target_pairs={{0,16},{4,20},{8,24},{12,28},{16,0},{20,4},{24,8},{28,12},{1,17},{... | collective-permute-start | bytes 442376 | tf_op jit(solution)/shard_map/down_grad_dp/ppermute | solution.py:578
  265.1 13.0 %collective-permute-start.33 = (bf16[192,768]{1,0:T(8,128)(2,1)}, bf16[192,768]{1,0:T(8,128)(2,1)}, u32[]{:S(2)}, u32[]{:S(2)}) collective-permute-start(bf16[192,768]{1,0:T(8,128)(2,1)} %dynamic-slice_convert_fusion.4), channel_id=1, source_target_pairs={{0,8},{4,12},{8,0},{12,4},{16,24},{20,28},{24,16},{28,20},{1,9},{5... | collective-permute-start | bytes 884744 | tf_op jit(solution)/shard_map/up_grad_dp/ppermute | solution.py:578
  265.9 13.2 %collective-permute-start.34 = (bf16[384,768]{1,0:T(8,128)(2,1)}, bf16[384,768]{1,0:T(8,128)(2,1)}, u32[]{:S(2)}, u32[]{:S(2)}) collective-permute-start(bf16[384,768]{1,0:T(8,128)(2,1)} %dynamic-slice_convert_fusion), channel_id=1, source_target_pairs={{0,4},{4,0},{8,12},{12,8},{16,20},{20,16},{24,28},{28,24},{1,5},{5... | collective-permute-start | bytes 1769480 | tf_op jit(solution)/shard_map/tail_grad_dp/ppermute | solution.py:578
  267.5 11.7 %copy-start.6 = (f32[768,768]{1,0:T(8,128)S(1)}, f32[768,768]{1,0:T(8,128)}, u32[]{:S(2)}) copy-start(f32[768,768]{1,0:T(8,128)} %copy-done.5) | copy-start | bytes 7077892
  277.2 26.6 %collective-permute-start.19 = (bf16[1024,768]{1,0:T(8,128)(2,1)}, bf16[1024,768]{1,0:T(8,128)(2,1)S(1)}, u32[]{:S(2)}, u32[]{:S(2)}) collective-permute-start(bf16[1024,768]{1,0:T(8,128)(2,1)} %get-tuple-element.107), channel_id=1, source_target_pairs={{0,1},{1,0},{2,3},{3,2},{4,5},{5,4},{6,7},{7,6},{8,9},{9,8},{10,11... | collective-permute-start | bytes 4718600 | tf_op jit(solution)/shard_map/first_core/ppermute | solution.py:29
  281.0 10.6 %collective-permute-start.36 = (bf16[96,768]{1,0:T(8,128)(2,1)}, bf16[96,768]{1,0:T(8,128)(2,1)}, u32[]{:S(2)}, u32[]{:S(2)}) collective-permute-start(bf16[96,768]{1,0:T(8,128)(2,1)} %dynamic-slice_convert_fusion.7), channel_id=1, source_target_pairs={{0,16},{4,20},{8,24},{12,28},{16,0},{20,4},{24,8},{28,12},{1,17},{... | collective-permute-start | bytes 442376 | tf_op jit(solution)/shard_map/up_grad_dp/ppermute | solution.py:578
  282.7 39.8 %collective-permute-start.17 = (bf16[768,768]{1,0:T(8,128)(2,1)}, bf16[768,768]{1,0:T(8,128)(2,1)S(1)}, u32[]{:S(2)}, u32[]{:S(2)}) collective-permute-start(bf16[768,768]{1,0:T(8,128)(2,1)} %get-tuple-element.104), channel_id=1, source_target_pairs={{0,1},{1,0},{2,3},{3,2},{4,5},{5,4},{6,7},{7,6},{8,9},{9,8},{10,11... | collective-permute-start | bytes 3538952 | tf_op jit(solution)/shard_map/block_out/ppermute | solution.py:29
  283.3 11.6 %collective-permute-start.35 = (bf16[96,768]{1,0:T(8,128)(2,1)S(1)}, bf16[96,768]{1,0:T(8,128)(2,1)S(1)}, u32[]{:S(2)}, u32[]{:S(2)}) collective-permute-start(bf16[96,768]{1,0:T(8,128)(2,1)S(1)} %convert_add_fusion.10), channel_id=1, source_target_pairs={{0,16},{4,20},{8,24},{12,28},{16,0},{20,4},{24,8},{28,12},{1,17},{... | collective-permute-start | bytes 442376 | tf_op jit(solution)/shard_map/down_grad_dp/ppermute | solution.py:578
  285.9 14.8 %collective-permute-start.37 = (bf16[192,768]{1,0:T(8,128)(2,1)S(1)}, bf16[192,768]{1,0:T(8,128)(2,1)S(1)}, u32[]{:S(2)}, u32[]{:S(2)}) collective-permute-start(bf16[192,768]{1,0:T(8,128)(2,1)S(1)} %dynamic-slice_convert_fusion.3), channel_id=1, source_target_pairs={{0,8},{4,12},{8,0},{12,4},{16,24},{20,28},{24,16},{28,20},{1,9},{5... | collective-permute-start | bytes 884744 | tf_op jit(solution)/shard_map/tail_grad_dp/ppermute | solution.py:578
  300.8 12.4 %collective-permute-start.40 = (bf16[96,768]{1,0:T(8,128)(2,1)S(1)}, bf16[96,768]{1,0:T(8,128)(2,1)S(1)}, u32[]{:S(2)}, u32[]{:S(2)}) collective-permute-start(bf16[96,768]{1,0:T(8,128)(2,1)S(1)} %dynamic-slice_convert_fusion.6), channel_id=1, source_target_pairs={{0,16},{4,20},{8,24},{12,28},{16,0},{20,4},{24,8},{28,12},{1,17},{... | collective-permute-start | bytes 442376 | tf_op jit(solution)/shard_map/tail_grad_dp/ppermute | solution.py:578
  300.9 12.2 %collective-permute-start.39 = (bf16[96,768]{1,0:T(8,128)(2,1)S(1)}, bf16[96,768]{1,0:T(8,128)(2,1)S(1)}, u32[]{:S(2)}, u32[]{:S(2)}) collective-permute-start(bf16[96,768]{1,0:T(8,128)(2,1)S(1)} %convert_add_fusion.9), channel_id=1, source_target_pairs={{0,16},{4,20},{8,24},{12,28},{16,0},{20,4},{24,8},{28,12},{1,17},{... | collective-permute-start | bytes 442376 | tf_op jit(solution)/shard_map/up_grad_dp/ppermute | solution.py:578
  303.8 17.3 %copy-start.4 = (bf16[1024,768]{1,0:T(8,128)(2,1)}, bf16[1024,768]{1,0:T(8,128)(2,1)S(1)}, u32[]{:S(2)}) copy-start(bf16[1024,768]{1,0:T(8,128)(2,1)S(1)} %collective-permute-done.19.got_ref) | copy-start | bytes 4718596
  303.8 18.8 %copy-start.11 = (f32[768,768]{1,0:T(8,128)S(1)}, f32[768,768]{1,0:T(8,128)}, u32[]{:S(2)}) copy-start(f32[768,768]{1,0:T(8,128)} %get-tuple-element.90) | copy-start | bytes 7077892
  305.3 24.6 %collective-permute-start.21 = (bf16[256,768]{1,0:T(8,128)(2,1)S(1)}, bf16[256,768]{1,0:T(8,128)(2,1)S(1)}, u32[]{:S(2)}, u32[]{:S(2)}) collective-permute-start(bf16[256,768]{1,0:T(8,128)(2,1)S(1)} %add_convert_fusion.1), channel_id=1, source_target_pairs={{0,2},{1,3},{2,0},{3,1},{4,6},{5,7},{6,4},{7,5},{8,10},{9,11},{10,... | collective-permute-start | bytes 1179656 | tf_op jit(solution)/shard_map/first_mid_x/ppermute | solution.py:25
  307.4 13.4 %collective-permute-start.38 = (bf16[192,768]{1,0:T(8,128)(2,1)S(1)}, bf16[192,768]{1,0:T(8,128)(2,1)S(1)}, u32[]{:S(2)}, u32[]{:S(2)}) collective-permute-start(bf16[192,768]{1,0:T(8,128)(2,1)S(1)} %maximum_select_fusion.9), channel_id=1, source_target_pairs={{0,8},{4,12},{8,0},{12,4},{16,24},{20,28},{24,16},{28,20},{1,9},{5... | collective-permute-start | bytes 884744 | tf_op jit(solution)/shard_map/down_grad_dp/ppermute | solution.py:578
  321.1 24.2 %collective-permute-start.41 = (bf16[384,768]{1,0:T(8,128)(2,1)S(1)}, bf16[384,768]{1,0:T(8,128)(2,1)S(1)}, u32[]{:S(2)}, u32[]{:S(2)}) collective-permute-start(bf16[384,768]{1,0:T(8,128)(2,1)S(1)} %maximum_select_fusion.6), channel_id=1, source_target_pairs={{0,4},{4,0},{8,12},{12,8},{16,20},{20,16},{24,28},{28,24},{1,5},{5... | collective-permute-start | bytes 1769480 | tf_op jit(solution)/shard_map/down_grad_dp/ppermute | solution.py:578
  323.0 25.6 %collective-permute-start.18 = (bf16[256,768]{1,0:T(8,128)(2,1)S(1)}, bf16[256,768]{1,0:T(8,128)(2,1)S(1)}, u32[]{:S(2)}, u32[]{:S(2)}) collective-permute-start(bf16[256,768]{1,0:T(8,128)(2,1)S(1)} %slice.234), channel_id=1, source_target_pairs={{0,2},{1,3},{2,0},{3,1},{4,6},{5,7},{6,4},{7,5},{8,10},{9,11},{10,... | collective-permute-start | bytes 1179656 | tf_op jit(solution)/shard_map/block_out/ppermute | solution.py:25
  328.2 35.5 %collective-permute-start.20 = (bf16[256,768]{1,0:T(8,128)(2,1)S(1)}, bf16[256,768]{1,0:T(8,128)(2,1)}, u32[]{:S(2)}, u32[]{:S(2)}) collective-permute-start(bf16[256,768]{1,0:T(8,128)(2,1)S(1)} %slice.191), channel_id=1, source_target_pairs={{0,2},{1,3},{2,0},{3,1},{4,6},{5,7},{6,4},{7,5},{8,10},{9,11},{10,... | collective-permute-start | bytes 1179656 | tf_op jit(solution)/shard_map/in_grad_x/ppermute | solution.py:25
  333.7 7.6 %collective-permute-start.43 = (bf16[96,768]{1,0:T(8,128)(2,1)S(1)}, bf16[96,768]{1,0:T(8,128)(2,1)S(1)}, u32[]{:S(2)}, u32[]{:S(2)}) collective-permute-start(bf16[96,768]{1,0:T(8,128)(2,1)S(1)} %convert_add_fusion.8), channel_id=1, source_target_pairs={{0,16},{4,20},{8,24},{12,28},{16,0},{20,4},{24,8},{28,12},{1,17},{... | collective-permute-start | bytes 442376 | tf_op jit(solution)/shard_map/tail_grad_dp/ppermute | solution.py:578
  333.7 11.3 %collective-permute-start.42 = (bf16[192,768]{1,0:T(8,128)(2,1)S(1)}, bf16[192,768]{1,0:T(8,128)(2,1)S(1)}, u32[]{:S(2)}, u32[]{:S(2)}) collective-permute-start(bf16[192,768]{1,0:T(8,128)(2,1)S(1)} %maximum_select_fusion.10), channel_id=1, source_target_pairs={{0,8},{4,12},{8,0},{12,4},{16,24},{20,28},{24,16},{28,20},{1,9},{5... | collective-permute-start | bytes 884744 | tf_op jit(solution)/shard_map/up_grad_dp/ppermute | solution.py:578
  341.3 5.0 %collective-permute-start.22 = (f32[12,768]{1,0:T(8,128)S(1)}, f32[12,768]{1,0:T(8,128)S(1)}, u32[]{:S(2)}, u32[]{:S(2)}) collective-permute-start(f32[12,768]{1,0:T(8,128)S(1)} %pad_maximum_fusion.9), channel_id=1, source_target_pairs={{0,1},{1,0},{2,3},{3,2},{4,5},{5,4},{6,7},{7,6},{8,9},{9,8},{10,11... | collective-permute-start | bytes 110600 | tf_op jit(solution)/shard_map/small_sums/ppermute | solution.py:29
  345.7 16.9 %collective-permute-start.44 = (bf16[384,768]{1,0:T(8,128)(2,1)S(1)}, bf16[384,768]{1,0:T(8,128)(2,1)S(1)}, u32[]{:S(2)}, u32[]{:S(2)}) collective-permute-start(bf16[384,768]{1,0:T(8,128)(2,1)S(1)} %maximum_select_fusion.7), channel_id=1, source_target_pairs={{0,4},{4,0},{8,12},{12,8},{16,20},{20,16},{24,28},{28,24},{1,5},{5... | collective-permute-start | bytes 1769480 | tf_op jit(solution)/shard_map/up_grad_dp/ppermute | solution.py:578
  346.4 4.2 %collective-permute-start.23 = (f32[12,768]{1,0:T(8,128)S(1)}, f32[12,768]{1,0:T(8,128)S(1)}, u32[]{:S(2)}, u32[]{:S(2)}) collective-permute-start(f32[12,768]{1,0:T(8,128)S(1)} %fusion.35), channel_id=1, source_target_pairs={{0,2},{1,3},{2,0},{3,1},{4,6},{5,7},{6,4},{7,5},{8,10},{9,11},{10,... | collective-permute-start | bytes 110600 | tf_op jit(solution)/shard_map/small_sums/ppermute | solution.py:25
  346.8 15.6 %collective-permute-start.45 = (bf16[192,768]{1,0:T(8,128)(2,1)S(1)}, bf16[192,768]{1,0:T(8,128)(2,1)S(1)}, u32[]{:S(2)}, u32[]{:S(2)}) collective-permute-start(bf16[192,768]{1,0:T(8,128)(2,1)S(1)} %maximum_select_fusion.11), channel_id=1, source_target_pairs={{0,8},{4,12},{8,0},{12,4},{16,24},{20,28},{24,16},{28,20},{1,9},{5... | collective-permute-start | bytes 884744 | tf_op jit(solution)/shard_map/tail_grad_dp/ppermute | solution.py:578
  350.6 9.4 %collective-permute-start.24 = (f32[12,768]{1,0:T(8,128)S(1)}, f32[12,768]{1,0:T(8,128)S(1)}, u32[]{:S(2)}, u32[]{:S(2)}) collective-permute-start(f32[12,768]{1,0:T(8,128)S(1)} %add.171), channel_id=1, source_target_pairs={{0,4},{4,0},{8,12},{12,8},{16,20},{20,16},{24,28},{28,24},{1,5},{5... | collective-permute-start | bytes 110600 | tf_op jit(solution)/shard_map/small_sums/ppermute | solution.py:578
  360.0 4.8 %collective-permute-start.25 = (f32[12,768]{1,0:T(8,128)S(1)}, f32[12,768]{1,0:T(8,128)S(1)}, u32[]{:S(2)}, u32[]{:S(2)}) collective-permute-start(f32[12,768]{1,0:T(8,128)S(1)} %add.172), channel_id=1, source_target_pairs={{0,8},{4,12},{8,0},{12,4},{16,24},{20,28},{24,16},{28,20},{1,9},{5... | collective-permute-start | bytes 110600 | tf_op jit(solution)/shard_map/small_sums/ppermute | solution.py:578
  363.0 12.6 %collective-permute-start.46 = (bf16[384,768]{1,0:T(8,128)(2,1)S(1)}, bf16[384,768]{1,0:T(8,128)(2,1)S(1)}, u32[]{:S(2)}, u32[]{:S(2)}) collective-permute-start(bf16[384,768]{1,0:T(8,128)(2,1)S(1)} %maximum_select_fusion.8), channel_id=1, source_target_pairs={{0,4},{4,0},{8,12},{12,8},{16,20},{20,16},{24,28},{28,24},{1,5},{5... | collective-permute-start | bytes 1769480 | tf_op jit(solution)/shard_map/tail_grad_dp/ppermute | solution.py:578
  364.8 5.1 %collective-permute-start.26 = (f32[12,768]{1,0:T(8,128)S(1)}, f32[12,768]{1,0:T(8,128)S(1)}, u32[]{:S(2)}, u32[]{:S(2)}) collective-permute-start(f32[12,768]{1,0:T(8,128)S(1)} %add.173), channel_id=1, source_target_pairs={{0,16},{4,20},{8,24},{12,28},{16,0},{20,4},{24,8},{28,12},{1,17},{... | collective-permute-start | bytes 110600 | tf_op jit(solution)/shard_map/small_sums/ppermute | solution.py:578
  (27 other events, 87.8 us)
where the time goes:
time: 387 us; the launch traced here: 382 us
  Pallas kernels  109 us (28%)
  waiting for transfers between devices  102 us (26%)
  starting transfers between devices  54.6 us (14%)
  local copies, waits for them, and re-layouts  44 us (11%)
  other arithmetic  41.9 us (11%)
  matrix products  27.9 us (7%)
    ppermute x24, waiting for transfers between devices, dp_swap(): return lax.ppermute(value, 'dp', dp_partners(lax.axis_size('dp'), bit))  69.6 us
    ppermute x24, starting transfers between devices, dp_swap(): return lax.ppermute(value, 'dp', dp_partners(lax.axis_size('dp'), bit))  33.7 us
    ppermute x14, waiting for transfers between devices, x_swap(): return lax.ppermute(value, 'tensor', X_SWAP)  32.4 us
    pallas_call x2, Pallas kernels, attend_backward(): pl.pallas_call(functools.partial(attend_backward_kernel, size), grid_spec...  28.7 us
    dot_general x7, matrix products, tn(): lax.dot_general(left, right, (((0,), (0,)), ((), ())), preferred_element_...  25.4 us
    pallas_call x1, Pallas kernels, mlp(): pl.pallas_call(mlp_kernel, grid=(rows // size,), in_specs=[block, block,...  25.4 us
    ppermute x14, starting transfers between devices, x_swap(): return lax.ppermute(value, 'tensor', X_SWAP)  19.4 us
    pallas_call x1, Pallas kernels, attend_forward(): pl.pallas_call(functools.partial(attend_forward_kernel, size), grid_spec=...  17 us
  transfers between devices with their start and end apart: 47, of which 16 were waited for; matrix products, arithmetic and copies ran while one was open for 24% of the time, Pallas kernels for 22%

commit v1 on v0

v1 whole, which is shorter than its diff:
```python
import functools

import jax
import jax.numpy as jnp
from jax import lax
from jax.experimental import pallas as pl
from jax.experimental.pallas import tpu as pltpu
from jax.sharding import PartitionSpec as P

HEAD_DIM = 64
NORM_EPS = 1e-05
MASKED = -1e30
BF = jnp.bfloat16
F32 = jnp.float32
VMEM_LIMIT = 56 * 1024 * 1024

SLOT = ((0, 2, 4, 5), (1, 3, 6, 7))
SLOT_ROW = (0, 1, 0, 1, 0, 0)
SLOT_K = (0, 0, 1, 1, 2, 3)
X_SWAP = ((0, 2), (1, 3), (2, 0), (3, 1))
CORE_SWAP = ((0, 1), (1, 0), (2, 3), (3, 2))


def x_swap(value):
    return lax.ppermute(value, "tensor", X_SWAP)


def core_swap(value):
    return lax.ppermute(value, "tensor", CORE_SWAP)


def params(semantics=None):
    return pltpu.CompilerParams(vmem_limit_bytes=VMEM_LIMIT)


def fixed(shape):
    return pl.BlockSpec(shape, lambda *ids: (0,) * len(shape), pipeline_mode=pl.Buffered(1))


def nt(left, right):
    return lax.dot_general(left, right, (((1,), (1,)), ((), ())), preferred_element_type=F32)


def nn(left, right):
    return lax.dot_general(left, right, (((1,), (0,)), ((), ())), preferred_element_type=F32)


def tn(left, right):
    return lax.dot_general(left, right, (((0,), (0,)), ((), ())), preferred_element_type=F32)


SMALL_COST = pl.CostEstimate(flops=1, bytes_accessed=1, transcendentals=0)


def key_mask(start_row, key_first, size, diagonal):
    keys = lax.broadcasted_iota(jnp.int32, (size, size), 0)
    mask = keys >= start_row - key_first
    if diagonal:
        mask = mask & (keys <= lax.broadcasted_iota(jnp.int32, (size, size), 1))
    return mask


def head_rows(size):
    lane = lax.broadcasted_iota(jnp.int32, (size, 2 * HEAD_DIM), 1)

    def select(value):
        zero = jnp.zeros((size, 2 * HEAD_DIM), value.dtype)
        pair = value[:, : 2 * HEAD_DIM]
        return (
            jnp.where(lane < HEAD_DIM, pair, zero),
            jnp.where(lane < HEAD_DIM, zero, pair),
            value[:, 2 * HEAD_DIM :],
        )

    return select


def pair_lanes(value, head):
    first = 2 * HEAD_DIM * (head // 2)
    return value[:, first : first + 2 * HEAD_DIM]


def attend_forward_kernel(size, table, start_ref, q_ref, k_ref, v_ref, out_ref, lse_ref):
    slot = pl.program_id(1)
    row, block, low = table[0, slot], table[1, slot], table[2, slot]
    start_row = start_ref[0:1, :]
    select = head_rows(size)
    heads = select(q_ref[...] * jnp.asarray(HEAD_DIM**-0.5, BF))

    def load(key_block):
        at = pl.multiple_of(table[3 + row, key_block] * size, size)
        return k_ref[pl.ds(at, size), :], jnp.transpose(v_ref[pl.ds(at, size), :])

    key, value_t = load(block)
    mask = key_mask(start_row, block * size, size, True)
    all_scores = [nt(pair_lanes(key, head), heads[head]) for head in range(3)]
    carry = []
    for head in range(3):
        scores = jnp.where(mask, all_scores[head], MASKED)
        top = jnp.max(scores, axis=0, keepdims=True)
        weight = jnp.exp(scores - top)
        total = jnp.sum(weight, axis=0, keepdims=True)
        acc = nn(value_t[head * HEAD_DIM : (head + 1) * HEAD_DIM], weight.astype(BF))
        carry += [top, total, acc]

    def earlier(step, carry):
        key_block = block - 1 - step
        key, value_t = load(key_block)
        mask = key_mask(start_row, key_block * size, size, False)
        all_scores = [nt(pair_lanes(key, head), heads[head]) for head in range(3)]
        new = []
        for head in range(3):
            top, total, acc = carry[3 * head : 3 * head + 3]
            scores = jnp.where(mask, all_scores[head], MASKED)
            higher = jnp.maximum(top, jnp.max(scores, axis=0, keepdims=True))
            shrink = jnp.exp(top - higher)
            weight = jnp.exp(scores - higher)
            total = total * shrink + jnp.sum(weight, axis=0, keepdims=True)
            acc = acc * shrink + nn(
                value_t[head * HEAD_DIM : (head + 1) * HEAD_DIM], weight.astype(BF)
            )
            new += [higher, total, acc]
        return tuple(new)

    carry = lax.fori_loop(0, block - low, earlier, tuple(carry))
    parts = [carry[3 * head + 2] / carry[3 * head + 1] for head in range(3)]
    parts.append(jnp.zeros_like(parts[0]))
    out_ref[...] = jnp.transpose(jnp.concatenate(parts, axis=0)).astype(BF)
    for head in range(3):
        lse_ref[head : head + 1, :] = carry[3 * head] + jnp.log(carry[3 * head + 1])


def attend_forward(qkv, table, starts, size):
    width = 4 * HEAD_DIM
    tokens = qkv.shape[0]
    return pl.pallas_call(
        functools.partial(attend_forward_kernel, size),
        grid_spec=pltpu.PrefetchScalarGridSpec(
            num_scalar_prefetch=1,
            grid=(2, 6),
            in_specs=[
                pl.BlockSpec((8, size), lambda p, s, *_: (0, s)),
                pl.BlockSpec((size, width), lambda p, s, *_: (s, 3 * p)),
                pl.BlockSpec((tokens, width), lambda p, s, *_: (0, 3 * p + 1)),
                pl.BlockSpec((tokens, width), lambda p, s, *_: (0, 3 * p + 2)),
            ],
            out_specs=[
                pl.BlockSpec((size, width), lambda p, s, *_: (s, p)),
                pl.BlockSpec((8, size), lambda p, s, *_: (p, s)),
            ],
        ),
        out_shape=[
            jax.ShapeDtypeStruct((6 * size, 2 * width), BF),
            jax.ShapeDtypeStruct((16, 6 * size), F32),
        ],
        compiler_params=params(),
        cost_estimate=SMALL_COST,
        name="attend_forward",
    )(table, starts, qkv, qkv, qkv)


def attend_backward_kernel(
    size, table, start_ref, q_ref, k_ref, v_ref, out_ref, grad_ref, lse_ref,
    d_ref, sum_ref, dk_acc, dv_acc,
):
    slot = pl.program_id(0)
    width = 4 * HEAD_DIM
    row, block, low = table[0, slot], table[1, slot], table[2, slot]
    start_row = start_ref[0:1, :]
    select = head_rows(size)
    q_heads = select(q_ref[...] * jnp.asarray(HEAD_DIM**-0.5, BF))
    grad = grad_ref[...]
    g_heads = select(grad)
    products = jnp.transpose(grad.astype(F32) * out_ref[...].astype(F32))
    deltas = [
        jnp.sum(products[head * HEAD_DIM : (head + 1) * HEAD_DIM], axis=0, keepdims=True)
        for head in range(3)
    ]

    @pl.when(slot == 0)
    def _():
        dk_acc[...] = jnp.zeros_like(dk_acc)
        dv_acc[...] = jnp.zeros_like(dv_acc)
        sum_ref[...] = jnp.zeros_like(sum_ref)

    def one_block(key_block, diagonal):
        at = pl.multiple_of(table[3 + row, key_block] * size, size)
        key, value = k_ref[pl.ds(at, size), :], v_ref[pl.ds(at, size), :]
        key_t = jnp.transpose(key)
        mask = key_mask(start_row, key_block * size, size, diagonal)
        all_scores = [nt(pair_lanes(key, head), q_heads[head]) for head in range(3)]
        all_grads = [nt(pair_lanes(value, head), g_heads[head]) for head in range(3)]
        dq_parts, dk_parts, dv_parts = [], [], []
        for head in range(3):
            scores = jnp.where(mask, all_scores[head], MASKED)
            prob = jnp.exp(scores - lse_ref[head : head + 1, :])
            score_grad = (prob * (all_grads[head] - deltas[head])).astype(BF)
            dk_parts.append(nn(score_grad, q_heads[head]))
            dv_parts.append(nn(prob.astype(BF), g_heads[head]))
            dq_parts.append(nn(key_t[head * HEAD_DIM : (head + 1) * HEAD_DIM], score_grad))
        dk_acc[pl.ds(at, size), : width // 2] += dk_parts[0] + dk_parts[1]
        dk_acc[pl.ds(at, size), width // 2 :] += dk_parts[2]
        dv_acc[pl.ds(at, size), : width // 2] += dv_parts[0] + dv_parts[1]
        dv_acc[pl.ds(at, size), width // 2 :] += dv_parts[2]
        return jnp.concatenate(dq_parts, axis=0)

    dq_t = one_block(block, True)
    dq_t = lax.fori_loop(
        0, block - low, lambda step, acc: acc + one_block(block - 1 - step, False), dq_t
    )
    dq_t = jnp.concatenate([dq_t, jnp.zeros((HEAD_DIM, size), F32)], axis=0)
    dq = (jnp.transpose(dq_t) * HEAD_DIM**-0.5).astype(BF)
    d_ref[pl.ds(pl.multiple_of(slot * size, size), size), :width] = dq
    sum_ref[0:1, :] += jnp.sum(dq.astype(F32), axis=0, keepdims=True)

    @pl.when(slot == pl.num_programs(0) - 1)
    def _():
        d_ref[6 * size :, :width] = jnp.zeros((2 * size, width), BF)
        d_ref[:, width : 2 * width] = dk_acc[...].astype(BF)
        dv = dv_acc[...].astype(BF)
        d_ref[:, 2 * width :] = dv
        sum_ref[1:2, :] = jnp.sum(dv.astype(F32), axis=0, keepdims=True)


def attend_backward(qkv, attended, grad, lse, table, starts, size, shard):
    tokens = qkv.shape[0]
    width = 4 * HEAD_DIM
    block = pl.BlockSpec((size, width), lambda s, *_: (s, shard))
    return pl.pallas_call(
        functools.partial(attend_backward_kernel, size),
        grid_spec=pltpu.PrefetchScalarGridSpec(
            num_scalar_prefetch=1,
            grid=(6,),
            in_specs=[
                pl.BlockSpec((8, size), lambda s, *_: (0, s)),
                pl.BlockSpec((size, width), lambda s, *_: (s, 3 * shard)),
                pl.BlockSpec((tokens, width), lambda s, *_: (0, 3 * shard + 1)),
                pl.BlockSpec((tokens, width), lambda s, *_: (0, 3 * shard + 2)),
                block,
                block,
                pl.BlockSpec((8, size), lambda s, *_: (shard, s)),
            ],
            out_specs=[
                pl.BlockSpec((tokens, 3 * width), lambda s, *_: (0, 0)),
                pl.BlockSpec((8, width), lambda s, *_: (0, 0)),
            ],
            scratch_shapes=[pltpu.VMEM((tokens, width), F32), pltpu.VMEM((tokens, width), F32)],
        ),
        out_shape=[
            jax.ShapeDtypeStruct((tokens, 3 * width), BF),
            jax.ShapeDtypeStruct((8, width), F32),
        ],
        compiler_params=params(),
        cost_estimate=SMALL_COST,
        name="attend_backward",
    )(table, starts, qkv, qkv, qkv, attended, grad, lse)


def prepare_kernel(size, place_ref, ids_ref, *refs):
    vectors, (start_ref, table_ref, vec_ref, rows_ref) = refs[:-4], refs[-4:]
    for i, ref in enumerate(vectors):
        vec_ref[i : i + 1, :] = ref[...].astype(F32).reshape(1, -1)
    vec_ref[len(vectors) :, :] = jnp.zeros((8 - len(vectors), vec_ref.shape[1]), F32)
    place = place_ref[0]
    ids = ids_ref[...]
    length = ids.shape[1]
    position = lax.broadcasted_iota(jnp.int32, ids.shape, 1)
    starts = position
    for doc in range(8):
        here = ids == doc
        first_one = jnp.min(jnp.where(here, position, length), axis=1, keepdims=True)
        starts = jnp.where(here, first_one, starts)
    rows_ref[...] = starts
    for i in range(8):
        for j in range(8):
            table_ref[i, j] = 0
    for slot in range(6):
        row, block = SLOT_ROW[slot], SLOT_K[slot] ^ place
        source = jnp.where(place >= 2, 2, 0) if row == 0 else 1
        at = pl.ds(pl.multiple_of(block * size, size), size)
        first_row, second_row, third_row = rows_ref[0:1, at], rows_ref[1:2, at], rows_ref[2:3, at]
        mine = second_row if row else jnp.where(source == 2, third_row, first_row)
        start_ref[:, slot * size : (slot + 1) * size] = jnp.broadcast_to(mine, (8, size))
        table_ref[0, slot] = row
        table_ref[1, slot] = block
        table_ref[2, slot] = jnp.min(mine) // size
    for row in range(2):
        for block in range(4):
            slots = SLOT[row]
            near = block ^ place
            table_ref[3 + row, block] = jnp.where(
                near < 2,
                jnp.where(near == 0, slots[0], slots[1]),
                jnp.where(near == 2, slots[2], slots[3]),
            )


def prepare(doc_ids, place, vectors, size):
    ids = jnp.pad(jnp.transpose(doc_ids), ((0, 5), (0, 0)), constant_values=-1)
    vmem, smem = pl.BlockSpec(memory_space=pltpu.VMEM), pl.BlockSpec(memory_space=pltpu.SMEM)
    return pl.pallas_call(
        functools.partial(prepare_kernel, size),
        in_specs=[smem, vmem] + [vmem] * len(vectors),
        out_specs=[vmem, smem, vmem],
        out_shape=[
            jax.ShapeDtypeStruct((8, 6 * size), jnp.int32),
            jax.ShapeDtypeStruct((8, 8), jnp.int32),
            jax.ShapeDtypeStruct((8, vectors[0].shape[0]), F32),
        ],
        scratch_shapes=[pltpu.VMEM(ids.shape, jnp.int32)],
        cost_estimate=SMALL_COST,
        name="prepare",
    )(place.reshape(1).astype(jnp.int32), ids, *vectors)


GELU_C = 0.7978845608028654
GELU_A = 0.044715


def two_blocks(step, refs, held_ref):
    home_ref, near_ref, far_ref, far_near_ref = refs
    half = home_ref.shape[0] // 2

    @pl.when(step == 0)
    def _():
        held_ref[...] = home_ref[...]

    @pl.when(step == 1)
    def _():
        held_ref[...] = near_ref[...]

    @pl.when(step == 2)
    def _():
        held_ref[:half] = far_ref[:half]
        held_ref[half:] = far_near_ref[:half]

    if far_ref.shape[0] > half:

        @pl.when(step == 3)
        def _():
            held_ref[:half] = far_ref[half:]
            held_ref[half:] = far_near_ref[half:]

    return held_ref[...]


def other_core(ref, step):
    value = ref[...].astype(F32)
    half = value.shape[0] // 2
    turned = jnp.concatenate([value[half:], value[:half]], axis=0)
    return jnp.where(step == 2, turned, value)


def other_pair(step):
    return jnp.where(step == 2, 2, 1 - step)


def mlp_kernel(
    x0, x1, x2, x3, own_ref, other_ref, b0, b1, b2, b3, vec_ref, upb_own, upb_far, up_own, up_far, dn_own, dn_far,
    res_ref, mid_ref, act_ref, hg_ref, out_ref, give_ref, midin_ref, upbg_ref, bg_ref, held_ref,
):
    step = pl.program_id(0)
    proj_bias, gain, shift = vec_ref[0:1, :], vec_ref[1:2, :], vec_ref[2:3, :]
    residual = two_blocks(step, (x0, x1, x2, x3), held_ref).astype(F32) + own_ref[...].astype(F32)
    residual = residual + other_core(other_ref, step) + proj_bias
    res_ref[...] = residual
    centered = residual - jnp.mean(residual, axis=-1, keepdims=True)
    variance = jnp.mean(centered * centered, axis=-1, keepdims=True)
    mid = (centered * lax.rsqrt(variance + NORM_EPS) * gain + shift).astype(BF)
    mid_ref[...] = mid
    bg = two_blocks(step, (b0, b1, b2, b3), bg_ref)

    @pl.when(step == 0)
    def _():
        upbg_ref[...] = jnp.zeros_like(upbg_ref)

    out = None
    midin = None
    weights = ((up_own[...], dn_own[...], upb_own[...]), (up_far[0], dn_far[0], upb_far[...]))
    for part, (up_w, dn_w, up_bias) in enumerate(weights):
        hidden = nn(mid, up_w) + up_bias[1:2].astype(F32)
        act_grad = nt(bg, dn_w)
        square = hidden * hidden
        bent = jnp.tanh(GELU_C * (hidden + GELU_A * hidden * square))
        half = 0.5 * (1.0 + bent)
        act = (hidden * half).astype(BF)
        slope = half + 0.5 * hidden * (1.0 - bent * bent) * (GELU_C + 3.0 * GELU_C * GELU_A * square)
        grad = (act_grad * slope).astype(BF)
        act_ref[part] = act
        hg_ref[part] = grad
        upbg_ref[part : part + 1, :] += jnp.sum(grad.astype(F32), axis=0, keepdims=True)
        out_part = nn(act, dn_w)
        midin_part = nt(grad, up_w)
        out = out_part if out is None else out + out_part
        midin = midin_part if midin is None else midin + midin_part
    midin_ref[...] = midin.astype(BF)
    size = out.shape[0] // 2

    @pl.when(step == 0)
    def _():
        out_ref[: 2 * size] = out + residual + vec_ref[3:4, :]

    @pl.when(step == 1)
    def _():
        give_ref[: 2 * size] = out.astype(BF)

    @pl.when(step == 2)
    def _():
        out_ref[2 * size :] = (out + residual)[:size] + vec_ref[3:4, :]
        give_ref[2 * size :] = out[size:].astype(BF)


def mlp(tokens, own, other, bg, vectors, qkv_own, qkv_far, up_own, down_own, far, size):
    rows, width = own.shape
    inner = up_own.shape[1]
    block = pl.BlockSpec((2 * size, width), lambda i: (i, 0))
    wide = pl.BlockSpec((2, 2 * size, inner), lambda i: (0, i, 0))
    half = pl.BlockSpec((rows // 2, width), lambda i: (0, 0))
    return pl.pallas_call(
        mlp_kernel,
        grid=(3,),
        in_specs=[fixed((2 * size, width))] * 4
        + [
            block,
            pl.BlockSpec((2 * size, width), lambda i: (other_pair(i), 0)),
        ]
        + [fixed(value.shape) for value in bg]
        + [
            fixed((8, width)),
            pl.BlockSpec((16, width), lambda i: (9 * HEAD_DIM // 16, 0)),
            pl.BlockSpec((16, width), lambda i: (9 * HEAD_DIM // 16, 0)),
            fixed((width, inner)),
            pl.BlockSpec((1, width, inner), lambda i: (0, 0, 0), pipeline_mode=pl.Buffered(1)),
            fixed((inner, width)),
            pl.BlockSpec((1, inner, width), lambda i: (1, 0, 0), pipeline_mode=pl.Buffered(1)),
        ],
        out_specs=[
            block, block, wide, wide, half, half, block,
            pl.BlockSpec((8, inner), lambda i: (0, 0)),
            block,
        ],
        out_shape=[
            jax.ShapeDtypeStruct((rows, width), F32),
            jax.ShapeDtypeStruct((rows, width), BF),
            jax.ShapeDtypeStruct((2, rows, inner), BF),
            jax.ShapeDtypeStruct((2, rows, inner), BF),
            jax.ShapeDtypeStruct((rows // 2, width), F32),
            jax.ShapeDtypeStruct((rows // 2, width), BF),
            jax.ShapeDtypeStruct((rows, width), BF),
            jax.ShapeDtypeStruct((8, inner), F32),
            jax.ShapeDtypeStruct((rows, width), BF),
        ],
        scratch_shapes=[pltpu.VMEM((2 * size, width), BF)],
        compiler_params=params(),
        cost_estimate=SMALL_COST,
        name="mlp",
    )(*tokens, own, other, *bg, vectors, qkv_own, qkv_far, up_own, far, down_own, far)


def sum_tokens_kernel(rows, has_extra, left_ref, right_ref, *refs):
    left = left_ref[0] if len(left_ref.shape) == 3 else left_ref[...]
    right = right_ref[0] if len(right_ref.shape) == 3 else right_ref[...]
    total = tn(left, right)[:rows]
    if has_extra:
        total = total + refs[0][...].astype(F32)
    refs[-1][...] = total.astype(refs[-1].dtype)


def sum_tokens(
    left, right, extra=None, dtype=BF, part=0, rows=256, first=0, count=None, room=0, into=None
):
    block = 256
    count = count or left.shape[-1] // block
    tokens, width = right.shape[-2:]

    def spec(value, lanes, at):
        if value.ndim == 3:
            return pl.BlockSpec((1, tokens, lanes), lambda i: (part, 0, at(i)))
        return pl.BlockSpec((tokens, lanes), lambda i: (0, at(i)))

    base = 0 if into is None else into.shape[0] // rows - count
    out = pl.BlockSpec((rows, width), lambda i: (base + i, 0))
    specs = [spec(left, block, lambda i: first + i), spec(right, width, lambda i: 0)]
    operands = [left, right]
    if extra is not None:
        specs.append(out)
        operands.append(extra)
    aliases = {}
    shape = jax.ShapeDtypeStruct((count * rows + room, width), dtype)
    if into is not None:
        specs.append(pl.BlockSpec(memory_space=pl.ANY))
        aliases = {len(operands): 0}
        operands.append(into)
        shape = jax.ShapeDtypeStruct(into.shape, into.dtype)
    return pl.pallas_call(
        functools.partial(sum_tokens_kernel, rows, extra is not None),
        grid=(count,),
        in_specs=specs,
        out_specs=out,
        out_shape=shape,
        input_output_aliases=aliases,
        compiler_params=params(),
        cost_estimate=SMALL_COST,
        name="sum_tokens",
    )(*operands)


def project_kernel(heads_ref, far_w, own_w, out_ref):
    lanes = 4 * HEAD_DIM
    feats = far_w.shape[0]
    total = nn(heads_ref[:, :feats], far_w[...])
    out_ref[...] = (total + nn(heads_ref[:, lanes : lanes + feats], own_w[...])).astype(BF)


def project(heads, far_w, own_w, size):
    rows, lanes = heads.shape
    width = far_w.shape[1]
    return pl.pallas_call(
        project_kernel,
        grid=(3,),
        in_specs=[
            pl.BlockSpec((2 * size, lanes), lambda i: (i, 0)), fixed(far_w.shape), fixed(own_w.shape)
        ],
        out_specs=pl.BlockSpec((2 * size, width), lambda i: (i, 0)),
        out_shape=jax.ShapeDtypeStruct((rows, width), BF),
        compiler_params=params(),
        cost_estimate=SMALL_COST,
        name="project",
    )(heads, far_w, own_w)


def mid_backward_kernel(
    res_ref, own_ref, other_ref, bg_ref, vec_ref, far_w, own_w, rg_ref, ag_ref, atg_ref, sum_ref
):
    step = pl.program_id(0)
    gain = vec_ref[1:2, :]
    residual = res_ref[...]
    centered = residual - jnp.mean(residual, axis=-1, keepdims=True)
    rstd = lax.rsqrt(jnp.mean(centered * centered, axis=-1, keepdims=True) + NORM_EPS)
    xhat = centered * rstd
    mid_in = own_ref[...].astype(F32) + other_core(other_ref, step)
    gy = mid_in * gain
    through = rstd * (
        gy
        - jnp.mean(gy, axis=-1, keepdims=True)
        - xhat * jnp.mean(gy * xhat, axis=-1, keepdims=True)
    )
    total = bg_ref[...].astype(F32) + through
    low = total.astype(BF)
    ag_ref[...] = low
    lanes = 4 * HEAD_DIM
    feats = far_w.shape[0]
    for shard, w_ref in enumerate((far_w, own_w)):
        atg_ref[:, shard * lanes : shard * lanes + feats] = nt(low, w_ref[...]).astype(BF)
        atg_ref[:, shard * lanes + feats : (shard + 1) * lanes] = jnp.zeros(
            (low.shape[0], lanes - feats), BF
        )
    size = total.shape[0] // 2

    @pl.when(step == 0)
    def _():
        rg_ref[: 2 * size] = total
        sum_ref[...] = jnp.zeros_like(sum_ref)

    @pl.when(step == 2)
    def _():
        rg_ref[2 * size :] = total[:size]

    sum_ref[0:1, :] += jnp.sum(mid_in * xhat, axis=0, keepdims=True)
    sum_ref[1:2, :] += jnp.sum(mid_in, axis=0, keepdims=True)
    sum_ref[2:3, :] += jnp.sum(low.astype(F32), axis=0, keepdims=True)
    sum_ref[3:4, :] += jnp.sum(bg_ref[...].astype(F32), axis=0, keepdims=True)


def mid_backward(residual, own, other, bg, vectors, far_w, own_w, size):
    rows, width = own.shape
    lanes = 8 * HEAD_DIM
    block = pl.BlockSpec((2 * size, width), lambda i: (i, 0))
    return pl.pallas_call(
        mid_backward_kernel,
        grid=(3,),
        in_specs=[
            block,
            block,
            pl.BlockSpec((2 * size, width), lambda i: (other_pair(i), 0)),
            block,
            fixed((8, width)),
            fixed(far_w.shape),
            fixed(own_w.shape),
        ],
        out_specs=[
            pl.BlockSpec((rows // 2, width), lambda i: (0, 0)),
            block,
            pl.BlockSpec((2 * size, lanes), lambda i: (i, 0)),
            pl.BlockSpec((8, width), lambda i: (0, 0)),
        ],
        out_shape=[
            jax.ShapeDtypeStruct((rows // 2, width), F32),
            jax.ShapeDtypeStruct((rows, width), BF),
            jax.ShapeDtypeStruct((rows, lanes), BF),
            jax.ShapeDtypeStruct((8, width), F32),
        ],
        compiler_params=params(),
        cost_estimate=SMALL_COST,
        name="mid_backward",
    )(residual, own, other, bg, vectors, far_w, own_w)


def bias_row(ref):
    return ref[9 * HEAD_DIM : 9 * HEAD_DIM + 1].astype(F32)


def pad_heads(w_ref, padded_ref):
    lanes, feats = 4 * HEAD_DIM, 3 * HEAD_DIM
    for i in range(3):
        padded_ref[i * lanes : i * lanes + feats] = w_ref[i * feats : (i + 1) * feats]
        padded_ref[i * lanes + feats : (i + 1) * lanes] = jnp.zeros(
            (lanes - feats, w_ref.shape[1]), BF
        )


def first_kernel(x0, x1, x2, x3, vec_ref, far_ref, own_ref, normed_ref, qkv_ref, far_w, own_w, held_ref):
    @pl.when(pl.program_id(0) == 0)
    def _():
        pad_heads(far_ref, far_w)
        pad_heads(own_ref, own_w)

    stream = two_blocks(pl.program_id(0), (x0, x1, x2, x3), held_ref).astype(F32)
    centered = stream - jnp.mean(stream, axis=-1, keepdims=True)
    variance = jnp.mean(centered * centered, axis=-1, keepdims=True)
    normed = (
        centered * lax.rsqrt(variance + NORM_EPS) * vec_ref[4:5, :] + vec_ref[5:6, :]
    ).astype(BF)
    normed_ref[...] = normed
    third = far_w.shape[0]
    qkv_ref[:, :third] = (nt(normed, far_w[...]) + bias_row(far_ref)).astype(BF)
    qkv_ref[:, third:] = (nt(normed, own_w[...]) + bias_row(own_ref)).astype(BF)


def first(tokens, vectors, far, own, size):
    width = tokens[0].shape[1]
    rows = 8 * size
    outs = 6 * 4 * HEAD_DIM
    block = pl.BlockSpec((2 * size, width), lambda i: (i, 0))
    return pl.pallas_call(
        first_kernel,
        grid=(4,),
        in_specs=[fixed((2 * size, width))] * 4
        + [fixed((8, width)), fixed(far.shape), fixed(own.shape)],
        out_specs=[block, pl.BlockSpec((2 * size, outs), lambda i: (i, 0))],
        out_shape=[
            jax.ShapeDtypeStruct((rows, width), BF),
            jax.ShapeDtypeStruct((rows, outs), BF),
        ],
        scratch_shapes=[pltpu.VMEM((outs // 2, width), BF)] * 2
        + [pltpu.VMEM((2 * size, width), BF)],
        compiler_params=params(),
        cost_estimate=SMALL_COST,
        name="first_norm_qkv",
    )(*tokens, vectors, far, own)


def first_in_kernel(far_d, own_d, far_ref, own_w_ref, own_ref, give_ref, far_w, own_w):
    step = pl.program_id(0)
    half = far_d.shape[0] // 2

    @pl.when(step == 0)
    def _():
        pad_heads(far_ref, far_w)
        pad_heads(own_w_ref, own_w)

    total = (nn(far_d[...], far_w[...]) + nn(own_d[...], own_w[...])).astype(BF)

    @pl.when(step == 0)
    def _():
        own_ref[: 2 * half] = total

    @pl.when(step == 1)
    def _():
        give_ref[: 2 * half] = total

    @pl.when(step == 2)
    def _():
        own_ref[2 * half : 3 * half] = total[:half]
        give_ref[2 * half : 3 * half] = total[half:]

    @pl.when(step == 3)
    def _():
        own_ref[3 * half :] = total[:half]
        give_ref[3 * half :] = total[half:]


def first_in(far_grad, own_grad, far, own, size):
    rows, lanes = far_grad.shape
    width = far.shape[1]
    block = pl.BlockSpec((2 * size, lanes), lambda i: (i, 0))
    whole = pl.BlockSpec((rows // 2, width), lambda i: (0, 0))
    return pl.pallas_call(
        first_in_kernel,
        grid=(4,),
        in_specs=[block, block, fixed(far.shape), fixed(own.shape)],
        out_specs=[whole, whole],
        out_shape=[jax.ShapeDtypeStruct((rows // 2, width), BF)] * 2,
        scratch_shapes=[pltpu.VMEM((lanes, width), BF)] * 2,
        compiler_params=params(),
        cost_estimate=SMALL_COST,
        name="first_in",
    )(far_grad, own_grad, far, own)


def first_backward_kernel(home_ref, away_ref, own_ref, got_ref, rg_ref, vec_ref, *refs):
    extra_ref, (in_ref, sum_ref) = (refs[0] if len(refs) == 3 else None), refs[-2:]
    stream = jnp.where(pl.program_id(0) == 0, home_ref[...], away_ref[...]).astype(F32)
    centered = stream - jnp.mean(stream, axis=-1, keepdims=True)
    rstd = lax.rsqrt(jnp.mean(centered * centered, axis=-1, keepdims=True) + NORM_EPS)
    xhat = centered * rstd
    grad = own_ref[...].astype(F32) + got_ref[...].astype(F32)
    if extra_ref is not None:
        grad = grad + extra_ref[...].astype(F32)
    gy = grad * vec_ref[4:5, :]
    through = rstd * (
        gy
        - jnp.mean(gy, axis=-1, keepdims=True)
        - xhat * jnp.mean(gy * xhat, axis=-1, keepdims=True)
    )
    in_ref[...] = (rg_ref[...] + through).astype(BF)

    @pl.when(pl.program_id(0) == 0)
    def _():
        sum_ref[...] = jnp.zeros_like(sum_ref)

    sum_ref[0:1, :] += jnp.sum(grad * xhat, axis=0, keepdims=True)
    sum_ref[1:2, :] += jnp.sum(grad, axis=0, keepdims=True)


def first_backward(tokens, own, got, residual_grad, vectors, extra, size, owned):
    width = tokens[0].shape[1]
    stride = owned[1] - owned[0] if len(owned) > 1 else 1
    block = pl.BlockSpec((size, width), lambda i: (owned[0] + stride * i, 0))
    home = pl.BlockSpec((size, width), lambda i: (owned[0], 0))
    away = pl.BlockSpec((size, width), lambda i: (0, 0))
    more = () if extra is None else (extra,)
    return pl.pallas_call(
        first_backward_kernel,
        grid=(len(owned),),
        in_specs=[home, away, block, block, block, fixed((8, width))]
        + [pl.BlockSpec((size, width), lambda i: (0, 0))] * len(more),
        out_specs=[
            pl.BlockSpec((size, width), lambda i: (i, 0)),
            pl.BlockSpec((8, width), lambda i: (0, 0)),
        ],
        out_shape=[
            jax.ShapeDtypeStruct((len(owned) * size, width), BF),
            jax.ShapeDtypeStruct((8, width), F32),
        ],
        compiler_params=params(),
        cost_estimate=SMALL_COST,
        name="first_backward",
    )(tokens[0], tokens[2], own, got, residual_grad, vectors, *more)


def dp_partners(count, bit):
    return [(d, d ^ bit) for d in range(count)]


def dp_bits():
    return [1 << i for i in range(lax.axis_size("dp").bit_length() - 1)]


def dp_swap(value, bit):
    return lax.ppermute(value, "dp", dp_partners(lax.axis_size("dp"), bit))


def upper(bit):
    return (lax.axis_index("dp") & bit) != 0


def in_order(value, got, bit, axis=0):
    return jnp.where(
        upper(bit),
        jnp.concatenate([got, value], axis=axis),
        jnp.concatenate([value, got], axis=axis),
    )


def double(value, bit, axis=0):
    return in_order(value, dp_swap(value, bit), bit, axis)


def dp_part(value, axis):
    bits = dp_bits()
    place = sum(jnp.where(upper(bit), value.shape[axis] // (2 * bit), 0) for bit in bits)
    return lax.dynamic_slice_in_dim(value, place, value.shape[axis] // (2 * bits[-1]), axis)


def dp_stages():
    bits = dp_bits()
    return [bits[:1]] + [bits[i : i + 2] for i in range(1, len(bits), 2)]


def masks(bits):
    if len(bits) == 1:
        return [bits[0]]
    return [bits[1], bits[0], bits[0] | bits[1]]


def member(bits):
    place = jnp.where(upper(bits[-1]), 1, 0)
    return place if len(bits) == 1 else place + jnp.where(upper(bits[0]), 2, 0)


class Step:
    def whole(self, value):
        with jax.named_scope(self.name):
            kept, give = self.split(value)
            return self.join(kept, [dp_swap(x, mask) for x, mask in zip(give, self.masks)])


class Scatter(Step):
    def __init__(self, name, bits):
        self.name, self.masks = name, masks(bits)
        self.bits = bits

    def split(self, value):
        rows = value.shape[0] // (2 ** len(self.bits))
        mine = member(self.bits)
        pieces = [
            lax.dynamic_slice_in_dim(value, (mine ^ distance) * rows, rows, 0)
            for distance in range(2 ** len(self.bits))
        ]
        return pieces[0], [piece.astype(BF) for piece in pieces[1:]]

    def join(self, kept, got):
        total = kept.astype(F32)
        for piece in got:
            total = total + piece.astype(F32)
        return total


class Gather(Step):
    def __init__(self, name, bits):
        self.name, self.masks = name, masks(bits)
        self.bits = bits

    def split(self, value):
        value = value.astype(BF)
        return value, [value] * len(self.masks)

    def join(self, kept, got):
        if len(self.bits) == 1:
            return in_order(kept, got[0], self.bits[0])
        low = in_order(kept, got[0], self.bits[1])
        return in_order(low, in_order(got[1], got[2], self.bits[1]), self.bits[0])


class GatherAndAdd(Gather):
    def split(self, value):
        pieces, total = value
        rows = -(-total.shape[0] // 16) * 16
        total_low = jnp.pad(total.astype(BF), ((0, rows - total.shape[0]), (0, 0)))
        message = jnp.concatenate([total_low, pieces], axis=0)
        return (pieces, total), [message] * len(self.masks)

    def join(self, kept, got):
        pieces, total = kept
        rows = -(-total.shape[0] // 16) * 16
        for message in got:
            total = total + message[: total.shape[0]].astype(F32)
        return super().join(pieces, [message[rows:] for message in got]), total


def exchange(values, steps, *held):
    values, held = lax.optimization_barrier((tuple(values), held))
    halves = []
    for value, step in zip(values, steps):
        with jax.named_scope(step.name):
            halves.append(step.split(value))
    halves, held = lax.optimization_barrier((halves, held))
    joined = []
    for (kept, give), step in zip(halves, steps):
        with jax.named_scope(step.name):
            got = [dp_swap(piece, mask) for piece, mask in zip(give, step.masks)]
            joined.append((kept, got))

    def finish():
        out = []
        for (kept, got), step in zip(joined, steps):
            with jax.named_scope(step.name):
                out.append(step.join(kept, got))
        return out

    return finish, held


def sum_over_tensor(value):
    diagonal = ((0, 3), (1, 2), (2, 1), (3, 0))
    return value + core_swap(value) + x_swap(value) + lax.ppermute(value, "tensor", diagonal)


def after(value, *earlier):
    return lax.optimization_barrier((value,) + earlier)[0]


def body(
    hidden_in,
    doc_ids,
    first_gain,
    first_shift,
    qkv_weight,
    qv_bias,
    proj_weight,
    proj_bias,
    second_gain,
    second_shift,
    up_weight,
    up_bias,
    down_weight,
    down_bias,
    out_grad,
):
    size, rows_dev, width = hidden_in.shape
    length = doc_ids.shape[0]
    place = lax.axis_index("tensor")
    right = place >= 2
    feats = qkv_weight.shape[2]
    inner = up_weight.shape[1]

    def split_rows(value):
        first, mid, last = value[:, 0], value[:, 1], value[:, 2]
        return jnp.where(right, last, first), mid, jnp.where(right, first, last)

    def join_rows(main, mid, other):
        return jnp.stack(
            [jnp.where(right, other, main), mid, jnp.where(right, main, other)], axis=1
        )

    def head_sums(sums_own, sums_far, up_sums):
        slots = []
        for own, away in (
            (up_sums[0:1], up_sums[1:2]),
            (sums_own[:2, :feats].reshape(1, -1), sums_far[:2, :feats].reshape(1, -1)),
        ):
            index = lax.broadcasted_iota(jnp.int32, (4, own.shape[1]), 0)
            value = jnp.where(index == place, own, jnp.where(index == place ^ 2, away, 0.0))
            slots.append(value.reshape(-1, width))
        return slots

    pieces = jnp.stack([dp_part(up_weight, 0), dp_part(down_weight, 0)])
    with jax.named_scope("mlp_weights_x"):
        far_mlp = x_swap(pieces)

    space = jnp.zeros((4 * HEAD_DIM - feats,), BF)
    biases = jnp.concatenate(
        [qv_bias[0], space, jnp.zeros((4 * HEAD_DIM,), BF), qv_bias[1], space, up_bias]
    ).reshape(2, width)
    qkv_own = jnp.concatenate(
        [
            jnp.transpose(qkv_weight, (1, 2, 0)).reshape(3 * feats, width),
            jnp.pad(biases, ((0, 14), (0, 0))),
        ],
        axis=0,
    )

    main, mid, away = split_rows(hidden_in)
    home = jnp.concatenate([main, mid], axis=0)
    with jax.named_scope("tokens"):
        far = x_swap(jnp.concatenate([away, mid], axis=0))
        near = core_swap(home)
        far_near = core_swap(far)
    tokens = (home, near, far, far_near)

    with jax.named_scope("qkv_weights_x"):
        qkv_far = x_swap(qkv_own)
    local_ids = lax.dynamic_slice_in_dim(doc_ids, place * size, size, 0)
    cot = jnp.where((local_ids >= 0)[:, :, None], out_grad, jnp.zeros_like(out_grad))
    g_main, g_mid, g_away = split_rows(cot)
    g_home = jnp.concatenate([g_main, g_mid], axis=0)
    start_rows, table, vectors = prepare(
        doc_ids,
        place,
        (proj_bias, second_gain, second_shift, down_bias, first_gain, first_shift),
        size,
    )

    with jax.named_scope("mlp_weights_dp"):
        far_mlp, qkv_own, g_home, g_away = lax.optimization_barrier(
            (far_mlp, qkv_own, g_home, g_away)
        )
        for bit in reversed(dp_bits()[1:]):
            far_mlp, table, start_rows, vectors = lax.optimization_barrier(
                (double(far_mlp, bit, 1), table, start_rows, vectors)
            )
        far_mlp, held, tokens = lax.optimization_barrier((far_mlp, qkv_far, tokens))
        got_mlp = dp_swap(far_mlp, dp_bits()[0])

    with jax.named_scope("cotangent"):
        g_near = core_swap(g_home)
        g_far = x_swap(after(g_away, held))
        g_far_near = core_swap(g_far)

    with jax.named_scope("proj_weight_x"):
        proj_far = x_swap(after(proj_weight, held))
    normed, qkv = first(tokens, vectors, held, qkv_own, size)
    attended, lse = attend_forward(qkv, table, start_rows, size)
    attn_part = project(after(attended, g_far, g_near, got_mlp), proj_far, proj_weight, size)
    with jax.named_scope("attn_core"):
        attn_other = core_swap(attn_part)
    far_mlp = in_order(far_mlp, got_mlp, dp_bits()[0], 1)

    residual, normed_mid, act, hidden_grad, out_own, out_give, mid_part, up_sums, branch_grad = mlp(
        tokens, attn_part, attn_other, (g_home, g_near, g_far, g_far_near), vectors, qkv_own, held,
        up_weight, down_weight, far_mlp, size,
    )

    stages = dp_stages()
    first_stage, high_stages = stages[0], stages[1:]

    with jax.named_scope("mid_core"):
        mid_other = core_swap(mid_part)
    down_away = sum_tokens(act, branch_grad, part=1)
    with jax.named_scope("down_grad_x"):
        down_got = x_swap(down_away)
    residual_grad, attn_grad, attended_grad, mid_sums = mid_backward(
        after(residual, down_away), mid_part, mid_other, branch_grad, vectors,
        proj_far, proj_weight, size,
    )

    act, hidden_grad, out_own, out_give, attended_grad = lax.optimization_barrier(
        (act, hidden_grad, out_own, out_give, attended_grad)
    )
    up_away = sum_tokens(normed_mid, hidden_grad, part=1, room=feats)
    up_away = sum_tokens(attended, attn_grad, rows=feats, count=1, into=up_away)
    with jax.named_scope("up_proj_grad_x"):
        up_got = x_swap(up_away)
    d_far, sums_far = attend_backward(
        qkv, attended, after(attended_grad, up_away), lse, table, start_rows, size, 0
    )
    qkv_away = sum_tokens(d_far, normed, rows=feats)
    with jax.named_scope("qkv_grad_x"):
        qkv_got = x_swap(qkv_away)
    down = sum_tokens(act, after(branch_grad, qkv_away), down_got, F32)
    with jax.named_scope("block_out"):
        out_got = core_swap(after(out_give, down))
    d_own, sums_own = attend_backward(
        qkv, attended, after(attended_grad, down), lse, table, start_rows, size, 1
    )
    d, u, t, n = "down_grad_dp", "up_proj_grad_dp", "qkv_grad_dp", "small_sums"
    finish, (attended_grad,) = exchange([down], [Scatter(d, first_stage)], attended_grad)
    d_own, sums_own = attend_backward(
        qkv, attended, attended_grad, lse, table, start_rows, size, 1
    )
    (down,) = finish()
    d_own, down, up_got, out_got = lax.optimization_barrier((d_own, down, up_got, out_got))

    singles = [[bit] for bit in dp_bits()[1:]]
    finish, (hidden_grad, up_got) = exchange(
        [down], [Scatter(d, singles[0])], hidden_grad, up_got
    )
    up = sum_tokens(normed_mid, hidden_grad, up_got, F32, room=feats)
    up = sum_tokens(attended, attn_grad, up_got, F32, rows=feats, first=1, count=1, into=up)
    with jax.named_scope("block_out"):
        out_full = (out_own + out_got.astype(F32)).astype(BF)
    (down,) = finish()
    up, down, out_full = lax.optimization_barrier((up, down, out_full))

    finish, (d_own, qkv_got, out_full) = exchange(
        [up, down], [Scatter(u, first_stage), Scatter(d, singles[1])], d_own, qkv_got, out_full
    )
    tail = sum_tokens(d_own, normed, qkv_got, F32, rows=feats)
    own_in, give_in = first_in(d_far, after(d_own, tail), held, qkv_own, size)
    up, down = finish()
    for bits in singles[2:]:
        finish, _ = exchange([down], [Scatter(d, bits)])
        (down,) = finish()

    up_gathers = [Gather(u, bits) for bits in reversed(singles)]
    down_gathers = [Gather(d, bits) for bits in reversed(singles)]
    for step in down_gathers[:-2]:
        finish, _ = exchange([down], [step])
        (down,) = finish()
    steps = [Scatter(t, first_stage), Scatter(u, high_stages[0]), down_gathers[-2]]
    finish, (own_in, give_in, out_full) = exchange(
        [tail, up, down], steps, own_in, give_in, out_full
    )
    with jax.named_scope("first_core"):
        got_in = core_swap(give_in)
    mid_sum = (own_in[3 * size :].astype(F32) + got_in[3 * size :].astype(F32)).astype(BF)
    with jax.named_scope("first_mid_x"):
        extra = x_swap(mid_sum)
    in_main, sums_main = first_backward(
        tokens, own_in, got_in, residual_grad, vectors, None, size, (0, 2)
    )
    tail, up, down = finish()
    for bits in high_stages[1:]:
        finish, _ = exchange([up], [Scatter(u, bits)])
        (up,) = finish()
    for step in up_gathers[:-2]:
        finish, _ = exchange([up], [step])
        (up,) = finish()

    steps = [Scatter(t, high_stages[0]), up_gathers[-2], down_gathers[-1]]
    finish, (in_main, extra, out_full) = exchange(
        [tail, up, down], steps, in_main, extra, out_full
    )
    with jax.named_scope("in_grad_x"):
        in_away = x_swap(in_main[size:])
    in_mid, sums_mid = first_backward(
        tokens, own_in, got_in, residual_grad, vectors, extra, size, (1,)
    )
    tail, up, down = finish()
    small = jnp.concatenate(
        [(sums_main + sums_mid)[:2], 0.5 * mid_sums[:4], *head_sums(sums_own, sums_far, up_sums)],
        axis=0,
    )
    for bits in high_stages[1:]:
        finish, _ = exchange([tail], [Scatter(t, bits)])
        (tail,) = finish()

    finish, (tail, up, small, in_away, out_full) = exchange(
        [down], [Gather(d, first_stage)], tail, up, small, in_away, out_full
    )
    with jax.named_scope("small_sums"):
        small = sum_over_tensor(small)
    with jax.named_scope("block_out"):
        out_away = x_swap(out_full[2 * size :])
    (down,) = finish()
    steps = [GatherAndAdd(t, first_stage), up_gathers[-1]]
    finish, (down, out_away) = exchange([(tail.astype(BF), small), up], steps, down, out_away)
    (tail, small), up = finish()
    last = high_stages[-1] if len(high_stages[-1]) == 2 else high_stages[-2]
    rest = [bits for bits in high_stages if bits is not last]
    for bits in reversed(rest):
        finish, _ = exchange([(tail, small)], [GatherAndAdd(t, bits)])
        ((tail, small),) = finish()
    steps = [GatherAndAdd(t, last), Gather(u, first_stage)]
    finish, _ = exchange([(tail, small), up], steps)
    (tail, small), up = finish()
    tail = tail.reshape(-1, 2, tail.shape[0] // (2 ** len(dp_bits())), width)
    tail = jnp.transpose(tail, (1, 0, 2, 3)).reshape(3 * feats, width)

    block_out = join_rows(out_full[:size], out_full[size : 2 * size], out_away)
    in_grad = join_rows(in_main[:size], in_mid, in_away)

    up_bias_grad = lax.dynamic_slice_in_dim(small, 6 + place, 1, 0)[0]
    qv_all = small[10:].reshape(4, 2, feats)
    qv_bias_grad = lax.dynamic_slice_in_dim(qv_all, place, 1, 0)[0]

    qkv_weight_grad = jnp.transpose(
        tail.reshape(3, feats, width), (2, 0, 1)
    ).astype(F32)
    return (
        block_out,
        in_grad,
        small[0],
        small[1],
        qkv_weight_grad,
        qv_bias_grad,
        up[inner:].astype(F32),
        small[4],
        small[2],
        small[3],
        up[:inner].astype(F32),
        up_bias_grad,
        down.astype(F32),
        small[5],
    )


def solution(mesh):
    in_specs = (
        P("tensor", "dp", None),
        P(None, "dp"),
        P(),
        P(),
        P(None, None, "tensor"),
        P(None, "tensor"),
        P("tensor", None),
        P(),
        P(),
        P(),
        P(None, "tensor"),
        P("tensor"),
        P("tensor", None),
        P(),
        P("tensor", "dp", None),
    )
    out_specs = (
        P("tensor", "dp", None),
        P("tensor", "dp", None),
        P(),
        P(),
        P(None, None, "tensor"),
        P(None, "tensor"),
        P("tensor", None),
        P(),
        P(),
        P(),
        P(None, "tensor"),
        P("tensor"),
        P("tensor", None),
        P(),
    )
    return jax.shard_map(body, mesh=mesh, in_specs=in_specs, out_specs=out_specs, check_vma=False)
```

time: 387 us -> 364 us (0.941)
  Pallas kernels: 109 us -> 162 us
  matrix products: 27.9 us -> 0 us
  local copies, waits for them, and re-layouts: 44 us -> 22.3 us
  other arithmetic: 41.9 us -> 25.8 us
  starting transfers between devices: 54.6 us -> 46.9 us
    pallas_call x5 -> x15, Pallas kernels: 54 us -> 107 us  [the longest x8 44.2 us: sum_tokens(): pl.pallas_call(functools.partial(sum_tokens_kernel, rows, extra is not No...]
    dot_general x8 -> x0, matrix products: 27.9 us -> none  [the longest x7 25.4 us: tn(): lax.dot_general(left, right, (((0,), (0,)), ((), ())), preferred_element_...]
    another operation x21 -> x0, local copies, waits for them, and re-layouts: 9.9 us -> none  [the longest x7 8.38 us: body(): jnp.stack([proj_bias, second_gain, second_shift, down_bias, first_gain, f...]
    ppermute x14 -> x12, waiting for transfers between devices: 32.4 us -> 23 us  [x_swap(): return lax.ppermute(value, 'tensor', X_SWAP)]
    unnamed x96 -> x62, local copies, waits for them, and re-layouts: 14.3 us -> 7.64 us
    ppermute x24, starting transfers between devices: 33.7 us -> 29.5 us  [dp_swap(): return lax.ppermute(value, 'dp', dp_partners(lax.axis_size('dp'), bit))]
    ppermute x14 -> x12, starting transfers between devices: 19.4 us -> 15.3 us  [x_swap(): return lax.ppermute(value, 'tensor', X_SWAP)]
    convert_element_type x7 -> x6, other arithmetic: 7.9 us -> 4.17 us  [the longest x1 1.58 us: body(): up[:inner].astype(F32)]
  transfers between devices with their start and end apart: 47 -> 46, of which waited for: 16 -> 20; matrix products, arithmetic and copies ran while one was open for 24% -> 8% of each run, Pallas kernels for 22% -> 36%
where the time goes in v1:
time: 364 us; the launch traced here: 357 us
  Pallas kernels  162 us (45%)
  waiting for transfers between devices  98.6 us (27%)
  starting transfers between devices  46.9 us (13%)
  other arithmetic  25.8 us (7%)
  local copies, waits for them, and re-layouts  22.3 us (6%)
    ppermute x24, waiting for transfers between devices, dp_swap(): return lax.ppermute(value, 'dp', dp_partners(lax.axis_size('dp'), bit))  72.2 us
    pallas_call x8, Pallas kernels, sum_tokens(): pl.pallas_call(functools.partial(sum_tokens_kernel, rows, extra is not No...  44.2 us
    ppermute x24, starting transfers between devices, dp_swap(): return lax.ppermute(value, 'dp', dp_partners(lax.axis_size('dp'), bit))  29.5 us
    pallas_call x2, Pallas kernels, attend_backward(): pl.pallas_call(functools.partial(attend_backward_kernel, size), grid_spec...  28 us
    pallas_call x1, Pallas kernels, mlp(): pl.pallas_call(mlp_kernel, grid=(3,), in_specs=[fixed((2 * size, width))]...  27.9 us
    ppermute x12, waiting for transfers between devices, x_swap(): return lax.ppermute(value, 'tensor', X_SWAP)  23 us
    pallas_call x1, Pallas kernels, attend_forward(): pl.pallas_call(functools.partial(attend_forward_kernel, size), grid_spec=...  17 us
    ppermute x12, starting transfers between devices, x_swap(): return lax.ppermute(value, 'tensor', X_SWAP)  15.3 us
  transfers between devices with their start and end apart: 46, of which 20 were waited for; matrix products, arithmetic and copies ran while one was open for 8% of the time, Pallas kernels for 36%

profile of v1, /device:TPU:8, one launch (start us, length us, event | category | flops | bytes accessed | tf_op | source)
XLA Modules:
  0.0 357.2 jit_solution(13635990502794203915)
XLA Ops:
  2.5 1.5 collective-permute-start
  9.1 3.7 %collective-permute-done = bf16[2,96,768]{2,1,0:T(8,128)(2,1)} collective-permute-done((bf16[2,96,768]{2,1,0:T(8,128)(2,1)}, bf16[2,96,768]{2,1,0:T(8,128)(2,1)}, u32[]{:S(2)}, u32[]{:S(2)}) %collective-permute-start) | collective-permute-done | bytes 294944 | tf_op jit(solution)/shard_map/mlp_weights_x/ppermute | solution.py:25
  12.7 2.6 collective-permute-start.1
  15.3 1.5 collective-permute-start.3
  17.4 1.8 prepare.1
  19.3 10.2 %collective-permute-done.5.x2.away_ref = bf16[512,768]{1,0:T(8,128)(2,1)S(1)} collective-permute-done((bf16[512,768]{1,0:T(8,128)(2,1)}, bf16[512,768]{1,0:T(8,128)(2,1)S(1)}, u32[]{:S(2)}, u32[]{:S(2)}) %collective-permute-start.5) | collective-permute-done | bytes 786464 | tf_op jit(solution)/shard_map/tokens/ppermute | solution.py:25
  29.5 1.7 maximum_select_fusion.6
  31.3 15.4 %collective-permute-done.2 = bf16[2,192,768]{2,1,0:T(8,128)(2,1)S(1)} collective-permute-done((bf16[2,192,768]{2,1,0:T(8,128)(2,1)S(1)}, bf16[2,192,768]{2,1,0:T(8,128)(2,1)S(1)}, u32[]{:S(2)}, u32[]{:S(2)}) %collective-permute-start.2) | collective-permute-done | bytes 589856 | tf_op jit(solution)/shard_map/mlp_weights_dp/ppermute | solution.py:771
  47.8 1.6 collective-permute-start.9
  49.4 1.5 collective-permute-start.7
  51.5 11.1 %first_norm_qkv.1 = (bf16[2048,768]{1,0:T(8,128)(2,1)}, bf16[2048,1536]{1,0:T(8,128)(2,1)}) custom-call(bf16[512,768]{1,0:T(8,128)(2,1)} %copy-done.1, bf16[512,768]{1,0:T(8,128)(2,1)} %collective-permute-done.4.x1, bf16[512,768]{1,0:T(8,128)(2,1)} %copy-done.3, bf16[512,768]{1,0:T(8,128)(2,1)} %copy-done.9, f32[8,768]{1,0:T(8,128)} %get-tuple-element.190.vec_ref, ...), custom_call_target="tpu_custom_call" | custom-call | flops 1 | bytes 1 | tf_op jit(solution)/shard_map/first_norm_qkv/pallas_call | solution.py:645
  62.6 17.0 %attend_forward.1 = (bf16[1536,512]{1,0:T(8,128)(2,1)}, f32[16,1536]{1,0:T(8,128)}) custom-call(s32[8,8]{1,0:T(8,128)} %get-tuple-element.183.table, s32[8,1536]{1,0:T(8,128)} %get-tuple-element.184.start_ref, bf16[2048,1536]{1,0:T(8,128)(2,1)} %get-tuple-element.193.q_ref.k_ref.v_ref, bf16[2048,1536]{1,0:T(8,128)(2,1)} %get-tuple-element.193.q_ref.k_ref.v_ref, ...), custom_call_target="tpu_custom_call" | custom-call | flops 1 | bytes 1 | tf_op jit(solution)/shard_map/attend_forward/pallas_call | solution.py:136
  81.1 4.6 %project.1.own_ref = bf16[1536,768]{1,0:T(8,128)(2,1)} custom-call(bf16[1536,512]{1,0:T(8,128)(2,1)} %get-tuple-element.199.heads_ref.left_ref.out_ref, bf16[192,768]{1,0:T(8,128)(2,1)} %copy-done.15, bf16[192,768]{1,0:T(8,128)(2,1)} %own_w.3), custom_call_target="tpu_custom_call" | custom-call | flops 1 | bytes 1 | tf_op jit(solution)/shard_map/project/pallas_call | solution.py:518
  86.2 1.7 maximum_select_fusion.up_far.dn_far
  87.9 3.1 collective-permute-done.12.b3
  91.7 1.4 copy-done.11
  93.1 27.9 %mlp.1 = (f32[1536,768]{1,0:T(8,128)}, bf16[1536,768]{1,0:T(8,128)(2,1)}, bf16[2,1536,768]{2,1,0:T(8,128)(2,1)}, bf16[2,1536,768]{2,1,0:T(8,128)(2,1)}, f32[768,...) custom-call(bf16[512,768]{1,0:T(8,128)(2,1)} %copy-done.1, ...), custom_call_target="tpu_custom_call" | custom-call | flops 1 | bytes 1 | tf_op jit(solution)/shard_map/mlp/pallas_call | solution.py:419
  121.2 5.6 %sum_tokens.8 = bf16[768,768]{1,0:T(8,128)(2,1)} custom-call(bf16[2,1536,768]{2,1,0:T(8,128)(2,1)} %get-tuple-element.211.left_ref, bf16[1536,768]{1,0:T(8,128)(2,1)} %get-tuple-element.219.right_ref.bg_ref), custom_call_target="tpu_custom_call" | custom-call | flops 1 | bytes 1 | tf_op jit(solution)/shard_map/sum_tokens/pallas_call | solution.py:495
  126.8 3.8 %collective-permute-start.14 = (bf16[768,768]{1,0:T(8,128)(2,1)}, bf16[768,768]{1,0:T(8,128)(2,1)S(1)}, u32[]{:S(2)}, u32[]{:S(2)}) collective-permute-start(bf16[768,768]{1,0:T(8,128)(2,1)} %sum_tokens.8), channel_id=1, source_target_pairs={{0,2},{1,3},{2,0},{3,1},{4,6},{5,7},{6,4},{7,5},{8,10},{9,11},{10,... | collective-permute-start | bytes 3538952 | tf_op jit(solution)/shard_map/down_grad_x/ppermute | solution.py:25
  130.7 1.4 copy-done.13
  132.1 10.4 %mid_backward.1 = (f32[768,768]{1,0:T(8,128)}, bf16[1536,768]{1,0:T(8,128)(2,1)}, bf16[1536,512]{1,0:T(8,128)(2,1)}, f32[8,768]{1,0:T(8,128)}) custom-call(f32[1536,768]{1,0:T(8,128)} %get-tuple-element.204.res_ref, bf16[1536,768]{1,0:T(8,128)(2,1)} %get-tuple-element.205.own_ref, bf16[1536,768]{1,0:T(8,128)(2,1)} %copy-done.13, ...), custom_call_target="tpu_custom_call" | custom-call | flops 1 | bytes 1 | tf_op jit(solution)/shard_map/mid_backward/pallas_call | solution.py:579
  142.5 5.6 %sum_tokens.9.refs_0_ = bf16[960,768]{1,0:T(8,128)(2,1)} custom-call(bf16[1536,768]{1,0:T(8,128)(2,1)} %get-tuple-element.213.left_ref, bf16[2,1536,768]{2,1,0:T(8,128)(2,1)} %get-tuple-element.234.right_ref), custom_call_target="tpu_custom_call" | custom-call | flops 1 | bytes 1 | tf_op jit(solution)/shard_map/sum_tokens/pallas_call | solution.py:495
  148.1 3.4 sum_tokens.10
  151.6 14.0 %attend_backward.2 = (bf16[2048,768]{1,0:T(8,128)(2,1)}, f32[8,256]{1,0:T(8,128)}) custom-call(s32[8,8]{1,0:T(8,128)} %get-tuple-element.183.table, s32[8,1536]{1,0:T(8,128)} %get-tuple-element.184.start_ref, bf16[2048,1536]{1,0:T(8,128)(2,1)} %get-tuple-element.193.q_ref.k_ref.v_ref, bf16[2048,1536]{1,0:T(8,128)(2,1)} %get-tuple-element.193.q_ref.k_ref.v_ref, ...), custom_call_target="tpu_custom_call" | custom-call | flops 1 | bytes 1 | tf_op jit(solution)/shard_map/attend_backward/pallas_call | solution.py:229
  165.6 6.3 %sum_tokens.11 = bf16[576,768]{1,0:T(8,128)(2,1)} custom-call(bf16[2048,768]{1,0:T(8,128)(2,1)} %get-tuple-element.217.left_ref.far_d, bf16[2048,768]{1,0:T(8,128)(2,1)} %get-tuple-element.218.right_ref), custom_call_target="tpu_custom_call" | custom-call | flops 1 | bytes 1 | tf_op jit(solution)/shard_map/sum_tokens/pallas_call | solution.py:495
  172.9 6.1 %sum_tokens.12 = f32[768,768]{1,0:T(8,128)} custom-call(bf16[2,1536,768]{2,1,0:T(8,128)(2,1)} %get-tuple-element.211.left_ref, bf16[1536,768]{1,0:T(8,128)(2,1)} %get-tuple-element.219.right_ref.bg_ref, bf16[768,768]{1,0:T(8,128)(2,1)} %copy-done.18), custom_call_target="tpu_custom_call" | custom-call | flops 1 | bytes 1 | tf_op jit(solution)/shard_map/sum_tokens/pallas_call | solution.py:495
  180.4 1.4 constant_dynamic-slice_fusion.8
  182.1 3.2 collective-permute-start.19
  185.3 14.0 %attend_backward.3 = (bf16[2048,768]{1,0:T(8,128)(2,1)}, f32[8,256]{1,0:T(8,128)}) custom-call(s32[8,8]{1,0:T(8,128)} %get-tuple-element.183.table, s32[8,1536]{1,0:T(8,128)} %get-tuple-element.184.start_ref, bf16[2048,1536]{1,0:T(8,128)(2,1)} %get-tuple-element.193.q_ref.k_ref.v_ref, bf16[2048,1536]{1,0:T(8,128)(2,1)} %get-tuple-element.193.q_ref.k_ref.v_ref, ...), custom_call_target="tpu_custom_call" | custom-call | flops 1 | bytes 1 | tf_op jit(solution)/shard_map/attend_backward/pallas_call | solution.py:229
  201.6 6.4 %sum_tokens.13.refs_1_ = f32[960,768]{1,0:T(8,128)} custom-call(bf16[1536,768]{1,0:T(8,128)(2,1)} %get-tuple-element.213.left_ref, bf16[2,1536,768]{2,1,0:T(8,128)(2,1)} %get-tuple-element.234.right_ref, bf16[960,768]{1,0:T(8,128)(2,1)} %copy-done.6), custom_call_target="tpu_custom_call" | custom-call | flops 1 | bytes 1 | tf_op jit(solution)/shard_map/sum_tokens/pallas_call | solution.py:495
  208.1 3.7 %sum_tokens.14 = f32[960,768]{1,0:T(8,128)} custom-call(bf16[1536,512]{1,0:T(8,128)(2,1)} %get-tuple-element.199.heads_ref.left_ref.out_ref, bf16[1536,768]{1,0:T(8,128)(2,1)} %get-tuple-element.206.right_ref, bf16[960,768]{1,0:T(8,128)(2,1)} %copy-done.6, f32[960,768]{1,0:T(8,128)} %sum_tokens.13.refs_1_), custom_call_target="tpu_custom_call", output_to_operand_aliasing={{}: (3, {})} | custom-call | flops 1 | bytes 1 | tf_op jit(solution)/shard_map/sum_tokens/pallas_call | solution.py:495
  211.8 1.7 add_convert_fusion
  213.5 3.8 %collective-permute-done.18 = bf16[192,768]{1,0:T(8,128)(2,1)S(1)} collective-permute-done((bf16[192,768]{1,0:T(8,128)(2,1)S(1)}, bf16[192,768]{1,0:T(8,128)(2,1)S(1)}, u32[]{:S(2)}, u32[]{:S(2)}) %collective-permute-start.18) | collective-permute-done | bytes 294944 | tf_op jit(solution)/shard_map/down_grad_dp/ppermute | solution.py:771
  218.4 2.4 collective-permute-start.20
  220.8 1.9 collective-permute-start.21
  222.7 7.0 %sum_tokens.15 = f32[576,768]{1,0:T(8,128)} custom-call(bf16[2048,768]{1,0:T(8,128)(2,1)} %get-tuple-element.254.left_ref.own_d, bf16[2048,768]{1,0:T(8,128)(2,1)} %get-tuple-element.218.right_ref, bf16[576,768]{1,0:T(8,128)(2,1)} %collective-permute-done.19.refs_0_), custom_call_target="tpu_custom_call" | custom-call | flops 1 | bytes 1 | tf_op jit(solution)/shard_map/sum_tokens/pallas_call | solution.py:495
  229.8 9.7 %first_in.1 = (bf16[1024,768]{1,0:T(8,128)(2,1)}, bf16[1024,768]{1,0:T(8,128)(2,1)}) custom-call(bf16[2048,768]{1,0:T(8,128)(2,1)} %get-tuple-element.217.left_ref.far_d, bf16[2048,768]{1,0:T(8,128)(2,1)} %get-tuple-element.254.left_ref.own_d, bf16[592,768]{1,0:T(8,128)(2,1)} %copy-done.4, bf16[592,768]{1,0:T(8,128)(2,1)} %copy-done.2), custom_call_target="tpu_custom_call" | custom-call | flops 1 | bytes 1 | tf_op jit(solution)/shard_map/first_in/pallas_call | solution.py:698
  239.6 1.4 convert_add_fusion
  247.7 2.0 collective-permute-start.23
  251.3 7.1 %collective-permute-done.26 = bf16[96,768]{1,0:T(8,128)(2,1)S(1)} collective-permute-done((bf16[96,768]{1,0:T(8,128)(2,1)S(1)}, bf16[96,768]{1,0:T(8,128)(2,1)S(1)}, u32[]{:S(2)}, u32[]{:S(2)}) %collective-permute-start.26) | collective-permute-done | bytes 147488 | tf_op jit(solution)/shard_map/down_grad_dp/ppermute | solution.py:771
  258.5 1.4 add_convert_fusion.1
  259.9 1.4 collective-permute-start.28
  261.3 5.0 %collective-permute-done.23 = bf16[120,768]{1,0:T(8,128)(2,1)S(1)} collective-permute-done((bf16[120,768]{1,0:T(8,128)(2,1)}, bf16[120,768]{1,0:T(8,128)(2,1)S(1)}, u32[]{:S(2)}, u32[]{:S(2)}) %collective-permute-start.23) | collective-permute-done | bytes 184352 | tf_op jit(solution)/shard_map/up_proj_grad_dp/ppermute | solution.py:771
  266.4 5.3 %collective-permute-done.25 = bf16[120,768]{1,0:T(8,128)(2,1)S(1)} collective-permute-done((bf16[120,768]{1,0:T(8,128)(2,1)S(1)}, bf16[120,768]{1,0:T(8,128)(2,1)S(1)}, u32[]{:S(2)}, u32[]{:S(2)}) %collective-permute-start.25) | collective-permute-done | bytes 184352 | tf_op jit(solution)/shard_map/up_proj_grad_dp/ppermute | solution.py:771
  271.8 3.9 %first_backward.2 = (bf16[512,768]{1,0:T(8,128)(2,1)}, f32[8,768]{1,0:T(8,128)}) custom-call(bf16[512,768]{1,0:T(8,128)(2,1)} %copy-done.1, bf16[512,768]{1,0:T(8,128)(2,1)} %copy-done.3, bf16[1024,768]{1,0:T(8,128)(2,1)} %get-tuple-element.272.own_ref, bf16[1024,768]{1,0:T(8,128)(2,1)} %copy-done.5, f32[768,768]{1,0:T(8,128)} %get-tuple-element.274.rg_ref, ...), custom_call_target="tpu_custom_call" | custom-call | flops 1 | bytes 1 | tf_op jit(solution)/shard_map/first_backward/pallas_call | solution.py:743
  275.8 2.4 collective-permute-start.33
  278.8 1.5 collective-permute-start.31
  283.8 3.2 first_backward.3
  287.7 5.5 %collective-permute-done.30 = bf16[72,768]{1,0:T(8,128)(2,1)S(1)} collective-permute-done((bf16[72,768]{1,0:T(8,128)(2,1)S(1)}, bf16[72,768]{1,0:T(8,128)(2,1)S(1)}, u32[]{:S(2)}, u32[]{:S(2)}) %collective-permute-start.30) | collective-permute-done | bytes 110624 | tf_op jit(solution)/shard_map/qkv_grad_dp/ppermute | solution.py:771
  293.6 1.7 collective-permute-done.32
  296.6 6.4 %collective-permute-done.34 = bf16[256,768]{1,0:T(8,128)(2,1)S(1)} collective-permute-done((bf16[256,768]{1,0:T(8,128)(2,1)S(1)}, bf16[256,768]{1,0:T(8,128)(2,1)S(1)}, u32[]{:S(2)}, u32[]{:S(2)}) %collective-permute-start.34) | collective-permute-done | bytes 393248 | tf_op jit(solution)/shard_map/in_grad_x/ppermute | solution.py:25
  304.4 1.5 collective-permute-start.37
  306.5 2.1 collective-permute-done.36
  308.9 7.7 %collective-permute-done.38 = bf16[384,768]{1,0:T(8,128)(2,1)} collective-permute-done((bf16[384,768]{1,0:T(8,128)(2,1)S(1)}, bf16[384,768]{1,0:T(8,128)(2,1)}, u32[]{:S(2)}, u32[]{:S(2)}) %collective-permute-start.38) | collective-permute-done | bytes 589856 | tf_op jit(solution)/shard_map/down_grad_dp/ppermute | solution.py:771
  316.5 1.6 maximum_select_fusion.3
  318.7 1.4 collective-permute-start.40
  321.2 2.5 collective-permute-done.40
  323.8 4.2 %collective-permute-done.41 = bf16[240,768]{1,0:T(8,128)(2,1)S(1)} collective-permute-done((bf16[240,768]{1,0:T(8,128)(2,1)S(1)}, bf16[240,768]{1,0:T(8,128)(2,1)S(1)}, u32[]{:S(2)}, u32[]{:S(2)}) %collective-permute-start.41) | collective-permute-done | bytes 368672 | tf_op jit(solution)/shard_map/up_proj_grad_dp/ppermute | solution.py:771
  328.3 2.3 collective-permute-start.44
  330.6 2.6 collective-permute-start.43
  333.3 1.6 convert_element_type.180
  337.0 10.2 %collective-permute-done.44 = bf16[160,768]{1,0:T(8,128)(2,1)S(1)} collective-permute-done((bf16[160,768]{1,0:T(8,128)(2,1)S(1)}, bf16[160,768]{1,0:T(8,128)(2,1)S(1)}, u32[]{:S(2)}, u32[]{:S(2)}) %collective-permute-start.44) | collective-permute-done | bytes 245792 | tf_op jit(solution)/shard_map/qkv_grad_dp/ppermute | solution.py:771
  347.4 3.0 collective-permute-done.42
  354.3 1.6 slice_convert_fusion
  (203 shorter events, 45.2 us)
Async XLA Ops:
  0.6 3.4 copy-start.16
  2.5 10.2 %collective-permute-start = (bf16[2,96,768]{2,1,0:T(8,128)(2,1)}, bf16[2,96,768]{2,1,0:T(8,128)(2,1)}, u32[]{:S(2)}, u32[]{:S(2)}) collective-permute-start(bf16[2,96,768]{2,1,0:T(8,128)(2,1)} %pad_maximum_fusion.5), channel_id=1, source_target_pairs={{0,2},{1,3},{2,0},{3,1},{4,6},{5,7},{6,4},{7,5},{8,10},{9,11},{10,... | collective-permute-start | bytes 884744 | tf_op jit(solution)/shard_map/mlp_weights_x/ppermute | solution.py:25
  5.2 11.7 %copy-start.1 = (bf16[512,768]{1,0:T(8,128)(2,1)}, bf16[512,768]{1,0:T(8,128)(2,1)S(1)}, u32[]{:S(2)}) copy-start(bf16[512,768]{1,0:T(8,128)(2,1)S(1)} %get-tuple-element.186.x0.home_ref) | copy-start | bytes 2359300
  5.2 24.3 %collective-permute-start.5 = (bf16[512,768]{1,0:T(8,128)(2,1)}, bf16[512,768]{1,0:T(8,128)(2,1)S(1)}, u32[]{:S(2)}, u32[]{:S(2)}) collective-permute-start(bf16[512,768]{1,0:T(8,128)(2,1)} %get-tuple-element.364), channel_id=1, source_target_pairs={{0,2},{1,3},{2,0},{3,1},{4,6},{5,7},{6,4},{7,5},{8,10},{9,11},{10,... | collective-permute-start | bytes 2359304 | tf_op jit(solution)/shard_map/tokens/ppermute | solution.py:25
  9.1 38.1 %copy-start.2 = (bf16[592,768]{1,0:T(8,128)(2,1)}, bf16[592,768]{1,0:T(8,128)(2,1)S(1)}, u32[]{:S(2)}) copy-start(bf16[592,768]{1,0:T(8,128)(2,1)S(1)} %fusion.1.own_ref.upb_own.own_w_ref) | copy-start | bytes 2727940
  12.7 16.8 %collective-permute-start.1 = (bf16[2,96,768]{2,1,0:T(8,128)(2,1)}, bf16[2,96,768]{2,1,0:T(8,128)(2,1)}, u32[]{:S(2)}, u32[]{:S(2)}) collective-permute-start(bf16[2,96,768]{2,1,0:T(8,128)(2,1)} %collective-permute-done), channel_id=1, source_target_pairs={{0,16},{4,20},{8,24},{12,28},{16,0},{20,4},{24,8},{28,12},{1,17},{... | collective-permute-start | bytes 884744 | tf_op jit(solution)/shard_map/mlp_weights_dp/ppermute | solution.py:771
  15.3 32.5 %collective-permute-start.3 = (bf16[592,768]{1,0:T(8,128)(2,1)S(1)}, bf16[592,768]{1,0:T(8,128)(2,1)S(1)}, u32[]{:S(2)}, u32[]{:S(2)}) collective-permute-start(bf16[592,768]{1,0:T(8,128)(2,1)S(1)} %fusion.1.own_ref.upb_own.own_w_ref), channel_id=1, source_target_pairs={{0,2},{1,3},{2,0},{3,1},{4,6},{5,7},{6,4},{7,5},{8,10},{9,11},{10,... | collective-permute-start | bytes 2727944 | tf_op jit(solution)/shard_map/qkv_weights_x/ppermute | solution.py:25
  16.8 30.4 %collective-permute-start.4 = (bf16[512,768]{1,0:T(8,128)(2,1)S(1)}, bf16[512,768]{1,0:T(8,128)(2,1)}, u32[]{:S(2)}, u32[]{:S(2)}) collective-permute-start(bf16[512,768]{1,0:T(8,128)(2,1)S(1)} %get-tuple-element.186.x0.home_ref), channel_id=1, source_target_pairs={{0,1},{1,0},{2,3},{3,2},{4,5},{5,4},{6,7},{7,6},{8,9},{9,8},{10,11... | collective-permute-start | bytes 2359304 | tf_op jit(solution)/shard_map/tokens/ppermute | solution.py:29
  29.5 17.7 %copy-start.3 = (bf16[512,768]{1,0:T(8,128)(2,1)}, bf16[512,768]{1,0:T(8,128)(2,1)S(1)}, u32[]{:S(2)}) copy-start(bf16[512,768]{1,0:T(8,128)(2,1)S(1)} %collective-permute-done.5.x2.away_ref) | copy-start | bytes 2359300
  29.5 18.3 %collective-permute-start.6 = (bf16[512,768]{1,0:T(8,128)(2,1)S(1)}, bf16[512,768]{1,0:T(8,128)(2,1)S(1)}, u32[]{:S(2)}, u32[]{:S(2)}) collective-permute-start(bf16[512,768]{1,0:T(8,128)(2,1)S(1)} %collective-permute-done.5.x2.away_ref), channel_id=1, source_target_pairs={{0,1},{1,0},{2,3},{3,2},{4,5},{5,4},{6,7},{7,6},{8,9},{9,8},{10,11... | collective-permute-start | bytes 2359304 | tf_op jit(solution)/shard_map/tokens/ppermute | solution.py:29
  31.2 18.3 %copy-start.10 = (bf16[512,768]{1,0:T(8,128)(2,1)S(1)}, bf16[512,768]{1,0:T(8,128)(2,1)}, u32[]{:S(2)}) copy-start(bf16[512,768]{1,0:T(8,128)(2,1)} %pad_maximum_fusion.4.b0) | copy-start | bytes 2359300
  31.2 19.7 %copy-start.14 = (bf16[192,768]{1,0:T(8,128)(2,1)S(1)}, bf16[192,768]{1,0:T(8,128)(2,1)}, u32[]{:S(2)}) copy-start(bf16[192,768]{1,0:T(8,128)(2,1)} %own_w.3) | copy-start | bytes 884740
  31.2 15.5 %collective-permute-start.2 = (bf16[2,192,768]{2,1,0:T(8,128)(2,1)S(1)}, bf16[2,192,768]{2,1,0:T(8,128)(2,1)S(1)}, u32[]{:S(2)}, u32[]{:S(2)}) collective-permute-start(bf16[2,192,768]{2,1,0:T(8,128)(2,1)S(1)} %maximum_select_fusion.6), channel_id=1, source_target_pairs={{0,8},{4,12},{8,0},{12,4},{16,24},{20,28},{24,16},{28,20},{1,9},{5... | collective-permute-start | bytes 1769480 | tf_op jit(solution)/shard_map/mlp_weights_dp/ppermute | solution.py:771
  47.8 3.6 %copy-start.4 = (bf16[592,768]{1,0:T(8,128)(2,1)}, bf16[592,768]{1,0:T(8,128)(2,1)S(1)}, u32[]{:S(2)}) copy-start(bf16[592,768]{1,0:T(8,128)(2,1)S(1)} %collective-permute-done.3.far_ref.upb_far) | copy-start | bytes 2727940
  47.8 3.6 %copy-start.9 = (bf16[512,768]{1,0:T(8,128)(2,1)}, bf16[512,768]{1,0:T(8,128)(2,1)S(1)}, u32[]{:S(2)}) copy-start(bf16[512,768]{1,0:T(8,128)(2,1)S(1)} %collective-permute-done.6.x3) | copy-start | bytes 2359300
  47.8 31.8 %collective-permute-start.9 = (bf16[2,384,768]{2,1,0:T(8,128)(2,1)S(1)}, bf16[2,384,768]{2,1,0:T(8,128)(2,1)S(1)}, u32[]{:S(2)}, u32[]{:S(2)}) collective-permute-start(bf16[2,384,768]{2,1,0:T(8,128)(2,1)S(1)} %maximum_select_fusion.2), channel_id=1, source_target_pairs={{0,4},{4,0},{8,12},{12,8},{16,20},{20,16},{24,28},{28,24},{1,5},{5... | collective-permute-start | bytes 3538952 | tf_op jit(solution)/shard_map/mlp_weights_dp/ppermute | solution.py:771
  49.4 30.2 %collective-permute-start.8 = (bf16[512,768]{1,0:T(8,128)(2,1)S(1)}, bf16[512,768]{1,0:T(8,128)(2,1)S(1)}, u32[]{:S(2)}, u32[]{:S(2)}) collective-permute-start(bf16[512,768]{1,0:T(8,128)(2,1)S(1)} %copy-done.10), channel_id=1, source_target_pairs={{0,1},{1,0},{2,3},{3,2},{4,5},{5,4},{6,7},{7,6},{8,9},{9,8},{10,11... | collective-permute-start | bytes 2359304 | tf_op jit(solution)/shard_map/cotangent/ppermute | solution.py:29
  49.4 30.2 %collective-permute-start.7 = (bf16[256,768]{1,0:T(8,128)(2,1)}, bf16[256,768]{1,0:T(8,128)(2,1)S(1)}, u32[]{:S(2)}, u32[]{:S(2)}) collective-permute-start(bf16[256,768]{1,0:T(8,128)(2,1)} %get-tuple-element.196), channel_id=1, source_target_pairs={{0,2},{1,3},{2,0},{3,1},{4,6},{5,7},{6,4},{7,5},{8,10},{9,11},{10,... | collective-permute-start | bytes 1179656 | tf_op jit(solution)/shard_map/cotangent/ppermute | solution.py:25
  50.9 28.7 %collective-permute-start.10 = (bf16[192,768]{1,0:T(8,128)(2,1)S(1)}, bf16[192,768]{1,0:T(8,128)(2,1)S(1)}, u32[]{:S(2)}, u32[]{:S(2)}) collective-permute-start(bf16[192,768]{1,0:T(8,128)(2,1)S(1)} %copy-done.14), channel_id=1, source_target_pairs={{0,2},{1,3},{2,0},{3,1},{4,6},{5,7},{6,4},{7,5},{8,10},{9,11},{10,... | collective-permute-start | bytes 884744 | tf_op jit(solution)/shard_map/proj_weight_x/ppermute | solution.py:25
  79.6 8.3 %copy-start.19 = (bf16[512,768]{1,0:T(8,128)(2,1)}, bf16[512,768]{1,0:T(8,128)(2,1)S(1)}, u32[]{:S(2)}) copy-start(bf16[512,768]{1,0:T(8,128)(2,1)S(1)} %collective-permute-done.8.b1) | copy-start | bytes 2359300
  85.7 5.3 %collective-permute-start.11 = (bf16[1536,768]{1,0:T(8,128)(2,1)}, bf16[1536,768]{1,0:T(8,128)(2,1)S(1)}, u32[]{:S(2)}, u32[]{:S(2)}) collective-permute-start(bf16[1536,768]{1,0:T(8,128)(2,1)} %project.1.own_ref), channel_id=1, source_target_pairs={{0,1},{1,0},{2,3},{3,2},{4,5},{5,4},{6,7},{7,6},{8,9},{9,8},{10,11... | collective-permute-start | bytes 7077896 | tf_op jit(solution)/shard_map/attn_core/ppermute | solution.py:29
  85.7 5.3 %collective-permute-start.12 = (bf16[256,768]{1,0:T(8,128)(2,1)}, bf16[256,768]{1,0:T(8,128)(2,1)S(1)}, u32[]{:S(2)}, u32[]{:S(2)}) collective-permute-start(bf16[256,768]{1,0:T(8,128)(2,1)} %copy-done.23), channel_id=1, source_target_pairs={{0,1},{1,0},{2,3},{3,2},{4,5},{5,4},{6,7},{7,6},{8,9},{9,8},{10,11... | collective-permute-start | bytes 1179656 | tf_op jit(solution)/shard_map/cotangent/ppermute | solution.py:29
  121.0 9.7 %collective-permute-start.13 = (bf16[1536,768]{1,0:T(8,128)(2,1)}, bf16[1536,768]{1,0:T(8,128)(2,1)S(1)}, u32[]{:S(2)}, u32[]{:S(2)}) collective-permute-start(bf16[1536,768]{1,0:T(8,128)(2,1)} %get-tuple-element.205.own_ref), channel_id=1, source_target_pairs={{0,1},{1,0},{2,3},{3,2},{4,5},{5,4},{6,7},{7,6},{8,9},{9,8},{10,11... | collective-permute-start | bytes 7077896 | tf_op jit(solution)/shard_map/mid_core/ppermute | solution.py:29
  126.8 45.1 %collective-permute-start.14 = (bf16[768,768]{1,0:T(8,128)(2,1)}, bf16[768,768]{1,0:T(8,128)(2,1)S(1)}, u32[]{:S(2)}, u32[]{:S(2)}) collective-permute-start(bf16[768,768]{1,0:T(8,128)(2,1)} %sum_tokens.8), channel_id=1, source_target_pairs={{0,2},{1,3},{2,0},{3,1},{4,6},{5,7},{6,4},{7,5},{8,10},{9,11},{10,... | collective-permute-start | bytes 3538952 | tf_op jit(solution)/shard_map/down_grad_x/ppermute | solution.py:25
  151.6 49.0 %collective-permute-start.16 = (bf16[960,768]{1,0:T(8,128)(2,1)}, bf16[960,768]{1,0:T(8,128)(2,1)S(1)}, u32[]{:S(2)}, u32[]{:S(2)}) collective-permute-start(bf16[960,768]{1,0:T(8,128)(2,1)} %sum_tokens.10), channel_id=1, source_target_pairs={{0,2},{1,3},{2,0},{3,1},{4,6},{5,7},{6,4},{7,5},{8,10},{9,11},{10,... | collective-permute-start | bytes 4423688 | tf_op jit(solution)/shard_map/up_proj_grad_x/ppermute | solution.py:25
  179.0 21.5 %collective-permute-start.17 = (bf16[768,768]{1,0:T(8,128)(2,1)}, bf16[768,768]{1,0:T(8,128)(2,1)}, u32[]{:S(2)}, u32[]{:S(2)}) collective-permute-start(bf16[768,768]{1,0:T(8,128)(2,1)} %get-tuple-element.227), channel_id=1, source_target_pairs={{0,1},{1,0},{2,3},{3,2},{4,5},{5,4},{6,7},{7,6},{8,9},{9,8},{10,11... | collective-permute-start | bytes 3538952 | tf_op jit(solution)/shard_map/block_out/ppermute | solution.py:29
  181.7 17.6 %collective-permute-start.15 = (bf16[384,768]{1,0:T(8,128)(2,1)S(1)}, bf16[384,768]{1,0:T(8,128)(2,1)}, u32[]{:S(2)}, u32[]{:S(2)}) collective-permute-start(bf16[384,768]{1,0:T(8,128)(2,1)S(1)} %dynamic-slice_convert_fusion.1), channel_id=1, source_target_pairs={{0,4},{4,0},{8,12},{12,8},{16,20},{20,16},{24,28},{28,24},{1,5},{5... | collective-permute-start | bytes 1769480 | tf_op jit(solution)/shard_map/down_grad_dp/ppermute | solution.py:771
  182.1 35.1 %collective-permute-start.19 = (bf16[576,768]{1,0:T(8,128)(2,1)}, bf16[576,768]{1,0:T(8,128)(2,1)}, u32[]{:S(2)}, u32[]{:S(2)}) collective-permute-start(bf16[576,768]{1,0:T(8,128)(2,1)} %sum_tokens.11), channel_id=1, source_target_pairs={{0,2},{1,3},{2,0},{3,1},{4,6},{5,7},{6,4},{7,5},{8,10},{9,11},{10,... | collective-permute-start | bytes 2654216 | tf_op jit(solution)/shard_map/qkv_grad_x/ppermute | solution.py:25
  208.0 9.2 %collective-permute-start.18 = (bf16[192,768]{1,0:T(8,128)(2,1)S(1)}, bf16[192,768]{1,0:T(8,128)(2,1)S(1)}, u32[]{:S(2)}, u32[]{:S(2)}) collective-permute-start(bf16[192,768]{1,0:T(8,128)(2,1)S(1)} %dynamic-slice_convert_fusion.3), channel_id=1, source_target_pairs={{0,8},{4,12},{8,0},{12,4},{16,24},{20,28},{24,16},{28,20},{1,9},{5... | collective-permute-start | bytes 884744 | tf_op jit(solution)/shard_map/down_grad_dp/ppermute | solution.py:771
  208.1 3.7 %copy-start.12 = (f32[768,768]{1,0:T(8,128)S(1)}, f32[768,768]{1,0:T(8,128)}, u32[]{:S(2)}) copy-start(f32[768,768]{1,0:T(8,128)} %get-tuple-element.237) | copy-start | bytes 7077892
  211.8 5.5 %copy-start = (f32[960,768]{1,0:T(8,128)S(1)}, f32[960,768]{1,0:T(8,128)}, u32[]{:S(2)}) copy-start(f32[960,768]{1,0:T(8,128)} %sum_tokens.14) | copy-start | bytes 8847364
  218.4 21.1 %collective-permute-start.20 = (bf16[480,768]{1,0:T(8,128)(2,1)}, bf16[480,768]{1,0:T(8,128)(2,1)}, u32[]{:S(2)}, u32[]{:S(2)}) collective-permute-start(bf16[480,768]{1,0:T(8,128)(2,1)} %dynamic-slice_convert_fusion), channel_id=1, source_target_pairs={{0,4},{4,0},{8,12},{12,8},{16,20},{20,16},{24,28},{28,24},{1,5},{5... | collective-permute-start | bytes 2211848 | tf_op jit(solution)/shard_map/up_proj_grad_dp/ppermute | solution.py:771
  220.8 18.7 %collective-permute-start.21 = (bf16[96,768]{1,0:T(8,128)(2,1)S(1)}, bf16[96,768]{1,0:T(8,128)(2,1)S(1)}, u32[]{:S(2)}, u32[]{:S(2)}) collective-permute-start(bf16[96,768]{1,0:T(8,128)(2,1)S(1)} %dynamic-slice_convert_fusion.7), channel_id=1, source_target_pairs={{0,16},{4,20},{8,24},{12,28},{16,0},{20,4},{24,8},{28,12},{1,17},{... | collective-permute-start | bytes 442376 | tf_op jit(solution)/shard_map/down_grad_dp/ppermute | solution.py:771
  239.5 1.7 copy-start.7
  242.2 4.4 %copy-start.26 = (f32[8,768]{1,0:T(8,128)S(1)}, f32[8,768]{1,0:T(8,128)}, u32[]{:S(2)}) copy-start(f32[8,768]{1,0:T(8,128)} %get-tuple-element.294) | copy-start | bytes 73732
  243.9 14.6 %collective-permute-start.27 = (bf16[1024,768]{1,0:T(8,128)(2,1)}, bf16[1024,768]{1,0:T(8,128)(2,1)S(1)}, u32[]{:S(2)}, u32[]{:S(2)}) collective-permute-start(bf16[1024,768]{1,0:T(8,128)(2,1)} %get-tuple-element.273), channel_id=1, source_target_pairs={{0,1},{1,0},{2,3},{3,2},{4,5},{5,4},{6,7},{7,6},{8,9},{9,8},{10,11... | collective-permute-start | bytes 4718600 | tf_op jit(solution)/shard_map/first_core/ppermute | solution.py:29
  246.6 25.1 %copy-start.8 = (f32[288,768]{1,0:T(8,128)S(1)}, f32[288,768]{1,0:T(8,128)}, u32[]{:S(2)}) copy-start(f32[288,768]{1,0:T(8,128)} %constant_dynamic-slice_fusion.4) | copy-start | bytes 2654212
  246.6 11.7 %collective-permute-start.26 = (bf16[96,768]{1,0:T(8,128)(2,1)S(1)}, bf16[96,768]{1,0:T(8,128)(2,1)S(1)}, u32[]{:S(2)}, u32[]{:S(2)}) collective-permute-start(bf16[96,768]{1,0:T(8,128)(2,1)S(1)} %convert_add_fusion.5), channel_id=1, source_target_pairs={{0,16},{4,20},{8,24},{12,28},{16,0},{20,4},{24,8},{28,12},{1,17},{... | collective-permute-start | bytes 442376 | tf_op jit(solution)/shard_map/down_grad_dp/ppermute | solution.py:771
  247.7 18.6 %collective-permute-start.23 = (bf16[120,768]{1,0:T(8,128)(2,1)}, bf16[120,768]{1,0:T(8,128)(2,1)S(1)}, u32[]{:S(2)}, u32[]{:S(2)}) collective-permute-start(bf16[120,768]{1,0:T(8,128)(2,1)} %get-tuple-element.267), channel_id=1, source_target_pairs={{0,16},{4,20},{8,24},{12,28},{16,0},{20,4},{24,8},{28,12},{1,17},{... | collective-permute-start | bytes 552968 | tf_op jit(solution)/shard_map/up_proj_grad_dp/ppermute | solution.py:771
  249.7 16.7 %collective-permute-start.24 = (bf16[120,768]{1,0:T(8,128)(2,1)}, bf16[120,768]{1,0:T(8,128)(2,1)S(1)}, u32[]{:S(2)}, u32[]{:S(2)}) collective-permute-start(bf16[120,768]{1,0:T(8,128)(2,1)} %get-tuple-element.268), channel_id=1, source_target_pairs={{0,8},{4,12},{8,0},{12,4},{16,24},{20,28},{24,16},{28,20},{1,9},{5... | collective-permute-start | bytes 552968 | tf_op jit(solution)/shard_map/up_proj_grad_dp/ppermute | solution.py:771
  250.0 21.7 %collective-permute-start.25 = (bf16[120,768]{1,0:T(8,128)(2,1)S(1)}, bf16[120,768]{1,0:T(8,128)(2,1)S(1)}, u32[]{:S(2)}, u32[]{:S(2)}) collective-permute-start(bf16[120,768]{1,0:T(8,128)(2,1)S(1)} %get-tuple-element.269), channel_id=1, source_target_pairs={{0,24},{4,28},{8,16},{12,20},{16,8},{20,12},{24,0},{28,4},{1,25},{... | collective-permute-start | bytes 552968 | tf_op jit(solution)/shard_map/up_proj_grad_dp/ppermute | solution.py:771
  258.3 13.4 %collective-permute-start.22 = (bf16[288,768]{1,0:T(8,128)(2,1)}, bf16[288,768]{1,0:T(8,128)(2,1)S(1)}, u32[]{:S(2)}, u32[]{:S(2)}) collective-permute-start(bf16[288,768]{1,0:T(8,128)(2,1)} %dynamic-slice_convert_fusion.2), channel_id=1, source_target_pairs={{0,4},{4,0},{8,12},{12,8},{16,20},{20,16},{24,28},{28,24},{1,5},{5... | collective-permute-start | bytes 1327112 | tf_op jit(solution)/shard_map/qkv_grad_dp/ppermute | solution.py:771
  258.5 13.3 %copy-start.5 = (bf16[1024,768]{1,0:T(8,128)(2,1)}, bf16[1024,768]{1,0:T(8,128)(2,1)S(1)}, u32[]{:S(2)}) copy-start(bf16[1024,768]{1,0:T(8,128)(2,1)S(1)} %collective-permute-done.27.got_ref) | copy-start | bytes 4718596
  259.9 15.8 %collective-permute-start.28 = (bf16[256,768]{1,0:T(8,128)(2,1)S(1)}, bf16[256,768]{1,0:T(8,128)(2,1)S(1)}, u32[]{:S(2)}, u32[]{:S(2)}) collective-permute-start(bf16[256,768]{1,0:T(8,128)(2,1)S(1)} %add_convert_fusion.1), channel_id=1, source_target_pairs={{0,2},{1,3},{2,0},{3,1},{4,6},{5,7},{6,4},{7,5},{8,10},{9,11},{10,... | collective-permute-start | bytes 1179656 | tf_op jit(solution)/shard_map/first_mid_x/ppermute | solution.py:25
  275.7 8.1 %copy-start.21 = (bf16[256,768]{1,0:T(8,128)(2,1)}, bf16[256,768]{1,0:T(8,128)(2,1)S(1)}, u32[]{:S(2)}) copy-start(bf16[256,768]{1,0:T(8,128)(2,1)S(1)} %collective-permute-done.28.refs_0_) | copy-start | bytes 1179652
  275.8 19.5 %collective-permute-start.33 = (bf16[120,768]{1,0:T(8,128)(2,1)S(1)}, bf16[120,768]{1,0:T(8,128)(2,1)S(1)}, u32[]{:S(2)}, u32[]{:S(2)}) collective-permute-start(bf16[120,768]{1,0:T(8,128)(2,1)S(1)} %convert_add_fusion.4), channel_id=1, source_target_pairs={{0,16},{4,20},{8,24},{12,28},{16,0},{20,4},{24,8},{28,12},{1,17},{... | collective-permute-start | bytes 552968 | tf_op jit(solution)/shard_map/up_proj_grad_dp/ppermute | solution.py:771
  278.2 15.0 %collective-permute-start.30 = (bf16[72,768]{1,0:T(8,128)(2,1)S(1)}, bf16[72,768]{1,0:T(8,128)(2,1)S(1)}, u32[]{:S(2)}, u32[]{:S(2)}) collective-permute-start(bf16[72,768]{1,0:T(8,128)(2,1)S(1)} %get-tuple-element.286), channel_id=1, source_target_pairs={{0,16},{4,20},{8,24},{12,28},{16,0},{20,4},{24,8},{28,12},{1,17},{... | collective-permute-start | bytes 331784 | tf_op jit(solution)/shard_map/qkv_grad_dp/ppermute | solution.py:771
  278.8 14.8 %collective-permute-start.31 = (bf16[72,768]{1,0:T(8,128)(2,1)S(1)}, bf16[72,768]{1,0:T(8,128)(2,1)S(1)}, u32[]{:S(2)}, u32[]{:S(2)}) collective-permute-start(bf16[72,768]{1,0:T(8,128)(2,1)S(1)} %get-tuple-element.287), channel_id=1, source_target_pairs={{0,8},{4,12},{8,0},{12,4},{16,24},{20,28},{24,16},{28,20},{1,9},{5... | collective-permute-start | bytes 331784 | tf_op jit(solution)/shard_map/qkv_grad_dp/ppermute | solution.py:771
  280.3 14.9 %collective-permute-start.32 = (bf16[72,768]{1,0:T(8,128)(2,1)S(1)}, bf16[72,768]{1,0:T(8,128)(2,1)S(1)}, u32[]{:S(2)}, u32[]{:S(2)}) collective-permute-start(bf16[72,768]{1,0:T(8,128)(2,1)S(1)} %get-tuple-element.288), channel_id=1, source_target_pairs={{0,24},{4,28},{8,16},{12,20},{16,8},{20,12},{24,0},{28,4},{1,25},{... | collective-permute-start | bytes 331784 | tf_op jit(solution)/shard_map/qkv_grad_dp/ppermute | solution.py:771
  281.7 14.7 %collective-permute-start.29 = (bf16[192,768]{1,0:T(8,128)(2,1)S(1)}, bf16[192,768]{1,0:T(8,128)(2,1)S(1)}, u32[]{:S(2)}, u32[]{:S(2)}) collective-permute-start(bf16[192,768]{1,0:T(8,128)(2,1)S(1)} %maximum_select_fusion.11), channel_id=1, source_target_pairs={{0,8},{4,12},{8,0},{12,4},{16,24},{20,28},{24,16},{28,20},{1,9},{5... | collective-permute-start | bytes 884744 | tf_op jit(solution)/shard_map/down_grad_dp/ppermute | solution.py:771
  293.2 9.8 %collective-permute-start.34 = (bf16[256,768]{1,0:T(8,128)(2,1)S(1)}, bf16[256,768]{1,0:T(8,128)(2,1)S(1)}, u32[]{:S(2)}, u32[]{:S(2)}) collective-permute-start(bf16[256,768]{1,0:T(8,128)(2,1)S(1)} %slice.130), channel_id=1, source_target_pairs={{0,2},{1,3},{2,0},{3,1},{4,6},{5,7},{6,4},{7,5},{8,10},{9,11},{10,... | collective-permute-start | bytes 1179656 | tf_op jit(solution)/shard_map/in_grad_x/ppermute | solution.py:25
  295.3 11.1 %copy-start.20 = (bf16[512,768]{1,0:T(8,128)(2,1)S(1)}, bf16[512,768]{1,0:T(8,128)(2,1)}, u32[]{:S(2)}) copy-start(bf16[512,768]{1,0:T(8,128)(2,1)} %get-tuple-element.298) | copy-start | bytes 2359300
  303.0 13.5 %collective-permute-start.38 = (bf16[384,768]{1,0:T(8,128)(2,1)S(1)}, bf16[384,768]{1,0:T(8,128)(2,1)}, u32[]{:S(2)}, u32[]{:S(2)}) collective-permute-start(bf16[384,768]{1,0:T(8,128)(2,1)S(1)} %maximum_select_fusion.7), channel_id=1, source_target_pairs={{0,4},{4,0},{8,12},{12,8},{16,20},{20,16},{24,28},{28,24},{1,5},{5... | collective-permute-start | bytes 1769480 | tf_op jit(solution)/shard_map/down_grad_dp/ppermute | solution.py:771
  304.0 2.4 collective-permute-start.35
  304.0 4.5 %collective-permute-start.36 = (f32[12,768]{1,0:T(8,128)S(1)}, f32[12,768]{1,0:T(8,128)S(1)}, u32[]{:S(2)}, u32[]{:S(2)}) collective-permute-start(f32[12,768]{1,0:T(8,128)S(1)} %pad_maximum_fusion.6), channel_id=1, source_target_pairs={{0,2},{1,3},{2,0},{3,1},{4,6},{5,7},{6,4},{7,5},{8,10},{9,11},{10,... | collective-permute-start | bytes 110600 | tf_op jit(solution)/shard_map/small_sums/ppermute | solution.py:25
  304.4 4.4 %collective-permute-start.37 = (f32[12,768]{1,0:T(8,128)S(1)}, f32[12,768]{1,0:T(8,128)S(1)}, u32[]{:S(2)}, u32[]{:S(2)}) collective-permute-start(f32[12,768]{1,0:T(8,128)S(1)} %pad_maximum_fusion.6), channel_id=1, source_target_pairs={{0,3},{1,2},{2,1},{3,0},{4,7},{5,6},{6,5},{7,4},{8,11},{9,10},{10,... | collective-permute-start | bytes 110600 | tf_op jit(solution)/shard_map/small_sums/ppermute | solution.py:897
  305.9 12.3 %collective-permute-start.39 = (bf16[256,768]{1,0:T(8,128)(2,1)S(1)}, bf16[256,768]{1,0:T(8,128)(2,1)S(1)}, u32[]{:S(2)}, u32[]{:S(2)}) collective-permute-start(bf16[256,768]{1,0:T(8,128)(2,1)S(1)} %slice.131), channel_id=1, source_target_pairs={{0,2},{1,3},{2,0},{3,1},{4,6},{5,7},{6,4},{7,5},{8,10},{9,11},{10,... | collective-permute-start | bytes 1179656 | tf_op jit(solution)/shard_map/block_out/ppermute | solution.py:25
  306.4 13.7 %copy-start.22 = (bf16[256,768]{1,0:T(8,128)(2,1)S(1)}, bf16[256,768]{1,0:T(8,128)(2,1)}, u32[]{:S(2)}) copy-start(bf16[256,768]{1,0:T(8,128)(2,1)} %get-tuple-element.319) | copy-start | bytes 1179652
  318.2 9.8 %collective-permute-start.41 = (bf16[240,768]{1,0:T(8,128)(2,1)S(1)}, bf16[240,768]{1,0:T(8,128)(2,1)S(1)}, u32[]{:S(2)}, u32[]{:S(2)}) collective-permute-start(bf16[240,768]{1,0:T(8,128)(2,1)S(1)} %maximum_select_fusion.10), channel_id=1, source_target_pairs={{0,8},{4,12},{8,0},{12,4},{16,24},{20,28},{24,16},{28,20},{1,9},{5... | collective-permute-start | bytes 1105928 | tf_op jit(solution)/shard_map/up_proj_grad_dp/ppermute | solution.py:771
  318.7 5.0 %collective-permute-start.40 = (bf16[88,768]{1,0:T(8,128)(2,1)S(1)}, bf16[88,768]{1,0:T(8,128)(2,1)S(1)}, u32[]{:S(2)}, u32[]{:S(2)}) collective-permute-start(bf16[88,768]{1,0:T(8,128)(2,1)S(1)} %fusion.5), channel_id=1, source_target_pairs={{0,4},{4,0},{8,12},{12,8},{16,20},{20,16},{24,28},{28,24},{1,5},{5... | collective-permute-start | bytes 405512 | tf_op jit(solution)/shard_map/qkv_grad_dp/ppermute | solution.py:771
  328.3 18.9 %collective-permute-start.44 = (bf16[160,768]{1,0:T(8,128)(2,1)S(1)}, bf16[160,768]{1,0:T(8,128)(2,1)S(1)}, u32[]{:S(2)}, u32[]{:S(2)}) collective-permute-start(bf16[160,768]{1,0:T(8,128)(2,1)S(1)} %fusion.4), channel_id=1, source_target_pairs={{0,24},{4,28},{8,16},{12,20},{16,8},{20,12},{24,0},{28,4},{1,25},{... | collective-permute-start | bytes 737288 | tf_op jit(solution)/shard_map/qkv_grad_dp/ppermute | solution.py:771
  330.6 16.6 %collective-permute-start.43 = (bf16[160,768]{1,0:T(8,128)(2,1)S(1)}, bf16[160,768]{1,0:T(8,128)(2,1)S(1)}, u32[]{:S(2)}, u32[]{:S(2)}) collective-permute-start(bf16[160,768]{1,0:T(8,128)(2,1)S(1)} %fusion.4), channel_id=1, source_target_pairs={{0,8},{4,12},{8,0},{12,4},{16,24},{20,28},{24,16},{28,20},{1,9},{5... | collective-permute-start | bytes 737288 | tf_op jit(solution)/shard_map/qkv_grad_dp/ppermute | solution.py:771
  334.9 15.5 %collective-permute-start.42 = (bf16[160,768]{1,0:T(8,128)(2,1)S(1)}, bf16[160,768]{1,0:T(8,128)(2,1)S(1)}, u32[]{:S(2)}, u32[]{:S(2)}) collective-permute-start(bf16[160,768]{1,0:T(8,128)(2,1)S(1)} %fusion.4), channel_id=1, source_target_pairs={{0,16},{4,20},{8,24},{12,28},{16,0},{20,4},{24,8},{28,12},{1,17},{... | collective-permute-start | bytes 737288 | tf_op jit(solution)/shard_map/qkv_grad_dp/ppermute | solution.py:771
  336.0 17.7 %collective-permute-start.45 = (bf16[480,768]{1,0:T(8,128)(2,1)S(1)}, bf16[480,768]{1,0:T(8,128)(2,1)S(1)}, u32[]{:S(2)}, u32[]{:S(2)}) collective-permute-start(bf16[480,768]{1,0:T(8,128)(2,1)S(1)} %maximum_select_fusion.5), channel_id=1, source_target_pairs={{0,4},{4,0},{8,12},{12,8},{16,20},{20,16},{24,28},{28,24},{1,5},{5... | collective-permute-start | bytes 2211848 | tf_op jit(solution)/shard_map/up_proj_grad_dp/ppermute | solution.py:771
  (11 other events, 12.1 us)

commit v2 on v1

--- a/solution.py
+++ b/solution.py
@@ -52,12 +52,19 @@
 SMALL_COST = pl.CostEstimate(flops=1, bytes_accessed=1, transcendentals=0)
 
 
-def key_mask(start_row, key_first, size, diagonal):
-    keys = lax.broadcasted_iota(jnp.int32, (size, size), 0)
-    mask = keys >= start_row - key_first
+def key_mask(start_row, key_first, keys, size, diagonal):
+    key = lax.broadcasted_iota(jnp.int32, (keys, size), 0)
+    mask = key >= start_row - key_first
     if diagonal:
-        mask = mask & (keys <= lax.broadcasted_iota(jnp.int32, (size, size), 1))
+        mask = mask & (key <= lax.broadcasted_iota(jnp.int32, (keys, size), 1))
     return mask
+
+
+KEYS = 128
+
+
+def key_rows(table, row, first, size):
+    return table[3 + row, first // size] * size + first % size
 
 
 def head_rows(size):
@@ -87,12 +94,12 @@
     select = head_rows(size)
     heads = select(q_ref[...] * jnp.asarray(HEAD_DIM**-0.5, BF))
 
-    def load(key_block):
-        at = pl.multiple_of(table[3 + row, key_block] * size, size)
-        return k_ref[pl.ds(at, size), :], jnp.transpose(v_ref[pl.ds(at, size), :])
-
-    key, value_t = load(block)
-    mask = key_mask(start_row, block * size, size, True)
+    def load(first, keys):
+        at = pl.multiple_of(key_rows(table, row, first, size), keys)
+        return k_ref[pl.ds(at, keys), :], jnp.transpose(v_ref[pl.ds(at, keys), :])
+
+    key, value_t = load(block * size, size)
+    mask = key_mask(start_row, block * size, size, size, True)
     all_scores = [nt(pair_lanes(key, head), heads[head]) for head in range(3)]
     carry = []
     for head in range(3):
@@ -104,9 +111,9 @@
         carry += [top, total, acc]
 
     def earlier(step, carry):
-        key_block = block - 1 - step
-        key, value_t = load(key_block)
-        mask = key_mask(start_row, key_block * size, size, False)
+        first = block * size - (step + 1) * KEYS
+        key, value_t = load(first, KEYS)
+        mask = key_mask(start_row, first, KEYS, size, False)
         all_scores = [nt(pair_lanes(key, head), heads[head]) for head in range(3)]
         new = []
         for head in range(3):
@@ -122,7 +129,7 @@
             new += [higher, total, acc]
         return tuple(new)
 
-    carry = lax.fori_loop(0, block - low, earlier, tuple(carry))
+    carry = lax.fori_loop(0, block * (size // KEYS) - low, earlier, tuple(carry))
     parts = [carry[3 * head + 2] / carry[3 * head + 1] for head in range(3)]
     parts.append(jnp.zeros_like(parts[0]))
     out_ref[...] = jnp.transpose(jnp.concatenate(parts, axis=0)).astype(BF)
@@ -183,11 +190,11 @@
         dv_acc[...] = jnp.zeros_like(dv_acc)
         sum_ref[...] = jnp.zeros_like(sum_ref)
 
-    def one_block(key_block, diagonal):
-        at = pl.multiple_of(table[3 + row, key_block] * size, size)
-        key, value = k_ref[pl.ds(at, size), :], v_ref[pl.ds(at, size), :]
+    def one_block(first, keys, diagonal):
+        at = pl.multiple_of(key_rows(table, row, first, size), keys)
+        key, value = k_ref[pl.ds(at, keys), :], v_ref[pl.ds(at, keys), :]
         key_t = jnp.transpose(key)
-        mask = key_mask(start_row, key_block * size, size, diagonal)
+        mask = key_mask(start_row, first, keys, size, diagonal)
         all_scores = [nt(pair_lanes(key, head), q_heads[head]) for head in range(3)]
         all_grads = [nt(pair_lanes(value, head), g_heads[head]) for head in range(3)]
         dq_parts, dk_parts, dv_parts = [], [], []
@@ -198,15 +205,18 @@
             dk_parts.append(nn(score_grad, q_heads[head]))
             dv_parts.append(nn(prob.astype(BF), g_heads[head]))
             dq_parts.append(nn(key_t[head * HEAD_DIM : (head + 1) * HEAD_DIM], score_grad))
-        dk_acc[pl.ds(at, size), : width // 2] += dk_parts[0] + dk_parts[1]
-        dk_acc[pl.ds(at, size), width // 2 :] += dk_parts[2]
-        dv_acc[pl.ds(at, size), : width // 2] += dv_parts[0] + dv_parts[1]
-        dv_acc[pl.ds(at, size), width // 2 :] += dv_parts[2]
+        dk_acc[pl.ds(at, keys), : width // 2] += dk_parts[0] + dk_parts[1]
+        dk_acc[pl.ds(at, keys), width // 2 :] += dk_parts[2]
+        dv_acc[pl.ds(at, keys), : width // 2] += dv_parts[0] + dv_parts[1]
+        dv_acc[pl.ds(at, keys), width // 2 :] += dv_parts[2]
         return jnp.concatenate(dq_parts, axis=0)
 
-    dq_t = one_block(block, True)
+    dq_t = one_block(block * size, size, True)
     dq_t = lax.fori_loop(
-        0, block - low, lambda step, acc: acc + one_block(block - 1 - step, False), dq_t
+        0,
+        block * (size // KEYS) - low,
+        lambda step, acc: acc + one_block(block * size - (step + 1) * KEYS, KEYS, False),
+        dq_t,
     )
     dq_t = jnp.concatenate([dq_t, jnp.zeros((HEAD_DIM, size), F32)], axis=0)
     dq = (jnp.transpose(dq_t) * HEAD_DIM**-0.5).astype(BF)
@@ -283,7 +293,7 @@
         start_ref[:, slot * size : (slot + 1) * size] = jnp.broadcast_to(mine, (8, size))
         table_ref[0, slot] = row
         table_ref[1, slot] = block
-        table_ref[2, slot] = jnp.min(mine) // size
+        table_ref[2, slot] = jnp.min(mine) // KEYS
     for row in range(2):
         for block in range(4):
             slots = SLOT[row]
@@ -357,16 +367,17 @@
 
 def mlp_kernel(
     x0, x1, x2, x3, own_ref, other_ref, b0, b1, b2, b3, vec_ref, upb_own, upb_far, up_own, up_far, dn_own, dn_far,
-    res_ref, mid_ref, act_ref, hg_ref, out_ref, give_ref, midin_ref, upbg_ref, bg_ref, held_ref,
+    rstd_ref, mid_ref, act_ref, hg_ref, out_ref, give_ref, midin_ref, upbg_ref, bg_ref, held_ref,
 ):
     step = pl.program_id(0)
     proj_bias, gain, shift = vec_ref[0:1, :], vec_ref[1:2, :], vec_ref[2:3, :]
     residual = two_blocks(step, (x0, x1, x2, x3), held_ref).astype(F32) + own_ref[...].astype(F32)
     residual = residual + other_core(other_ref, step) + proj_bias
-    res_ref[...] = residual
     centered = residual - jnp.mean(residual, axis=-1, keepdims=True)
     variance = jnp.mean(centered * centered, axis=-1, keepdims=True)
-    mid = (centered * lax.rsqrt(variance + NORM_EPS) * gain + shift).astype(BF)
+    rstd = lax.rsqrt(variance + NORM_EPS)
+    rstd_ref[...] = jnp.broadcast_to(rstd, rstd_ref.shape)
+    mid = (centered * rstd * gain + shift).astype(BF)
     mid_ref[...] = mid
     bg = two_blocks(step, (b0, b1, b2, b3), bg_ref)
 
@@ -435,12 +446,13 @@
             pl.BlockSpec((1, inner, width), lambda i: (1, 0, 0), pipeline_mode=pl.Buffered(1)),
         ],
         out_specs=[
-            block, block, wide, wide, half, half, block,
+            pl.BlockSpec((2 * size, 128), lambda i: (i, 0)),
+            block, wide, wide, half, half, block,
             pl.BlockSpec((8, inner), lambda i: (0, 0)),
             block,
         ],
         out_shape=[
-            jax.ShapeDtypeStruct((rows, width), F32),
+            jax.ShapeDtypeStruct((rows, 128), F32),
             jax.ShapeDtypeStruct((rows, width), BF),
             jax.ShapeDtypeStruct((2, rows, inner), BF),
             jax.ShapeDtypeStruct((2, rows, inner), BF),
@@ -467,13 +479,16 @@
 
 
 def sum_tokens(
-    left, right, extra=None, dtype=BF, part=0, rows=256, first=0, count=None, room=0, into=None
+    left, right, extra=None, dtype=BF, part=0, parts=1, rows=256, first=0, count=None, room=0, into=None
 ):
     block = 256
-    count = count or left.shape[-1] // block
+    blocks = left.shape[-1] // block
+    count = count or parts * blocks
     tokens, width = right.shape[-2:]
 
     def spec(value, lanes, at):
+        if value.ndim == 3 and parts > 1:
+            return pl.BlockSpec((1, tokens, lanes), lambda i: (i // blocks, 0, i % blocks))
         if value.ndim == 3:
             return pl.BlockSpec((1, tokens, lanes), lambda i: (part, 0, at(i)))
         return pl.BlockSpec((tokens, lanes), lambda i: (0, at(i)))
@@ -483,7 +498,7 @@
     specs = [spec(left, block, lambda i: first + i), spec(right, width, lambda i: 0)]
     operands = [left, right]
     if extra is not None:
-        specs.append(out)
+        specs.append(pl.BlockSpec((rows, width), lambda i: (i, 0)))
         operands.append(extra)
     aliases = {}
     shape = jax.ShapeDtypeStruct((count * rows + room, width), dtype)
@@ -530,14 +545,13 @@
 
 
 def mid_backward_kernel(
-    res_ref, own_ref, other_ref, bg_ref, vec_ref, far_w, own_w, rg_ref, ag_ref, atg_ref, sum_ref
+    mid_ref, rstd_ref, own_ref, other_ref, bg_ref, vec_ref, far_w, own_w,
+    rg_ref, ag_ref, atg_ref, sum_ref,
 ):
     step = pl.program_id(0)
-    gain = vec_ref[1:2, :]
-    residual = res_ref[...]
-    centered = residual - jnp.mean(residual, axis=-1, keepdims=True)
-    rstd = lax.rsqrt(jnp.mean(centered * centered, axis=-1, keepdims=True) + NORM_EPS)
-    xhat = centered * rstd
+    gain, shift = vec_ref[1:2, :], vec_ref[2:3, :]
+    rstd = rstd_ref[:, 0:1]
+    xhat = (mid_ref[...].astype(F32) - shift) * (1.0 / gain)
     mid_in = own_ref[...].astype(F32) + other_core(other_ref, step)
     gy = mid_in * gain
     through = rstd * (
@@ -572,7 +586,7 @@
     sum_ref[3:4, :] += jnp.sum(bg_ref[...].astype(F32), axis=0, keepdims=True)
 
 
-def mid_backward(residual, own, other, bg, vectors, far_w, own_w, size):
+def mid_backward(mid, rstd, own, other, bg, vectors, far_w, own_w, size):
     rows, width = own.shape
     lanes = 8 * HEAD_DIM
     block = pl.BlockSpec((2 * size, width), lambda i: (i, 0))
@@ -581,6 +595,7 @@
         grid=(3,),
         in_specs=[
             block,
+            pl.BlockSpec((2 * size, 128), lambda i: (i, 0)),
             block,
             pl.BlockSpec((2 * size, width), lambda i: (other_pair(i), 0)),
             block,
@@ -603,7 +618,7 @@
         compiler_params=params(),
         cost_estimate=SMALL_COST,
         name="mid_backward",
-    )(residual, own, other, bg, vectors, far_w, own_w)
+    )(mid, rstd, own, other, bg, vectors, far_w, own_w)
 
 
 def bias_row(ref):
@@ -822,10 +837,11 @@
         self.bits = bits
 
     def split(self, value):
-        rows = value.shape[0] // (2 ** len(self.bits))
+        axis = value.ndim - 2
+        rows = value.shape[axis] // (2 ** len(self.bits))
         mine = member(self.bits)
         pieces = [
-            lax.dynamic_slice_in_dim(value, (mine ^ distance) * rows, rows, 0)
+            lax.dynamic_slice_in_dim(value, (mine ^ distance) * rows, rows, axis)
             for distance in range(2 ** len(self.bits))
         ]
         return pieces[0], [piece.astype(BF) for piece in pieces[1:]]
@@ -882,9 +898,11 @@
             got = [dp_swap(piece, mask) for piece, mask in zip(give, step.masks)]
             joined.append((kept, got))
 
-    def finish():
+    def finish(*late):
+        gots = [got for _, got in joined]
+        gots, _ = lax.optimization_barrier((gots, late))
         out = []
-        for (kept, got), step in zip(joined, steps):
+        for (kept, _), got, step in zip(joined, gots, steps):
             with jax.named_scope(step.name):
                 out.append(step.join(kept, got))
         return out
@@ -1007,7 +1025,7 @@
         attn_other = core_swap(attn_part)
     far_mlp = in_order(far_mlp, got_mlp, dp_bits()[0], 1)
 
-    residual, normed_mid, act, hidden_grad, out_own, out_give, mid_part, up_sums, branch_grad = mlp(
+    mid_rstd, normed_mid, act, hidden_grad, out_own, out_give, mid_part, up_sums, branch_grad = mlp(
         tokens, attn_part, attn_other, (g_home, g_near, g_far, g_far_near), vectors, qkv_own, held,
         up_weight, down_weight, far_mlp, size,
     )
@@ -1015,73 +1033,84 @@
     stages = dp_stages()
     first_stage, high_stages = stages[0], stages[1:]
 
+    d, u, t = "down_grad_dp", "up_proj_grad_dp", "qkv_grad_dp"
+    singles = [[bit] for bit in dp_bits()[1:]]
+
     with jax.named_scope("mid_core"):
         mid_other = core_swap(mid_part)
-    down_away = sum_tokens(act, branch_grad, part=1)
-    with jax.named_scope("down_grad_x"):
-        down_got = x_swap(down_away)
+    up_away = sum_tokens(normed_mid, hidden_grad, part=1)
+    with jax.named_scope("up_grad_x"):
+        up_got = x_swap(up_away)
+
+    down = sum_tokens(act, after(branch_grad, up_away), parts=2).reshape(2, inner, width)
+    finish, (mid_rstd, mid_part, attended, hidden_grad, out_give) = exchange(
+        [down], [Scatter(d, first_stage)], mid_rstd, mid_part, attended, hidden_grad, out_give
+    )
     residual_grad, attn_grad, attended_grad, mid_sums = mid_backward(
-        after(residual, down_away), mid_part, mid_other, branch_grad, vectors,
+        normed_mid, mid_rstd, mid_part, mid_other, branch_grad, vectors,
         proj_far, proj_weight, size,
     )
-
-    act, hidden_grad, out_own, out_give, attended_grad = lax.optimization_barrier(
-        (act, hidden_grad, out_own, out_give, attended_grad)
-    )
-    up_away = sum_tokens(normed_mid, hidden_grad, part=1, room=feats)
-    up_away = sum_tokens(attended, attn_grad, rows=feats, count=1, into=up_away)
-    with jax.named_scope("up_proj_grad_x"):
-        up_got = x_swap(up_away)
+    proj_away = sum_tokens(attended, attn_grad, rows=feats, count=1)
+    with jax.named_scope("proj_grad_x"):
+        proj_got = x_swap(proj_away)
     d_far, sums_far = attend_backward(
-        qkv, attended, after(attended_grad, up_away), lse, table, start_rows, size, 0
+        qkv, attended, after(attended_grad, proj_away), lse, table, start_rows, size, 0
     )
     qkv_away = sum_tokens(d_far, normed, rows=feats)
     with jax.named_scope("qkv_grad_x"):
         qkv_got = x_swap(qkv_away)
-    down = sum_tokens(act, after(branch_grad, qkv_away), down_got, F32)
+    (down,) = finish(qkv_away)
+
+    finish, (attended_grad, out_give) = exchange(
+        [down], [Scatter(d, singles[0])], after(attended_grad, qkv_away), out_give
+    )
     with jax.named_scope("block_out"):
-        out_got = core_swap(after(out_give, down))
-    d_own, sums_own = attend_backward(
-        qkv, attended, after(attended_grad, down), lse, table, start_rows, size, 1
-    )
-    d, u, t, n = "down_grad_dp", "up_proj_grad_dp", "qkv_grad_dp", "small_sums"
-    finish, (attended_grad,) = exchange([down], [Scatter(d, first_stage)], attended_grad)
+        out_got = core_swap(out_give)
     d_own, sums_own = attend_backward(
         qkv, attended, attended_grad, lse, table, start_rows, size, 1
     )
-    (down,) = finish()
-    d_own, down, up_got, out_got = lax.optimization_barrier((d_own, down, up_got, out_got))
-
-    singles = [[bit] for bit in dp_bits()[1:]]
-    finish, (hidden_grad, up_got) = exchange(
-        [down], [Scatter(d, singles[0])], hidden_grad, up_got
+    (down,) = finish(d_own)
+
+    finish, (d_own, up_got, out_got, hidden_grad) = exchange(
+        [down], [Scatter(d, singles[1])], d_own, up_got, out_got, hidden_grad
     )
     up = sum_tokens(normed_mid, hidden_grad, up_got, F32, room=feats)
-    up = sum_tokens(attended, attn_grad, up_got, F32, rows=feats, first=1, count=1, into=up)
-    with jax.named_scope("block_out"):
-        out_full = (out_own + out_got.astype(F32)).astype(BF)
-    (down,) = finish()
-    up, down, out_full = lax.optimization_barrier((up, down, out_full))
-
-    finish, (d_own, qkv_got, out_full) = exchange(
-        [up, down], [Scatter(u, first_stage), Scatter(d, singles[1])], d_own, qkv_got, out_full
-    )
-    tail = sum_tokens(d_own, normed, qkv_got, F32, rows=feats)
-    own_in, give_in = first_in(d_far, after(d_own, tail), held, qkv_own, size)
-    up, down = finish()
+    up, qkv_got, proj_got = lax.optimization_barrier((up, qkv_got, proj_got))
+    up = sum_tokens(
+        attended, attn_grad, proj_got, F32, rows=feats, first=1, count=1, into=up
+    )
+    (down,) = finish(up)
     for bits in singles[2:]:
         finish, _ = exchange([down], [Scatter(d, bits)])
         (down,) = finish()
-
-    up_gathers = [Gather(u, bits) for bits in reversed(singles)]
-    down_gathers = [Gather(d, bits) for bits in reversed(singles)]
-    for step in down_gathers[:-2]:
+    down_own, down_away = down[0], down[1].astype(BF)
+
+    finish_up, (d_own, qkv_got, down_own, down_away) = exchange(
+        [up], [Scatter(u, first_stage)], d_own, qkv_got, down_own, down_away
+    )
+    with jax.named_scope("down_grad_x"):
+        down_got = x_swap(down_away)
+    tail = sum_tokens(d_own, normed, qkv_got, F32, rows=feats)
+    down_got, tail = lax.optimization_barrier((down_got, tail))
+    down = down_own + down_got.astype(F32)
+
+    down_gathers = [Gather(d, bits) for bits in reversed(singles)] + [Gather(d, first_stage)]
+    for step in down_gathers[:-3]:
         finish, _ = exchange([down], [step])
         (down,) = finish()
-    steps = [Scatter(t, first_stage), Scatter(u, high_stages[0]), down_gathers[-2]]
-    finish, (own_in, give_in, out_full) = exchange(
-        [tail, up, down], steps, own_in, give_in, out_full
-    )
+    steps = [Scatter(t, first_stage), down_gathers[-3]]
+    finish, (d_own, out_got) = exchange([tail, down], steps, d_own, out_got)
+    own_in, give_in = first_in(d_far, d_own, held, qkv_own, size)
+    with jax.named_scope("block_out"):
+        out_full = (out_own + out_got.astype(F32)).astype(BF)
+        out_away = x_swap(out_full[2 * size :])
+    (up,) = finish_up(own_in, out_away)
+
+    finish_high, (own_in, give_in) = exchange(
+        [up], [Scatter(u, high_stages[0])], own_in, give_in
+    )
+    tail, down = finish()
+    finish, (own_in, give_in) = exchange([down], [down_gathers[-2]], own_in, give_in)
     with jax.named_scope("first_core"):
         got_in = core_swap(give_in)
     mid_sum = (own_in[3 * size :].astype(F32) + got_in[3 * size :].astype(F32)).astype(BF)
@@ -1090,49 +1119,44 @@
     in_main, sums_main = first_backward(
         tokens, own_in, got_in, residual_grad, vectors, None, size, (0, 2)
     )
-    tail, up, down = finish()
+    (up,) = finish_high(in_main)
+    (down,) = finish(in_main)
     for bits in high_stages[1:]:
         finish, _ = exchange([up], [Scatter(u, bits)])
         (up,) = finish()
-    for step in up_gathers[:-2]:
+
+    up_gathers = [Gather(u, bits) for bits in reversed(singles)] + [Gather(u, first_stage)]
+    for step in up_gathers[:-3]:
         finish, _ = exchange([up], [step])
         (up,) = finish()
-
-    steps = [Scatter(t, high_stages[0]), up_gathers[-2], down_gathers[-1]]
-    finish, (in_main, extra, out_full) = exchange(
-        [tail, up, down], steps, in_main, extra, out_full
-    )
+    steps = [Scatter(t, high_stages[0]), up_gathers[-3], down_gathers[-1]]
+    finish, (in_main, extra) = exchange([tail, up, down], steps, in_main, extra)
     with jax.named_scope("in_grad_x"):
         in_away = x_swap(in_main[size:])
     in_mid, sums_mid = first_backward(
         tokens, own_in, got_in, residual_grad, vectors, extra, size, (1,)
     )
-    tail, up, down = finish()
+    tail, up, down = finish(in_mid, in_away)
+    for bits in high_stages[1:]:
+        finish, _ = exchange([tail], [Scatter(t, bits)])
+        (tail,) = finish()
     small = jnp.concatenate(
         [(sums_main + sums_mid)[:2], 0.5 * mid_sums[:4], *head_sums(sums_own, sums_far, up_sums)],
         axis=0,
     )
-    for bits in high_stages[1:]:
-        finish, _ = exchange([tail], [Scatter(t, bits)])
-        (tail,) = finish()
-
-    finish, (tail, up, small, in_away, out_full) = exchange(
-        [down], [Gather(d, first_stage)], tail, up, small, in_away, out_full
-    )
+
+    steps = [Gather(t, first_stage), up_gathers[-2]]
+    finish, (small, in_away, down) = exchange([tail, up], steps, small, in_away, down)
     with jax.named_scope("small_sums"):
         small = sum_over_tensor(small)
-    with jax.named_scope("block_out"):
-        out_away = x_swap(out_full[2 * size :])
-    (down,) = finish()
-    steps = [GatherAndAdd(t, first_stage), up_gathers[-1]]
-    finish, (down, out_away) = exchange([(tail.astype(BF), small), up], steps, down, out_away)
-    (tail, small), up = finish()
+        small = small + dp_swap(small, first_stage[0])
+    tail, up = finish(small)
+
     last = high_stages[-1] if len(high_stages[-1]) == 2 else high_stages[-2]
-    rest = [bits for bits in high_stages if bits is not last]
-    for bits in reversed(rest):
+    for bits in reversed([bits for bits in high_stages if bits is not last]):
         finish, _ = exchange([(tail, small)], [GatherAndAdd(t, bits)])
         ((tail, small),) = finish()
-    steps = [GatherAndAdd(t, last), Gather(u, first_stage)]
+    steps = [GatherAndAdd(t, last), up_gathers[-1]]
     finish, _ = exchange([(tail, small), up], steps)
     (tail, small), up = finish()
     tail = tail.reshape(-1, 2, tail.shape[0] // (2 ** len(dp_bits())), width)

time: 364 us -> 352 us (0.967); the launches traced: 357 us -> 349 us
  waiting for transfers between devices: 98.6 us -> 73.9 us
  starting transfers between devices: 46.9 us -> 57.5 us
  local copies, waits for them, and re-layouts: 22.3 us -> 30.3 us
  Pallas kernels: 162 us -> 157 us
    ppermute x24 -> x25, waiting for transfers between devices: 72.2 us -> 50 us  [dp_swap(): return lax.ppermute(value, 'dp', dp_partners(lax.axis_size('dp'), bit))]
    ppermute x24 -> x25, starting transfers between devices: 29.5 us -> 40.4 us  [dp_swap(): return lax.ppermute(value, 'dp', dp_partners(lax.axis_size('dp'), bit))]
    dynamic_slice x7, local copies, waits for them, and re-layouts: 2.55 us -> 8.3 us  [split(): lax.dynamic_slice_in_dim(value, (mine ^ distance) * rows, rows, axis)]
    pallas_call x8 -> x7, Pallas kernels: 44.2 us -> 41.2 us  [sum_tokens(): pl.pallas_call(functools.partial(sum_tokens_kernel, rows, extra is not No...]
    ppermute x12 -> x13, waiting for transfers between devices: 23 us -> 20.5 us  [x_swap(): return lax.ppermute(value, 'tensor', X_SWAP)]
    unnamed x62 -> x82, local copies, waits for them, and re-layouts: 7.64 us -> 6.02 us
    select_n x13 -> x12, other arithmetic: 7.27 us -> 8.67 us  [in_order(): jnp.where(upper(bit), jnp.concatenate([got, value], axis=axis), jnp.conca...]
    ppermute x12 -> x13, starting transfers between devices: 15.3 us -> 14.7 us  [x_swap(): return lax.ppermute(value, 'tensor', X_SWAP)]
  transfers between devices with their start and end apart: 46 -> 48, of which waited for: 20 -> 19; matrix products, arithmetic and copies ran while one was open for 8% -> 9% of each run, Pallas kernels for 36% -> 36%
where the time goes in v2:
time: 352 us; the launch traced here: 349 us
  Pallas kernels  157 us (45%)
  waiting for transfers between devices  73.9 us (21%)
  starting transfers between devices  57.5 us (16%)
  local copies, waits for them, and re-layouts  30.3 us (9%)
  other arithmetic  28.9 us (8%)
    ppermute x25, waiting for transfers between devices, dp_swap(): return lax.ppermute(value, 'dp', dp_partners(lax.axis_size('dp'), bit))  50 us
    pallas_call x7, Pallas kernels, sum_tokens(): pl.pallas_call(functools.partial(sum_tokens_kernel, rows, extra is not No...  41.2 us
    ppermute x25, starting transfers between devices, dp_swap(): return lax.ppermute(value, 'dp', dp_partners(lax.axis_size('dp'), bit))  40.4 us
    pallas_call x2, Pallas kernels, attend_backward(): pl.pallas_call(functools.partial(attend_backward_kernel, size), grid_spec...  27.4 us
    pallas_call x1, Pallas kernels, mlp(): pl.pallas_call(mlp_kernel, grid=(3,), in_specs=[fixed((2 * size, width))]...  27.4 us
    ppermute x13, waiting for transfers between devices, x_swap(): return lax.ppermute(value, 'tensor', X_SWAP)  20.5 us
    pallas_call x1, Pallas kernels, attend_forward(): pl.pallas_call(functools.partial(attend_forward_kernel, size), grid_spec=...  16.9 us
    ppermute x13, starting transfers between devices, x_swap(): return lax.ppermute(value, 'tensor', X_SWAP)  14.7 us
  transfers between devices with their start and end apart: 48, of which 19 were waited for; matrix products, arithmetic and copies ran while one was open for 9% of the time, Pallas kernels for 36%

profile of v2, /device:TPU:8, one launch (start us, length us, event | category | flops | bytes accessed | tf_op | source)
XLA Modules:
  0.0 349.3 jit_solution(18340731124400819373)
XLA Ops:
  3.4 1.5 collective-permute-start
  8.7 4.8 %collective-permute-done = bf16[2,96,768]{2,1,0:T(8,128)(2,1)} collective-permute-done((bf16[2,96,768]{2,1,0:T(8,128)(2,1)}, bf16[2,96,768]{2,1,0:T(8,128)(2,1)}, u32[]{:S(2)}, u32[]{:S(2)}) %collective-permute-start) | collective-permute-done | bytes 294944 | tf_op jit(solution)/shard_map/mlp_weights_x/ppermute | solution.py:25
  13.6 2.6 collective-permute-start.1
  16.2 1.5 collective-permute-start.3
  18.3 1.8 prepare.1
  20.1 10.2 %collective-permute-done.5.x2.away_ref = bf16[512,768]{1,0:T(8,128)(2,1)S(1)} collective-permute-done((bf16[512,768]{1,0:T(8,128)(2,1)}, bf16[512,768]{1,0:T(8,128)(2,1)S(1)}, u32[]{:S(2)}, u32[]{:S(2)}) %collective-permute-start.5) | collective-permute-done | bytes 786464 | tf_op jit(solution)/shard_map/tokens/ppermute | solution.py:25
  30.3 1.7 maximum_select_fusion.6
  32.1 15.5 %collective-permute-done.2 = bf16[2,192,768]{2,1,0:T(8,128)(2,1)S(1)} collective-permute-done((bf16[2,192,768]{2,1,0:T(8,128)(2,1)S(1)}, bf16[2,192,768]{2,1,0:T(8,128)(2,1)S(1)}, u32[]{:S(2)}, u32[]{:S(2)}) %collective-permute-start.2) | collective-permute-done | bytes 589856 | tf_op jit(solution)/shard_map/mlp_weights_dp/ppermute | solution.py:786
  48.7 1.6 collective-permute-start.9
  50.3 1.5 collective-permute-start.7
  52.3 11.1 %first_norm_qkv.1 = (bf16[2048,768]{1,0:T(8,128)(2,1)}, bf16[2048,1536]{1,0:T(8,128)(2,1)}) custom-call(bf16[512,768]{1,0:T(8,128)(2,1)} %copy-done, bf16[512,768]{1,0:T(8,128)(2,1)} %collective-permute-done.4.x1, bf16[512,768]{1,0:T(8,128)(2,1)} %copy-done.2, bf16[512,768]{1,0:T(8,128)(2,1)} %copy-done.6, f32[8,768]{1,0:T(8,128)} %get-tuple-element.214.vec_ref, ...), custom_call_target="tpu_custom_call" | custom-call | flops 1 | bytes 1 | tf_op jit(solution)/shard_map/first_norm_qkv/pallas_call | solution.py:660
  63.4 16.9 %attend_forward.1 = (bf16[1536,512]{1,0:T(8,128)(2,1)}, f32[16,1536]{1,0:T(8,128)}) custom-call(s32[8,8]{1,0:T(8,128)} %get-tuple-element.212.table, s32[8,1536]{1,0:T(8,128)} %get-tuple-element.213.start_ref, bf16[2048,1536]{1,0:T(8,128)(2,1)} %get-tuple-element.217.q_ref.k_ref.v_ref, bf16[2048,1536]{1,0:T(8,128)(2,1)} %get-tuple-element.217.q_ref.k_ref.v_ref, ...), custom_call_target="tpu_custom_call" | custom-call | flops 1 | bytes 1 | tf_op jit(solution)/shard_map/attend_forward/pallas_call | solution.py:143
  81.2 4.6 %project.1.own_ref = bf16[1536,768]{1,0:T(8,128)(2,1)} custom-call(bf16[1536,512]{1,0:T(8,128)(2,1)} %get-tuple-element.240.heads_ref.left_ref.out_ref, bf16[192,768]{1,0:T(8,128)(2,1)} %copy-done.13, bf16[192,768]{1,0:T(8,128)(2,1)} %own_w.3), custom_call_target="tpu_custom_call" | custom-call | flops 1 | bytes 1 | tf_op jit(solution)/shard_map/project/pallas_call | solution.py:533
  86.2 1.7 maximum_select_fusion.up_far.dn_far
  87.9 2.5 collective-permute-done.12.b3
  91.2 1.4 copy-done.8
  92.6 27.4 %mlp.1 = (f32[1536,128]{1,0:T(8,128)}, bf16[1536,768]{1,0:T(8,128)(2,1)}, bf16[2,1536,768]{2,1,0:T(8,128)(2,1)}, bf16[2,1536,768]{2,1,0:T(8,128)(2,1)}, f32[768,...) custom-call(bf16[512,768]{1,0:T(8,128)(2,1)} %copy-done, ...), custom_call_target="tpu_custom_call" | custom-call | flops 1 | bytes 1 | tf_op jit(solution)/shard_map/mlp/pallas_call | solution.py:430
  120.5 5.6 %sum_tokens.7 = bf16[768,768]{1,0:T(8,128)(2,1)} custom-call(bf16[1536,768]{1,0:T(8,128)(2,1)} %get-tuple-element.228.left_ref.mid_ref, bf16[2,1536,768]{2,1,0:T(8,128)(2,1)} %get-tuple-element.269.right_ref), custom_call_target="tpu_custom_call" | custom-call | flops 1 | bytes 1 | tf_op jit(solution)/shard_map/sum_tokens/pallas_call | solution.py:510
  126.1 8.7 %sum_tokens.8 = bf16[1536,768]{1,0:T(8,128)(2,1)} custom-call(bf16[2,1536,768]{2,1,0:T(8,128)(2,1)} %get-tuple-element.226.left_ref, bf16[1536,768]{1,0:T(8,128)(2,1)} %get-tuple-element.230.right_ref.bg_ref), custom_call_target="tpu_custom_call" | custom-call | flops 1 | bytes 1 | tf_op jit(solution)/shard_map/sum_tokens/pallas_call | solution.py:510
  134.8 2.9 constant_dynamic-slice_fusion.8
  138.7 1.9 collective-permute-start.16
  140.7 1.4 copy-done.10
  142.1 9.9 %mid_backward.1 = (f32[768,768]{1,0:T(8,128)}, bf16[1536,768]{1,0:T(8,128)(2,1)}, bf16[1536,512]{1,0:T(8,128)(2,1)}, f32[8,768]{1,0:T(8,128)}) custom-call(bf16[1536,768]{1,0:T(8,128)(2,1)} %get-tuple-element.228.left_ref.mid_ref, f32[1536,128]{1,0:T(8,128)} %get-tuple-element.241.rstd_ref, bf16[1536,768]{1,0:T(8,128)(2,1)} %get-tuple-element.242.own_ref, ...), custom_call_target="tpu_custom_call" | custom-call | flops 1 | bytes 1 | tf_op jit(solution)/shard_map/mid_backward/pallas_call | solution.py:593
  152.0 3.4 sum_tokens.9
  155.4 13.7 %attend_backward.2 = (bf16[2048,768]{1,0:T(8,128)(2,1)}, f32[8,256]{1,0:T(8,128)}) custom-call(s32[8,8]{1,0:T(8,128)} %get-tuple-element.212.table, s32[8,1536]{1,0:T(8,128)} %get-tuple-element.213.start_ref, bf16[2048,1536]{1,0:T(8,128)(2,1)} %get-tuple-element.217.q_ref.k_ref.v_ref, bf16[2048,1536]{1,0:T(8,128)(2,1)} %get-tuple-element.217.q_ref.k_ref.v_ref, ...), custom_call_target="tpu_custom_call" | custom-call | flops 1 | bytes 1 | tf_op jit(solution)/shard_map/attend_backward/pallas_call | solution.py:239
  169.2 6.3 %sum_tokens.10 = bf16[576,768]{1,0:T(8,128)(2,1)} custom-call(bf16[2048,768]{1,0:T(8,128)(2,1)} %get-tuple-element.249.left_ref.far_d, bf16[2048,768]{1,0:T(8,128)(2,1)} %get-tuple-element.250.right_ref), custom_call_target="tpu_custom_call" | custom-call | flops 1 | bytes 1 | tf_op jit(solution)/shard_map/sum_tokens/pallas_call | solution.py:510
  175.5 1.5 convert_add_fusion
  179.4 1.8 collective-permute-start.19
  181.2 13.7 %attend_backward.3 = (bf16[2048,768]{1,0:T(8,128)(2,1)}, f32[8,256]{1,0:T(8,128)}) custom-call(s32[8,8]{1,0:T(8,128)} %get-tuple-element.212.table, s32[8,1536]{1,0:T(8,128)} %get-tuple-element.213.start_ref, bf16[2048,1536]{1,0:T(8,128)(2,1)} %get-tuple-element.217.q_ref.k_ref.v_ref, bf16[2048,1536]{1,0:T(8,128)(2,1)} %get-tuple-element.217.q_ref.k_ref.v_ref, ...), custom_call_target="tpu_custom_call" | custom-call | flops 1 | bytes 1 | tf_op jit(solution)/shard_map/attend_backward/pallas_call | solution.py:239
  196.2 2.8 collective-permute-start.20
  198.9 6.1 %sum_tokens.11.refs_1_ = f32[960,768]{1,0:T(8,128)} custom-call(bf16[1536,768]{1,0:T(8,128)(2,1)} %get-tuple-element.228.left_ref.mid_ref, bf16[2,1536,768]{2,1,0:T(8,128)(2,1)} %get-tuple-element.269.right_ref, bf16[768,768]{1,0:T(8,128)(2,1)} %collective-permute-done.16.refs_0_), custom_call_target="tpu_custom_call" | custom-call | flops 1 | bytes 1 | tf_op jit(solution)/shard_map/sum_tokens/pallas_call | solution.py:510
  205.1 2.5 collective-permute-done.19.refs_0_
  207.6 3.9 %sum_tokens.12 = f32[960,768]{1,0:T(8,128)} custom-call(bf16[1536,512]{1,0:T(8,128)(2,1)} %get-tuple-element.240.heads_ref.left_ref.out_ref, bf16[1536,768]{1,0:T(8,128)(2,1)} %get-tuple-element.243.right_ref, bf16[192,768]{1,0:T(8,128)(2,1)} %collective-permute-done.19.refs_0_, f32[960,768]{1,0:T(8,128)} %sum_tokens.11.refs_1_), custom_call_target="tpu_custom_call", output_to_operand_aliasing={{}: (3, {})} | custom-call | flops 1 | bytes 1 | tf_op jit(solution)/shard_map/sum_tokens/pallas_call | solution.py:510
  211.7 1.5 constant_dynamic-slice_fusion.5
  213.2 2.3 dynamic-slice_convert_fusion
  215.5 2.2 collective-permute-start.21
  217.8 2.0 collective-permute-start.25
  219.8 7.1 %sum_tokens.13 = f32[576,768]{1,0:T(8,128)} custom-call(bf16[2048,768]{1,0:T(8,128)(2,1)} %get-tuple-element.301.left_ref.own_d, bf16[2048,768]{1,0:T(8,128)(2,1)} %get-tuple-element.250.right_ref, bf16[576,768]{1,0:T(8,128)(2,1)} %copy-done.20), custom_call_target="tpu_custom_call" | custom-call | flops 1 | bytes 1 | tf_op jit(solution)/shard_map/sum_tokens/pallas_call | solution.py:510
  226.9 2.3 constant_dynamic-slice_fusion.4
  229.2 2.0 dynamic-slice_convert_fusion.2
  232.9 3.4 collective-permute-start.24
  236.2 9.7 %first_in.1 = (bf16[1024,768]{1,0:T(8,128)(2,1)}, bf16[1024,768]{1,0:T(8,128)(2,1)}) custom-call(bf16[2048,768]{1,0:T(8,128)(2,1)} %get-tuple-element.249.left_ref.far_d, bf16[2048,768]{1,0:T(8,128)(2,1)} %get-tuple-element.301.left_ref.own_d, bf16[592,768]{1,0:T(8,128)(2,1)} %copy-done.3, bf16[592,768]{1,0:T(8,128)(2,1)} %copy-done.1), custom_call_target="tpu_custom_call" | custom-call | flops 1 | bytes 1 | tf_op jit(solution)/shard_map/first_in/pallas_call | solution.py:713
  251.2 1.9 collective-permute-start.30
  253.9 1.9 collective-permute-start.27
  259.5 3.9 %first_backward.2 = (bf16[512,768]{1,0:T(8,128)(2,1)}, f32[8,768]{1,0:T(8,128)}) custom-call(bf16[512,768]{1,0:T(8,128)(2,1)} %copy-done, bf16[512,768]{1,0:T(8,128)(2,1)} %copy-done.2, bf16[1024,768]{1,0:T(8,128)(2,1)} %get-tuple-element.319.own_ref, bf16[1024,768]{1,0:T(8,128)(2,1)} %copy-done.4, f32[768,768]{1,0:T(8,128)} %get-tuple-element.321.rg_ref, ...), custom_call_target="tpu_custom_call" | custom-call | flops 1 | bytes 1 | tf_op jit(solution)/shard_map/first_backward/pallas_call | solution.py:758
  265.7 3.4 collective-permute-done.27
  270.9 1.9 collective-permute-start.36
  275.1 1.6 collective-permute-start.37
  277.4 6.0 %collective-permute-start.35 = (bf16[120,768]{1,0:T(8,128)(2,1)S(1)}, bf16[120,768]{1,0:T(8,128)(2,1)S(1)}, u32[]{:S(2)}, u32[]{:S(2)}) collective-permute-start(bf16[120,768]{1,0:T(8,128)(2,1)S(1)} %convert_add_fusion.5), channel_id=1, source_target_pairs={{0,16},{4,20},{8,24},{12,28},{16,0},{20,4},{24,8},{28,12},{1,17},{... | collective-permute-start | bytes 552968 | tf_op jit(solution)/shard_map/up_proj_grad_dp/ppermute | solution.py:786
  283.5 2.1 collective-permute-start.33
  285.5 3.2 first_backward.3
  289.5 5.1 %collective-permute-done.32 = bf16[72,768]{1,0:T(8,128)(2,1)S(1)} collective-permute-done((bf16[72,768]{1,0:T(8,128)(2,1)}, bf16[72,768]{1,0:T(8,128)(2,1)S(1)}, u32[]{:S(2)}, u32[]{:S(2)}) %collective-permute-start.32) | collective-permute-done | bytes 110624 | tf_op jit(solution)/shard_map/qkv_grad_dp/ppermute | solution.py:786
  295.7 3.8 %collective-permute-done.34 = bf16[72,768]{1,0:T(8,128)(2,1)S(1)} collective-permute-done((bf16[72,768]{1,0:T(8,128)(2,1)S(1)}, bf16[72,768]{1,0:T(8,128)(2,1)S(1)}, u32[]{:S(2)}, u32[]{:S(2)}) %collective-permute-start.34) | collective-permute-done | bytes 110624 | tf_op jit(solution)/shard_map/qkv_grad_dp/ppermute | solution.py:786
  300.3 1.6 maximum_select_fusion.3
  302.1 4.8 %collective-permute-start.39 = (bf16[240,768]{1,0:T(8,128)(2,1)S(1)}, bf16[240,768]{1,0:T(8,128)(2,1)S(1)}, u32[]{:S(2)}, u32[]{:S(2)}) collective-permute-start(bf16[240,768]{1,0:T(8,128)(2,1)S(1)} %maximum_select_fusion.10), channel_id=1, source_target_pairs={{0,8},{4,12},{8,0},{12,4},{16,24},{20,28},{24,16},{28,20},{1,9},{5... | collective-permute-start | bytes 1105928 | tf_op jit(solution)/shard_map/up_proj_grad_dp/ppermute | solution.py:786
  309.1 2.4 collective-permute-done.41
  312.1 3.9 %collective-permute-done.43 = f32[12,768]{1,0:T(8,128)S(1)} collective-permute-done((f32[12,768]{1,0:T(8,128)S(1)}, f32[12,768]{1,0:T(8,128)S(1)}, u32[]{:S(2)}, u32[]{:S(2)}) %collective-permute-start.43) | collective-permute-done | bytes 36896 | tf_op jit(solution)/shard_map/small_sums/ppermute | solution.py:786
  319.5 1.6 collective-permute-start.45
  322.2 1.6 convert_element_type.180
  323.7 1.7 pad_maximum_fusion
  325.4 6.5 %collective-permute-done.44 = bf16[160,768]{1,0:T(8,128)(2,1)S(1)} collective-permute-done((bf16[160,768]{1,0:T(8,128)(2,1)S(1)}, bf16[160,768]{1,0:T(8,128)(2,1)S(1)}, u32[]{:S(2)}, u32[]{:S(2)}) %collective-permute-start.44) | collective-permute-done | bytes 245792 | tf_op jit(solution)/shard_map/qkv_grad_dp/ppermute | solution.py:786
  333.2 8.1 %collective-permute-done.46 = bf16[160,768]{1,0:T(8,128)(2,1)S(1)} collective-permute-done((bf16[160,768]{1,0:T(8,128)(2,1)S(1)}, bf16[160,768]{1,0:T(8,128)(2,1)S(1)}, u32[]{:S(2)}, u32[]{:S(2)}) %collective-permute-start.46) | collective-permute-done | bytes 245792 | tf_op jit(solution)/shard_map/qkv_grad_dp/ppermute | solution.py:786
  341.3 1.9 maximum_select_fusion.1
  343.2 1.6 slice_convert_fusion
  (225 shorter events, 50.5 us)
Async XLA Ops:
  3.4 10.2 %collective-permute-start = (bf16[2,96,768]{2,1,0:T(8,128)(2,1)}, bf16[2,96,768]{2,1,0:T(8,128)(2,1)}, u32[]{:S(2)}, u32[]{:S(2)}) collective-permute-start(bf16[2,96,768]{2,1,0:T(8,128)(2,1)} %pad_maximum_fusion.5), channel_id=1, source_target_pairs={{0,2},{1,3},{2,0},{3,1},{4,6},{5,7},{6,4},{7,5},{8,10},{9,11},{10,... | collective-permute-start | bytes 884744 | tf_op jit(solution)/shard_map/mlp_weights_x/ppermute | solution.py:25
  6.0 11.7 %copy-start = (bf16[512,768]{1,0:T(8,128)(2,1)}, bf16[512,768]{1,0:T(8,128)(2,1)S(1)}, u32[]{:S(2)}) copy-start(bf16[512,768]{1,0:T(8,128)(2,1)S(1)} %get-tuple-element.208.x0.home_ref) | copy-start | bytes 2359300
  6.0 24.4 %collective-permute-start.5 = (bf16[512,768]{1,0:T(8,128)(2,1)}, bf16[512,768]{1,0:T(8,128)(2,1)S(1)}, u32[]{:S(2)}, u32[]{:S(2)}) collective-permute-start(bf16[512,768]{1,0:T(8,128)(2,1)} %get-tuple-element.414), channel_id=1, source_target_pairs={{0,2},{1,3},{2,0},{3,1},{4,6},{5,7},{6,4},{7,5},{8,10},{9,11},{10,... | collective-permute-start | bytes 2359304 | tf_op jit(solution)/shard_map/tokens/ppermute | solution.py:25
  8.7 39.4 %copy-start.1 = (bf16[592,768]{1,0:T(8,128)(2,1)}, bf16[592,768]{1,0:T(8,128)(2,1)S(1)}, u32[]{:S(2)}) copy-start(bf16[592,768]{1,0:T(8,128)(2,1)S(1)} %fusion.1.own_ref.upb_own.own_w_ref) | copy-start | bytes 2727940
  13.6 16.8 %collective-permute-start.1 = (bf16[2,96,768]{2,1,0:T(8,128)(2,1)}, bf16[2,96,768]{2,1,0:T(8,128)(2,1)}, u32[]{:S(2)}, u32[]{:S(2)}) collective-permute-start(bf16[2,96,768]{2,1,0:T(8,128)(2,1)} %collective-permute-done), channel_id=1, source_target_pairs={{0,16},{4,20},{8,24},{12,28},{16,0},{20,4},{24,8},{28,12},{1,17},{... | collective-permute-start | bytes 884744 | tf_op jit(solution)/shard_map/mlp_weights_dp/ppermute | solution.py:786
  16.2 32.5 %collective-permute-start.3 = (bf16[592,768]{1,0:T(8,128)(2,1)S(1)}, bf16[592,768]{1,0:T(8,128)(2,1)S(1)}, u32[]{:S(2)}, u32[]{:S(2)}) collective-permute-start(bf16[592,768]{1,0:T(8,128)(2,1)S(1)} %fusion.1.own_ref.upb_own.own_w_ref), channel_id=1, source_target_pairs={{0,2},{1,3},{2,0},{3,1},{4,6},{5,7},{6,4},{7,5},{8,10},{9,11},{10,... | collective-permute-start | bytes 2727944 | tf_op jit(solution)/shard_map/qkv_weights_x/ppermute | solution.py:25
  17.7 30.4 %collective-permute-start.4 = (bf16[512,768]{1,0:T(8,128)(2,1)S(1)}, bf16[512,768]{1,0:T(8,128)(2,1)}, u32[]{:S(2)}, u32[]{:S(2)}) collective-permute-start(bf16[512,768]{1,0:T(8,128)(2,1)S(1)} %get-tuple-element.208.x0.home_ref), channel_id=1, source_target_pairs={{0,1},{1,0},{2,3},{3,2},{4,5},{5,4},{6,7},{7,6},{8,9},{9,8},{10,11... | collective-permute-start | bytes 2359304 | tf_op jit(solution)/shard_map/tokens/ppermute | solution.py:29
  30.3 17.8 %copy-start.2 = (bf16[512,768]{1,0:T(8,128)(2,1)}, bf16[512,768]{1,0:T(8,128)(2,1)S(1)}, u32[]{:S(2)}) copy-start(bf16[512,768]{1,0:T(8,128)(2,1)S(1)} %collective-permute-done.5.x2.away_ref) | copy-start | bytes 2359300
  30.3 18.3 %collective-permute-start.6 = (bf16[512,768]{1,0:T(8,128)(2,1)S(1)}, bf16[512,768]{1,0:T(8,128)(2,1)S(1)}, u32[]{:S(2)}, u32[]{:S(2)}) collective-permute-start(bf16[512,768]{1,0:T(8,128)(2,1)S(1)} %collective-permute-done.5.x2.away_ref), channel_id=1, source_target_pairs={{0,1},{1,0},{2,3},{3,2},{4,5},{5,4},{6,7},{7,6},{8,9},{9,8},{10,11... | collective-permute-start | bytes 2359304 | tf_op jit(solution)/shard_map/tokens/ppermute | solution.py:29
  32.0 18.3 %copy-start.7 = (bf16[512,768]{1,0:T(8,128)(2,1)S(1)}, bf16[512,768]{1,0:T(8,128)(2,1)}, u32[]{:S(2)}) copy-start(bf16[512,768]{1,0:T(8,128)(2,1)} %pad_maximum_fusion.4.b0) | copy-start | bytes 2359300
  32.0 19.7 %copy-start.12 = (bf16[192,768]{1,0:T(8,128)(2,1)S(1)}, bf16[192,768]{1,0:T(8,128)(2,1)}, u32[]{:S(2)}) copy-start(bf16[192,768]{1,0:T(8,128)(2,1)} %own_w.3) | copy-start | bytes 884740
  32.0 15.6 %collective-permute-start.2 = (bf16[2,192,768]{2,1,0:T(8,128)(2,1)S(1)}, bf16[2,192,768]{2,1,0:T(8,128)(2,1)S(1)}, u32[]{:S(2)}, u32[]{:S(2)}) collective-permute-start(bf16[2,192,768]{2,1,0:T(8,128)(2,1)S(1)} %maximum_select_fusion.6), channel_id=1, source_target_pairs={{0,8},{4,12},{8,0},{12,4},{16,24},{20,28},{24,16},{28,20},{1,9},{5... | collective-permute-start | bytes 1769480 | tf_op jit(solution)/shard_map/mlp_weights_dp/ppermute | solution.py:786
  48.7 31.7 %collective-permute-start.9 = (bf16[2,384,768]{2,1,0:T(8,128)(2,1)S(1)}, bf16[2,384,768]{2,1,0:T(8,128)(2,1)S(1)}, u32[]{:S(2)}, u32[]{:S(2)}) collective-permute-start(bf16[2,384,768]{2,1,0:T(8,128)(2,1)S(1)} %maximum_select_fusion.2), channel_id=1, source_target_pairs={{0,4},{4,0},{8,12},{12,8},{16,20},{20,16},{24,28},{28,24},{1,5},{5... | collective-permute-start | bytes 3538952 | tf_op jit(solution)/shard_map/mlp_weights_dp/ppermute | solution.py:786
  50.3 30.1 %collective-permute-start.8 = (bf16[512,768]{1,0:T(8,128)(2,1)S(1)}, bf16[512,768]{1,0:T(8,128)(2,1)S(1)}, u32[]{:S(2)}, u32[]{:S(2)}) collective-permute-start(bf16[512,768]{1,0:T(8,128)(2,1)S(1)} %copy-done.7), channel_id=1, source_target_pairs={{0,1},{1,0},{2,3},{3,2},{4,5},{5,4},{6,7},{7,6},{8,9},{9,8},{10,11... | collective-permute-start | bytes 2359304 | tf_op jit(solution)/shard_map/cotangent/ppermute | solution.py:29
  50.3 30.1 %collective-permute-start.7 = (bf16[256,768]{1,0:T(8,128)(2,1)}, bf16[256,768]{1,0:T(8,128)(2,1)S(1)}, u32[]{:S(2)}, u32[]{:S(2)}) collective-permute-start(bf16[256,768]{1,0:T(8,128)(2,1)} %get-tuple-element.220), channel_id=1, source_target_pairs={{0,2},{1,3},{2,0},{3,1},{4,6},{5,7},{6,4},{7,5},{8,10},{9,11},{10,... | collective-permute-start | bytes 1179656 | tf_op jit(solution)/shard_map/cotangent/ppermute | solution.py:25
  51.8 28.6 %collective-permute-start.10 = (bf16[192,768]{1,0:T(8,128)(2,1)S(1)}, bf16[192,768]{1,0:T(8,128)(2,1)S(1)}, u32[]{:S(2)}, u32[]{:S(2)}) collective-permute-start(bf16[192,768]{1,0:T(8,128)(2,1)S(1)} %copy-done.12), channel_id=1, source_target_pairs={{0,2},{1,3},{2,0},{3,1},{4,6},{5,7},{6,4},{7,5},{8,10},{9,11},{10,... | collective-permute-start | bytes 884744 | tf_op jit(solution)/shard_map/proj_weight_x/ppermute | solution.py:25
  80.3 7.6 %copy-start.23 = (bf16[512,768]{1,0:T(8,128)(2,1)}, bf16[512,768]{1,0:T(8,128)(2,1)S(1)}, u32[]{:S(2)}) copy-start(bf16[512,768]{1,0:T(8,128)(2,1)S(1)} %collective-permute-done.8.b1) | copy-start | bytes 2359300
  80.3 7.6 %copy-start.30 = (bf16[256,768]{1,0:T(8,128)(2,1)}, bf16[256,768]{1,0:T(8,128)(2,1)S(1)}, u32[]{:S(2)}) copy-start(bf16[256,768]{1,0:T(8,128)(2,1)S(1)} %collective-permute-done.7.b2) | copy-start | bytes 1179652
  85.7 5.3 %collective-permute-start.11 = (bf16[1536,768]{1,0:T(8,128)(2,1)}, bf16[1536,768]{1,0:T(8,128)(2,1)S(1)}, u32[]{:S(2)}, u32[]{:S(2)}) collective-permute-start(bf16[1536,768]{1,0:T(8,128)(2,1)} %project.1.own_ref), channel_id=1, source_target_pairs={{0,1},{1,0},{2,3},{3,2},{4,5},{5,4},{6,7},{7,6},{8,9},{9,8},{10,11... | collective-permute-start | bytes 7077896 | tf_op jit(solution)/shard_map/attn_core/ppermute | solution.py:29
  85.7 4.7 %collective-permute-start.12 = (bf16[256,768]{1,0:T(8,128)(2,1)S(1)}, bf16[256,768]{1,0:T(8,128)(2,1)S(1)}, u32[]{:S(2)}, u32[]{:S(2)}) collective-permute-start(bf16[256,768]{1,0:T(8,128)(2,1)S(1)} %collective-permute-done.7.b2), channel_id=1, source_target_pairs={{0,1},{1,0},{2,3},{3,2},{4,5},{5,4},{6,7},{7,6},{8,9},{9,8},{10,11... | collective-permute-start | bytes 1179656 | tf_op jit(solution)/shard_map/cotangent/ppermute | solution.py:29
  120.1 20.6 %collective-permute-start.13 = (bf16[1536,768]{1,0:T(8,128)(2,1)}, bf16[1536,768]{1,0:T(8,128)(2,1)S(1)}, u32[]{:S(2)}, u32[]{:S(2)}) collective-permute-start(bf16[1536,768]{1,0:T(8,128)(2,1)} %get-tuple-element.242.own_ref), channel_id=1, source_target_pairs={{0,1},{1,0},{2,3},{3,2},{4,5},{5,4},{6,7},{7,6},{8,9},{9,8},{10,11... | collective-permute-start | bytes 7077896 | tf_op jit(solution)/shard_map/mid_core/ppermute | solution.py:29
  137.7 37.8 %collective-permute-start.14 = (bf16[2,384,768]{2,1,0:T(8,128)(2,1)}, bf16[2,384,768]{2,1,0:T(8,128)(2,1)}, u32[]{:S(2)}, u32[]{:S(2)}) collective-permute-start(bf16[2,384,768]{2,1,0:T(8,128)(2,1)} %get-tuple-element.245), channel_id=1, source_target_pairs={{0,4},{4,0},{8,12},{12,8},{16,20},{20,16},{24,28},{28,24},{1,5},{5... | collective-permute-start | bytes 3538952 | tf_op jit(solution)/shard_map/down_grad_dp/ppermute | solution.py:786
  138.7 57.3 %collective-permute-start.16 = (bf16[768,768]{1,0:T(8,128)(2,1)}, bf16[768,768]{1,0:T(8,128)(2,1)}, u32[]{:S(2)}, u32[]{:S(2)}) collective-permute-start(bf16[768,768]{1,0:T(8,128)(2,1)} %sum_tokens.7), channel_id=1, source_target_pairs={{0,2},{1,3},{2,0},{3,1},{4,6},{5,7},{6,4},{7,5},{8,10},{9,11},{10,... | collective-permute-start | bytes 3538952 | tf_op jit(solution)/shard_map/up_grad_x/ppermute | solution.py:25
  178.0 18.0 %collective-permute-start.17 = (bf16[768,768]{1,0:T(8,128)(2,1)}, bf16[768,768]{1,0:T(8,128)(2,1)S(1)}, u32[]{:S(2)}, u32[]{:S(2)}) collective-permute-start(bf16[768,768]{1,0:T(8,128)(2,1)} %get-tuple-element.262), channel_id=1, source_target_pairs={{0,1},{1,0},{2,3},{3,2},{4,5},{5,4},{6,7},{7,6},{8,9},{9,8},{10,11... | collective-permute-start | bytes 3538952 | tf_op jit(solution)/shard_map/block_out/ppermute | solution.py:29
  178.1 16.8 %collective-permute-start.15 = (bf16[2,192,768]{2,1,0:T(8,128)(2,1)}, bf16[2,192,768]{2,1,0:T(8,128)(2,1)}, u32[]{:S(2)}, u32[]{:S(2)}) collective-permute-start(bf16[2,192,768]{2,1,0:T(8,128)(2,1)} %dynamic-slice_convert_fusion.1), channel_id=1, source_target_pairs={{0,8},{4,12},{8,0},{12,4},{16,24},{20,28},{24,16},{28,20},{1,9},{5... | collective-permute-start | bytes 1769480 | tf_op jit(solution)/shard_map/down_grad_dp/ppermute | solution.py:786
  179.1 28.4 %collective-permute-start.18 = (bf16[576,768]{1,0:T(8,128)(2,1)}, bf16[576,768]{1,0:T(8,128)(2,1)S(1)}, u32[]{:S(2)}, u32[]{:S(2)}) collective-permute-start(bf16[576,768]{1,0:T(8,128)(2,1)} %sum_tokens.10), channel_id=1, source_target_pairs={{0,2},{1,3},{2,0},{3,1},{4,6},{5,7},{6,4},{7,5},{8,10},{9,11},{10,... | collective-permute-start | bytes 2654216 | tf_op jit(solution)/shard_map/qkv_grad_x/ppermute | solution.py:25
  179.4 28.2 %collective-permute-start.19 = (bf16[192,768]{1,0:T(8,128)(2,1)S(1)}, bf16[192,768]{1,0:T(8,128)(2,1)}, u32[]{:S(2)}, u32[]{:S(2)}) collective-permute-start(bf16[192,768]{1,0:T(8,128)(2,1)S(1)} %copy-done.32), channel_id=1, source_target_pairs={{0,2},{1,3},{2,0},{3,1},{4,6},{5,7},{6,4},{7,5},{8,10},{9,11},{10,... | collective-permute-start | bytes 884744 | tf_op jit(solution)/shard_map/proj_grad_x/ppermute | solution.py:25
  196.1 9.0 %copy-start.18 = (bf16[768,768]{1,0:T(8,128)(2,1)}, bf16[768,768]{1,0:T(8,128)(2,1)S(1)}, u32[]{:S(2)}) copy-start(bf16[768,768]{1,0:T(8,128)(2,1)S(1)} %collective-permute-done.17) | copy-start | bytes 3538948
  196.2 15.4 %collective-permute-start.20 = (bf16[2,96,768]{2,1,0:T(8,128)(2,1)S(1)}, bf16[2,96,768]{2,1,0:T(8,128)(2,1)S(1)}, u32[]{:S(2)}, u32[]{:S(2)}) collective-permute-start(bf16[2,96,768]{2,1,0:T(8,128)(2,1)S(1)} %dynamic-slice_convert_fusion.3), channel_id=1, source_target_pairs={{0,16},{4,20},{8,24},{12,28},{16,0},{20,4},{24,8},{28,12},{1,17},{... | collective-permute-start | bytes 884744 | tf_op jit(solution)/shard_map/down_grad_dp/ppermute | solution.py:786
  215.5 11.4 %collective-permute-start.21 = (bf16[96,768]{1,0:T(8,128)(2,1)S(1)}, bf16[96,768]{1,0:T(8,128)(2,1)S(1)}, u32[]{:S(2)}, u32[]{:S(2)}) collective-permute-start(bf16[96,768]{1,0:T(8,128)(2,1)S(1)} %fusion.4), channel_id=1, source_target_pairs={{0,2},{1,3},{2,0},{3,1},{4,6},{5,7},{6,4},{7,5},{8,10},{9,11},{10,... | collective-permute-start | bytes 442376 | tf_op jit(solution)/shard_map/down_grad_x/ppermute | solution.py:25
  217.8 28.3 %collective-permute-start.25 = (bf16[480,768]{1,0:T(8,128)(2,1)}, bf16[480,768]{1,0:T(8,128)(2,1)}, u32[]{:S(2)}, u32[]{:S(2)}) collective-permute-start(bf16[480,768]{1,0:T(8,128)(2,1)} %dynamic-slice_convert_fusion), channel_id=1, source_target_pairs={{0,4},{4,0},{8,12},{12,8},{16,20},{20,16},{24,28},{28,24},{1,5},{5... | collective-permute-start | bytes 2211848 | tf_op jit(solution)/shard_map/up_proj_grad_dp/ppermute | solution.py:786
  219.8 11.4 %copy-start.19 = (bf16[768,768]{1,0:T(8,128)(2,1)S(1)}, bf16[768,768]{1,0:T(8,128)(2,1)}, u32[]{:S(2)}) copy-start(bf16[768,768]{1,0:T(8,128)(2,1)} %copy-done.18) | copy-start | bytes 3538948
  231.2 14.7 %collective-permute-start.23 = (bf16[288,768]{1,0:T(8,128)(2,1)}, bf16[288,768]{1,0:T(8,128)(2,1)}, u32[]{:S(2)}, u32[]{:S(2)}) collective-permute-start(bf16[288,768]{1,0:T(8,128)(2,1)} %dynamic-slice_convert_fusion.2), channel_id=1, source_target_pairs={{0,4},{4,0},{8,12},{12,8},{16,20},{20,16},{24,28},{28,24},{1,5},{5... | collective-permute-start | bytes 1327112 | tf_op jit(solution)/shard_map/qkv_grad_dp/ppermute | solution.py:786
  232.3 13.7 %collective-permute-start.22 = (bf16[256,768]{1,0:T(8,128)(2,1)}, bf16[256,768]{1,0:T(8,128)(2,1)}, u32[]{:S(2)}, u32[]{:S(2)}) collective-permute-start(bf16[256,768]{1,0:T(8,128)(2,1)} %slice.158), channel_id=1, source_target_pairs={{0,2},{1,3},{2,0},{3,1},{4,6},{5,7},{6,4},{7,5},{8,10},{9,11},{10,... | collective-permute-start | bytes 1179656 | tf_op jit(solution)/shard_map/block_out/ppermute | solution.py:25
  232.9 13.1 %collective-permute-start.24 = (bf16[96,768]{1,0:T(8,128)(2,1)S(1)}, bf16[96,768]{1,0:T(8,128)(2,1)S(1)}, u32[]{:S(2)}, u32[]{:S(2)}) collective-permute-start(bf16[96,768]{1,0:T(8,128)(2,1)S(1)} %convert_add_fusion.6), channel_id=1, source_target_pairs={{0,16},{4,20},{8,24},{12,28},{16,0},{20,4},{24,8},{28,12},{1,17},{... | collective-permute-start | bytes 442376 | tf_op jit(solution)/shard_map/down_grad_dp/ppermute | solution.py:786
  246.0 5.2 %copy-start.16 = (bf16[192,768]{1,0:T(8,128)(2,1)}, bf16[192,768]{1,0:T(8,128)(2,1)S(1)}, u32[]{:S(2)}) copy-start(bf16[192,768]{1,0:T(8,128)(2,1)S(1)} %maximum_select_fusion.11) | copy-start | bytes 884740
  248.9 7.7 %collective-permute-start.29 = (bf16[1024,768]{1,0:T(8,128)(2,1)}, bf16[1024,768]{1,0:T(8,128)(2,1)S(1)}, u32[]{:S(2)}, u32[]{:S(2)}) collective-permute-start(bf16[1024,768]{1,0:T(8,128)(2,1)} %get-tuple-element.320), channel_id=1, source_target_pairs={{0,1},{1,0},{2,3},{3,2},{4,5},{5,4},{6,7},{7,6},{8,9},{9,8},{10,11... | collective-permute-start | bytes 4718600 | tf_op jit(solution)/shard_map/first_core/ppermute | solution.py:29
  250.3 8.1 %copy-start.5 = (f32[288,768]{1,0:T(8,128)S(1)}, f32[288,768]{1,0:T(8,128)}, u32[]{:S(2)}) copy-start(f32[288,768]{1,0:T(8,128)} %constant_dynamic-slice_fusion.4) | copy-start | bytes 2654212
  251.2 13.2 %collective-permute-start.30 = (bf16[192,768]{1,0:T(8,128)(2,1)S(1)}, bf16[192,768]{1,0:T(8,128)(2,1)S(1)}, u32[]{:S(2)}, u32[]{:S(2)}) collective-permute-start(bf16[192,768]{1,0:T(8,128)(2,1)S(1)} %maximum_select_fusion.11), channel_id=1, source_target_pairs={{0,8},{4,12},{8,0},{12,4},{16,24},{20,28},{24,16},{28,20},{1,9},{5... | collective-permute-start | bytes 884744 | tf_op jit(solution)/shard_map/down_grad_dp/ppermute | solution.py:786
  253.1 12.6 %collective-permute-start.26 = (bf16[120,768]{1,0:T(8,128)(2,1)}, bf16[120,768]{1,0:T(8,128)(2,1)S(1)}, u32[]{:S(2)}, u32[]{:S(2)}) collective-permute-start(bf16[120,768]{1,0:T(8,128)(2,1)} %get-tuple-element.309), channel_id=1, source_target_pairs={{0,16},{4,20},{8,24},{12,28},{16,0},{20,4},{24,8},{28,12},{1,17},{... | collective-permute-start | bytes 552968 | tf_op jit(solution)/shard_map/up_proj_grad_dp/ppermute | solution.py:786
  253.9 15.2 %collective-permute-start.27 = (bf16[120,768]{1,0:T(8,128)(2,1)S(1)}, bf16[120,768]{1,0:T(8,128)(2,1)S(1)}, u32[]{:S(2)}, u32[]{:S(2)}) collective-permute-start(bf16[120,768]{1,0:T(8,128)(2,1)S(1)} %get-tuple-element.310), channel_id=1, source_target_pairs={{0,8},{4,12},{8,0},{12,4},{16,24},{20,28},{24,16},{28,20},{1,9},{5... | collective-permute-start | bytes 552968 | tf_op jit(solution)/shard_map/up_proj_grad_dp/ppermute | solution.py:786
  255.8 13.2 %collective-permute-start.28 = (bf16[120,768]{1,0:T(8,128)(2,1)S(1)}, bf16[120,768]{1,0:T(8,128)(2,1)S(1)}, u32[]{:S(2)}, u32[]{:S(2)}) collective-permute-start(bf16[120,768]{1,0:T(8,128)(2,1)S(1)} %get-tuple-element.311), channel_id=1, source_target_pairs={{0,24},{4,28},{8,16},{12,20},{16,8},{20,12},{24,0},{28,4},{1,25},{... | collective-permute-start | bytes 552968 | tf_op jit(solution)/shard_map/up_proj_grad_dp/ppermute | solution.py:786
  258.0 11.4 %collective-permute-start.31 = (bf16[256,768]{1,0:T(8,128)(2,1)S(1)}, bf16[256,768]{1,0:T(8,128)(2,1)S(1)}, u32[]{:S(2)}, u32[]{:S(2)}) collective-permute-start(bf16[256,768]{1,0:T(8,128)(2,1)S(1)} %add_convert_fusion.1), channel_id=1, source_target_pairs={{0,2},{1,3},{2,0},{3,1},{4,6},{5,7},{6,4},{7,5},{8,10},{9,11},{10,... | collective-permute-start | bytes 1179656 | tf_op jit(solution)/shard_map/first_mid_x/ppermute | solution.py:25
  259.5 9.6 %copy-start.17 = (bf16[192,768]{1,0:T(8,128)(2,1)S(1)}, bf16[192,768]{1,0:T(8,128)(2,1)}, u32[]{:S(2)}) copy-start(bf16[192,768]{1,0:T(8,128)(2,1)} %copy-done.16) | copy-start | bytes 884740
  259.5 9.8 %copy-start.11 = (f32[120,768]{1,0:T(8,128)S(1)}, f32[120,768]{1,0:T(8,128)}, u32[]{:S(2)}) copy-start(f32[120,768]{1,0:T(8,128)} %constant_dynamic-slice_fusion.3) | copy-start | bytes 1105924
  264.4 8.4 %copy-start.36 = (f32[8,768]{1,0:T(8,128)S(1)}, f32[8,768]{1,0:T(8,128)}, u32[]{:S(2)}) copy-start(f32[8,768]{1,0:T(8,128)} %get-tuple-element.350) | copy-start | bytes 73732
  264.4 10.6 %copy-start.24 = (bf16[512,768]{1,0:T(8,128)(2,1)S(1)}, bf16[512,768]{1,0:T(8,128)(2,1)}, u32[]{:S(2)}) copy-start(bf16[512,768]{1,0:T(8,128)(2,1)} %get-tuple-element.342) | copy-start | bytes 2359300
  270.9 28.7 %collective-permute-start.36 = (bf16[384,768]{1,0:T(8,128)(2,1)S(1)}, bf16[384,768]{1,0:T(8,128)(2,1)}, u32[]{:S(2)}, u32[]{:S(2)}) collective-permute-start(bf16[384,768]{1,0:T(8,128)(2,1)S(1)} %maximum_select_fusion.7), channel_id=1, source_target_pairs={{0,4},{4,0},{8,12},{12,8},{16,20},{20,16},{24,28},{28,24},{1,5},{5... | collective-permute-start | bytes 1769480 | tf_op jit(solution)/shard_map/down_grad_dp/ppermute | solution.py:786
  275.1 24.5 %collective-permute-start.37 = (bf16[256,768]{1,0:T(8,128)(2,1)S(1)}, bf16[256,768]{1,0:T(8,128)(2,1)S(1)}, u32[]{:S(2)}, u32[]{:S(2)}) collective-permute-start(bf16[256,768]{1,0:T(8,128)(2,1)S(1)} %slice.130), channel_id=1, source_target_pairs={{0,2},{1,3},{2,0},{3,1},{4,6},{5,7},{6,4},{7,5},{8,10},{9,11},{10,... | collective-permute-start | bytes 1179656 | tf_op jit(solution)/shard_map/in_grad_x/ppermute | solution.py:25
  277.4 17.2 %copy-start.34 = (bf16[72,768]{1,0:T(8,128)(2,1)S(1)}, bf16[72,768]{1,0:T(8,128)(2,1)}, u32[]{:S(2)}) copy-start(bf16[72,768]{1,0:T(8,128)(2,1)} %get-tuple-element.337) | copy-start | bytes 331780
  277.4 22.2 %collective-permute-start.35 = (bf16[120,768]{1,0:T(8,128)(2,1)S(1)}, bf16[120,768]{1,0:T(8,128)(2,1)S(1)}, u32[]{:S(2)}, u32[]{:S(2)}) collective-permute-start(bf16[120,768]{1,0:T(8,128)(2,1)S(1)} %convert_add_fusion.5), channel_id=1, source_target_pairs={{0,16},{4,20},{8,24},{12,28},{16,0},{20,4},{24,8},{28,12},{1,17},{... | collective-permute-start | bytes 552968 | tf_op jit(solution)/shard_map/up_proj_grad_dp/ppermute | solution.py:786
  283.4 11.2 %collective-permute-start.32 = (bf16[72,768]{1,0:T(8,128)(2,1)}, bf16[72,768]{1,0:T(8,128)(2,1)S(1)}, u32[]{:S(2)}, u32[]{:S(2)}) collective-permute-start(bf16[72,768]{1,0:T(8,128)(2,1)} %get-tuple-element.335), channel_id=1, source_target_pairs={{0,16},{4,20},{8,24},{12,28},{16,0},{20,4},{24,8},{28,12},{1,17},{... | collective-permute-start | bytes 331784 | tf_op jit(solution)/shard_map/qkv_grad_dp/ppermute | solution.py:786
  283.5 12.3 %collective-permute-start.33 = (bf16[72,768]{1,0:T(8,128)(2,1)}, bf16[72,768]{1,0:T(8,128)(2,1)S(1)}, u32[]{:S(2)}, u32[]{:S(2)}) collective-permute-start(bf16[72,768]{1,0:T(8,128)(2,1)} %get-tuple-element.336), channel_id=1, source_target_pairs={{0,8},{4,12},{8,0},{12,4},{16,24},{20,28},{24,16},{28,20},{1,9},{5... | collective-permute-start | bytes 331784 | tf_op jit(solution)/shard_map/qkv_grad_dp/ppermute | solution.py:786
  294.6 5.0 %collective-permute-start.34 = (bf16[72,768]{1,0:T(8,128)(2,1)S(1)}, bf16[72,768]{1,0:T(8,128)(2,1)S(1)}, u32[]{:S(2)}, u32[]{:S(2)}) collective-permute-start(bf16[72,768]{1,0:T(8,128)(2,1)S(1)} %copy-done.34), channel_id=1, source_target_pairs={{0,24},{4,28},{8,16},{12,20},{16,8},{20,12},{24,0},{28,4},{1,25},{... | collective-permute-start | bytes 331784 | tf_op jit(solution)/shard_map/qkv_grad_dp/ppermute | solution.py:786
  302.1 13.9 %collective-permute-start.39 = (bf16[240,768]{1,0:T(8,128)(2,1)S(1)}, bf16[240,768]{1,0:T(8,128)(2,1)S(1)}, u32[]{:S(2)}, u32[]{:S(2)}) collective-permute-start(bf16[240,768]{1,0:T(8,128)(2,1)S(1)} %maximum_select_fusion.10), channel_id=1, source_target_pairs={{0,8},{4,12},{8,0},{12,4},{16,24},{20,28},{24,16},{28,20},{1,9},{5... | collective-permute-start | bytes 1105928 | tf_op jit(solution)/shard_map/up_proj_grad_dp/ppermute | solution.py:786
  306.9 2.2 collective-permute-start.40
  306.9 4.5 %collective-permute-start.41 = (f32[12,768]{1,0:T(8,128)S(1)}, f32[12,768]{1,0:T(8,128)S(1)}, u32[]{:S(2)}, u32[]{:S(2)}) collective-permute-start(f32[12,768]{1,0:T(8,128)S(1)} %pad_maximum_fusion.6), channel_id=1, source_target_pairs={{0,2},{1,3},{2,0},{3,1},{4,6},{5,7},{6,4},{7,5},{8,10},{9,11},{10,... | collective-permute-start | bytes 110600 | tf_op jit(solution)/shard_map/small_sums/ppermute | solution.py:25
  307.4 4.3 %collective-permute-start.42 = (f32[12,768]{1,0:T(8,128)S(1)}, f32[12,768]{1,0:T(8,128)S(1)}, u32[]{:S(2)}, u32[]{:S(2)}) collective-permute-start(f32[12,768]{1,0:T(8,128)S(1)} %pad_maximum_fusion.6), channel_id=1, source_target_pairs={{0,3},{1,2},{2,1},{3,0},{4,7},{5,6},{6,5},{7,4},{8,11},{9,10},{10,... | collective-permute-start | bytes 110600 | tf_op jit(solution)/shard_map/small_sums/ppermute | solution.py:915
  308.8 7.2 %collective-permute-start.38 = (bf16[72,768]{1,0:T(8,128)(2,1)S(1)}, bf16[72,768]{1,0:T(8,128)(2,1)S(1)}, u32[]{:S(2)}, u32[]{:S(2)}) collective-permute-start(bf16[72,768]{1,0:T(8,128)(2,1)S(1)} %convert_add_fusion.7), channel_id=1, source_target_pairs={{0,4},{4,0},{8,12},{12,8},{16,20},{20,16},{24,28},{28,24},{1,5},{5... | collective-permute-start | bytes 331784 | tf_op jit(solution)/shard_map/qkv_grad_dp/ppermute | solution.py:786
  311.7 4.2 %collective-permute-start.43 = (f32[12,768]{1,0:T(8,128)S(1)}, f32[12,768]{1,0:T(8,128)S(1)}, u32[]{:S(2)}, u32[]{:S(2)}) collective-permute-start(f32[12,768]{1,0:T(8,128)S(1)} %add_add_fusion), channel_id=1, source_target_pairs={{0,4},{4,0},{8,12},{12,8},{16,20},{20,16},{24,28},{28,24},{1,5},{5... | collective-permute-start | bytes 110600 | tf_op jit(solution)/shard_map/small_sums/ppermute | solution.py:786
  317.0 24.3 %collective-permute-start.47 = (bf16[480,768]{1,0:T(8,128)(2,1)S(1)}, bf16[480,768]{1,0:T(8,128)(2,1)}, u32[]{:S(2)}, u32[]{:S(2)}) collective-permute-start(bf16[480,768]{1,0:T(8,128)(2,1)S(1)} %maximum_select_fusion.5), channel_id=1, source_target_pairs={{0,4},{4,0},{8,12},{12,8},{16,20},{20,16},{24,28},{28,24},{1,5},{5... | collective-permute-start | bytes 2211848 | tf_op jit(solution)/shard_map/up_proj_grad_dp/ppermute | solution.py:786
  318.5 13.4 %collective-permute-start.44 = (bf16[160,768]{1,0:T(8,128)(2,1)S(1)}, bf16[160,768]{1,0:T(8,128)(2,1)S(1)}, u32[]{:S(2)}, u32[]{:S(2)}) collective-permute-start(bf16[160,768]{1,0:T(8,128)(2,1)S(1)} %copy-done.33), channel_id=1, source_target_pairs={{0,16},{4,20},{8,24},{12,28},{16,0},{20,4},{24,8},{28,12},{1,17},{... | collective-permute-start | bytes 737288 | tf_op jit(solution)/shard_map/qkv_grad_dp/ppermute | solution.py:786
  319.5 13.7 %collective-permute-start.45 = (bf16[160,768]{1,0:T(8,128)(2,1)S(1)}, bf16[160,768]{1,0:T(8,128)(2,1)S(1)}, u32[]{:S(2)}, u32[]{:S(2)}) collective-permute-start(bf16[160,768]{1,0:T(8,128)(2,1)S(1)} %copy-done.33), channel_id=1, source_target_pairs={{0,8},{4,12},{8,0},{12,4},{16,24},{20,28},{24,16},{28,20},{1,9},{5... | collective-permute-start | bytes 737288 | tf_op jit(solution)/shard_map/qkv_grad_dp/ppermute | solution.py:786
  321.1 20.2 %collective-permute-start.46 = (bf16[160,768]{1,0:T(8,128)(2,1)S(1)}, bf16[160,768]{1,0:T(8,128)(2,1)S(1)}, u32[]{:S(2)}, u32[]{:S(2)}) collective-permute-start(bf16[160,768]{1,0:T(8,128)(2,1)S(1)} %copy-done.33), channel_id=1, source_target_pairs={{0,24},{4,28},{8,16},{12,20},{16,8},{20,12},{24,0},{28,4},{1,25},{... | collective-permute-start | bytes 737288 | tf_op jit(solution)/shard_map/qkv_grad_dp/ppermute | solution.py:786
  (23 other events, 52.3 us)

commit v3 on v2

--- a/solution.py
+++ b/solution.py
@@ -1074,10 +1074,10 @@
     finish, (d_own, up_got, out_got, hidden_grad) = exchange(
         [down], [Scatter(d, singles[1])], d_own, up_got, out_got, hidden_grad
     )
-    up = sum_tokens(normed_mid, hidden_grad, up_got, F32, room=feats)
+    up = sum_tokens(normed_mid, hidden_grad, up_got, room=feats)
     up, qkv_got, proj_got = lax.optimization_barrier((up, qkv_got, proj_got))
     up = sum_tokens(
-        attended, attn_grad, proj_got, F32, rows=feats, first=1, count=1, into=up
+        attended, attn_grad, proj_got, rows=feats, first=1, count=1, into=up
     )
     (down,) = finish(up)
     for bits in singles[2:]:
@@ -1090,7 +1090,7 @@
     )
     with jax.named_scope("down_grad_x"):
         down_got = x_swap(down_away)
-    tail = sum_tokens(d_own, normed, qkv_got, F32, rows=feats)
+    tail = sum_tokens(d_own, normed, qkv_got, rows=feats)
     down_got, tail = lax.optimization_barrier((down_got, tail))
     down = down_own + down_got.astype(F32)
 
@@ -1130,13 +1130,14 @@
         finish, _ = exchange([up], [step])
         (up,) = finish()
     steps = [Scatter(t, high_stages[0]), up_gathers[-3], down_gathers[-1]]
-    finish, (in_main, extra) = exchange([tail, up, down], steps, in_main, extra)
-    with jax.named_scope("in_grad_x"):
-        in_away = x_swap(in_main[size:])
+    finish, (in_main, extra, out_full, out_away) = exchange(
+        [tail, up, down], steps, in_main, extra, out_full, out_away
+    )
+    block_out = join_rows(out_full[:size], out_full[size : 2 * size], out_away)
     in_mid, sums_mid = first_backward(
         tokens, own_in, got_in, residual_grad, vectors, extra, size, (1,)
     )
-    tail, up, down = finish(in_mid, in_away)
+    tail, up, down = finish(in_mid, block_out)
     for bits in high_stages[1:]:
         finish, _ = exchange([tail], [Scatter(t, bits)])
         (tail,) = finish()
@@ -1146,23 +1147,27 @@
     )
 
     steps = [Gather(t, first_stage), up_gathers[-2]]
-    finish, (small, in_away, down) = exchange([tail, up], steps, small, in_away, down)
+    finish, (small, in_main, down) = exchange([tail, up], steps, small, in_main, down)
     with jax.named_scope("small_sums"):
         small = sum_over_tensor(small)
         small = small + dp_swap(small, first_stage[0])
-    tail, up = finish(small)
+    with jax.named_scope("in_grad_x"):
+        in_away = x_swap(after(in_main[size:], small))
+    down = down.astype(F32)
+    tail, up = finish(small, down)
 
     last = high_stages[-1] if len(high_stages[-1]) == 2 else high_stages[-2]
     for bits in reversed([bits for bits in high_stages if bits is not last]):
         finish, _ = exchange([(tail, small)], [GatherAndAdd(t, bits)])
         ((tail, small),) = finish()
-    steps = [GatherAndAdd(t, last), up_gathers[-1]]
-    finish, _ = exchange([(tail, small), up], steps)
-    (tail, small), up = finish()
+    finish_up, (tail, small) = exchange([up], [up_gathers[-1]], tail, small)
+    finish, _ = exchange([(tail, small)], [GatherAndAdd(t, last)])
+    (up,) = finish_up()
+    up_weight_grad, proj_weight_grad = up[:inner].astype(F32), up[inner:].astype(F32)
+    ((tail, small),) = finish(up_weight_grad, proj_weight_grad)
     tail = tail.reshape(-1, 2, tail.shape[0] // (2 ** len(dp_bits())), width)
     tail = jnp.transpose(tail, (1, 0, 2, 3)).reshape(3 * feats, width)
 
-    block_out = join_rows(out_full[:size], out_full[size : 2 * size], out_away)
     in_grad = join_rows(in_main[:size], in_mid, in_away)
 
     up_bias_grad = lax.dynamic_slice_in_dim(small, 6 + place, 1, 0)[0]
@@ -1179,13 +1184,13 @@
         small[1],
         qkv_weight_grad,
         qv_bias_grad,
-        up[inner:].astype(F32),
+        proj_weight_grad,
         small[4],
         small[2],
         small[3],
-        up[:inner].astype(F32),
+        up_weight_grad,
         up_bias_grad,
-        down.astype(F32),
+        down,
         small[5],
     )
 

time: 352 us -> 335 us (0.952)
  starting transfers between devices: 57.5 us -> 49.3 us
  local copies, waits for them, and re-layouts: 30.3 us -> 23.9 us
    ppermute x25, starting transfers between devices: 40.4 us -> 30.6 us  [dp_swap(): return lax.ppermute(value, 'dp', dp_partners(lax.axis_size('dp'), bit))]
    convert_element_type x6 -> x4, local copies, waits for them, and re-layouts: 6.72 us -> 1.79 us  [split(): return (pieces[0], [piece.astype(BF) for piece in pieces[1:]])]
    ppermute x13, waiting for transfers between devices: 20.5 us -> 25 us  [x_swap(): return lax.ppermute(value, 'tensor', X_SWAP)]
  transfers between devices with their start and end apart: 48 -> 48, of which waited for: 19 -> 19; matrix products, arithmetic and copies ran while one was open for 9% -> 10% of each run, Pallas kernels for 36% -> 37%
where the time goes in v3:
time: 335 us; the launch traced here: 333 us
  Pallas kernels  157 us (47%)
  waiting for transfers between devices  75.8 us (23%)
  starting transfers between devices  49.3 us (15%)
  other arithmetic  25.6 us (8%)
  local copies, waits for them, and re-layouts  23.9 us (7%)
    ppermute x25, waiting for transfers between devices, dp_swap(): return lax.ppermute(value, 'dp', dp_partners(lax.axis_size('dp'), bit))  46.7 us
    pallas_call x7, Pallas kernels, sum_tokens(): pl.pallas_call(functools.partial(sum_tokens_kernel, rows, extra is not No...  40.3 us
    ppermute x25, starting transfers between devices, dp_swap(): return lax.ppermute(value, 'dp', dp_partners(lax.axis_size('dp'), bit))  30.6 us
    pallas_call x2, Pallas kernels, attend_backward(): pl.pallas_call(functools.partial(attend_backward_kernel, size), grid_spec...  27.5 us
    pallas_call x1, Pallas kernels, mlp(): pl.pallas_call(mlp_kernel, grid=(3,), in_specs=[fixed((2 * size, width))]...  27.4 us
    ppermute x13, waiting for transfers between devices, x_swap(): return lax.ppermute(value, 'tensor', X_SWAP)  25 us
    ppermute x13, starting transfers between devices, x_swap(): return lax.ppermute(value, 'tensor', X_SWAP)  17.2 us
    pallas_call x1, Pallas kernels, attend_forward(): pl.pallas_call(functools.partial(attend_forward_kernel, size), grid_spec=...  16.9 us
  transfers between devices with their start and end apart: 48, of which 19 were waited for; matrix products, arithmetic and copies ran while one was open for 10% of the time, Pallas kernels for 37%

profile of v3, /device:TPU:8, one launch (start us, length us, event | category | flops | bytes accessed | tf_op | source)
XLA Modules:
  0.0 332.5 jit_solution(4983052121975961456)
XLA Ops:
  3.4 1.5 collective-permute-start
  8.7 4.9 %collective-permute-done = bf16[2,96,768]{2,1,0:T(8,128)(2,1)} collective-permute-done((bf16[2,96,768]{2,1,0:T(8,128)(2,1)}, bf16[2,96,768]{2,1,0:T(8,128)(2,1)}, u32[]{:S(2)}, u32[]{:S(2)}) %collective-permute-start) | collective-permute-done | bytes 294944 | tf_op jit(solution)/shard_map/mlp_weights_x/ppermute | solution.py:25
  13.6 2.6 collective-permute-start.1
  16.2 1.5 collective-permute-start.3
  18.3 1.8 prepare.1
  20.1 10.2 %collective-permute-done.5.x2.away_ref = bf16[512,768]{1,0:T(8,128)(2,1)S(1)} collective-permute-done((bf16[512,768]{1,0:T(8,128)(2,1)}, bf16[512,768]{1,0:T(8,128)(2,1)S(1)}, u32[]{:S(2)}, u32[]{:S(2)}) %collective-permute-start.5) | collective-permute-done | bytes 786464 | tf_op jit(solution)/shard_map/tokens/ppermute | solution.py:25
  30.3 1.7 maximum_select_fusion.6
  32.1 15.4 %collective-permute-done.2 = bf16[2,192,768]{2,1,0:T(8,128)(2,1)S(1)} collective-permute-done((bf16[2,192,768]{2,1,0:T(8,128)(2,1)S(1)}, bf16[2,192,768]{2,1,0:T(8,128)(2,1)S(1)}, u32[]{:S(2)}, u32[]{:S(2)}) %collective-permute-start.2) | collective-permute-done | bytes 589856 | tf_op jit(solution)/shard_map/mlp_weights_dp/ppermute | solution.py:786
  48.7 1.6 collective-permute-start.9
  50.3 1.5 collective-permute-start.7
  52.3 11.1 %first_norm_qkv.1 = (bf16[2048,768]{1,0:T(8,128)(2,1)}, bf16[2048,1536]{1,0:T(8,128)(2,1)}) custom-call(bf16[512,768]{1,0:T(8,128)(2,1)} %copy-done, bf16[512,768]{1,0:T(8,128)(2,1)} %collective-permute-done.4.x1, bf16[512,768]{1,0:T(8,128)(2,1)} %copy-done.3, bf16[512,768]{1,0:T(8,128)(2,1)} %copy-done.6, f32[8,768]{1,0:T(8,128)} %get-tuple-element.222.vec_ref, ...), custom_call_target="tpu_custom_call" | custom-call | flops 1 | bytes 1 | tf_op jit(solution)/shard_map/first_norm_qkv/pallas_call | solution.py:660
  63.4 16.9 %attend_forward.1 = (bf16[1536,512]{1,0:T(8,128)(2,1)}, f32[16,1536]{1,0:T(8,128)}) custom-call(s32[8,8]{1,0:T(8,128)} %get-tuple-element.220.table, s32[8,1536]{1,0:T(8,128)} %get-tuple-element.221.start_ref, bf16[2048,1536]{1,0:T(8,128)(2,1)} %get-tuple-element.225.q_ref.k_ref.v_ref, bf16[2048,1536]{1,0:T(8,128)(2,1)} %get-tuple-element.225.q_ref.k_ref.v_ref, ...), custom_call_target="tpu_custom_call" | custom-call | flops 1 | bytes 1 | tf_op jit(solution)/shard_map/attend_forward/pallas_call | solution.py:143
  81.2 4.6 %project.1.own_ref = bf16[1536,768]{1,0:T(8,128)(2,1)} custom-call(bf16[1536,512]{1,0:T(8,128)(2,1)} %get-tuple-element.247.heads_ref.left_ref.out_ref, bf16[192,768]{1,0:T(8,128)(2,1)} %copy-done.13, bf16[192,768]{1,0:T(8,128)(2,1)} %own_w.3), custom_call_target="tpu_custom_call" | custom-call | flops 1 | bytes 1 | tf_op jit(solution)/shard_map/project/pallas_call | solution.py:533
  86.3 1.7 maximum_select_fusion.up_far.dn_far
  88.0 2.5 collective-permute-done.12.b3
  91.3 1.4 copy-done.8
  92.7 27.4 %mlp.1 = (f32[1536,128]{1,0:T(8,128)}, bf16[1536,768]{1,0:T(8,128)(2,1)}, bf16[2,1536,768]{2,1,0:T(8,128)(2,1)}, bf16[2,1536,768]{2,1,0:T(8,128)(2,1)}, f32[768,...) custom-call(bf16[512,768]{1,0:T(8,128)(2,1)} %copy-done, ...), custom_call_target="tpu_custom_call" | custom-call | flops 1 | bytes 1 | tf_op jit(solution)/shard_map/mlp/pallas_call | solution.py:430
  120.5 5.6 %sum_tokens.7 = bf16[768,768]{1,0:T(8,128)(2,1)} custom-call(bf16[1536,768]{1,0:T(8,128)(2,1)} %get-tuple-element.235.left_ref.mid_ref, bf16[2,1536,768]{2,1,0:T(8,128)(2,1)} %get-tuple-element.276.right_ref), custom_call_target="tpu_custom_call" | custom-call | flops 1 | bytes 1 | tf_op jit(solution)/shard_map/sum_tokens/pallas_call | solution.py:510
  126.1 8.7 %sum_tokens.8 = bf16[1536,768]{1,0:T(8,128)(2,1)} custom-call(bf16[2,1536,768]{2,1,0:T(8,128)(2,1)} %get-tuple-element.233.left_ref, bf16[1536,768]{1,0:T(8,128)(2,1)} %get-tuple-element.237.right_ref.bg_ref), custom_call_target="tpu_custom_call" | custom-call | flops 1 | bytes 1 | tf_op jit(solution)/shard_map/sum_tokens/pallas_call | solution.py:510
  134.8 2.9 constant_dynamic-slice_fusion.10
  138.2 4.0 %collective-permute-start.16 = (bf16[768,768]{1,0:T(8,128)(2,1)}, bf16[768,768]{1,0:T(8,128)(2,1)}, u32[]{:S(2)}, u32[]{:S(2)}) collective-permute-start(bf16[768,768]{1,0:T(8,128)(2,1)} %sum_tokens.7), channel_id=1, source_target_pairs={{0,2},{1,3},{2,0},{3,1},{4,6},{5,7},{6,4},{7,5},{8,10},{9,11},{10,... | collective-permute-start | bytes 3538952 | tf_op jit(solution)/shard_map/up_grad_x/ppermute | solution.py:25
  142.2 1.4 copy-done.10
  143.6 9.9 %mid_backward.1 = (f32[768,768]{1,0:T(8,128)}, bf16[1536,768]{1,0:T(8,128)(2,1)}, bf16[1536,512]{1,0:T(8,128)(2,1)}, f32[8,768]{1,0:T(8,128)}) custom-call(bf16[1536,768]{1,0:T(8,128)(2,1)} %get-tuple-element.235.left_ref.mid_ref, f32[1536,128]{1,0:T(8,128)} %get-tuple-element.248.rstd_ref, bf16[1536,768]{1,0:T(8,128)(2,1)} %get-tuple-element.249.own_ref, ...), custom_call_target="tpu_custom_call" | custom-call | flops 1 | bytes 1 | tf_op jit(solution)/shard_map/mid_backward/pallas_call | solution.py:593
  153.5 3.4 %sum_tokens.9 = bf16[192,768]{1,0:T(8,128)(2,1)} custom-call(bf16[1536,512]{1,0:T(8,128)(2,1)} %get-tuple-element.247.heads_ref.left_ref.out_ref, bf16[1536,768]{1,0:T(8,128)(2,1)} %get-tuple-element.250.right_ref), custom_call_target="tpu_custom_call" | custom-call | flops 1 | bytes 1 | tf_op jit(solution)/shard_map/sum_tokens/pallas_call | solution.py:510
  157.0 13.8 %attend_backward.2 = (bf16[2048,768]{1,0:T(8,128)(2,1)}, f32[8,256]{1,0:T(8,128)}) custom-call(s32[8,8]{1,0:T(8,128)} %get-tuple-element.220.table, s32[8,1536]{1,0:T(8,128)} %get-tuple-element.221.start_ref, bf16[2048,1536]{1,0:T(8,128)(2,1)} %get-tuple-element.225.q_ref.k_ref.v_ref, bf16[2048,1536]{1,0:T(8,128)(2,1)} %get-tuple-element.225.q_ref.k_ref.v_ref, ...), custom_call_target="tpu_custom_call" | custom-call | flops 1 | bytes 1 | tf_op jit(solution)/shard_map/attend_backward/pallas_call | solution.py:239
  170.7 6.3 %sum_tokens.10 = bf16[576,768]{1,0:T(8,128)(2,1)} custom-call(bf16[2048,768]{1,0:T(8,128)(2,1)} %get-tuple-element.256.left_ref.far_d, bf16[2048,768]{1,0:T(8,128)(2,1)} %get-tuple-element.257.right_ref), custom_call_target="tpu_custom_call" | custom-call | flops 1 | bytes 1 | tf_op jit(solution)/shard_map/sum_tokens/pallas_call | solution.py:510
  177.1 1.5 convert_add_fusion
  179.9 1.3 collective-permute-start.18
  182.0 13.7 %attend_backward.3 = (bf16[2048,768]{1,0:T(8,128)(2,1)}, f32[8,256]{1,0:T(8,128)}) custom-call(s32[8,8]{1,0:T(8,128)} %get-tuple-element.220.table, s32[8,1536]{1,0:T(8,128)} %get-tuple-element.221.start_ref, bf16[2048,1536]{1,0:T(8,128)(2,1)} %get-tuple-element.225.q_ref.k_ref.v_ref, bf16[2048,1536]{1,0:T(8,128)(2,1)} %get-tuple-element.225.q_ref.k_ref.v_ref, ...), custom_call_target="tpu_custom_call" | custom-call | flops 1 | bytes 1 | tf_op jit(solution)/shard_map/attend_backward/pallas_call | solution.py:239
  197.0 2.0 collective-permute-start.20
  199.0 5.8 %sum_tokens.11.refs_1_ = bf16[960,768]{1,0:T(8,128)(2,1)} custom-call(bf16[1536,768]{1,0:T(8,128)(2,1)} %get-tuple-element.235.left_ref.mid_ref, bf16[2,1536,768]{2,1,0:T(8,128)(2,1)} %get-tuple-element.276.right_ref, bf16[768,768]{1,0:T(8,128)(2,1)} %collective-permute-done.16.refs_0_), custom_call_target="tpu_custom_call" | custom-call | flops 1 | bytes 1 | tf_op jit(solution)/shard_map/sum_tokens/pallas_call | solution.py:510
  204.8 3.2 collective-permute-done.19.refs_0_
  208.7 3.4 %sum_tokens.12 = bf16[960,768]{1,0:T(8,128)(2,1)} custom-call(bf16[1536,512]{1,0:T(8,128)(2,1)} %get-tuple-element.247.heads_ref.left_ref.out_ref, bf16[1536,768]{1,0:T(8,128)(2,1)} %get-tuple-element.250.right_ref, bf16[192,768]{1,0:T(8,128)(2,1)} %copy-done.28, bf16[960,768]{1,0:T(8,128)(2,1)} %sum_tokens.11.refs_1_), custom_call_target="tpu_custom_call", output_to_operand_aliasing={{}: (3, {})} | custom-call | flops 1 | bytes 1 | tf_op jit(solution)/shard_map/sum_tokens/pallas_call | solution.py:510
  215.7 1.7 collective-permute-start.24
  217.4 6.9 %sum_tokens.13 = bf16[576,768]{1,0:T(8,128)(2,1)} custom-call(bf16[2048,768]{1,0:T(8,128)(2,1)} %get-tuple-element.307.left_ref.own_d, bf16[2048,768]{1,0:T(8,128)(2,1)} %get-tuple-element.257.right_ref, bf16[576,768]{1,0:T(8,128)(2,1)} %collective-permute-done.18.refs_0_), custom_call_target="tpu_custom_call" | custom-call | flops 1 | bytes 1 | tf_op jit(solution)/shard_map/sum_tokens/pallas_call | solution.py:510
  224.3 2.1 constant_dynamic-slice_fusion.4
  227.9 1.4 collective-permute-start.25
  229.3 1.9 collective-permute-start.23
  231.2 10.0 %first_in.1 = (bf16[1024,768]{1,0:T(8,128)(2,1)}, bf16[1024,768]{1,0:T(8,128)(2,1)}) custom-call(bf16[2048,768]{1,0:T(8,128)(2,1)} %get-tuple-element.256.left_ref.far_d, bf16[2048,768]{1,0:T(8,128)(2,1)} %get-tuple-element.307.left_ref.own_d, bf16[592,768]{1,0:T(8,128)(2,1)} %copy-done.4, bf16[592,768]{1,0:T(8,128)(2,1)} %copy-done.1), custom_call_target="tpu_custom_call" | custom-call | flops 1 | bytes 1 | tf_op jit(solution)/shard_map/first_in/pallas_call | solution.py:713
  241.2 2.1 collective-permute-done.22
  243.4 1.4 convert_add_fusion.1
  249.2 2.3 collective-permute-start.30
  251.5 1.6 collective-permute-start.27
  253.1 1.9 collective-permute-start.28
  255.0 1.3 add_convert_fusion.1
  257.9 3.9 %first_backward.2 = (bf16[512,768]{1,0:T(8,128)(2,1)}, f32[8,768]{1,0:T(8,128)}) custom-call(bf16[512,768]{1,0:T(8,128)(2,1)} %copy-done, bf16[512,768]{1,0:T(8,128)(2,1)} %copy-done.3, bf16[1024,768]{1,0:T(8,128)(2,1)} %get-tuple-element.327.own_ref, bf16[1024,768]{1,0:T(8,128)(2,1)} %copy-done.5, f32[768,768]{1,0:T(8,128)} %get-tuple-element.329.rg_ref, ...), custom_call_target="tpu_custom_call" | custom-call | flops 1 | bytes 1 | tf_op jit(solution)/shard_map/first_backward/pallas_call | solution.py:758
  263.0 7.3 %collective-permute-done.27 = bf16[120,768]{1,0:T(8,128)(2,1)S(1)} collective-permute-done((bf16[120,768]{1,0:T(8,128)(2,1)}, bf16[120,768]{1,0:T(8,128)(2,1)S(1)}, u32[]{:S(2)}, u32[]{:S(2)}) %collective-permute-start.27) | collective-permute-done | bytes 184352 | tf_op jit(solution)/shard_map/up_proj_grad_dp/ppermute | solution.py:786
  270.9 4.3 %collective-permute-start.35 = (bf16[120,768]{1,0:T(8,128)(2,1)S(1)}, bf16[120,768]{1,0:T(8,128)(2,1)S(1)}, u32[]{:S(2)}, u32[]{:S(2)}) collective-permute-start(bf16[120,768]{1,0:T(8,128)(2,1)S(1)} %convert_add_fusion.5), channel_id=1, source_target_pairs={{0,16},{4,20},{8,24},{12,28},{16,0},{20,4},{24,8},{28,12},{1,17},{... | collective-permute-start | bytes 552968 | tf_op jit(solution)/shard_map/up_proj_grad_dp/ppermute | solution.py:786
  275.2 2.1 collective-permute-start.33
  277.2 1.4 collective-permute-start.34
  278.6 3.2 first_backward.3
  283.8 5.1 %collective-permute-done.32 = bf16[72,768]{1,0:T(8,128)(2,1)S(1)} collective-permute-done((bf16[72,768]{1,0:T(8,128)(2,1)S(1)}, bf16[72,768]{1,0:T(8,128)(2,1)S(1)}, u32[]{:S(2)}, u32[]{:S(2)}) %collective-permute-start.32) | collective-permute-done | bytes 110624 | tf_op jit(solution)/shard_map/qkv_grad_dp/ppermute | solution.py:786
  288.9 3.9 %collective-permute-done.34 = bf16[72,768]{1,0:T(8,128)(2,1)S(1)} collective-permute-done((bf16[72,768]{1,0:T(8,128)(2,1)S(1)}, bf16[72,768]{1,0:T(8,128)(2,1)S(1)}, u32[]{:S(2)}, u32[]{:S(2)}) %collective-permute-start.34) | collective-permute-done | bytes 110624 | tf_op jit(solution)/shard_map/qkv_grad_dp/ppermute | solution.py:786
  293.6 1.4 collective-permute-start.38
  296.4 1.3 collective-permute-done.38
  299.6 1.6 convert_element_type.169
  301.2 1.7 collective-permute-done.40
  305.4 1.6 collective-permute-start.44
  307.5 1.4 collective-permute-start.46
  308.9 4.8 %collective-permute-done.41 = bf16[256,768]{1,0:T(8,128)(2,1)} collective-permute-done((bf16[256,768]{1,0:T(8,128)(2,1)S(1)}, bf16[256,768]{1,0:T(8,128)(2,1)}, u32[]{:S(2)}, u32[]{:S(2)}) %collective-permute-start.41) | collective-permute-done | bytes 393248 | tf_op jit(solution)/shard_map/in_grad_x/ppermute | solution.py:25
  316.0 6.4 %collective-permute-done.47 = bf16[480,768]{1,0:T(8,128)(2,1)S(1)} collective-permute-done((bf16[480,768]{1,0:T(8,128)(2,1)S(1)}, bf16[480,768]{1,0:T(8,128)(2,1)S(1)}, u32[]{:S(2)}, u32[]{:S(2)}) %collective-permute-start.47) | collective-permute-done | bytes 737312 | tf_op jit(solution)/shard_map/up_proj_grad_dp/ppermute | solution.py:786
  323.0 1.6 slice_convert_fusion
  325.5 3.4 %collective-permute-done.46 = bf16[160,768]{1,0:T(8,128)(2,1)S(1)} collective-permute-done((bf16[160,768]{1,0:T(8,128)(2,1)S(1)}, bf16[160,768]{1,0:T(8,128)(2,1)S(1)}, u32[]{:S(2)}, u32[]{:S(2)}) %collective-permute-start.46) | collective-permute-done | bytes 245792 | tf_op jit(solution)/shard_map/qkv_grad_dp/ppermute | solution.py:786
  329.8 1.3 copy.30
  (212 shorter events, 43.5 us)
Async XLA Ops:
  0.6 4.2 %copy-start.14 = (bf16[256,3,768]{2,0,1:T(8,128)(2,1)S(1)}, bf16[256,3,768]{2,0,1:T(8,128)(2,1)}, u32[]{:S(2)}) copy-start(bf16[256,3,768]{2,0,1:T(8,128)(2,1)} %param.15) | copy-start | bytes 3538948
  3.4 10.2 %collective-permute-start = (bf16[2,96,768]{2,1,0:T(8,128)(2,1)}, bf16[2,96,768]{2,1,0:T(8,128)(2,1)}, u32[]{:S(2)}, u32[]{:S(2)}) collective-permute-start(bf16[2,96,768]{2,1,0:T(8,128)(2,1)} %pad_maximum_fusion.5), channel_id=1, source_target_pairs={{0,2},{1,3},{2,0},{3,1},{4,6},{5,7},{6,4},{7,5},{8,10},{9,11},{10,... | collective-permute-start | bytes 884744 | tf_op jit(solution)/shard_map/mlp_weights_x/ppermute | solution.py:25
  6.0 11.7 %copy-start = (bf16[512,768]{1,0:T(8,128)(2,1)}, bf16[512,768]{1,0:T(8,128)(2,1)S(1)}, u32[]{:S(2)}) copy-start(bf16[512,768]{1,0:T(8,128)(2,1)S(1)} %get-tuple-element.216.x0.home_ref) | copy-start | bytes 2359300
  6.0 24.4 %collective-permute-start.5 = (bf16[512,768]{1,0:T(8,128)(2,1)}, bf16[512,768]{1,0:T(8,128)(2,1)S(1)}, u32[]{:S(2)}, u32[]{:S(2)}) collective-permute-start(bf16[512,768]{1,0:T(8,128)(2,1)} %get-tuple-element.434), channel_id=1, source_target_pairs={{0,2},{1,3},{2,0},{3,1},{4,6},{5,7},{6,4},{7,5},{8,10},{9,11},{10,... | collective-permute-start | bytes 2359304 | tf_op jit(solution)/shard_map/tokens/ppermute | solution.py:25
  8.7 39.3 %copy-start.1 = (bf16[592,768]{1,0:T(8,128)(2,1)}, bf16[592,768]{1,0:T(8,128)(2,1)S(1)}, u32[]{:S(2)}) copy-start(bf16[592,768]{1,0:T(8,128)(2,1)S(1)} %fusion.1.own_ref.upb_own.own_w_ref) | copy-start | bytes 2727940
  13.6 16.8 %collective-permute-start.1 = (bf16[2,96,768]{2,1,0:T(8,128)(2,1)}, bf16[2,96,768]{2,1,0:T(8,128)(2,1)}, u32[]{:S(2)}, u32[]{:S(2)}) collective-permute-start(bf16[2,96,768]{2,1,0:T(8,128)(2,1)} %collective-permute-done), channel_id=1, source_target_pairs={{0,16},{4,20},{8,24},{12,28},{16,0},{20,4},{24,8},{28,12},{1,17},{... | collective-permute-start | bytes 884744 | tf_op jit(solution)/shard_map/mlp_weights_dp/ppermute | solution.py:786
  16.2 32.5 %collective-permute-start.3 = (bf16[592,768]{1,0:T(8,128)(2,1)S(1)}, bf16[592,768]{1,0:T(8,128)(2,1)S(1)}, u32[]{:S(2)}, u32[]{:S(2)}) collective-permute-start(bf16[592,768]{1,0:T(8,128)(2,1)S(1)} %fusion.1.own_ref.upb_own.own_w_ref), channel_id=1, source_target_pairs={{0,2},{1,3},{2,0},{3,1},{4,6},{5,7},{6,4},{7,5},{8,10},{9,11},{10,... | collective-permute-start | bytes 2727944 | tf_op jit(solution)/shard_map/qkv_weights_x/ppermute | solution.py:25
  17.7 30.4 %collective-permute-start.4 = (bf16[512,768]{1,0:T(8,128)(2,1)S(1)}, bf16[512,768]{1,0:T(8,128)(2,1)}, u32[]{:S(2)}, u32[]{:S(2)}) collective-permute-start(bf16[512,768]{1,0:T(8,128)(2,1)S(1)} %get-tuple-element.216.x0.home_ref), channel_id=1, source_target_pairs={{0,1},{1,0},{2,3},{3,2},{4,5},{5,4},{6,7},{7,6},{8,9},{9,8},{10,11... | collective-permute-start | bytes 2359304 | tf_op jit(solution)/shard_map/tokens/ppermute | solution.py:29
  30.3 17.7 %copy-start.3 = (bf16[512,768]{1,0:T(8,128)(2,1)}, bf16[512,768]{1,0:T(8,128)(2,1)S(1)}, u32[]{:S(2)}) copy-start(bf16[512,768]{1,0:T(8,128)(2,1)S(1)} %collective-permute-done.5.x2.away_ref) | copy-start | bytes 2359300
  30.3 18.3 %collective-permute-start.6 = (bf16[512,768]{1,0:T(8,128)(2,1)S(1)}, bf16[512,768]{1,0:T(8,128)(2,1)S(1)}, u32[]{:S(2)}, u32[]{:S(2)}) collective-permute-start(bf16[512,768]{1,0:T(8,128)(2,1)S(1)} %collective-permute-done.5.x2.away_ref), channel_id=1, source_target_pairs={{0,1},{1,0},{2,3},{3,2},{4,5},{5,4},{6,7},{7,6},{8,9},{9,8},{10,11... | collective-permute-start | bytes 2359304 | tf_op jit(solution)/shard_map/tokens/ppermute | solution.py:29
  32.0 18.3 %copy-start.7 = (bf16[512,768]{1,0:T(8,128)(2,1)S(1)}, bf16[512,768]{1,0:T(8,128)(2,1)}, u32[]{:S(2)}) copy-start(bf16[512,768]{1,0:T(8,128)(2,1)} %pad_maximum_fusion.4.b0) | copy-start | bytes 2359300
  32.0 19.7 %copy-start.12 = (bf16[192,768]{1,0:T(8,128)(2,1)S(1)}, bf16[192,768]{1,0:T(8,128)(2,1)}, u32[]{:S(2)}) copy-start(bf16[192,768]{1,0:T(8,128)(2,1)} %own_w.3) | copy-start | bytes 884740
  32.0 15.5 %collective-permute-start.2 = (bf16[2,192,768]{2,1,0:T(8,128)(2,1)S(1)}, bf16[2,192,768]{2,1,0:T(8,128)(2,1)S(1)}, u32[]{:S(2)}, u32[]{:S(2)}) collective-permute-start(bf16[2,192,768]{2,1,0:T(8,128)(2,1)S(1)} %maximum_select_fusion.6), channel_id=1, source_target_pairs={{0,8},{4,12},{8,0},{12,4},{16,24},{20,28},{24,16},{28,20},{1,9},{5... | collective-permute-start | bytes 1769480 | tf_op jit(solution)/shard_map/mlp_weights_dp/ppermute | solution.py:786
  48.7 3.6 %copy-start.4 = (bf16[592,768]{1,0:T(8,128)(2,1)}, bf16[592,768]{1,0:T(8,128)(2,1)S(1)}, u32[]{:S(2)}) copy-start(bf16[592,768]{1,0:T(8,128)(2,1)S(1)} %collective-permute-done.3.far_ref.upb_far) | copy-start | bytes 2727940
  48.7 31.7 %collective-permute-start.9 = (bf16[2,384,768]{2,1,0:T(8,128)(2,1)S(1)}, bf16[2,384,768]{2,1,0:T(8,128)(2,1)S(1)}, u32[]{:S(2)}, u32[]{:S(2)}) collective-permute-start(bf16[2,384,768]{2,1,0:T(8,128)(2,1)S(1)} %maximum_select_fusion.2), channel_id=1, source_target_pairs={{0,4},{4,0},{8,12},{12,8},{16,20},{20,16},{24,28},{28,24},{1,5},{5... | collective-permute-start | bytes 3538952 | tf_op jit(solution)/shard_map/mlp_weights_dp/ppermute | solution.py:786
  50.3 30.1 %collective-permute-start.8 = (bf16[512,768]{1,0:T(8,128)(2,1)S(1)}, bf16[512,768]{1,0:T(8,128)(2,1)S(1)}, u32[]{:S(2)}, u32[]{:S(2)}) collective-permute-start(bf16[512,768]{1,0:T(8,128)(2,1)S(1)} %copy-done.7), channel_id=1, source_target_pairs={{0,1},{1,0},{2,3},{3,2},{4,5},{5,4},{6,7},{7,6},{8,9},{9,8},{10,11... | collective-permute-start | bytes 2359304 | tf_op jit(solution)/shard_map/cotangent/ppermute | solution.py:29
  50.3 30.1 %collective-permute-start.7 = (bf16[256,768]{1,0:T(8,128)(2,1)}, bf16[256,768]{1,0:T(8,128)(2,1)S(1)}, u32[]{:S(2)}, u32[]{:S(2)}) collective-permute-start(bf16[256,768]{1,0:T(8,128)(2,1)} %get-tuple-element.228), channel_id=1, source_target_pairs={{0,2},{1,3},{2,0},{3,1},{4,6},{5,7},{6,4},{7,5},{8,10},{9,11},{10,... | collective-permute-start | bytes 1179656 | tf_op jit(solution)/shard_map/cotangent/ppermute | solution.py:25
  51.8 28.6 %collective-permute-start.10 = (bf16[192,768]{1,0:T(8,128)(2,1)S(1)}, bf16[192,768]{1,0:T(8,128)(2,1)S(1)}, u32[]{:S(2)}, u32[]{:S(2)}) collective-permute-start(bf16[192,768]{1,0:T(8,128)(2,1)S(1)} %copy-done.12), channel_id=1, source_target_pairs={{0,2},{1,3},{2,0},{3,1},{4,6},{5,7},{6,4},{7,5},{8,10},{9,11},{10,... | collective-permute-start | bytes 884744 | tf_op jit(solution)/shard_map/proj_weight_x/ppermute | solution.py:25
  80.3 7.6 %copy-start.20 = (bf16[512,768]{1,0:T(8,128)(2,1)}, bf16[512,768]{1,0:T(8,128)(2,1)S(1)}, u32[]{:S(2)}) copy-start(bf16[512,768]{1,0:T(8,128)(2,1)S(1)} %collective-permute-done.8.b1) | copy-start | bytes 2359300
  80.4 7.6 %copy-start.26 = (bf16[256,768]{1,0:T(8,128)(2,1)}, bf16[256,768]{1,0:T(8,128)(2,1)S(1)}, u32[]{:S(2)}) copy-start(bf16[256,768]{1,0:T(8,128)(2,1)S(1)} %collective-permute-done.7.b2) | copy-start | bytes 1179652
  85.7 5.3 %collective-permute-start.11 = (bf16[1536,768]{1,0:T(8,128)(2,1)}, bf16[1536,768]{1,0:T(8,128)(2,1)S(1)}, u32[]{:S(2)}, u32[]{:S(2)}) collective-permute-start(bf16[1536,768]{1,0:T(8,128)(2,1)} %project.1.own_ref), channel_id=1, source_target_pairs={{0,1},{1,0},{2,3},{3,2},{4,5},{5,4},{6,7},{7,6},{8,9},{9,8},{10,11... | collective-permute-start | bytes 7077896 | tf_op jit(solution)/shard_map/attn_core/ppermute | solution.py:29
  85.8 4.7 %collective-permute-start.12 = (bf16[256,768]{1,0:T(8,128)(2,1)S(1)}, bf16[256,768]{1,0:T(8,128)(2,1)S(1)}, u32[]{:S(2)}, u32[]{:S(2)}) collective-permute-start(bf16[256,768]{1,0:T(8,128)(2,1)S(1)} %collective-permute-done.7.b2), channel_id=1, source_target_pairs={{0,1},{1,0},{2,3},{3,2},{4,5},{5,4},{6,7},{7,6},{8,9},{9,8},{10,11... | collective-permute-start | bytes 1179656 | tf_op jit(solution)/shard_map/cotangent/ppermute | solution.py:29
  120.1 22.1 %collective-permute-start.13 = (bf16[1536,768]{1,0:T(8,128)(2,1)}, bf16[1536,768]{1,0:T(8,128)(2,1)S(1)}, u32[]{:S(2)}, u32[]{:S(2)}) collective-permute-start(bf16[1536,768]{1,0:T(8,128)(2,1)} %get-tuple-element.249.own_ref), channel_id=1, source_target_pairs={{0,1},{1,0},{2,3},{3,2},{4,5},{5,4},{6,7},{7,6},{8,9},{9,8},{10,11... | collective-permute-start | bytes 7077896 | tf_op jit(solution)/shard_map/mid_core/ppermute | solution.py:29
  137.7 39.4 %collective-permute-start.14 = (bf16[2,384,768]{2,1,0:T(8,128)(2,1)}, bf16[2,384,768]{2,1,0:T(8,128)(2,1)}, u32[]{:S(2)}, u32[]{:S(2)}) collective-permute-start(bf16[2,384,768]{2,1,0:T(8,128)(2,1)} %get-tuple-element.252), channel_id=1, source_target_pairs={{0,4},{4,0},{8,12},{12,8},{16,20},{20,16},{24,28},{28,24},{1,5},{5... | collective-permute-start | bytes 3538952 | tf_op jit(solution)/shard_map/down_grad_dp/ppermute | solution.py:786
  138.2 58.7 %collective-permute-start.16 = (bf16[768,768]{1,0:T(8,128)(2,1)}, bf16[768,768]{1,0:T(8,128)(2,1)}, u32[]{:S(2)}, u32[]{:S(2)}) collective-permute-start(bf16[768,768]{1,0:T(8,128)(2,1)} %sum_tokens.7), channel_id=1, source_target_pairs={{0,2},{1,3},{2,0},{3,1},{4,6},{5,7},{6,4},{7,5},{8,10},{9,11},{10,... | collective-permute-start | bytes 3538952 | tf_op jit(solution)/shard_map/up_grad_x/ppermute | solution.py:25
  179.6 17.3 %collective-permute-start.17 = (bf16[768,768]{1,0:T(8,128)(2,1)}, bf16[768,768]{1,0:T(8,128)(2,1)S(1)}, u32[]{:S(2)}, u32[]{:S(2)}) collective-permute-start(bf16[768,768]{1,0:T(8,128)(2,1)} %get-tuple-element.269), channel_id=1, source_target_pairs={{0,1},{1,0},{2,3},{3,2},{4,5},{5,4},{6,7},{7,6},{8,9},{9,8},{10,11... | collective-permute-start | bytes 3538952 | tf_op jit(solution)/shard_map/block_out/ppermute | solution.py:29
  179.6 16.1 %collective-permute-start.15 = (bf16[2,192,768]{2,1,0:T(8,128)(2,1)}, bf16[2,192,768]{2,1,0:T(8,128)(2,1)}, u32[]{:S(2)}, u32[]{:S(2)}) collective-permute-start(bf16[2,192,768]{2,1,0:T(8,128)(2,1)} %dynamic-slice_convert_fusion), channel_id=1, source_target_pairs={{0,8},{4,12},{8,0},{12,4},{16,24},{20,28},{24,16},{28,20},{1,9},{5... | collective-permute-start | bytes 1769480 | tf_op jit(solution)/shard_map/down_grad_dp/ppermute | solution.py:786
  179.9 28.0 %collective-permute-start.18 = (bf16[576,768]{1,0:T(8,128)(2,1)S(1)}, bf16[576,768]{1,0:T(8,128)(2,1)}, u32[]{:S(2)}, u32[]{:S(2)}) collective-permute-start(bf16[576,768]{1,0:T(8,128)(2,1)S(1)} %copy-done.18), channel_id=1, source_target_pairs={{0,2},{1,3},{2,0},{3,1},{4,6},{5,7},{6,4},{7,5},{8,10},{9,11},{10,... | collective-permute-start | bytes 2654216 | tf_op jit(solution)/shard_map/qkv_grad_x/ppermute | solution.py:25
  181.3 26.7 %collective-permute-start.19 = (bf16[192,768]{1,0:T(8,128)(2,1)}, bf16[192,768]{1,0:T(8,128)(2,1)S(1)}, u32[]{:S(2)}, u32[]{:S(2)}) collective-permute-start(bf16[192,768]{1,0:T(8,128)(2,1)} %sum_tokens.9), channel_id=1, source_target_pairs={{0,2},{1,3},{2,0},{3,1},{4,6},{5,7},{6,4},{7,5},{8,10},{9,11},{10,... | collective-permute-start | bytes 884744 | tf_op jit(solution)/shard_map/proj_grad_x/ppermute | solution.py:25
  196.9 7.9 %copy-start.16 = (bf16[768,768]{1,0:T(8,128)(2,1)}, bf16[768,768]{1,0:T(8,128)(2,1)S(1)}, u32[]{:S(2)}) copy-start(bf16[768,768]{1,0:T(8,128)(2,1)S(1)} %collective-permute-done.17) | copy-start | bytes 3538948
  197.0 15.1 %collective-permute-start.20 = (bf16[2,96,768]{2,1,0:T(8,128)(2,1)S(1)}, bf16[2,96,768]{2,1,0:T(8,128)(2,1)S(1)}, u32[]{:S(2)}, u32[]{:S(2)}) collective-permute-start(bf16[2,96,768]{2,1,0:T(8,128)(2,1)S(1)} %dynamic-slice_convert_fusion.1), channel_id=1, source_target_pairs={{0,16},{4,20},{8,24},{12,28},{16,0},{20,4},{24,8},{28,12},{1,17},{... | collective-permute-start | bytes 884744 | tf_op jit(solution)/shard_map/down_grad_dp/ppermute | solution.py:786
  214.5 9.8 %collective-permute-start.21 = (bf16[96,768]{1,0:T(8,128)(2,1)S(1)}, bf16[96,768]{1,0:T(8,128)(2,1)S(1)}, u32[]{:S(2)}, u32[]{:S(2)}) collective-permute-start(bf16[96,768]{1,0:T(8,128)(2,1)S(1)} %fusion.4), channel_id=1, source_target_pairs={{0,2},{1,3},{2,0},{3,1},{4,6},{5,7},{6,4},{7,5},{8,10},{9,11},{10,... | collective-permute-start | bytes 442376 | tf_op jit(solution)/shard_map/down_grad_x/ppermute | solution.py:25
  215.7 27.7 %collective-permute-start.24 = (bf16[480,768]{1,0:T(8,128)(2,1)}, bf16[480,768]{1,0:T(8,128)(2,1)}, u32[]{:S(2)}, u32[]{:S(2)}) collective-permute-start(bf16[480,768]{1,0:T(8,128)(2,1)} %get-tuple-element.306), channel_id=1, source_target_pairs={{0,4},{4,0},{8,12},{12,8},{16,20},{20,16},{24,28},{28,24},{1,5},{5... | collective-permute-start | bytes 2211848 | tf_op jit(solution)/shard_map/up_proj_grad_dp/ppermute | solution.py:786
  217.4 9.4 %copy-start.17 = (bf16[768,768]{1,0:T(8,128)(2,1)S(1)}, bf16[768,768]{1,0:T(8,128)(2,1)}, u32[]{:S(2)}) copy-start(bf16[768,768]{1,0:T(8,128)(2,1)} %copy-done.16) | copy-start | bytes 3538948
  226.5 16.8 %collective-permute-start.22 = (bf16[288,768]{1,0:T(8,128)(2,1)}, bf16[288,768]{1,0:T(8,128)(2,1)}, u32[]{:S(2)}, u32[]{:S(2)}) collective-permute-start(bf16[288,768]{1,0:T(8,128)(2,1)} %get-tuple-element.302), channel_id=1, source_target_pairs={{0,4},{4,0},{8,12},{12,8},{16,20},{20,16},{24,28},{28,24},{1,5},{5... | collective-permute-start | bytes 1327112 | tf_op jit(solution)/shard_map/qkv_grad_dp/ppermute | solution.py:786
  227.9 15.4 %collective-permute-start.25 = (bf16[256,768]{1,0:T(8,128)(2,1)}, bf16[256,768]{1,0:T(8,128)(2,1)S(1)}, u32[]{:S(2)}, u32[]{:S(2)}) collective-permute-start(bf16[256,768]{1,0:T(8,128)(2,1)} %slice.158), channel_id=1, source_target_pairs={{0,2},{1,3},{2,0},{3,1},{4,6},{5,7},{6,4},{7,5},{8,10},{9,11},{10,... | collective-permute-start | bytes 1179656 | tf_op jit(solution)/shard_map/block_out/ppermute | solution.py:25
  229.3 11.9 %collective-permute-start.23 = (bf16[96,768]{1,0:T(8,128)(2,1)S(1)}, bf16[96,768]{1,0:T(8,128)(2,1)S(1)}, u32[]{:S(2)}, u32[]{:S(2)}) collective-permute-start(bf16[96,768]{1,0:T(8,128)(2,1)S(1)} %convert_add_fusion.6), channel_id=1, source_target_pairs={{0,16},{4,20},{8,24},{12,28},{16,0},{20,4},{24,8},{28,12},{1,17},{... | collective-permute-start | bytes 442376 | tf_op jit(solution)/shard_map/down_grad_dp/ppermute | solution.py:786
  244.8 4.4 %copy-start.30 = (f32[8,768]{1,0:T(8,128)S(1)}, f32[8,768]{1,0:T(8,128)}, u32[]{:S(2)}) copy-start(f32[8,768]{1,0:T(8,128)} %get-tuple-element.361) | copy-start | bytes 73732
  246.4 8.6 %collective-permute-start.29 = (bf16[1024,768]{1,0:T(8,128)(2,1)}, bf16[1024,768]{1,0:T(8,128)(2,1)S(1)}, u32[]{:S(2)}, u32[]{:S(2)}) collective-permute-start(bf16[1024,768]{1,0:T(8,128)(2,1)} %get-tuple-element.328), channel_id=1, source_target_pairs={{0,1},{1,0},{2,3},{3,2},{4,5},{5,4},{6,7},{7,6},{8,9},{9,8},{10,11... | collective-permute-start | bytes 4718600 | tf_op jit(solution)/shard_map/first_core/ppermute | solution.py:29
  249.2 13.6 %collective-permute-start.30 = (bf16[192,768]{1,0:T(8,128)(2,1)S(1)}, bf16[192,768]{1,0:T(8,128)(2,1)S(1)}, u32[]{:S(2)}, u32[]{:S(2)}) collective-permute-start(bf16[192,768]{1,0:T(8,128)(2,1)S(1)} %maximum_select_fusion.11), channel_id=1, source_target_pairs={{0,8},{4,12},{8,0},{12,4},{16,24},{20,28},{24,16},{28,20},{1,9},{5... | collective-permute-start | bytes 884744 | tf_op jit(solution)/shard_map/down_grad_dp/ppermute | solution.py:786
  251.5 11.6 %collective-permute-start.26 = (bf16[120,768]{1,0:T(8,128)(2,1)}, bf16[120,768]{1,0:T(8,128)(2,1)S(1)}, u32[]{:S(2)}, u32[]{:S(2)}) collective-permute-start(bf16[120,768]{1,0:T(8,128)(2,1)} %get-tuple-element.317), channel_id=1, source_target_pairs={{0,16},{4,20},{8,24},{12,28},{16,0},{20,4},{24,8},{28,12},{1,17},{... | collective-permute-start | bytes 552968 | tf_op jit(solution)/shard_map/up_proj_grad_dp/ppermute | solution.py:786
  251.5 18.9 %collective-permute-start.27 = (bf16[120,768]{1,0:T(8,128)(2,1)}, bf16[120,768]{1,0:T(8,128)(2,1)S(1)}, u32[]{:S(2)}, u32[]{:S(2)}) collective-permute-start(bf16[120,768]{1,0:T(8,128)(2,1)} %get-tuple-element.318), channel_id=1, source_target_pairs={{0,8},{4,12},{8,0},{12,4},{16,24},{20,28},{24,16},{28,20},{1,9},{5... | collective-permute-start | bytes 552968 | tf_op jit(solution)/shard_map/up_proj_grad_dp/ppermute | solution.py:786
  253.1 17.3 %collective-permute-start.28 = (bf16[120,768]{1,0:T(8,128)(2,1)}, bf16[120,768]{1,0:T(8,128)(2,1)S(1)}, u32[]{:S(2)}, u32[]{:S(2)}) collective-permute-start(bf16[120,768]{1,0:T(8,128)(2,1)} %get-tuple-element.319), channel_id=1, source_target_pairs={{0,24},{4,28},{8,16},{12,20},{16,8},{20,12},{24,0},{28,4},{1,25},{... | collective-permute-start | bytes 552968 | tf_op jit(solution)/shard_map/up_proj_grad_dp/ppermute | solution.py:786
  256.3 14.4 %collective-permute-start.31 = (bf16[256,768]{1,0:T(8,128)(2,1)S(1)}, bf16[256,768]{1,0:T(8,128)(2,1)S(1)}, u32[]{:S(2)}, u32[]{:S(2)}) collective-permute-start(bf16[256,768]{1,0:T(8,128)(2,1)S(1)} %add_convert_fusion.1), channel_id=1, source_target_pairs={{0,2},{1,3},{2,0},{3,1},{4,6},{5,7},{6,4},{7,5},{8,10},{9,11},{10,... | collective-permute-start | bytes 1179656 | tf_op jit(solution)/shard_map/first_mid_x/ppermute | solution.py:25
  257.8 12.7 %copy-start.11 = (f32[120,768]{1,0:T(8,128)S(1)}, f32[120,768]{1,0:T(8,128)}, u32[]{:S(2)}) copy-start(f32[120,768]{1,0:T(8,128)} %constant_dynamic-slice_fusion.3) | copy-start | bytes 1105924
  270.7 7.9 %copy-start.22 = (bf16[256,768]{1,0:T(8,128)(2,1)}, bf16[256,768]{1,0:T(8,128)(2,1)S(1)}, u32[]{:S(2)}) copy-start(bf16[256,768]{1,0:T(8,128)(2,1)S(1)} %collective-permute-done.31.refs_0_) | copy-start | bytes 1179652
  270.8 11.8 %copy-start.24 = (bf16[256,768]{1,0:T(8,128)(2,1)S(1)}, bf16[256,768]{1,0:T(8,128)(2,1)}, u32[]{:S(2)}) copy-start(bf16[256,768]{1,0:T(8,128)(2,1)} %copy-done.23) | copy-start | bytes 1179652
  270.8 22.0 %collective-permute-start.36 = (bf16[384,768]{1,0:T(8,128)(2,1)S(1)}, bf16[384,768]{1,0:T(8,128)(2,1)S(1)}, u32[]{:S(2)}, u32[]{:S(2)}) collective-permute-start(bf16[384,768]{1,0:T(8,128)(2,1)S(1)} %maximum_select_fusion.7), channel_id=1, source_target_pairs={{0,4},{4,0},{8,12},{12,8},{16,20},{20,16},{24,28},{28,24},{1,5},{5... | collective-permute-start | bytes 1769480 | tf_op jit(solution)/shard_map/down_grad_dp/ppermute | solution.py:786
  270.9 21.9 %collective-permute-start.35 = (bf16[120,768]{1,0:T(8,128)(2,1)S(1)}, bf16[120,768]{1,0:T(8,128)(2,1)S(1)}, u32[]{:S(2)}, u32[]{:S(2)}) collective-permute-start(bf16[120,768]{1,0:T(8,128)(2,1)S(1)} %convert_add_fusion.5), channel_id=1, source_target_pairs={{0,16},{4,20},{8,24},{12,28},{16,0},{20,4},{24,8},{28,12},{1,17},{... | collective-permute-start | bytes 552968 | tf_op jit(solution)/shard_map/up_proj_grad_dp/ppermute | solution.py:786
  275.1 13.8 %collective-permute-start.32 = (bf16[72,768]{1,0:T(8,128)(2,1)S(1)}, bf16[72,768]{1,0:T(8,128)(2,1)S(1)}, u32[]{:S(2)}, u32[]{:S(2)}) collective-permute-start(bf16[72,768]{1,0:T(8,128)(2,1)S(1)} %get-tuple-element.347), channel_id=1, source_target_pairs={{0,16},{4,20},{8,24},{12,28},{16,0},{20,4},{24,8},{28,12},{1,17},{... | collective-permute-start | bytes 331784 | tf_op jit(solution)/shard_map/qkv_grad_dp/ppermute | solution.py:786
  275.2 13.7 %collective-permute-start.33 = (bf16[72,768]{1,0:T(8,128)(2,1)S(1)}, bf16[72,768]{1,0:T(8,128)(2,1)S(1)}, u32[]{:S(2)}, u32[]{:S(2)}) collective-permute-start(bf16[72,768]{1,0:T(8,128)(2,1)S(1)} %get-tuple-element.348), channel_id=1, source_target_pairs={{0,8},{4,12},{8,0},{12,4},{16,24},{20,28},{24,16},{28,20},{1,9},{5... | collective-permute-start | bytes 331784 | tf_op jit(solution)/shard_map/qkv_grad_dp/ppermute | solution.py:786
  277.2 15.6 %collective-permute-start.34 = (bf16[72,768]{1,0:T(8,128)(2,1)S(1)}, bf16[72,768]{1,0:T(8,128)(2,1)S(1)}, u32[]{:S(2)}, u32[]{:S(2)}) collective-permute-start(bf16[72,768]{1,0:T(8,128)(2,1)S(1)} %get-tuple-element.349), channel_id=1, source_target_pairs={{0,24},{4,28},{8,16},{12,20},{16,8},{20,12},{24,0},{28,4},{1,25},{... | collective-permute-start | bytes 331784 | tf_op jit(solution)/shard_map/qkv_grad_dp/ppermute | solution.py:786
  293.4 10.7 %collective-permute-start.43 = (bf16[240,768]{1,0:T(8,128)(2,1)S(1)}, bf16[240,768]{1,0:T(8,128)(2,1)S(1)}, u32[]{:S(2)}, u32[]{:S(2)}) collective-permute-start(bf16[240,768]{1,0:T(8,128)(2,1)S(1)} %maximum_select_fusion.10), channel_id=1, source_target_pairs={{0,8},{4,12},{8,0},{12,4},{16,24},{20,28},{24,16},{28,20},{1,9},{5... | collective-permute-start | bytes 1105928 | tf_op jit(solution)/shard_map/up_proj_grad_dp/ppermute | solution.py:786
  293.5 2.9 collective-permute-start.37
  293.6 4.2 %collective-permute-start.38 = (f32[12,768]{1,0:T(8,128)S(1)}, f32[12,768]{1,0:T(8,128)S(1)}, u32[]{:S(2)}, u32[]{:S(2)}) collective-permute-start(f32[12,768]{1,0:T(8,128)S(1)} %pad_maximum_fusion.6), channel_id=1, source_target_pairs={{0,2},{1,3},{2,0},{3,1},{4,6},{5,7},{6,4},{7,5},{8,10},{9,11},{10,... | collective-permute-start | bytes 110600 | tf_op jit(solution)/shard_map/small_sums/ppermute | solution.py:25
  295.0 3.7 %collective-permute-start.39 = (f32[12,768]{1,0:T(8,128)S(1)}, f32[12,768]{1,0:T(8,128)S(1)}, u32[]{:S(2)}, u32[]{:S(2)}) collective-permute-start(f32[12,768]{1,0:T(8,128)S(1)} %pad_maximum_fusion.6), channel_id=1, source_target_pairs={{0,3},{1,2},{2,1},{3,0},{4,7},{5,6},{6,5},{7,4},{8,11},{9,10},{10,... | collective-permute-start | bytes 110600 | tf_op jit(solution)/shard_map/small_sums/ppermute | solution.py:915
  295.4 8.6 %collective-permute-start.42 = (bf16[72,768]{1,0:T(8,128)(2,1)S(1)}, bf16[72,768]{1,0:T(8,128)(2,1)S(1)}, u32[]{:S(2)}, u32[]{:S(2)}) collective-permute-start(bf16[72,768]{1,0:T(8,128)(2,1)S(1)} %convert_add_fusion.7), channel_id=1, source_target_pairs={{0,4},{4,0},{8,12},{12,8},{16,20},{20,16},{24,28},{28,24},{1,5},{5... | collective-permute-start | bytes 331784 | tf_op jit(solution)/shard_map/qkv_grad_dp/ppermute | solution.py:786
  298.7 4.2 %collective-permute-start.40 = (f32[12,768]{1,0:T(8,128)S(1)}, f32[12,768]{1,0:T(8,128)S(1)}, u32[]{:S(2)}, u32[]{:S(2)}) collective-permute-start(f32[12,768]{1,0:T(8,128)S(1)} %add_add_fusion), channel_id=1, source_target_pairs={{0,4},{4,0},{8,12},{12,8},{16,20},{20,16},{24,28},{28,24},{1,5},{5... | collective-permute-start | bytes 110600 | tf_op jit(solution)/shard_map/small_sums/ppermute | solution.py:786
  302.9 10.9 %collective-permute-start.41 = (bf16[256,768]{1,0:T(8,128)(2,1)S(1)}, bf16[256,768]{1,0:T(8,128)(2,1)}, u32[]{:S(2)}, u32[]{:S(2)}) collective-permute-start(bf16[256,768]{1,0:T(8,128)(2,1)S(1)} %slice.136), channel_id=1, source_target_pairs={{0,2},{1,3},{2,0},{3,1},{4,6},{5,7},{6,4},{7,5},{8,10},{9,11},{10,... | collective-permute-start | bytes 1179656 | tf_op jit(solution)/shard_map/in_grad_x/ppermute | solution.py:25
  304.4 10.5 %copy-start.25 = (bf16[256,768]{1,0:T(8,128)(2,1)S(1)}, bf16[256,768]{1,0:T(8,128)(2,1)}, u32[]{:S(2)}) copy-start(bf16[256,768]{1,0:T(8,128)(2,1)} %get-tuple-element.353) | copy-start | bytes 1179652
  304.4 18.0 %collective-permute-start.47 = (bf16[480,768]{1,0:T(8,128)(2,1)S(1)}, bf16[480,768]{1,0:T(8,128)(2,1)S(1)}, u32[]{:S(2)}, u32[]{:S(2)}) collective-permute-start(bf16[480,768]{1,0:T(8,128)(2,1)S(1)} %maximum_select_fusion.5), channel_id=1, source_target_pairs={{0,4},{4,0},{8,12},{12,8},{16,20},{20,16},{24,28},{28,24},{1,5},{5... | collective-permute-start | bytes 2211848 | tf_op jit(solution)/shard_map/up_proj_grad_dp/ppermute | solution.py:786
  305.4 20.1 %collective-permute-start.44 = (bf16[160,768]{1,0:T(8,128)(2,1)S(1)}, bf16[160,768]{1,0:T(8,128)(2,1)S(1)}, u32[]{:S(2)}, u32[]{:S(2)}) collective-permute-start(bf16[160,768]{1,0:T(8,128)(2,1)S(1)} %fusion.3), channel_id=1, source_target_pairs={{0,16},{4,20},{8,24},{12,28},{16,0},{20,4},{24,8},{28,12},{1,17},{... | collective-permute-start | bytes 737288 | tf_op jit(solution)/shard_map/qkv_grad_dp/ppermute | solution.py:786
  307.0 18.4 %collective-permute-start.45 = (bf16[160,768]{1,0:T(8,128)(2,1)S(1)}, bf16[160,768]{1,0:T(8,128)(2,1)S(1)}, u32[]{:S(2)}, u32[]{:S(2)}) collective-permute-start(bf16[160,768]{1,0:T(8,128)(2,1)S(1)} %fusion.3), channel_id=1, source_target_pairs={{0,8},{4,12},{8,0},{12,4},{16,24},{20,28},{24,16},{28,20},{1,9},{5... | collective-permute-start | bytes 737288 | tf_op jit(solution)/shard_map/qkv_grad_dp/ppermute | solution.py:786
  307.5 21.4 %collective-permute-start.46 = (bf16[160,768]{1,0:T(8,128)(2,1)S(1)}, bf16[160,768]{1,0:T(8,128)(2,1)S(1)}, u32[]{:S(2)}, u32[]{:S(2)}) collective-permute-start(bf16[160,768]{1,0:T(8,128)(2,1)S(1)} %fusion.3), channel_id=1, source_target_pairs={{0,24},{4,28},{8,16},{12,20},{16,8},{20,12},{24,0},{28,4},{1,25},{... | collective-permute-start | bytes 737288 | tf_op jit(solution)/shard_map/qkv_grad_dp/ppermute | solution.py:786
  (17 other events, 27.5 us)

commit v4 on v3

--- a/solution.py
+++ b/solution.py
@@ -19,6 +19,7 @@
 SLOT_K = (0, 0, 1, 1, 2, 3)
 X_SWAP = ((0, 2), (1, 3), (2, 0), (3, 1))
 CORE_SWAP = ((0, 1), (1, 0), (2, 3), (3, 2))
+DIAGONAL = ((0, 3), (1, 2), (2, 1), (3, 0))
 
 
 def x_swap(value):
@@ -87,73 +88,89 @@
     return value[:, first : first + 2 * HEAD_DIM]
 
 
-def attend_forward_kernel(size, table, start_ref, q_ref, k_ref, v_ref, out_ref, lse_ref):
-    slot = pl.program_id(1)
+def attend_forward_kernel(size, table, start_ref, *refs):
+    parts = (refs[:3], refs[3:6])
+    out_ref, lse_ref = refs[6:]
+    slot = pl.program_id(0)
     row, block, low = table[0, slot], table[1, slot], table[2, slot]
     start_row = start_ref[0:1, :]
     select = head_rows(size)
-    heads = select(q_ref[...] * jnp.asarray(HEAD_DIM**-0.5, BF))
+    heads = [
+        head for q_ref, _, _ in parts for head in select(q_ref[...] * jnp.asarray(HEAD_DIM**-0.5, BF))
+    ]
+    count = len(heads)
 
     def load(first, keys):
         at = pl.multiple_of(key_rows(table, row, first, size), keys)
-        return k_ref[pl.ds(at, keys), :], jnp.transpose(v_ref[pl.ds(at, keys), :])
-
-    key, value_t = load(block * size, size)
+        loaded = [
+            (k_ref[pl.ds(at, keys), :], jnp.transpose(v_ref[pl.ds(at, keys), :]))
+            for _, k_ref, v_ref in parts
+        ]
+        scores = [
+            nt(pair_lanes(loaded[head // 3][0], head % 3), heads[head]) for head in range(count)
+        ]
+        values = [
+            loaded[head // 3][1][head % 3 * HEAD_DIM : (head % 3 + 1) * HEAD_DIM]
+            for head in range(count)
+        ]
+        return scores, values
+
+    all_scores, values = load(block * size, size)
     mask = key_mask(start_row, block * size, size, size, True)
-    all_scores = [nt(pair_lanes(key, head), heads[head]) for head in range(3)]
     carry = []
-    for head in range(3):
+    for head in range(count):
         scores = jnp.where(mask, all_scores[head], MASKED)
         top = jnp.max(scores, axis=0, keepdims=True)
         weight = jnp.exp(scores - top)
         total = jnp.sum(weight, axis=0, keepdims=True)
-        acc = nn(value_t[head * HEAD_DIM : (head + 1) * HEAD_DIM], weight.astype(BF))
-        carry += [top, total, acc]
+        carry += [top, total, nn(values[head], weight.astype(BF))]
 
     def earlier(step, carry):
         first = block * size - (step + 1) * KEYS
-        key, value_t = load(first, KEYS)
+        all_scores, values = load(first, KEYS)
         mask = key_mask(start_row, first, KEYS, size, False)
-        all_scores = [nt(pair_lanes(key, head), heads[head]) for head in range(3)]
         new = []
-        for head in range(3):
+        for head in range(count):
             top, total, acc = carry[3 * head : 3 * head + 3]
             scores = jnp.where(mask, all_scores[head], MASKED)
             higher = jnp.maximum(top, jnp.max(scores, axis=0, keepdims=True))
             shrink = jnp.exp(top - higher)
             weight = jnp.exp(scores - higher)
             total = total * shrink + jnp.sum(weight, axis=0, keepdims=True)
-            acc = acc * shrink + nn(
-                value_t[head * HEAD_DIM : (head + 1) * HEAD_DIM], weight.astype(BF)
-            )
-            new += [higher, total, acc]
+            new += [higher, total, acc * shrink + nn(values[head], weight.astype(BF))]
         return tuple(new)
 
     carry = lax.fori_loop(0, block * (size // KEYS) - low, earlier, tuple(carry))
-    parts = [carry[3 * head + 2] / carry[3 * head + 1] for head in range(3)]
-    parts.append(jnp.zeros_like(parts[0]))
-    out_ref[...] = jnp.transpose(jnp.concatenate(parts, axis=0)).astype(BF)
-    for head in range(3):
-        lse_ref[head : head + 1, :] = carry[3 * head] + jnp.log(carry[3 * head + 1])
+    for shard in range(2):
+        rows = []
+        for head in range(3 * shard, 3 * shard + 3):
+            rows.append(carry[3 * head + 2] / carry[3 * head + 1])
+            at = 8 * shard + head % 3
+            lse_ref[at : at + 1, :] = carry[3 * head] + jnp.log(carry[3 * head + 1])
+        rows.append(jnp.zeros_like(rows[0]))
+        lanes = slice(4 * HEAD_DIM * shard, 4 * HEAD_DIM * (shard + 1))
+        out_ref[:, lanes] = jnp.transpose(jnp.concatenate(rows, axis=0)).astype(BF)
 
 
 def attend_forward(qkv, table, starts, size):
     width = 4 * HEAD_DIM
     tokens = qkv.shape[0]
+    specs = [pl.BlockSpec((8, size), lambda s, *_: (0, s))]
+    for shard in range(2):
+        specs += [
+            pl.BlockSpec((size, width), functools.partial(lambda c, s, *_: (s, c), 3 * shard)),
+            pl.BlockSpec((tokens, width), functools.partial(lambda c, s, *_: (0, c), 3 * shard + 1)),
+            pl.BlockSpec((tokens, width), functools.partial(lambda c, s, *_: (0, c), 3 * shard + 2)),
+        ]
     return pl.pallas_call(
         functools.partial(attend_forward_kernel, size),
         grid_spec=pltpu.PrefetchScalarGridSpec(
             num_scalar_prefetch=1,
-            grid=(2, 6),
-            in_specs=[
-                pl.BlockSpec((8, size), lambda p, s, *_: (0, s)),
-                pl.BlockSpec((size, width), lambda p, s, *_: (s, 3 * p)),
-                pl.BlockSpec((tokens, width), lambda p, s, *_: (0, 3 * p + 1)),
-                pl.BlockSpec((tokens, width), lambda p, s, *_: (0, 3 * p + 2)),
-            ],
+            grid=(6,),
+            in_specs=specs,
             out_specs=[
-                pl.BlockSpec((size, width), lambda p, s, *_: (s, p)),
-                pl.BlockSpec((8, size), lambda p, s, *_: (p, s)),
+                pl.BlockSpec((size, 2 * width), lambda s, *_: (s, 0)),
+                pl.BlockSpec((16, size), lambda s, *_: (0, s)),
             ],
         ),
         out_shape=[
@@ -163,7 +180,7 @@
         compiler_params=params(),
         cost_estimate=SMALL_COST,
         name="attend_forward",
-    )(table, starts, qkv, qkv, qkv)
+    )(table, starts, *[qkv] * 6)
 
 
 def attend_backward_kernel(
@@ -911,8 +928,7 @@
 
 
 def sum_over_tensor(value):
-    diagonal = ((0, 3), (1, 2), (2, 1), (3, 0))
-    return value + core_swap(value) + x_swap(value) + lax.ppermute(value, "tensor", diagonal)
+    return value + core_swap(value) + x_swap(value) + lax.ppermute(value, "tensor", DIAGONAL)
 
 
 def after(value, *earlier):
@@ -1014,13 +1030,13 @@
     with jax.named_scope("cotangent"):
         g_near = core_swap(g_home)
         g_far = x_swap(after(g_away, held))
-        g_far_near = core_swap(g_far)
+        g_far_near = lax.ppermute(after(g_away, held), "tensor", DIAGONAL)
 
     with jax.named_scope("proj_weight_x"):
         proj_far = x_swap(after(proj_weight, held))
     normed, qkv = first(tokens, vectors, held, qkv_own, size)
     attended, lse = attend_forward(qkv, table, start_rows, size)
-    attn_part = project(after(attended, g_far, g_near, got_mlp), proj_far, proj_weight, size)
+    attn_part = project(after(attended, g_far, g_near, g_far_near, got_mlp), proj_far, proj_weight, size)
     with jax.named_scope("attn_core"):
         attn_other = core_swap(attn_part)
     far_mlp = in_order(far_mlp, got_mlp, dp_bits()[0], 1)

time: 335 us -> 334 us (level); the launches traced: 333 us -> 328 us
  Pallas kernels: 157 us -> 151 us
    pallas_call x1, Pallas kernels: 16.9 us -> 12.1 us  [attend_forward(): pl.pallas_call(functools.partial(attend_forward_kernel, size), grid_spec=...]
  transfers between devices with their start and end apart: 48 -> 48, of which waited for: 19 -> 20; matrix products, arithmetic and copies ran while one was open for 10% -> 10% of each run, Pallas kernels for 37% -> 36%
where the time goes in v4:
time: 334 us; the launch traced here: 328 us
  Pallas kernels  151 us (45%)
  waiting for transfers between devices  77 us (23%)
  starting transfers between devices  49 us (15%)
  other arithmetic  25.7 us (8%)
  local copies, waits for them, and re-layouts  23.7 us (7%)
    ppermute x25, waiting for transfers between devices, dp_swap(): return lax.ppermute(value, 'dp', dp_partners(lax.axis_size('dp'), bit))  48.4 us
    pallas_call x7, Pallas kernels, sum_tokens(): pl.pallas_call(functools.partial(sum_tokens_kernel, rows, extra is not No...  40.3 us
    ppermute x25, starting transfers between devices, dp_swap(): return lax.ppermute(value, 'dp', dp_partners(lax.axis_size('dp'), bit))  31.5 us
    pallas_call x1, Pallas kernels, mlp(): pl.pallas_call(mlp_kernel, grid=(3,), in_specs=[fixed((2 * size, width))]...  27.4 us
    pallas_call x2, Pallas kernels, attend_backward(): pl.pallas_call(functools.partial(attend_backward_kernel, size), grid_spec...  26.5 us
    ppermute x13, waiting for transfers between devices, x_swap(): return lax.ppermute(value, 'tensor', X_SWAP)  25.4 us
    ppermute x13, starting transfers between devices, x_swap(): return lax.ppermute(value, 'tensor', X_SWAP)  15.1 us
    pallas_call x1, Pallas kernels, attend_forward(): pl.pallas_call(functools.partial(attend_forward_kernel, size), grid_spec=...  12.1 us
  transfers between devices with their start and end apart: 48, of which 20 were waited for; matrix products, arithmetic and copies ran while one was open for 10% of the time, Pallas kernels for 36%

profile of v4, /device:TPU:8, one launch (start us, length us, event | category | flops | bytes accessed | tf_op | source)
XLA Modules:
  0.0 328.2 jit_solution(17698399337424432597)
XLA Ops:
  3.4 1.5 collective-permute-start
  8.7 4.9 %collective-permute-done = bf16[2,96,768]{2,1,0:T(8,128)(2,1)} collective-permute-done((bf16[2,96,768]{2,1,0:T(8,128)(2,1)}, bf16[2,96,768]{2,1,0:T(8,128)(2,1)}, u32[]{:S(2)}, u32[]{:S(2)}) %collective-permute-start) | collective-permute-done | bytes 294944 | tf_op jit(solution)/shard_map/mlp_weights_x/ppermute | solution.py:26
  13.6 2.6 collective-permute-start.1
  16.2 1.5 collective-permute-start.3
  18.3 1.8 prepare.1
  20.1 10.2 %collective-permute-done.5.x2.away_ref = bf16[512,768]{1,0:T(8,128)(2,1)S(1)} collective-permute-done((bf16[512,768]{1,0:T(8,128)(2,1)}, bf16[512,768]{1,0:T(8,128)(2,1)S(1)}, u32[]{:S(2)}, u32[]{:S(2)}) %collective-permute-start.5) | collective-permute-done | bytes 786464 | tf_op jit(solution)/shard_map/tokens/ppermute | solution.py:26
  30.3 1.7 maximum_select_fusion.6
  32.1 15.4 %collective-permute-done.2 = bf16[2,192,768]{2,1,0:T(8,128)(2,1)S(1)} collective-permute-done((bf16[2,192,768]{2,1,0:T(8,128)(2,1)S(1)}, bf16[2,192,768]{2,1,0:T(8,128)(2,1)S(1)}, u32[]{:S(2)}, u32[]{:S(2)}) %collective-permute-start.2) | collective-permute-done | bytes 589856 | tf_op jit(solution)/shard_map/mlp_weights_dp/ppermute | solution.py:803
  48.7 1.6 collective-permute-start.10
  50.3 1.5 collective-permute-start.7
  52.1 1.5 collective-permute-start.11
  53.6 11.4 %first_norm_qkv.1 = (bf16[2048,768]{1,0:T(8,128)(2,1)}, bf16[2048,1536]{1,0:T(8,128)(2,1)}) custom-call(bf16[512,768]{1,0:T(8,128)(2,1)} %copy-done, bf16[512,768]{1,0:T(8,128)(2,1)} %collective-permute-done.4.x1, bf16[512,768]{1,0:T(8,128)(2,1)} %copy-done.3, bf16[512,768]{1,0:T(8,128)(2,1)} %copy-done.6, f32[8,768]{1,0:T(8,128)} %get-tuple-element.222.vec_ref, ...), custom_call_target="tpu_custom_call" | custom-call | flops 1 | bytes 1 | tf_op jit(solution)/shard_map/first_norm_qkv/pallas_call | solution.py:677
  65.0 12.1 %attend_forward.1 = (bf16[1536,512]{1,0:T(8,128)(2,1)}, f32[16,1536]{1,0:T(8,128)}) custom-call(s32[8,8]{1,0:T(8,128)} %get-tuple-element.220.table, s32[8,1536]{1,0:T(8,128)} %get-tuple-element.221.start_ref, bf16[2048,1536]{1,0:T(8,128)(2,1)} %get-tuple-element.225.refs_0_.refs_1_.refs_2_.refs_3_.refs_4_.refs_5_.q_ref.k_ref.v_ref, ...), custom_call_target="tpu_custom_call" | custom-call | flops 1 | bytes 1 | tf_op jit(solution)/shard_map/attend_forward/pallas_call | solution.py:165
  78.1 4.6 %project.1.own_ref = bf16[1536,768]{1,0:T(8,128)(2,1)} custom-call(bf16[1536,512]{1,0:T(8,128)(2,1)} %get-tuple-element.247.heads_ref.left_ref.out_ref, bf16[192,768]{1,0:T(8,128)(2,1)} %copy-done.13, bf16[192,768]{1,0:T(8,128)(2,1)} %own_w.3), custom_call_target="tpu_custom_call" | custom-call | flops 1 | bytes 1 | tf_op jit(solution)/shard_map/project/pallas_call | solution.py:550
  82.7 1.7 maximum_select_fusion.up_far.dn_far
  84.4 3.0 collective-permute-done.12.other_ref
  87.4 1.4 copy-done.8
  88.8 27.4 %mlp.1 = (f32[1536,128]{1,0:T(8,128)}, bf16[1536,768]{1,0:T(8,128)(2,1)}, bf16[2,1536,768]{2,1,0:T(8,128)(2,1)}, bf16[2,1536,768]{2,1,0:T(8,128)(2,1)}, f32[768,...) custom-call(bf16[512,768]{1,0:T(8,128)(2,1)} %copy-done, ...), custom_call_target="tpu_custom_call" | custom-call | flops 1 | bytes 1 | tf_op jit(solution)/shard_map/mlp/pallas_call | solution.py:447
  116.4 5.6 %sum_tokens.7 = bf16[768,768]{1,0:T(8,128)(2,1)} custom-call(bf16[1536,768]{1,0:T(8,128)(2,1)} %get-tuple-element.235.left_ref.mid_ref, bf16[2,1536,768]{2,1,0:T(8,128)(2,1)} %get-tuple-element.276.right_ref), custom_call_target="tpu_custom_call" | custom-call | flops 1 | bytes 1 | tf_op jit(solution)/shard_map/sum_tokens/pallas_call | solution.py:527
  122.0 8.7 %sum_tokens.8 = bf16[1536,768]{1,0:T(8,128)(2,1)} custom-call(bf16[2,1536,768]{2,1,0:T(8,128)(2,1)} %get-tuple-element.233.left_ref, bf16[1536,768]{1,0:T(8,128)(2,1)} %get-tuple-element.237.right_ref.bg_ref), custom_call_target="tpu_custom_call" | custom-call | flops 1 | bytes 1 | tf_op jit(solution)/shard_map/sum_tokens/pallas_call | solution.py:527
  130.8 2.9 constant_dynamic-slice_fusion.10
  134.7 3.0 collective-permute-start.16
  137.7 1.4 copy-done.10
  139.2 10.1 %mid_backward.1 = (f32[768,768]{1,0:T(8,128)}, bf16[1536,768]{1,0:T(8,128)(2,1)}, bf16[1536,512]{1,0:T(8,128)(2,1)}, f32[8,768]{1,0:T(8,128)}) custom-call(bf16[1536,768]{1,0:T(8,128)(2,1)} %get-tuple-element.235.left_ref.mid_ref, f32[1536,128]{1,0:T(8,128)} %get-tuple-element.248.rstd_ref, bf16[1536,768]{1,0:T(8,128)(2,1)} %get-tuple-element.249.own_ref, ...), custom_call_target="tpu_custom_call" | custom-call | flops 1 | bytes 1 | tf_op jit(solution)/shard_map/mid_backward/pallas_call | solution.py:610
  149.2 3.4 %sum_tokens.9 = bf16[192,768]{1,0:T(8,128)(2,1)} custom-call(bf16[1536,512]{1,0:T(8,128)(2,1)} %get-tuple-element.247.heads_ref.left_ref.out_ref, bf16[1536,768]{1,0:T(8,128)(2,1)} %get-tuple-element.250.right_ref), custom_call_target="tpu_custom_call" | custom-call | flops 1 | bytes 1 | tf_op jit(solution)/shard_map/sum_tokens/pallas_call | solution.py:527
  152.7 13.3 %attend_backward.2 = (bf16[2048,768]{1,0:T(8,128)(2,1)}, f32[8,256]{1,0:T(8,128)}) custom-call(s32[8,8]{1,0:T(8,128)} %get-tuple-element.220.table, s32[8,1536]{1,0:T(8,128)} %get-tuple-element.221.start_ref, bf16[2048,1536]{1,0:T(8,128)(2,1)} %get-tuple-element.225.refs_0_.refs_1_.refs_2_.refs_3_.refs_4_.refs_5_.q_ref.k_ref.v_ref, ...), custom_call_target="tpu_custom_call" | custom-call | flops 1 | bytes 1 | tf_op jit(solution)/shard_map/attend_backward/pallas_call | solution.py:256
  165.9 6.3 %sum_tokens.10 = bf16[576,768]{1,0:T(8,128)(2,1)} custom-call(bf16[2048,768]{1,0:T(8,128)(2,1)} %get-tuple-element.256.left_ref.far_d, bf16[2048,768]{1,0:T(8,128)(2,1)} %get-tuple-element.257.right_ref), custom_call_target="tpu_custom_call" | custom-call | flops 1 | bytes 1 | tf_op jit(solution)/shard_map/sum_tokens/pallas_call | solution.py:527
  172.3 1.5 convert_add_fusion
  175.1 1.5 collective-permute-start.18
  177.2 13.2 %attend_backward.3 = (bf16[2048,768]{1,0:T(8,128)(2,1)}, f32[8,256]{1,0:T(8,128)}) custom-call(s32[8,8]{1,0:T(8,128)} %get-tuple-element.220.table, s32[8,1536]{1,0:T(8,128)} %get-tuple-element.221.start_ref, bf16[2048,1536]{1,0:T(8,128)(2,1)} %get-tuple-element.225.refs_0_.refs_1_.refs_2_.refs_3_.refs_4_.refs_5_.q_ref.k_ref.v_ref, ...), custom_call_target="tpu_custom_call" | custom-call | flops 1 | bytes 1 | tf_op jit(solution)/shard_map/attend_backward/pallas_call | solution.py:256
  192.1 1.6 collective-permute-start.20
  193.7 5.8 %sum_tokens.11.refs_1_ = bf16[960,768]{1,0:T(8,128)(2,1)} custom-call(bf16[1536,768]{1,0:T(8,128)(2,1)} %get-tuple-element.235.left_ref.mid_ref, bf16[2,1536,768]{2,1,0:T(8,128)(2,1)} %get-tuple-element.276.right_ref, bf16[768,768]{1,0:T(8,128)(2,1)} %collective-permute-done.16.refs_0_), custom_call_target="tpu_custom_call" | custom-call | flops 1 | bytes 1 | tf_op jit(solution)/shard_map/sum_tokens/pallas_call | solution.py:527
  199.6 3.6 %collective-permute-done.19.refs_0_ = bf16[192,768]{1,0:T(8,128)(2,1)S(1)} collective-permute-done((bf16[192,768]{1,0:T(8,128)(2,1)}, bf16[192,768]{1,0:T(8,128)(2,1)S(1)}, u32[]{:S(2)}, u32[]{:S(2)}) %collective-permute-start.19) | collective-permute-done | bytes 294944 | tf_op jit(solution)/shard_map/proj_grad_x/ppermute | solution.py:26
  203.9 3.4 %sum_tokens.12 = bf16[960,768]{1,0:T(8,128)(2,1)} custom-call(bf16[1536,512]{1,0:T(8,128)(2,1)} %get-tuple-element.247.heads_ref.left_ref.out_ref, bf16[1536,768]{1,0:T(8,128)(2,1)} %get-tuple-element.250.right_ref, bf16[192,768]{1,0:T(8,128)(2,1)} %copy-done.28, bf16[960,768]{1,0:T(8,128)(2,1)} %sum_tokens.11.refs_1_), custom_call_target="tpu_custom_call", output_to_operand_aliasing={{}: (3, {})} | custom-call | flops 1 | bytes 1 | tf_op jit(solution)/shard_map/sum_tokens/pallas_call | solution.py:527
  209.7 1.5 collective-permute-start.21
  211.2 1.3 collective-permute-start.24
  212.5 6.9 %sum_tokens.13 = bf16[576,768]{1,0:T(8,128)(2,1)} custom-call(bf16[2048,768]{1,0:T(8,128)(2,1)} %get-tuple-element.307.left_ref.own_d, bf16[2048,768]{1,0:T(8,128)(2,1)} %get-tuple-element.257.right_ref, bf16[576,768]{1,0:T(8,128)(2,1)} %collective-permute-done.18.refs_0_), custom_call_target="tpu_custom_call" | custom-call | flops 1 | bytes 1 | tf_op jit(solution)/shard_map/sum_tokens/pallas_call | solution.py:527
  219.5 2.1 constant_dynamic-slice_fusion.4
  223.9 1.8 collective-permute-start.23
  225.7 9.9 %first_in.1 = (bf16[1024,768]{1,0:T(8,128)(2,1)}, bf16[1024,768]{1,0:T(8,128)(2,1)}) custom-call(bf16[2048,768]{1,0:T(8,128)(2,1)} %get-tuple-element.256.left_ref.far_d, bf16[2048,768]{1,0:T(8,128)(2,1)} %get-tuple-element.307.left_ref.own_d, bf16[592,768]{1,0:T(8,128)(2,1)} %copy-done.4, bf16[592,768]{1,0:T(8,128)(2,1)} %copy-done.1), custom_call_target="tpu_custom_call" | custom-call | flops 1 | bytes 1 | tf_op jit(solution)/shard_map/first_in/pallas_call | solution.py:730
  235.6 2.8 collective-permute-done.22
  238.5 1.4 convert_add_fusion.1
  244.3 2.7 collective-permute-start.30
  247.1 1.4 collective-permute-start.27
  248.5 2.0 collective-permute-start.28
  250.5 1.3 add_convert_fusion.1
  253.3 3.9 %first_backward.2 = (bf16[512,768]{1,0:T(8,128)(2,1)}, f32[8,768]{1,0:T(8,128)}) custom-call(bf16[512,768]{1,0:T(8,128)(2,1)} %copy-done, bf16[512,768]{1,0:T(8,128)(2,1)} %copy-done.3, bf16[1024,768]{1,0:T(8,128)(2,1)} %get-tuple-element.327.own_ref, bf16[1024,768]{1,0:T(8,128)(2,1)} %copy-done.5, f32[768,768]{1,0:T(8,128)} %get-tuple-element.329.rg_ref, ...), custom_call_target="tpu_custom_call" | custom-call | flops 1 | bytes 1 | tf_op jit(solution)/shard_map/first_backward/pallas_call | solution.py:775
  258.9 7.0 %collective-permute-done.27 = bf16[120,768]{1,0:T(8,128)(2,1)S(1)} collective-permute-done((bf16[120,768]{1,0:T(8,128)(2,1)}, bf16[120,768]{1,0:T(8,128)(2,1)S(1)}, u32[]{:S(2)}, u32[]{:S(2)}) %collective-permute-start.27) | collective-permute-done | bytes 184352 | tf_op jit(solution)/shard_map/up_proj_grad_dp/ppermute | solution.py:803
  266.4 3.8 %collective-permute-start.35 = (bf16[120,768]{1,0:T(8,128)(2,1)S(1)}, bf16[120,768]{1,0:T(8,128)(2,1)S(1)}, u32[]{:S(2)}, u32[]{:S(2)}) collective-permute-start(bf16[120,768]{1,0:T(8,128)(2,1)S(1)} %convert_add_fusion.5), channel_id=1, source_target_pairs={{0,16},{4,20},{8,24},{12,28},{16,0},{20,4},{24,8},{28,12},{1,17},{... | collective-permute-start | bytes 552968 | tf_op jit(solution)/shard_map/up_proj_grad_dp/ppermute | solution.py:803
  270.3 2.7 collective-permute-start.33
  273.8 3.2 first_backward.3
  278.9 5.5 %collective-permute-done.32 = bf16[72,768]{1,0:T(8,128)(2,1)S(1)} collective-permute-done((bf16[72,768]{1,0:T(8,128)(2,1)S(1)}, bf16[72,768]{1,0:T(8,128)(2,1)S(1)}, u32[]{:S(2)}, u32[]{:S(2)}) %collective-permute-start.32) | collective-permute-done | bytes 110624 | tf_op jit(solution)/shard_map/qkv_grad_dp/ppermute | solution.py:803
  284.5 3.7 %collective-permute-done.34 = bf16[72,768]{1,0:T(8,128)(2,1)S(1)} collective-permute-done((bf16[72,768]{1,0:T(8,128)(2,1)S(1)}, bf16[72,768]{1,0:T(8,128)(2,1)S(1)}, u32[]{:S(2)}, u32[]{:S(2)}) %collective-permute-start.34) | collective-permute-done | bytes 110624 | tf_op jit(solution)/shard_map/qkv_grad_dp/ppermute | solution.py:803
  289.2 1.6 collective-permute-start.39
  291.9 1.6 collective-permute-done.38
  294.9 1.6 convert_element_type.169
  296.5 1.5 collective-permute-done.40
  300.9 1.3 collective-permute-start.44
  302.7 1.7 collective-permute-start.46
  304.4 4.5 %collective-permute-done.41 = bf16[256,768]{1,0:T(8,128)(2,1)} collective-permute-done((bf16[256,768]{1,0:T(8,128)(2,1)S(1)}, bf16[256,768]{1,0:T(8,128)(2,1)}, u32[]{:S(2)}, u32[]{:S(2)}) %collective-permute-start.41) | collective-permute-done | bytes 393248 | tf_op jit(solution)/shard_map/in_grad_x/ppermute | solution.py:26
  311.2 6.1 %collective-permute-done.47 = bf16[480,768]{1,0:T(8,128)(2,1)S(1)} collective-permute-done((bf16[480,768]{1,0:T(8,128)(2,1)S(1)}, bf16[480,768]{1,0:T(8,128)(2,1)S(1)}, u32[]{:S(2)}, u32[]{:S(2)}) %collective-permute-start.47) | collective-permute-done | bytes 737312 | tf_op jit(solution)/shard_map/up_proj_grad_dp/ppermute | solution.py:803
  317.9 1.6 slice_convert_fusion
  320.4 3.9 %collective-permute-done.46 = bf16[160,768]{1,0:T(8,128)(2,1)S(1)} collective-permute-done((bf16[160,768]{1,0:T(8,128)(2,1)S(1)}, bf16[160,768]{1,0:T(8,128)(2,1)S(1)}, u32[]{:S(2)}, u32[]{:S(2)}) %collective-permute-start.46) | collective-permute-done | bytes 245792 | tf_op jit(solution)/shard_map/qkv_grad_dp/ppermute | solution.py:803
  325.2 1.3 copy.30
  (212 shorter events, 43.6 us)
Async XLA Ops:
  3.4 10.2 %collective-permute-start = (bf16[2,96,768]{2,1,0:T(8,128)(2,1)}, bf16[2,96,768]{2,1,0:T(8,128)(2,1)}, u32[]{:S(2)}, u32[]{:S(2)}) collective-permute-start(bf16[2,96,768]{2,1,0:T(8,128)(2,1)} %pad_maximum_fusion.5), channel_id=1, source_target_pairs={{0,2},{1,3},{2,0},{3,1},{4,6},{5,7},{6,4},{7,5},{8,10},{9,11},{10,... | collective-permute-start | bytes 884744 | tf_op jit(solution)/shard_map/mlp_weights_x/ppermute | solution.py:26
  6.0 11.7 %copy-start = (bf16[512,768]{1,0:T(8,128)(2,1)}, bf16[512,768]{1,0:T(8,128)(2,1)S(1)}, u32[]{:S(2)}) copy-start(bf16[512,768]{1,0:T(8,128)(2,1)S(1)} %get-tuple-element.216.x0.home_ref) | copy-start | bytes 2359300
  6.0 24.4 %collective-permute-start.5 = (bf16[512,768]{1,0:T(8,128)(2,1)}, bf16[512,768]{1,0:T(8,128)(2,1)S(1)}, u32[]{:S(2)}, u32[]{:S(2)}) collective-permute-start(bf16[512,768]{1,0:T(8,128)(2,1)} %get-tuple-element.434), channel_id=1, source_target_pairs={{0,2},{1,3},{2,0},{3,1},{4,6},{5,7},{6,4},{7,5},{8,10},{9,11},{10,... | collective-permute-start | bytes 2359304 | tf_op jit(solution)/shard_map/tokens/ppermute | solution.py:26
  8.7 39.3 %copy-start.1 = (bf16[592,768]{1,0:T(8,128)(2,1)}, bf16[592,768]{1,0:T(8,128)(2,1)S(1)}, u32[]{:S(2)}) copy-start(bf16[592,768]{1,0:T(8,128)(2,1)S(1)} %fusion.1.own_ref.upb_own.own_w_ref) | copy-start | bytes 2727940
  13.6 16.8 %collective-permute-start.1 = (bf16[2,96,768]{2,1,0:T(8,128)(2,1)}, bf16[2,96,768]{2,1,0:T(8,128)(2,1)}, u32[]{:S(2)}, u32[]{:S(2)}) collective-permute-start(bf16[2,96,768]{2,1,0:T(8,128)(2,1)} %collective-permute-done), channel_id=1, source_target_pairs={{0,16},{4,20},{8,24},{12,28},{16,0},{20,4},{24,8},{28,12},{1,17},{... | collective-permute-start | bytes 884744 | tf_op jit(solution)/shard_map/mlp_weights_dp/ppermute | solution.py:803
  16.2 32.5 %collective-permute-start.3 = (bf16[592,768]{1,0:T(8,128)(2,1)S(1)}, bf16[592,768]{1,0:T(8,128)(2,1)S(1)}, u32[]{:S(2)}, u32[]{:S(2)}) collective-permute-start(bf16[592,768]{1,0:T(8,128)(2,1)S(1)} %fusion.1.own_ref.upb_own.own_w_ref), channel_id=1, source_target_pairs={{0,2},{1,3},{2,0},{3,1},{4,6},{5,7},{6,4},{7,5},{8,10},{9,11},{10,... | collective-permute-start | bytes 2727944 | tf_op jit(solution)/shard_map/qkv_weights_x/ppermute | solution.py:26
  17.7 30.4 %collective-permute-start.4 = (bf16[512,768]{1,0:T(8,128)(2,1)S(1)}, bf16[512,768]{1,0:T(8,128)(2,1)}, u32[]{:S(2)}, u32[]{:S(2)}) collective-permute-start(bf16[512,768]{1,0:T(8,128)(2,1)S(1)} %get-tuple-element.216.x0.home_ref), channel_id=1, source_target_pairs={{0,1},{1,0},{2,3},{3,2},{4,5},{5,4},{6,7},{7,6},{8,9},{9,8},{10,11... | collective-permute-start | bytes 2359304 | tf_op jit(solution)/shard_map/tokens/ppermute | solution.py:30
  30.3 17.7 %copy-start.3 = (bf16[512,768]{1,0:T(8,128)(2,1)}, bf16[512,768]{1,0:T(8,128)(2,1)S(1)}, u32[]{:S(2)}) copy-start(bf16[512,768]{1,0:T(8,128)(2,1)S(1)} %collective-permute-done.5.x2.away_ref) | copy-start | bytes 2359300
  30.3 18.3 %collective-permute-start.6 = (bf16[512,768]{1,0:T(8,128)(2,1)S(1)}, bf16[512,768]{1,0:T(8,128)(2,1)S(1)}, u32[]{:S(2)}, u32[]{:S(2)}) collective-permute-start(bf16[512,768]{1,0:T(8,128)(2,1)S(1)} %collective-permute-done.5.x2.away_ref), channel_id=1, source_target_pairs={{0,1},{1,0},{2,3},{3,2},{4,5},{5,4},{6,7},{7,6},{8,9},{9,8},{10,11... | collective-permute-start | bytes 2359304 | tf_op jit(solution)/shard_map/tokens/ppermute | solution.py:30
  32.0 18.3 %copy-start.7 = (bf16[512,768]{1,0:T(8,128)(2,1)S(1)}, bf16[512,768]{1,0:T(8,128)(2,1)}, u32[]{:S(2)}) copy-start(bf16[512,768]{1,0:T(8,128)(2,1)} %pad_maximum_fusion.4.b0) | copy-start | bytes 2359300
  32.0 20.1 %copy-start.12 = (bf16[192,768]{1,0:T(8,128)(2,1)S(1)}, bf16[192,768]{1,0:T(8,128)(2,1)}, u32[]{:S(2)}) copy-start(bf16[192,768]{1,0:T(8,128)(2,1)} %own_w.3) | copy-start | bytes 884740
  32.0 15.5 %collective-permute-start.2 = (bf16[2,192,768]{2,1,0:T(8,128)(2,1)S(1)}, bf16[2,192,768]{2,1,0:T(8,128)(2,1)S(1)}, u32[]{:S(2)}, u32[]{:S(2)}) collective-permute-start(bf16[2,192,768]{2,1,0:T(8,128)(2,1)S(1)} %maximum_select_fusion.6), channel_id=1, source_target_pairs={{0,8},{4,12},{8,0},{12,4},{16,24},{20,28},{24,16},{28,20},{1,9},{5... | collective-permute-start | bytes 1769480 | tf_op jit(solution)/shard_map/mlp_weights_dp/ppermute | solution.py:803
  48.7 4.9 %copy-start.4 = (bf16[592,768]{1,0:T(8,128)(2,1)}, bf16[592,768]{1,0:T(8,128)(2,1)S(1)}, u32[]{:S(2)}) copy-start(bf16[592,768]{1,0:T(8,128)(2,1)S(1)} %collective-permute-done.3.far_ref.upb_far) | copy-start | bytes 2727940
  48.7 4.9 %copy-start.6 = (bf16[512,768]{1,0:T(8,128)(2,1)}, bf16[512,768]{1,0:T(8,128)(2,1)S(1)}, u32[]{:S(2)}) copy-start(bf16[512,768]{1,0:T(8,128)(2,1)S(1)} %collective-permute-done.6.x3) | copy-start | bytes 2359300
  48.7 28.6 %collective-permute-start.10 = (bf16[2,384,768]{2,1,0:T(8,128)(2,1)S(1)}, bf16[2,384,768]{2,1,0:T(8,128)(2,1)S(1)}, u32[]{:S(2)}, u32[]{:S(2)}) collective-permute-start(bf16[2,384,768]{2,1,0:T(8,128)(2,1)S(1)} %maximum_select_fusion.2), channel_id=1, source_target_pairs={{0,4},{4,0},{8,12},{12,8},{16,20},{20,16},{24,28},{28,24},{1,5},{5... | collective-permute-start | bytes 3538952 | tf_op jit(solution)/shard_map/mlp_weights_dp/ppermute | solution.py:803
  50.3 26.9 %collective-permute-start.8 = (bf16[512,768]{1,0:T(8,128)(2,1)S(1)}, bf16[512,768]{1,0:T(8,128)(2,1)S(1)}, u32[]{:S(2)}, u32[]{:S(2)}) collective-permute-start(bf16[512,768]{1,0:T(8,128)(2,1)S(1)} %copy-done.7), channel_id=1, source_target_pairs={{0,1},{1,0},{2,3},{3,2},{4,5},{5,4},{6,7},{7,6},{8,9},{9,8},{10,11... | collective-permute-start | bytes 2359304 | tf_op jit(solution)/shard_map/cotangent/ppermute | solution.py:30
  50.3 26.9 %collective-permute-start.7 = (bf16[256,768]{1,0:T(8,128)(2,1)}, bf16[256,768]{1,0:T(8,128)(2,1)S(1)}, u32[]{:S(2)}, u32[]{:S(2)}) collective-permute-start(bf16[256,768]{1,0:T(8,128)(2,1)} %get-tuple-element.228), channel_id=1, source_target_pairs={{0,2},{1,3},{2,0},{3,1},{4,6},{5,7},{6,4},{7,5},{8,10},{9,11},{10,... | collective-permute-start | bytes 1179656 | tf_op jit(solution)/shard_map/cotangent/ppermute | solution.py:26
  51.8 25.5 %collective-permute-start.9 = (bf16[256,768]{1,0:T(8,128)(2,1)}, bf16[256,768]{1,0:T(8,128)(2,1)S(1)}, u32[]{:S(2)}, u32[]{:S(2)}) collective-permute-start(bf16[256,768]{1,0:T(8,128)(2,1)} %get-tuple-element.228), channel_id=1, source_target_pairs={{0,3},{1,2},{2,1},{3,0},{4,7},{5,6},{6,5},{7,4},{8,11},{9,10},{10,... | collective-permute-start | bytes 1179656 | tf_op jit(solution)/shard_map/cotangent/ppermute | solution.py:1033
  52.1 25.1 %collective-permute-start.11 = (bf16[192,768]{1,0:T(8,128)(2,1)S(1)}, bf16[192,768]{1,0:T(8,128)(2,1)S(1)}, u32[]{:S(2)}, u32[]{:S(2)}) collective-permute-start(bf16[192,768]{1,0:T(8,128)(2,1)S(1)} %copy-done.12), channel_id=1, source_target_pairs={{0,2},{1,3},{2,0},{3,1},{4,6},{5,7},{6,4},{7,5},{8,10},{9,11},{10,... | collective-permute-start | bytes 884744 | tf_op jit(solution)/shard_map/proj_weight_x/ppermute | solution.py:26
  77.2 7.2 %copy-start.20 = (bf16[512,768]{1,0:T(8,128)(2,1)}, bf16[512,768]{1,0:T(8,128)(2,1)S(1)}, u32[]{:S(2)}) copy-start(bf16[512,768]{1,0:T(8,128)(2,1)S(1)} %collective-permute-done.8.b1) | copy-start | bytes 2359300
  77.2 7.2 %copy-start.26 = (bf16[256,768]{1,0:T(8,128)(2,1)}, bf16[256,768]{1,0:T(8,128)(2,1)S(1)}, u32[]{:S(2)}) copy-start(bf16[256,768]{1,0:T(8,128)(2,1)S(1)} %collective-permute-done.7.b2) | copy-start | bytes 1179652
  77.2 7.2 %copy-start.27 = (bf16[256,768]{1,0:T(8,128)(2,1)}, bf16[256,768]{1,0:T(8,128)(2,1)S(1)}, u32[]{:S(2)}) copy-start(bf16[256,768]{1,0:T(8,128)(2,1)S(1)} %collective-permute-done.9.b3) | copy-start | bytes 1179652
  82.7 4.7 %collective-permute-start.12 = (bf16[1536,768]{1,0:T(8,128)(2,1)}, bf16[1536,768]{1,0:T(8,128)(2,1)S(1)}, u32[]{:S(2)}, u32[]{:S(2)}) collective-permute-start(bf16[1536,768]{1,0:T(8,128)(2,1)} %project.1.own_ref), channel_id=1, source_target_pairs={{0,1},{1,0},{2,3},{3,2},{4,5},{5,4},{6,7},{7,6},{8,9},{9,8},{10,11... | collective-permute-start | bytes 7077896 | tf_op jit(solution)/shard_map/attn_core/ppermute | solution.py:30
  116.2 21.5 %collective-permute-start.13 = (bf16[1536,768]{1,0:T(8,128)(2,1)}, bf16[1536,768]{1,0:T(8,128)(2,1)S(1)}, u32[]{:S(2)}, u32[]{:S(2)}) collective-permute-start(bf16[1536,768]{1,0:T(8,128)(2,1)} %get-tuple-element.249.own_ref), channel_id=1, source_target_pairs={{0,1},{1,0},{2,3},{3,2},{4,5},{5,4},{6,7},{7,6},{8,9},{9,8},{10,11... | collective-permute-start | bytes 7077896 | tf_op jit(solution)/shard_map/mid_core/ppermute | solution.py:30
  133.6 38.7 %collective-permute-start.14 = (bf16[2,384,768]{2,1,0:T(8,128)(2,1)}, bf16[2,384,768]{2,1,0:T(8,128)(2,1)}, u32[]{:S(2)}, u32[]{:S(2)}) collective-permute-start(bf16[2,384,768]{2,1,0:T(8,128)(2,1)} %get-tuple-element.252), channel_id=1, source_target_pairs={{0,4},{4,0},{8,12},{12,8},{16,20},{20,16},{24,28},{28,24},{1,5},{5... | collective-permute-start | bytes 3538952 | tf_op jit(solution)/shard_map/down_grad_dp/ppermute | solution.py:803
  134.7 57.3 %collective-permute-start.16 = (bf16[768,768]{1,0:T(8,128)(2,1)}, bf16[768,768]{1,0:T(8,128)(2,1)}, u32[]{:S(2)}, u32[]{:S(2)}) collective-permute-start(bf16[768,768]{1,0:T(8,128)(2,1)} %sum_tokens.7), channel_id=1, source_target_pairs={{0,2},{1,3},{2,0},{3,1},{4,6},{5,7},{6,4},{7,5},{8,10},{9,11},{10,... | collective-permute-start | bytes 3538952 | tf_op jit(solution)/shard_map/up_grad_x/ppermute | solution.py:26
  174.8 17.2 %collective-permute-start.17 = (bf16[768,768]{1,0:T(8,128)(2,1)}, bf16[768,768]{1,0:T(8,128)(2,1)S(1)}, u32[]{:S(2)}, u32[]{:S(2)}) collective-permute-start(bf16[768,768]{1,0:T(8,128)(2,1)} %get-tuple-element.269), channel_id=1, source_target_pairs={{0,1},{1,0},{2,3},{3,2},{4,5},{5,4},{6,7},{7,6},{8,9},{9,8},{10,11... | collective-permute-start | bytes 3538952 | tf_op jit(solution)/shard_map/block_out/ppermute | solution.py:30
  174.8 16.1 %collective-permute-start.15 = (bf16[2,192,768]{2,1,0:T(8,128)(2,1)}, bf16[2,192,768]{2,1,0:T(8,128)(2,1)}, u32[]{:S(2)}, u32[]{:S(2)}) collective-permute-start(bf16[2,192,768]{2,1,0:T(8,128)(2,1)} %dynamic-slice_convert_fusion), channel_id=1, source_target_pairs={{0,8},{4,12},{8,0},{12,4},{16,24},{20,28},{24,16},{28,20},{1,9},{5... | collective-permute-start | bytes 1769480 | tf_op jit(solution)/shard_map/down_grad_dp/ppermute | solution.py:803
  175.1 28.0 %collective-permute-start.18 = (bf16[576,768]{1,0:T(8,128)(2,1)S(1)}, bf16[576,768]{1,0:T(8,128)(2,1)}, u32[]{:S(2)}, u32[]{:S(2)}) collective-permute-start(bf16[576,768]{1,0:T(8,128)(2,1)S(1)} %copy-done.18), channel_id=1, source_target_pairs={{0,2},{1,3},{2,0},{3,1},{4,6},{5,7},{6,4},{7,5},{8,10},{9,11},{10,... | collective-permute-start | bytes 2654216 | tf_op jit(solution)/shard_map/qkv_grad_x/ppermute | solution.py:26
  176.7 26.5 %collective-permute-start.19 = (bf16[192,768]{1,0:T(8,128)(2,1)}, bf16[192,768]{1,0:T(8,128)(2,1)S(1)}, u32[]{:S(2)}, u32[]{:S(2)}) collective-permute-start(bf16[192,768]{1,0:T(8,128)(2,1)} %sum_tokens.9), channel_id=1, source_target_pairs={{0,2},{1,3},{2,0},{3,1},{4,6},{5,7},{6,4},{7,5},{8,10},{9,11},{10,... | collective-permute-start | bytes 884744 | tf_op jit(solution)/shard_map/proj_grad_x/ppermute | solution.py:26
  192.0 7.6 %copy-start.16 = (bf16[768,768]{1,0:T(8,128)(2,1)}, bf16[768,768]{1,0:T(8,128)(2,1)S(1)}, u32[]{:S(2)}) copy-start(bf16[768,768]{1,0:T(8,128)(2,1)S(1)} %collective-permute-done.17) | copy-start | bytes 3538948
  192.1 15.2 %collective-permute-start.20 = (bf16[2,96,768]{2,1,0:T(8,128)(2,1)S(1)}, bf16[2,96,768]{2,1,0:T(8,128)(2,1)S(1)}, u32[]{:S(2)}, u32[]{:S(2)}) collective-permute-start(bf16[2,96,768]{2,1,0:T(8,128)(2,1)S(1)} %dynamic-slice_convert_fusion.1), channel_id=1, source_target_pairs={{0,16},{4,20},{8,24},{12,28},{16,0},{20,4},{24,8},{28,12},{1,17},{... | collective-permute-start | bytes 884744 | tf_op jit(solution)/shard_map/down_grad_dp/ppermute | solution.py:803
  209.7 9.7 %collective-permute-start.21 = (bf16[96,768]{1,0:T(8,128)(2,1)S(1)}, bf16[96,768]{1,0:T(8,128)(2,1)S(1)}, u32[]{:S(2)}, u32[]{:S(2)}) collective-permute-start(bf16[96,768]{1,0:T(8,128)(2,1)S(1)} %fusion.4), channel_id=1, source_target_pairs={{0,2},{1,3},{2,0},{3,1},{4,6},{5,7},{6,4},{7,5},{8,10},{9,11},{10,... | collective-permute-start | bytes 442376 | tf_op jit(solution)/shard_map/down_grad_x/ppermute | solution.py:26
  211.2 27.3 %collective-permute-start.24 = (bf16[480,768]{1,0:T(8,128)(2,1)}, bf16[480,768]{1,0:T(8,128)(2,1)}, u32[]{:S(2)}, u32[]{:S(2)}) collective-permute-start(bf16[480,768]{1,0:T(8,128)(2,1)} %get-tuple-element.306), channel_id=1, source_target_pairs={{0,4},{4,0},{8,12},{12,8},{16,20},{20,16},{24,28},{28,24},{1,5},{5... | collective-permute-start | bytes 2211848 | tf_op jit(solution)/shard_map/up_proj_grad_dp/ppermute | solution.py:803
  212.5 9.8 %copy-start.17 = (bf16[768,768]{1,0:T(8,128)(2,1)S(1)}, bf16[768,768]{1,0:T(8,128)(2,1)}, u32[]{:S(2)}) copy-start(bf16[768,768]{1,0:T(8,128)(2,1)} %copy-done.16) | copy-start | bytes 3538948
  221.6 16.8 %collective-permute-start.22 = (bf16[288,768]{1,0:T(8,128)(2,1)}, bf16[288,768]{1,0:T(8,128)(2,1)}, u32[]{:S(2)}, u32[]{:S(2)}) collective-permute-start(bf16[288,768]{1,0:T(8,128)(2,1)} %get-tuple-element.302), channel_id=1, source_target_pairs={{0,4},{4,0},{8,12},{12,8},{16,20},{20,16},{24,28},{28,24},{1,5},{5... | collective-permute-start | bytes 1327112 | tf_op jit(solution)/shard_map/qkv_grad_dp/ppermute | solution.py:803
  223.4 15.0 %collective-permute-start.25 = (bf16[256,768]{1,0:T(8,128)(2,1)}, bf16[256,768]{1,0:T(8,128)(2,1)S(1)}, u32[]{:S(2)}, u32[]{:S(2)}) collective-permute-start(bf16[256,768]{1,0:T(8,128)(2,1)} %slice.158), channel_id=1, source_target_pairs={{0,2},{1,3},{2,0},{3,1},{4,6},{5,7},{6,4},{7,5},{8,10},{9,11},{10,... | collective-permute-start | bytes 1179656 | tf_op jit(solution)/shard_map/block_out/ppermute | solution.py:26
  223.9 11.7 %collective-permute-start.23 = (bf16[96,768]{1,0:T(8,128)(2,1)S(1)}, bf16[96,768]{1,0:T(8,128)(2,1)S(1)}, u32[]{:S(2)}, u32[]{:S(2)}) collective-permute-start(bf16[96,768]{1,0:T(8,128)(2,1)S(1)} %convert_add_fusion.6), channel_id=1, source_target_pairs={{0,16},{4,20},{8,24},{12,28},{16,0},{20,4},{24,8},{28,12},{1,17},{... | collective-permute-start | bytes 442376 | tf_op jit(solution)/shard_map/down_grad_dp/ppermute | solution.py:803
  241.5 9.0 %collective-permute-start.29 = (bf16[1024,768]{1,0:T(8,128)(2,1)}, bf16[1024,768]{1,0:T(8,128)(2,1)S(1)}, u32[]{:S(2)}, u32[]{:S(2)}) collective-permute-start(bf16[1024,768]{1,0:T(8,128)(2,1)} %get-tuple-element.328), channel_id=1, source_target_pairs={{0,1},{1,0},{2,3},{3,2},{4,5},{5,4},{6,7},{7,6},{8,9},{9,8},{10,11... | collective-permute-start | bytes 4718600 | tf_op jit(solution)/shard_map/first_core/ppermute | solution.py:30
  244.3 14.0 %collective-permute-start.30 = (bf16[192,768]{1,0:T(8,128)(2,1)S(1)}, bf16[192,768]{1,0:T(8,128)(2,1)S(1)}, u32[]{:S(2)}, u32[]{:S(2)}) collective-permute-start(bf16[192,768]{1,0:T(8,128)(2,1)S(1)} %maximum_select_fusion.11), channel_id=1, source_target_pairs={{0,8},{4,12},{8,0},{12,4},{16,24},{20,28},{24,16},{28,20},{1,9},{5... | collective-permute-start | bytes 884744 | tf_op jit(solution)/shard_map/down_grad_dp/ppermute | solution.py:803
  247.0 11.9 %collective-permute-start.26 = (bf16[120,768]{1,0:T(8,128)(2,1)}, bf16[120,768]{1,0:T(8,128)(2,1)S(1)}, u32[]{:S(2)}, u32[]{:S(2)}) collective-permute-start(bf16[120,768]{1,0:T(8,128)(2,1)} %get-tuple-element.317), channel_id=1, source_target_pairs={{0,16},{4,20},{8,24},{12,28},{16,0},{20,4},{24,8},{28,12},{1,17},{... | collective-permute-start | bytes 552968 | tf_op jit(solution)/shard_map/up_proj_grad_dp/ppermute | solution.py:803
  247.1 18.8 %collective-permute-start.27 = (bf16[120,768]{1,0:T(8,128)(2,1)}, bf16[120,768]{1,0:T(8,128)(2,1)S(1)}, u32[]{:S(2)}, u32[]{:S(2)}) collective-permute-start(bf16[120,768]{1,0:T(8,128)(2,1)} %get-tuple-element.318), channel_id=1, source_target_pairs={{0,8},{4,12},{8,0},{12,4},{16,24},{20,28},{24,16},{28,20},{1,9},{5... | collective-permute-start | bytes 552968 | tf_op jit(solution)/shard_map/up_proj_grad_dp/ppermute | solution.py:803
  248.5 17.4 %collective-permute-start.28 = (bf16[120,768]{1,0:T(8,128)(2,1)}, bf16[120,768]{1,0:T(8,128)(2,1)S(1)}, u32[]{:S(2)}, u32[]{:S(2)}) collective-permute-start(bf16[120,768]{1,0:T(8,128)(2,1)} %get-tuple-element.319), channel_id=1, source_target_pairs={{0,24},{4,28},{8,16},{12,20},{16,8},{20,12},{24,0},{28,4},{1,25},{... | collective-permute-start | bytes 552968 | tf_op jit(solution)/shard_map/up_proj_grad_dp/ppermute | solution.py:803
  251.8 14.4 %collective-permute-start.31 = (bf16[256,768]{1,0:T(8,128)(2,1)S(1)}, bf16[256,768]{1,0:T(8,128)(2,1)S(1)}, u32[]{:S(2)}, u32[]{:S(2)}) collective-permute-start(bf16[256,768]{1,0:T(8,128)(2,1)S(1)} %add_convert_fusion.1), channel_id=1, source_target_pairs={{0,2},{1,3},{2,0},{3,1},{4,6},{5,7},{6,4},{7,5},{8,10},{9,11},{10,... | collective-permute-start | bytes 1179656 | tf_op jit(solution)/shard_map/first_mid_x/ppermute | solution.py:26
  253.3 12.8 %copy-start.11 = (f32[120,768]{1,0:T(8,128)S(1)}, f32[120,768]{1,0:T(8,128)}, u32[]{:S(2)}) copy-start(f32[120,768]{1,0:T(8,128)} %constant_dynamic-slice_fusion.3) | copy-start | bytes 1105924
  266.2 7.5 %copy-start.22 = (bf16[256,768]{1,0:T(8,128)(2,1)}, bf16[256,768]{1,0:T(8,128)(2,1)S(1)}, u32[]{:S(2)}) copy-start(bf16[256,768]{1,0:T(8,128)(2,1)S(1)} %collective-permute-done.31.refs_0_) | copy-start | bytes 1179652
  266.3 11.4 %copy-start.24 = (bf16[256,768]{1,0:T(8,128)(2,1)S(1)}, bf16[256,768]{1,0:T(8,128)(2,1)}, u32[]{:S(2)}) copy-start(bf16[256,768]{1,0:T(8,128)(2,1)} %copy-done.23) | copy-start | bytes 1179652
  266.3 21.8 %collective-permute-start.36 = (bf16[384,768]{1,0:T(8,128)(2,1)S(1)}, bf16[384,768]{1,0:T(8,128)(2,1)S(1)}, u32[]{:S(2)}, u32[]{:S(2)}) collective-permute-start(bf16[384,768]{1,0:T(8,128)(2,1)S(1)} %maximum_select_fusion.7), channel_id=1, source_target_pairs={{0,4},{4,0},{8,12},{12,8},{16,20},{20,16},{24,28},{28,24},{1,5},{5... | collective-permute-start | bytes 1769480 | tf_op jit(solution)/shard_map/down_grad_dp/ppermute | solution.py:803
  266.4 21.7 %collective-permute-start.35 = (bf16[120,768]{1,0:T(8,128)(2,1)S(1)}, bf16[120,768]{1,0:T(8,128)(2,1)S(1)}, u32[]{:S(2)}, u32[]{:S(2)}) collective-permute-start(bf16[120,768]{1,0:T(8,128)(2,1)S(1)} %convert_add_fusion.5), channel_id=1, source_target_pairs={{0,16},{4,20},{8,24},{12,28},{16,0},{20,4},{24,8},{28,12},{1,17},{... | collective-permute-start | bytes 552968 | tf_op jit(solution)/shard_map/up_proj_grad_dp/ppermute | solution.py:803
  270.3 14.2 %collective-permute-start.32 = (bf16[72,768]{1,0:T(8,128)(2,1)S(1)}, bf16[72,768]{1,0:T(8,128)(2,1)S(1)}, u32[]{:S(2)}, u32[]{:S(2)}) collective-permute-start(bf16[72,768]{1,0:T(8,128)(2,1)S(1)} %get-tuple-element.347), channel_id=1, source_target_pairs={{0,16},{4,20},{8,24},{12,28},{16,0},{20,4},{24,8},{28,12},{1,17},{... | collective-permute-start | bytes 331784 | tf_op jit(solution)/shard_map/qkv_grad_dp/ppermute | solution.py:803
  270.3 14.2 %collective-permute-start.33 = (bf16[72,768]{1,0:T(8,128)(2,1)S(1)}, bf16[72,768]{1,0:T(8,128)(2,1)S(1)}, u32[]{:S(2)}, u32[]{:S(2)}) collective-permute-start(bf16[72,768]{1,0:T(8,128)(2,1)S(1)} %get-tuple-element.348), channel_id=1, source_target_pairs={{0,8},{4,12},{8,0},{12,4},{16,24},{20,28},{24,16},{28,20},{1,9},{5... | collective-permute-start | bytes 331784 | tf_op jit(solution)/shard_map/qkv_grad_dp/ppermute | solution.py:803
  273.0 15.1 %collective-permute-start.34 = (bf16[72,768]{1,0:T(8,128)(2,1)S(1)}, bf16[72,768]{1,0:T(8,128)(2,1)S(1)}, u32[]{:S(2)}, u32[]{:S(2)}) collective-permute-start(bf16[72,768]{1,0:T(8,128)(2,1)S(1)} %get-tuple-element.349), channel_id=1, source_target_pairs={{0,24},{4,28},{8,16},{12,20},{16,8},{20,12},{24,0},{28,4},{1,25},{... | collective-permute-start | bytes 331784 | tf_op jit(solution)/shard_map/qkv_grad_dp/ppermute | solution.py:803
  288.8 10.6 %collective-permute-start.43 = (bf16[240,768]{1,0:T(8,128)(2,1)S(1)}, bf16[240,768]{1,0:T(8,128)(2,1)S(1)}, u32[]{:S(2)}, u32[]{:S(2)}) collective-permute-start(bf16[240,768]{1,0:T(8,128)(2,1)S(1)} %maximum_select_fusion.10), channel_id=1, source_target_pairs={{0,8},{4,12},{8,0},{12,4},{16,24},{20,28},{24,16},{28,20},{1,9},{5... | collective-permute-start | bytes 1105928 | tf_op jit(solution)/shard_map/up_proj_grad_dp/ppermute | solution.py:803
  288.8 3.1 collective-permute-start.37
  288.9 4.6 %collective-permute-start.38 = (f32[12,768]{1,0:T(8,128)S(1)}, f32[12,768]{1,0:T(8,128)S(1)}, u32[]{:S(2)}, u32[]{:S(2)}) collective-permute-start(f32[12,768]{1,0:T(8,128)S(1)} %pad_maximum_fusion.6), channel_id=1, source_target_pairs={{0,2},{1,3},{2,0},{3,1},{4,6},{5,7},{6,4},{7,5},{8,10},{9,11},{10,... | collective-permute-start | bytes 110600 | tf_op jit(solution)/shard_map/small_sums/ppermute | solution.py:26
  289.2 4.5 %collective-permute-start.39 = (f32[12,768]{1,0:T(8,128)S(1)}, f32[12,768]{1,0:T(8,128)S(1)}, u32[]{:S(2)}, u32[]{:S(2)}) collective-permute-start(f32[12,768]{1,0:T(8,128)S(1)} %pad_maximum_fusion.6), channel_id=1, source_target_pairs={{0,3},{1,2},{2,1},{3,0},{4,7},{5,6},{6,5},{7,4},{8,11},{9,10},{10,... | collective-permute-start | bytes 110600 | tf_op jit(solution)/shard_map/small_sums/ppermute | solution.py:931
  290.8 8.2 %collective-permute-start.42 = (bf16[72,768]{1,0:T(8,128)(2,1)S(1)}, bf16[72,768]{1,0:T(8,128)(2,1)S(1)}, u32[]{:S(2)}, u32[]{:S(2)}) collective-permute-start(bf16[72,768]{1,0:T(8,128)(2,1)S(1)} %convert_add_fusion.7), channel_id=1, source_target_pairs={{0,4},{4,0},{8,12},{12,8},{16,20},{20,16},{24,28},{28,24},{1,5},{5... | collective-permute-start | bytes 331784 | tf_op jit(solution)/shard_map/qkv_grad_dp/ppermute | solution.py:803
  293.7 4.3 %collective-permute-start.40 = (f32[12,768]{1,0:T(8,128)S(1)}, f32[12,768]{1,0:T(8,128)S(1)}, u32[]{:S(2)}, u32[]{:S(2)}) collective-permute-start(f32[12,768]{1,0:T(8,128)S(1)} %add_add_fusion), channel_id=1, source_target_pairs={{0,4},{4,0},{8,12},{12,8},{16,20},{20,16},{24,28},{28,24},{1,5},{5... | collective-permute-start | bytes 110600 | tf_op jit(solution)/shard_map/small_sums/ppermute | solution.py:803
  298.0 11.0 %collective-permute-start.41 = (bf16[256,768]{1,0:T(8,128)(2,1)S(1)}, bf16[256,768]{1,0:T(8,128)(2,1)}, u32[]{:S(2)}, u32[]{:S(2)}) collective-permute-start(bf16[256,768]{1,0:T(8,128)(2,1)S(1)} %slice.136), channel_id=1, source_target_pairs={{0,2},{1,3},{2,0},{3,1},{4,6},{5,7},{6,4},{7,5},{8,10},{9,11},{10,... | collective-permute-start | bytes 1179656 | tf_op jit(solution)/shard_map/in_grad_x/ppermute | solution.py:26
  299.6 10.4 %copy-start.25 = (bf16[256,768]{1,0:T(8,128)(2,1)S(1)}, bf16[256,768]{1,0:T(8,128)(2,1)}, u32[]{:S(2)}) copy-start(bf16[256,768]{1,0:T(8,128)(2,1)} %get-tuple-element.353) | copy-start | bytes 1179652
  299.7 17.6 %collective-permute-start.47 = (bf16[480,768]{1,0:T(8,128)(2,1)S(1)}, bf16[480,768]{1,0:T(8,128)(2,1)S(1)}, u32[]{:S(2)}, u32[]{:S(2)}) collective-permute-start(bf16[480,768]{1,0:T(8,128)(2,1)S(1)} %maximum_select_fusion.5), channel_id=1, source_target_pairs={{0,4},{4,0},{8,12},{12,8},{16,20},{20,16},{24,28},{28,24},{1,5},{5... | collective-permute-start | bytes 2211848 | tf_op jit(solution)/shard_map/up_proj_grad_dp/ppermute | solution.py:803
  300.9 19.5 %collective-permute-start.44 = (bf16[160,768]{1,0:T(8,128)(2,1)S(1)}, bf16[160,768]{1,0:T(8,128)(2,1)S(1)}, u32[]{:S(2)}, u32[]{:S(2)}) collective-permute-start(bf16[160,768]{1,0:T(8,128)(2,1)S(1)} %fusion.3), channel_id=1, source_target_pairs={{0,16},{4,20},{8,24},{12,28},{16,0},{20,4},{24,8},{28,12},{1,17},{... | collective-permute-start | bytes 737288 | tf_op jit(solution)/shard_map/qkv_grad_dp/ppermute | solution.py:803
  302.2 18.2 %collective-permute-start.45 = (bf16[160,768]{1,0:T(8,128)(2,1)S(1)}, bf16[160,768]{1,0:T(8,128)(2,1)S(1)}, u32[]{:S(2)}, u32[]{:S(2)}) collective-permute-start(bf16[160,768]{1,0:T(8,128)(2,1)S(1)} %fusion.3), channel_id=1, source_target_pairs={{0,8},{4,12},{8,0},{12,4},{16,24},{20,28},{24,16},{28,20},{1,9},{5... | collective-permute-start | bytes 737288 | tf_op jit(solution)/shard_map/qkv_grad_dp/ppermute | solution.py:803
  302.7 21.6 %collective-permute-start.46 = (bf16[160,768]{1,0:T(8,128)(2,1)S(1)}, bf16[160,768]{1,0:T(8,128)(2,1)S(1)}, u32[]{:S(2)}, u32[]{:S(2)}) collective-permute-start(bf16[160,768]{1,0:T(8,128)(2,1)S(1)} %fusion.3), channel_id=1, source_target_pairs={{0,24},{4,28},{8,16},{12,20},{16,8},{20,12},{24,0},{28,4},{1,25},{... | collective-permute-start | bytes 737288 | tf_op jit(solution)/shard_map/qkv_grad_dp/ppermute | solution.py:803
  (17 other events, 32.4 us)

commit v5 on v4

--- a/solution.py
+++ b/solution.py
@@ -853,18 +853,17 @@
         self.name, self.masks = name, masks(bits)
         self.bits = bits
 
-    def split(self, value):
+    def piece(self, value, distance):
         axis = value.ndim - 2
         rows = value.shape[axis] // (2 ** len(self.bits))
-        mine = member(self.bits)
-        pieces = [
-            lax.dynamic_slice_in_dim(value, (mine ^ distance) * rows, rows, axis)
-            for distance in range(2 ** len(self.bits))
-        ]
-        return pieces[0], [piece.astype(BF) for piece in pieces[1:]]
+        return lax.dynamic_slice_in_dim(value, (member(self.bits) ^ distance) * rows, rows, axis)
+
+    def split(self, value):
+        give = range(1, 2 ** len(self.bits))
+        return value, [self.piece(value, distance).astype(BF) for distance in give]
 
     def join(self, kept, got):
-        total = kept.astype(F32)
+        total = self.piece(kept, 0).astype(F32)
         for piece in got:
             total = total + piece.astype(F32)
         return total

time: 334 us -> 328 us (0.982); the launches traced: 328 us -> 326 us
  waiting for transfers between devices: 77 us -> 71.3 us
  local copies, waits for them, and re-layouts: 23.7 us -> 20.3 us
    ppermute x25, waiting for transfers between devices: 48.4 us -> 41.1 us  [dp_swap(): return lax.ppermute(value, 'dp', dp_partners(lax.axis_size('dp'), bit))]
    dynamic_slice x7 -> x3, local copies, waits for them, and re-layouts: 6.91 us -> 5.08 us  [piece(): lax.dynamic_slice_in_dim(value, (member(self.bits) ^ distance) * rows, ro...]
  transfers between devices with their start and end apart: 48 -> 48, of which waited for: 20 -> 19; matrix products, arithmetic and copies ran while one was open for 10% -> 10% of each run, Pallas kernels for 36% -> 37%
where the time goes in v5:
time: 328 us; the launch traced here: 326 us
  Pallas kernels  154 us (47%)
  waiting for transfers between devices  71.3 us (22%)
  starting transfers between devices  51.4 us (16%)
  other arithmetic  27.5 us (8%)
  local copies, waits for them, and re-layouts  20.3 us (6%)
    ppermute x25, waiting for transfers between devices, dp_swap(): return lax.ppermute(value, 'dp', dp_partners(lax.axis_size('dp'), bit))  41.1 us
    pallas_call x7, Pallas kernels, sum_tokens(): pl.pallas_call(functools.partial(sum_tokens_kernel, rows, extra is not No...  40.5 us
    ppermute x25, starting transfers between devices, dp_swap(): return lax.ppermute(value, 'dp', dp_partners(lax.axis_size('dp'), bit))  34 us
    pallas_call x2, Pallas kernels, attend_backward(): pl.pallas_call(functools.partial(attend_backward_kernel, size), grid_spec...  28.5 us
    pallas_call x1, Pallas kernels, mlp(): pl.pallas_call(mlp_kernel, grid=(3,), in_specs=[fixed((2 * size, width))]...  27.4 us
    ppermute x13, waiting for transfers between devices, x_swap(): return lax.ppermute(value, 'tensor', X_SWAP)  26.6 us
    ppermute x13, starting transfers between devices, x_swap(): return lax.ppermute(value, 'tensor', X_SWAP)  15.7 us
    pallas_call x1, Pallas kernels, attend_forward(): pl.pallas_call(functools.partial(attend_forward_kernel, size), grid_spec=...  13.4 us
  transfers between devices with their start and end apart: 48, of which 19 were waited for; matrix products, arithmetic and copies ran while one was open for 10% of the time, Pallas kernels for 37%

profile of v5, /device:TPU:8, one launch (start us, length us, event | category | flops | bytes accessed | tf_op | source)
XLA Modules:
  0.0 326.1 jit_solution(9533192731635460637)
XLA Ops:
  3.4 1.5 collective-permute-start
  8.8 4.8 %collective-permute-done = bf16[2,96,768]{2,1,0:T(8,128)(2,1)} collective-permute-done((bf16[2,96,768]{2,1,0:T(8,128)(2,1)}, bf16[2,96,768]{2,1,0:T(8,128)(2,1)}, u32[]{:S(2)}, u32[]{:S(2)}) %collective-permute-start) | collective-permute-done | bytes 294944 | tf_op jit(solution)/shard_map/mlp_weights_x/ppermute | solution.py:26
  13.6 2.6 collective-permute-start.1
  16.2 1.5 collective-permute-start.3
  18.3 1.8 prepare.1
  20.1 10.2 %collective-permute-done.5.x2.away_ref = bf16[512,768]{1,0:T(8,128)(2,1)S(1)} collective-permute-done((bf16[512,768]{1,0:T(8,128)(2,1)}, bf16[512,768]{1,0:T(8,128)(2,1)S(1)}, u32[]{:S(2)}, u32[]{:S(2)}) %collective-permute-start.5) | collective-permute-done | bytes 786464 | tf_op jit(solution)/shard_map/tokens/ppermute | solution.py:26
  30.3 1.7 maximum_select_fusion.6
  32.1 15.4 %collective-permute-done.2 = bf16[2,192,768]{2,1,0:T(8,128)(2,1)S(1)} collective-permute-done((bf16[2,192,768]{2,1,0:T(8,128)(2,1)S(1)}, bf16[2,192,768]{2,1,0:T(8,128)(2,1)S(1)}, u32[]{:S(2)}, u32[]{:S(2)}) %collective-permute-start.2) | collective-permute-done | bytes 589856 | tf_op jit(solution)/shard_map/mlp_weights_dp/ppermute | solution.py:803
  48.7 1.6 collective-permute-start.10
  50.3 1.5 collective-permute-start.7
  52.1 1.5 collective-permute-start.11
  53.6 11.1 %first_norm_qkv.1 = (bf16[2048,768]{1,0:T(8,128)(2,1)}, bf16[2048,1536]{1,0:T(8,128)(2,1)}) custom-call(bf16[512,768]{1,0:T(8,128)(2,1)} %copy-done, bf16[512,768]{1,0:T(8,128)(2,1)} %collective-permute-done.4.x1, bf16[512,768]{1,0:T(8,128)(2,1)} %copy-done.3, bf16[512,768]{1,0:T(8,128)(2,1)} %copy-done.9, f32[8,768]{1,0:T(8,128)} %get-tuple-element.222.vec_ref, ...), custom_call_target="tpu_custom_call" | custom-call | flops 1 | bytes 1 | tf_op jit(solution)/shard_map/first_norm_qkv/pallas_call | solution.py:677
  64.8 13.4 %attend_forward.1 = (bf16[1536,512]{1,0:T(8,128)(2,1)}, f32[16,1536]{1,0:T(8,128)}) custom-call(s32[8,8]{1,0:T(8,128)} %get-tuple-element.220.table, s32[8,1536]{1,0:T(8,128)} %get-tuple-element.221.start_ref, bf16[2048,1536]{1,0:T(8,128)(2,1)} %get-tuple-element.225.refs_0_.refs_1_.refs_2_.refs_3_.refs_4_.refs_5_.q_ref.k_ref.v_ref, ...), custom_call_target="tpu_custom_call" | custom-call | flops 1 | bytes 1 | tf_op jit(solution)/shard_map/attend_forward/pallas_call | solution.py:165
  79.0 4.6 %project.1.own_ref = bf16[1536,768]{1,0:T(8,128)(2,1)} custom-call(bf16[1536,512]{1,0:T(8,128)(2,1)} %get-tuple-element.247.heads_ref.left_ref.out_ref, bf16[192,768]{1,0:T(8,128)(2,1)} %copy-done.15, bf16[192,768]{1,0:T(8,128)(2,1)} %own_w.3), custom_call_target="tpu_custom_call" | custom-call | flops 1 | bytes 1 | tf_op jit(solution)/shard_map/project/pallas_call | solution.py:550
  83.6 1.8 maximum_select_fusion.up_far.dn_far
  85.4 2.9 collective-permute-done.12.other_ref
  88.3 1.4 copy-done.11
  89.7 27.4 %mlp.1 = (f32[1536,128]{1,0:T(8,128)}, bf16[1536,768]{1,0:T(8,128)(2,1)}, bf16[2,1536,768]{2,1,0:T(8,128)(2,1)}, bf16[2,1536,768]{2,1,0:T(8,128)(2,1)}, f32[768,...) custom-call(bf16[512,768]{1,0:T(8,128)(2,1)} %copy-done, ...), custom_call_target="tpu_custom_call" | custom-call | flops 1 | bytes 1 | tf_op jit(solution)/shard_map/mlp/pallas_call | solution.py:447
  117.4 5.6 %sum_tokens.7 = bf16[768,768]{1,0:T(8,128)(2,1)} custom-call(bf16[1536,768]{1,0:T(8,128)(2,1)} %get-tuple-element.235.left_ref.mid_ref, bf16[2,1536,768]{2,1,0:T(8,128)(2,1)} %get-tuple-element.276.right_ref), custom_call_target="tpu_custom_call" | custom-call | flops 1 | bytes 1 | tf_op jit(solution)/shard_map/sum_tokens/pallas_call | solution.py:527
  123.0 8.7 %sum_tokens.8 = bf16[1536,768]{1,0:T(8,128)(2,1)} custom-call(bf16[2,1536,768]{2,1,0:T(8,128)(2,1)} %get-tuple-element.233.left_ref, bf16[1536,768]{1,0:T(8,128)(2,1)} %get-tuple-element.237.right_ref.bg_ref), custom_call_target="tpu_custom_call" | custom-call | flops 1 | bytes 1 | tf_op jit(solution)/shard_map/sum_tokens/pallas_call | solution.py:527
  131.7 2.4 constant_dynamic-slice_fusion.4
  135.1 2.4 collective-permute-start.16
  137.6 1.4 copy-done.13
  139.0 9.9 %mid_backward.1 = (f32[768,768]{1,0:T(8,128)}, bf16[1536,768]{1,0:T(8,128)(2,1)}, bf16[1536,512]{1,0:T(8,128)(2,1)}, f32[8,768]{1,0:T(8,128)}) custom-call(bf16[1536,768]{1,0:T(8,128)(2,1)} %get-tuple-element.235.left_ref.mid_ref, f32[1536,128]{1,0:T(8,128)} %get-tuple-element.248.rstd_ref, bf16[1536,768]{1,0:T(8,128)(2,1)} %get-tuple-element.249.own_ref, ...), custom_call_target="tpu_custom_call" | custom-call | flops 1 | bytes 1 | tf_op jit(solution)/shard_map/mid_backward/pallas_call | solution.py:610
  148.9 3.4 %sum_tokens.9 = bf16[192,768]{1,0:T(8,128)(2,1)} custom-call(bf16[1536,512]{1,0:T(8,128)(2,1)} %get-tuple-element.247.heads_ref.left_ref.out_ref, bf16[1536,768]{1,0:T(8,128)(2,1)} %get-tuple-element.250.right_ref), custom_call_target="tpu_custom_call" | custom-call | flops 1 | bytes 1 | tf_op jit(solution)/shard_map/sum_tokens/pallas_call | solution.py:527
  152.3 14.2 %attend_backward.2 = (bf16[2048,768]{1,0:T(8,128)(2,1)}, f32[8,256]{1,0:T(8,128)}) custom-call(s32[8,8]{1,0:T(8,128)} %get-tuple-element.220.table, s32[8,1536]{1,0:T(8,128)} %get-tuple-element.221.start_ref, bf16[2048,1536]{1,0:T(8,128)(2,1)} %get-tuple-element.225.refs_0_.refs_1_.refs_2_.refs_3_.refs_4_.refs_5_.q_ref.k_ref.v_ref, ...), custom_call_target="tpu_custom_call" | custom-call | flops 1 | bytes 1 | tf_op jit(solution)/shard_map/attend_backward/pallas_call | solution.py:256
  166.6 6.5 %sum_tokens.10 = bf16[576,768]{1,0:T(8,128)(2,1)} custom-call(bf16[2048,768]{1,0:T(8,128)(2,1)} %get-tuple-element.256.left_ref.far_d, bf16[2048,768]{1,0:T(8,128)(2,1)} %get-tuple-element.257.right_ref), custom_call_target="tpu_custom_call" | custom-call | flops 1 | bytes 1 | tf_op jit(solution)/shard_map/sum_tokens/pallas_call | solution.py:527
  173.6 2.0 collective-permute-start.19
  175.6 14.3 %attend_backward.3 = (bf16[2048,768]{1,0:T(8,128)(2,1)}, f32[8,256]{1,0:T(8,128)}) custom-call(s32[8,8]{1,0:T(8,128)} %get-tuple-element.220.table, s32[8,1536]{1,0:T(8,128)} %get-tuple-element.221.start_ref, bf16[2048,1536]{1,0:T(8,128)(2,1)} %get-tuple-element.225.refs_0_.refs_1_.refs_2_.refs_3_.refs_4_.refs_5_.q_ref.k_ref.v_ref, ...), custom_call_target="tpu_custom_call" | custom-call | flops 1 | bytes 1 | tf_op jit(solution)/shard_map/attend_backward/pallas_call | solution.py:256
  189.9 1.2 convert_add_fusion.2
  191.2 1.4 collective-permute-start.20
  192.5 5.8 %sum_tokens.11.refs_1_ = bf16[960,768]{1,0:T(8,128)(2,1)} custom-call(bf16[1536,768]{1,0:T(8,128)(2,1)} %get-tuple-element.235.left_ref.mid_ref, bf16[2,1536,768]{2,1,0:T(8,128)(2,1)} %get-tuple-element.276.right_ref, bf16[768,768]{1,0:T(8,128)(2,1)} %collective-permute-done.16.refs_0_), custom_call_target="tpu_custom_call" | custom-call | flops 1 | bytes 1 | tf_op jit(solution)/shard_map/sum_tokens/pallas_call | solution.py:527
  198.4 3.8 %collective-permute-done.19.refs_0_ = bf16[192,768]{1,0:T(8,128)(2,1)} collective-permute-done((bf16[192,768]{1,0:T(8,128)(2,1)}, bf16[192,768]{1,0:T(8,128)(2,1)}, u32[]{:S(2)}, u32[]{:S(2)}) %collective-permute-start.19) | collective-permute-done | bytes 294944 | tf_op jit(solution)/shard_map/proj_grad_x/ppermute | solution.py:26
  202.2 3.4 %sum_tokens.12 = bf16[960,768]{1,0:T(8,128)(2,1)} custom-call(bf16[1536,512]{1,0:T(8,128)(2,1)} %get-tuple-element.247.heads_ref.left_ref.out_ref, bf16[1536,768]{1,0:T(8,128)(2,1)} %get-tuple-element.250.right_ref, bf16[192,768]{1,0:T(8,128)(2,1)} %collective-permute-done.19.refs_0_, ...), custom_call_target="tpu_custom_call", output_to_operand_aliasing={{}: (3, {})} | custom-call | flops 1 | bytes 1 | tf_op jit(solution)/shard_map/sum_tokens/pallas_call | solution.py:527
  205.7 1.3 copy-done.2
  208.4 2.0 collective-permute-start.24
  210.4 7.0 %sum_tokens.13 = bf16[576,768]{1,0:T(8,128)(2,1)} custom-call(bf16[2048,768]{1,0:T(8,128)(2,1)} %get-tuple-element.307.left_ref.own_d, bf16[2048,768]{1,0:T(8,128)(2,1)} %get-tuple-element.257.right_ref, bf16[576,768]{1,0:T(8,128)(2,1)} %collective-permute-done.18.refs_0_), custom_call_target="tpu_custom_call" | custom-call | flops 1 | bytes 1 | tf_op jit(solution)/shard_map/sum_tokens/pallas_call | solution.py:527
  217.4 1.8 constant_dynamic-slice_fusion.2
  219.3 1.5 add_convert_fusion
  221.6 1.5 collective-permute-start.25
  223.0 2.8 collective-permute-start.23
  225.8 10.0 %first_in.1 = (bf16[1024,768]{1,0:T(8,128)(2,1)}, bf16[1024,768]{1,0:T(8,128)(2,1)}) custom-call(bf16[2048,768]{1,0:T(8,128)(2,1)} %get-tuple-element.256.left_ref.far_d, bf16[2048,768]{1,0:T(8,128)(2,1)} %get-tuple-element.307.left_ref.own_d, bf16[592,768]{1,0:T(8,128)(2,1)} %copy-done.5, bf16[592,768]{1,0:T(8,128)(2,1)} %copy-done.1), custom_call_target="tpu_custom_call" | custom-call | flops 1 | bytes 1 | tf_op jit(solution)/shard_map/first_in/pallas_call | solution.py:730
  236.2 1.3 convert_add_fusion.1
  241.5 2.5 collective-permute-start.30
  245.2 1.6 collective-permute-start.27
  247.5 1.3 add_convert_fusion.1
  250.8 3.9 %first_backward.2 = (bf16[512,768]{1,0:T(8,128)(2,1)}, f32[8,768]{1,0:T(8,128)}) custom-call(bf16[512,768]{1,0:T(8,128)(2,1)} %copy-done, bf16[512,768]{1,0:T(8,128)(2,1)} %copy-done.3, bf16[1024,768]{1,0:T(8,128)(2,1)} %get-tuple-element.327.own_ref, bf16[1024,768]{1,0:T(8,128)(2,1)} %copy-done.6, f32[768,768]{1,0:T(8,128)} %get-tuple-element.329.rg_ref, ...), custom_call_target="tpu_custom_call" | custom-call | flops 1 | bytes 1 | tf_op jit(solution)/shard_map/first_backward/pallas_call | solution.py:775
  255.3 1.7 collective-permute-done.26
  256.9 2.9 collective-permute-done.27
  261.2 1.3 collective-permute-start.36
  262.5 6.7 %collective-permute-start.35 = (bf16[120,768]{1,0:T(8,128)(2,1)S(1)}, bf16[120,768]{1,0:T(8,128)(2,1)S(1)}, u32[]{:S(2)}, u32[]{:S(2)}) collective-permute-start(bf16[120,768]{1,0:T(8,128)(2,1)S(1)} %convert_add_fusion.5), channel_id=1, source_target_pairs={{0,16},{4,20},{8,24},{12,28},{16,0},{20,4},{24,8},{28,12},{1,17},{... | collective-permute-start | bytes 552968 | tf_op jit(solution)/shard_map/up_proj_grad_dp/ppermute | solution.py:803
  269.2 2.7 collective-permute-start.33
  272.7 3.2 first_backward.3
  278.9 4.7 %collective-permute-done.32 = bf16[72,768]{1,0:T(8,128)(2,1)S(1)} collective-permute-done((bf16[72,768]{1,0:T(8,128)(2,1)S(1)}, bf16[72,768]{1,0:T(8,128)(2,1)S(1)}, u32[]{:S(2)}, u32[]{:S(2)}) %collective-permute-start.32) | collective-permute-done | bytes 110624 | tf_op jit(solution)/shard_map/qkv_grad_dp/ppermute | solution.py:803
  283.6 3.3 %collective-permute-done.34 = bf16[72,768]{1,0:T(8,128)(2,1)S(1)} collective-permute-done((bf16[72,768]{1,0:T(8,128)(2,1)S(1)}, bf16[72,768]{1,0:T(8,128)(2,1)S(1)}, u32[]{:S(2)}, u32[]{:S(2)}) %collective-permute-start.34) | collective-permute-done | bytes 110624 | tf_op jit(solution)/shard_map/qkv_grad_dp/ppermute | solution.py:803
  289.9 2.1 collective-permute-done.38
  293.1 1.6 convert_element_type.169
  294.7 2.1 collective-permute-done.40
  298.9 2.4 collective-permute-start.44
  302.5 5.1 %collective-permute-done.41 = bf16[256,768]{1,0:T(8,128)(2,1)} collective-permute-done((bf16[256,768]{1,0:T(8,128)(2,1)S(1)}, bf16[256,768]{1,0:T(8,128)(2,1)}, u32[]{:S(2)}, u32[]{:S(2)}) %collective-permute-start.41) | collective-permute-done | bytes 393248 | tf_op jit(solution)/shard_map/in_grad_x/ppermute | solution.py:26
  309.7 6.3 %collective-permute-done.47 = bf16[480,768]{1,0:T(8,128)(2,1)S(1)} collective-permute-done((bf16[480,768]{1,0:T(8,128)(2,1)S(1)}, bf16[480,768]{1,0:T(8,128)(2,1)S(1)}, u32[]{:S(2)}, u32[]{:S(2)}) %collective-permute-start.47) | collective-permute-done | bytes 737312 | tf_op jit(solution)/shard_map/up_proj_grad_dp/ppermute | solution.py:803
  316.7 1.6 slice_convert_fusion
  319.1 3.3 %collective-permute-done.46 = bf16[160,768]{1,0:T(8,128)(2,1)S(1)} collective-permute-done((bf16[160,768]{1,0:T(8,128)(2,1)S(1)}, bf16[160,768]{1,0:T(8,128)(2,1)S(1)}, u32[]{:S(2)}, u32[]{:S(2)}) %collective-permute-start.46) | collective-permute-done | bytes 245792 | tf_op jit(solution)/shard_map/qkv_grad_dp/ppermute | solution.py:803
  323.4 1.3 copy.30
  (200 shorter events, 41.1 us)
Async XLA Ops:
  3.4 10.2 %collective-permute-start = (bf16[2,96,768]{2,1,0:T(8,128)(2,1)}, bf16[2,96,768]{2,1,0:T(8,128)(2,1)}, u32[]{:S(2)}, u32[]{:S(2)}) collective-permute-start(bf16[2,96,768]{2,1,0:T(8,128)(2,1)} %pad_maximum_fusion.5), channel_id=1, source_target_pairs={{0,2},{1,3},{2,0},{3,1},{4,6},{5,7},{6,4},{7,5},{8,10},{9,11},{10,... | collective-permute-start | bytes 884744 | tf_op jit(solution)/shard_map/mlp_weights_x/ppermute | solution.py:26
  6.0 11.7 %copy-start = (bf16[512,768]{1,0:T(8,128)(2,1)}, bf16[512,768]{1,0:T(8,128)(2,1)S(1)}, u32[]{:S(2)}) copy-start(bf16[512,768]{1,0:T(8,128)(2,1)S(1)} %get-tuple-element.216.x0.home_ref) | copy-start | bytes 2359300
  6.0 24.4 %collective-permute-start.5 = (bf16[512,768]{1,0:T(8,128)(2,1)}, bf16[512,768]{1,0:T(8,128)(2,1)S(1)}, u32[]{:S(2)}, u32[]{:S(2)}) collective-permute-start(bf16[512,768]{1,0:T(8,128)(2,1)} %get-tuple-element.428), channel_id=1, source_target_pairs={{0,2},{1,3},{2,0},{3,1},{4,6},{5,7},{6,4},{7,5},{8,10},{9,11},{10,... | collective-permute-start | bytes 2359304 | tf_op jit(solution)/shard_map/tokens/ppermute | solution.py:26
  8.8 39.2 %copy-start.1 = (bf16[592,768]{1,0:T(8,128)(2,1)}, bf16[592,768]{1,0:T(8,128)(2,1)S(1)}, u32[]{:S(2)}) copy-start(bf16[592,768]{1,0:T(8,128)(2,1)S(1)} %fusion.1.own_ref.upb_own.own_w_ref) | copy-start | bytes 2727940
  13.6 16.8 %collective-permute-start.1 = (bf16[2,96,768]{2,1,0:T(8,128)(2,1)}, bf16[2,96,768]{2,1,0:T(8,128)(2,1)}, u32[]{:S(2)}, u32[]{:S(2)}) collective-permute-start(bf16[2,96,768]{2,1,0:T(8,128)(2,1)} %collective-permute-done), channel_id=1, source_target_pairs={{0,16},{4,20},{8,24},{12,28},{16,0},{20,4},{24,8},{28,12},{1,17},{... | collective-permute-start | bytes 884744 | tf_op jit(solution)/shard_map/mlp_weights_dp/ppermute | solution.py:803
  16.2 32.5 %collective-permute-start.3 = (bf16[592,768]{1,0:T(8,128)(2,1)S(1)}, bf16[592,768]{1,0:T(8,128)(2,1)S(1)}, u32[]{:S(2)}, u32[]{:S(2)}) collective-permute-start(bf16[592,768]{1,0:T(8,128)(2,1)S(1)} %fusion.1.own_ref.upb_own.own_w_ref), channel_id=1, source_target_pairs={{0,2},{1,3},{2,0},{3,1},{4,6},{5,7},{6,4},{7,5},{8,10},{9,11},{10,... | collective-permute-start | bytes 2727944 | tf_op jit(solution)/shard_map/qkv_weights_x/ppermute | solution.py:26
  17.7 30.4 %collective-permute-start.4 = (bf16[512,768]{1,0:T(8,128)(2,1)S(1)}, bf16[512,768]{1,0:T(8,128)(2,1)}, u32[]{:S(2)}, u32[]{:S(2)}) collective-permute-start(bf16[512,768]{1,0:T(8,128)(2,1)S(1)} %get-tuple-element.216.x0.home_ref), channel_id=1, source_target_pairs={{0,1},{1,0},{2,3},{3,2},{4,5},{5,4},{6,7},{7,6},{8,9},{9,8},{10,11... | collective-permute-start | bytes 2359304 | tf_op jit(solution)/shard_map/tokens/ppermute | solution.py:30
  30.3 17.7 %copy-start.3 = (bf16[512,768]{1,0:T(8,128)(2,1)}, bf16[512,768]{1,0:T(8,128)(2,1)S(1)}, u32[]{:S(2)}) copy-start(bf16[512,768]{1,0:T(8,128)(2,1)S(1)} %collective-permute-done.5.x2.away_ref) | copy-start | bytes 2359300
  30.3 18.3 %collective-permute-start.6 = (bf16[512,768]{1,0:T(8,128)(2,1)S(1)}, bf16[512,768]{1,0:T(8,128)(2,1)S(1)}, u32[]{:S(2)}, u32[]{:S(2)}) collective-permute-start(bf16[512,768]{1,0:T(8,128)(2,1)S(1)} %collective-permute-done.5.x2.away_ref), channel_id=1, source_target_pairs={{0,1},{1,0},{2,3},{3,2},{4,5},{5,4},{6,7},{7,6},{8,9},{9,8},{10,11... | collective-permute-start | bytes 2359304 | tf_op jit(solution)/shard_map/tokens/ppermute | solution.py:30
  32.0 18.3 %copy-start.10 = (bf16[512,768]{1,0:T(8,128)(2,1)S(1)}, bf16[512,768]{1,0:T(8,128)(2,1)}, u32[]{:S(2)}) copy-start(bf16[512,768]{1,0:T(8,128)(2,1)} %pad_maximum_fusion.4.b0) | copy-start | bytes 2359300
  32.0 20.1 %copy-start.14 = (bf16[192,768]{1,0:T(8,128)(2,1)S(1)}, bf16[192,768]{1,0:T(8,128)(2,1)}, u32[]{:S(2)}) copy-start(bf16[192,768]{1,0:T(8,128)(2,1)} %own_w.3) | copy-start | bytes 884740
  32.0 15.5 %collective-permute-start.2 = (bf16[2,192,768]{2,1,0:T(8,128)(2,1)S(1)}, bf16[2,192,768]{2,1,0:T(8,128)(2,1)S(1)}, u32[]{:S(2)}, u32[]{:S(2)}) collective-permute-start(bf16[2,192,768]{2,1,0:T(8,128)(2,1)S(1)} %maximum_select_fusion.6), channel_id=1, source_target_pairs={{0,8},{4,12},{8,0},{12,4},{16,24},{20,28},{24,16},{28,20},{1,9},{5... | collective-permute-start | bytes 1769480 | tf_op jit(solution)/shard_map/mlp_weights_dp/ppermute | solution.py:803
  48.7 4.9 %copy-start.5 = (bf16[592,768]{1,0:T(8,128)(2,1)}, bf16[592,768]{1,0:T(8,128)(2,1)S(1)}, u32[]{:S(2)}) copy-start(bf16[592,768]{1,0:T(8,128)(2,1)S(1)} %collective-permute-done.3.far_ref.upb_far) | copy-start | bytes 2727940
  48.7 4.9 %copy-start.9 = (bf16[512,768]{1,0:T(8,128)(2,1)}, bf16[512,768]{1,0:T(8,128)(2,1)S(1)}, u32[]{:S(2)}) copy-start(bf16[512,768]{1,0:T(8,128)(2,1)S(1)} %collective-permute-done.6.x3) | copy-start | bytes 2359300
  48.7 29.5 %collective-permute-start.10 = (bf16[2,384,768]{2,1,0:T(8,128)(2,1)S(1)}, bf16[2,384,768]{2,1,0:T(8,128)(2,1)S(1)}, u32[]{:S(2)}, u32[]{:S(2)}) collective-permute-start(bf16[2,384,768]{2,1,0:T(8,128)(2,1)S(1)} %maximum_select_fusion.2), channel_id=1, source_target_pairs={{0,4},{4,0},{8,12},{12,8},{16,20},{20,16},{24,28},{28,24},{1,5},{5... | collective-permute-start | bytes 3538952 | tf_op jit(solution)/shard_map/mlp_weights_dp/ppermute | solution.py:803
  50.3 27.9 %collective-permute-start.8 = (bf16[512,768]{1,0:T(8,128)(2,1)S(1)}, bf16[512,768]{1,0:T(8,128)(2,1)S(1)}, u32[]{:S(2)}, u32[]{:S(2)}) collective-permute-start(bf16[512,768]{1,0:T(8,128)(2,1)S(1)} %copy-done.10), channel_id=1, source_target_pairs={{0,1},{1,0},{2,3},{3,2},{4,5},{5,4},{6,7},{7,6},{8,9},{9,8},{10,11... | collective-permute-start | bytes 2359304 | tf_op jit(solution)/shard_map/cotangent/ppermute | solution.py:30
  50.3 27.9 %collective-permute-start.7 = (bf16[256,768]{1,0:T(8,128)(2,1)}, bf16[256,768]{1,0:T(8,128)(2,1)S(1)}, u32[]{:S(2)}, u32[]{:S(2)}) collective-permute-start(bf16[256,768]{1,0:T(8,128)(2,1)} %get-tuple-element.228), channel_id=1, source_target_pairs={{0,2},{1,3},{2,0},{3,1},{4,6},{5,7},{6,4},{7,5},{8,10},{9,11},{10,... | collective-permute-start | bytes 1179656 | tf_op jit(solution)/shard_map/cotangent/ppermute | solution.py:26
  51.8 26.4 %collective-permute-start.9 = (bf16[256,768]{1,0:T(8,128)(2,1)}, bf16[256,768]{1,0:T(8,128)(2,1)S(1)}, u32[]{:S(2)}, u32[]{:S(2)}) collective-permute-start(bf16[256,768]{1,0:T(8,128)(2,1)} %get-tuple-element.228), channel_id=1, source_target_pairs={{0,3},{1,2},{2,1},{3,0},{4,7},{5,6},{6,5},{7,4},{8,11},{9,10},{10,... | collective-permute-start | bytes 1179656 | tf_op jit(solution)/shard_map/cotangent/ppermute | solution.py:1032
  52.1 26.1 %collective-permute-start.11 = (bf16[192,768]{1,0:T(8,128)(2,1)S(1)}, bf16[192,768]{1,0:T(8,128)(2,1)S(1)}, u32[]{:S(2)}, u32[]{:S(2)}) collective-permute-start(bf16[192,768]{1,0:T(8,128)(2,1)S(1)} %copy-done.14), channel_id=1, source_target_pairs={{0,2},{1,3},{2,0},{3,1},{4,6},{5,7},{6,4},{7,5},{8,10},{9,11},{10,... | collective-permute-start | bytes 884744 | tf_op jit(solution)/shard_map/proj_weight_x/ppermute | solution.py:26
  78.1 7.3 %copy-start.19 = (bf16[512,768]{1,0:T(8,128)(2,1)}, bf16[512,768]{1,0:T(8,128)(2,1)S(1)}, u32[]{:S(2)}) copy-start(bf16[512,768]{1,0:T(8,128)(2,1)S(1)} %collective-permute-done.8.b1) | copy-start | bytes 2359300
  78.1 7.2 %copy-start.23 = (bf16[256,768]{1,0:T(8,128)(2,1)}, bf16[256,768]{1,0:T(8,128)(2,1)S(1)}, u32[]{:S(2)}) copy-start(bf16[256,768]{1,0:T(8,128)(2,1)S(1)} %collective-permute-done.7.b2) | copy-start | bytes 1179652
  78.2 7.2 %copy-start.24 = (bf16[256,768]{1,0:T(8,128)(2,1)}, bf16[256,768]{1,0:T(8,128)(2,1)S(1)}, u32[]{:S(2)}) copy-start(bf16[256,768]{1,0:T(8,128)(2,1)S(1)} %collective-permute-done.9.b3) | copy-start | bytes 1179652
  83.6 4.7 %collective-permute-start.12 = (bf16[1536,768]{1,0:T(8,128)(2,1)}, bf16[1536,768]{1,0:T(8,128)(2,1)S(1)}, u32[]{:S(2)}, u32[]{:S(2)}) collective-permute-start(bf16[1536,768]{1,0:T(8,128)(2,1)} %project.1.own_ref), channel_id=1, source_target_pairs={{0,1},{1,0},{2,3},{3,2},{4,5},{5,4},{6,7},{7,6},{8,9},{9,8},{10,11... | collective-permute-start | bytes 7077896 | tf_op jit(solution)/shard_map/attn_core/ppermute | solution.py:30
  117.1 20.4 %collective-permute-start.13 = (bf16[1536,768]{1,0:T(8,128)(2,1)}, bf16[1536,768]{1,0:T(8,128)(2,1)S(1)}, u32[]{:S(2)}, u32[]{:S(2)}) collective-permute-start(bf16[1536,768]{1,0:T(8,128)(2,1)} %get-tuple-element.249.own_ref), channel_id=1, source_target_pairs={{0,1},{1,0},{2,3},{3,2},{4,5},{5,4},{6,7},{7,6},{8,9},{9,8},{10,11... | collective-permute-start | bytes 7077896 | tf_op jit(solution)/shard_map/mid_core/ppermute | solution.py:30
  134.0 39.0 %collective-permute-start.14 = (bf16[2,384,768]{2,1,0:T(8,128)(2,1)}, bf16[2,384,768]{2,1,0:T(8,128)(2,1)S(1)}, u32[]{:S(2)}, u32[]{:S(2)}) collective-permute-start(bf16[2,384,768]{2,1,0:T(8,128)(2,1)} %constant_dynamic-slice_fusion.4), channel_id=1, source_target_pairs={{0,4},{4,0},{8,12},{12,8},{16,20},{20,16},{24,28},{28,24},{1,5},{5... | collective-permute-start | bytes 3538952 | tf_op jit(solution)/shard_map/down_grad_dp/ppermute | solution.py:803
  135.1 56.0 %collective-permute-start.16 = (bf16[768,768]{1,0:T(8,128)(2,1)}, bf16[768,768]{1,0:T(8,128)(2,1)}, u32[]{:S(2)}, u32[]{:S(2)}) collective-permute-start(bf16[768,768]{1,0:T(8,128)(2,1)} %sum_tokens.7), channel_id=1, source_target_pairs={{0,2},{1,3},{2,0},{3,1},{4,6},{5,7},{6,4},{7,5},{8,10},{9,11},{10,... | collective-permute-start | bytes 3538952 | tf_op jit(solution)/shard_map/up_grad_x/ppermute | solution.py:26
  166.6 6.5 %copy-start.4 = (bf16[1536,768]{1,0:T(8,128)(2,1)S(1)}, bf16[1536,768]{1,0:T(8,128)(2,1)}, u32[]{:S(2)}) copy-start(bf16[1536,768]{1,0:T(8,128)(2,1)} %sum_tokens.8) | copy-start | bytes 7077892
  173.4 17.7 %collective-permute-start.17 = (bf16[768,768]{1,0:T(8,128)(2,1)}, bf16[768,768]{1,0:T(8,128)(2,1)}, u32[]{:S(2)}, u32[]{:S(2)}) collective-permute-start(bf16[768,768]{1,0:T(8,128)(2,1)} %get-tuple-element.269), channel_id=1, source_target_pairs={{0,1},{1,0},{2,3},{3,2},{4,5},{5,4},{6,7},{7,6},{8,9},{9,8},{10,11... | collective-permute-start | bytes 3538952 | tf_op jit(solution)/shard_map/block_out/ppermute | solution.py:30
  173.5 16.5 %collective-permute-start.15 = (bf16[2,192,768]{2,1,0:T(8,128)(2,1)S(1)}, bf16[2,192,768]{2,1,0:T(8,128)(2,1)}, u32[]{:S(2)}, u32[]{:S(2)}) collective-permute-start(bf16[2,192,768]{2,1,0:T(8,128)(2,1)S(1)} %dynamic-slice_convert_fusion), channel_id=1, source_target_pairs={{0,8},{4,12},{8,0},{12,4},{16,24},{20,28},{24,16},{28,20},{1,9},{5... | collective-permute-start | bytes 1769480 | tf_op jit(solution)/shard_map/down_grad_dp/ppermute | solution.py:803
  173.5 28.6 %collective-permute-start.18 = (bf16[576,768]{1,0:T(8,128)(2,1)}, bf16[576,768]{1,0:T(8,128)(2,1)}, u32[]{:S(2)}, u32[]{:S(2)}) collective-permute-start(bf16[576,768]{1,0:T(8,128)(2,1)} %sum_tokens.10), channel_id=1, source_target_pairs={{0,2},{1,3},{2,0},{3,1},{4,6},{5,7},{6,4},{7,5},{8,10},{9,11},{10,... | collective-permute-start | bytes 2654216 | tf_op jit(solution)/shard_map/qkv_grad_x/ppermute | solution.py:26
  173.6 28.5 %collective-permute-start.19 = (bf16[192,768]{1,0:T(8,128)(2,1)}, bf16[192,768]{1,0:T(8,128)(2,1)}, u32[]{:S(2)}, u32[]{:S(2)}) collective-permute-start(bf16[192,768]{1,0:T(8,128)(2,1)} %sum_tokens.9), channel_id=1, source_target_pairs={{0,2},{1,3},{2,0},{3,1},{4,6},{5,7},{6,4},{7,5},{8,10},{9,11},{10,... | collective-permute-start | bytes 884744 | tf_op jit(solution)/shard_map/proj_grad_x/ppermute | solution.py:26
  191.2 14.4 %collective-permute-start.20 = (bf16[2,96,768]{2,1,0:T(8,128)(2,1)S(1)}, bf16[2,96,768]{2,1,0:T(8,128)(2,1)S(1)}, u32[]{:S(2)}, u32[]{:S(2)}) collective-permute-start(bf16[2,96,768]{2,1,0:T(8,128)(2,1)S(1)} %dynamic-slice_convert_fusion.1), channel_id=1, source_target_pairs={{0,16},{4,20},{8,24},{12,28},{16,0},{20,4},{24,8},{28,12},{1,17},{... | collective-permute-start | bytes 884744 | tf_op jit(solution)/shard_map/down_grad_dp/ppermute | solution.py:803
  207.9 9.5 %collective-permute-start.21 = (bf16[96,768]{1,0:T(8,128)(2,1)S(1)}, bf16[96,768]{1,0:T(8,128)(2,1)S(1)}, u32[]{:S(2)}, u32[]{:S(2)}) collective-permute-start(bf16[96,768]{1,0:T(8,128)(2,1)S(1)} %fusion.4), channel_id=1, source_target_pairs={{0,2},{1,3},{2,0},{3,1},{4,6},{5,7},{6,4},{7,5},{8,10},{9,11},{10,... | collective-permute-start | bytes 442376 | tf_op jit(solution)/shard_map/down_grad_x/ppermute | solution.py:26
  208.4 27.8 %collective-permute-start.24 = (bf16[480,768]{1,0:T(8,128)(2,1)}, bf16[480,768]{1,0:T(8,128)(2,1)}, u32[]{:S(2)}, u32[]{:S(2)}) collective-permute-start(bf16[480,768]{1,0:T(8,128)(2,1)} %constant_dynamic-slice_fusion.3), channel_id=1, source_target_pairs={{0,4},{4,0},{8,12},{12,8},{16,20},{20,16},{24,28},{28,24},{1,5},{5... | collective-permute-start | bytes 2211848 | tf_op jit(solution)/shard_map/up_proj_grad_dp/ppermute | solution.py:803
  210.4 8.8 %copy-start.12 = (f32[768,768]{1,0:T(8,128)S(1)}, f32[768,768]{1,0:T(8,128)}, u32[]{:S(2)}) copy-start(f32[768,768]{1,0:T(8,128)} %get-tuple-element.309) | copy-start | bytes 7077892
  219.2 16.9 %collective-permute-start.22 = (bf16[288,768]{1,0:T(8,128)(2,1)}, bf16[288,768]{1,0:T(8,128)(2,1)}, u32[]{:S(2)}, u32[]{:S(2)}) collective-permute-start(bf16[288,768]{1,0:T(8,128)(2,1)} %constant_dynamic-slice_fusion.2), channel_id=1, source_target_pairs={{0,4},{4,0},{8,12},{12,8},{16,20},{20,16},{24,28},{28,24},{1,5},{5... | collective-permute-start | bytes 1327112 | tf_op jit(solution)/shard_map/qkv_grad_dp/ppermute | solution.py:803
  221.6 14.6 %collective-permute-start.25 = (bf16[256,768]{1,0:T(8,128)(2,1)}, bf16[256,768]{1,0:T(8,128)(2,1)}, u32[]{:S(2)}, u32[]{:S(2)}) collective-permute-start(bf16[256,768]{1,0:T(8,128)(2,1)} %slice.158), channel_id=1, source_target_pairs={{0,2},{1,3},{2,0},{3,1},{4,6},{5,7},{6,4},{7,5},{8,10},{9,11},{10,... | collective-permute-start | bytes 1179656 | tf_op jit(solution)/shard_map/block_out/ppermute | solution.py:26
  223.0 12.8 %collective-permute-start.23 = (bf16[96,768]{1,0:T(8,128)(2,1)S(1)}, bf16[96,768]{1,0:T(8,128)(2,1)S(1)}, u32[]{:S(2)}, u32[]{:S(2)}) collective-permute-start(bf16[96,768]{1,0:T(8,128)(2,1)S(1)} %convert_add_fusion.6), channel_id=1, source_target_pairs={{0,16},{4,20},{8,24},{12,28},{16,0},{20,4},{24,8},{28,12},{1,17},{... | collective-permute-start | bytes 442376 | tf_op jit(solution)/shard_map/down_grad_dp/ppermute | solution.py:803
  236.2 5.3 %copy-start.26 = (f32[8,768]{1,0:T(8,128)S(1)}, f32[8,768]{1,0:T(8,128)}, u32[]{:S(2)}) copy-start(f32[8,768]{1,0:T(8,128)} %get-tuple-element.361) | copy-start | bytes 73732
  238.7 8.8 %collective-permute-start.29 = (bf16[1024,768]{1,0:T(8,128)(2,1)}, bf16[1024,768]{1,0:T(8,128)(2,1)S(1)}, u32[]{:S(2)}, u32[]{:S(2)}) collective-permute-start(bf16[1024,768]{1,0:T(8,128)(2,1)} %get-tuple-element.328), channel_id=1, source_target_pairs={{0,1},{1,0},{2,3},{3,2},{4,5},{5,4},{6,7},{7,6},{8,9},{9,8},{10,11... | collective-permute-start | bytes 4718600 | tf_op jit(solution)/shard_map/first_core/ppermute | solution.py:30
  241.5 8.2 %copy-start.8 = (bf16[576,768]{1,0:T(8,128)(2,1)S(1)}, bf16[576,768]{1,0:T(8,128)(2,1)}, u32[]{:S(2)}) copy-start(bf16[576,768]{1,0:T(8,128)(2,1)} %sum_tokens.13) | copy-start | bytes 2654212
  241.5 13.8 %collective-permute-start.30 = (bf16[192,768]{1,0:T(8,128)(2,1)S(1)}, bf16[192,768]{1,0:T(8,128)(2,1)S(1)}, u32[]{:S(2)}, u32[]{:S(2)}) collective-permute-start(bf16[192,768]{1,0:T(8,128)(2,1)S(1)} %maximum_select_fusion.11), channel_id=1, source_target_pairs={{0,8},{4,12},{8,0},{12,4},{16,24},{20,28},{24,16},{28,20},{1,9},{5... | collective-permute-start | bytes 884744 | tf_op jit(solution)/shard_map/down_grad_dp/ppermute | solution.py:803
  244.0 12.9 %collective-permute-start.26 = (bf16[120,768]{1,0:T(8,128)(2,1)}, bf16[120,768]{1,0:T(8,128)(2,1)S(1)}, u32[]{:S(2)}, u32[]{:S(2)}) collective-permute-start(bf16[120,768]{1,0:T(8,128)(2,1)} %get-tuple-element.317), channel_id=1, source_target_pairs={{0,16},{4,20},{8,24},{12,28},{16,0},{20,4},{24,8},{28,12},{1,17},{... | collective-permute-start | bytes 552968 | tf_op jit(solution)/shard_map/up_proj_grad_dp/ppermute | solution.py:803
  245.2 14.7 %collective-permute-start.27 = (bf16[120,768]{1,0:T(8,128)(2,1)S(1)}, bf16[120,768]{1,0:T(8,128)(2,1)S(1)}, u32[]{:S(2)}, u32[]{:S(2)}) collective-permute-start(bf16[120,768]{1,0:T(8,128)(2,1)S(1)} %get-tuple-element.318), channel_id=1, source_target_pairs={{0,8},{4,12},{8,0},{12,4},{16,24},{20,28},{24,16},{28,20},{1,9},{5... | collective-permute-start | bytes 552968 | tf_op jit(solution)/shard_map/up_proj_grad_dp/ppermute | solution.py:803
  246.8 13.0 %collective-permute-start.28 = (bf16[120,768]{1,0:T(8,128)(2,1)S(1)}, bf16[120,768]{1,0:T(8,128)(2,1)S(1)}, u32[]{:S(2)}, u32[]{:S(2)}) collective-permute-start(bf16[120,768]{1,0:T(8,128)(2,1)S(1)} %get-tuple-element.319), channel_id=1, source_target_pairs={{0,24},{4,28},{8,16},{12,20},{16,8},{20,12},{24,0},{28,4},{1,25},{... | collective-permute-start | bytes 552968 | tf_op jit(solution)/shard_map/up_proj_grad_dp/ppermute | solution.py:803
  248.9 12.2 %collective-permute-start.31 = (bf16[256,768]{1,0:T(8,128)(2,1)S(1)}, bf16[256,768]{1,0:T(8,128)(2,1)S(1)}, u32[]{:S(2)}, u32[]{:S(2)}) collective-permute-start(bf16[256,768]{1,0:T(8,128)(2,1)S(1)} %add_convert_fusion.1), channel_id=1, source_target_pairs={{0,2},{1,3},{2,0},{3,1},{4,6},{5,7},{6,4},{7,5},{8,10},{9,11},{10,... | collective-permute-start | bytes 1179656 | tf_op jit(solution)/shard_map/first_mid_x/ppermute | solution.py:26
  261.1 11.6 %copy-start.21 = (bf16[256,768]{1,0:T(8,128)(2,1)}, bf16[256,768]{1,0:T(8,128)(2,1)S(1)}, u32[]{:S(2)}) copy-start(bf16[256,768]{1,0:T(8,128)(2,1)S(1)} %collective-permute-done.31.refs_0_) | copy-start | bytes 1179652
  261.2 25.7 %collective-permute-start.36 = (bf16[384,768]{1,0:T(8,128)(2,1)S(1)}, bf16[384,768]{1,0:T(8,128)(2,1)S(1)}, u32[]{:S(2)}, u32[]{:S(2)}) collective-permute-start(bf16[384,768]{1,0:T(8,128)(2,1)S(1)} %maximum_select_fusion.7), channel_id=1, source_target_pairs={{0,4},{4,0},{8,12},{12,8},{16,20},{20,16},{24,28},{28,24},{1,5},{5... | collective-permute-start | bytes 1769480 | tf_op jit(solution)/shard_map/down_grad_dp/ppermute | solution.py:803
  262.5 24.4 %collective-permute-start.35 = (bf16[120,768]{1,0:T(8,128)(2,1)S(1)}, bf16[120,768]{1,0:T(8,128)(2,1)S(1)}, u32[]{:S(2)}, u32[]{:S(2)}) collective-permute-start(bf16[120,768]{1,0:T(8,128)(2,1)S(1)} %convert_add_fusion.5), channel_id=1, source_target_pairs={{0,16},{4,20},{8,24},{12,28},{16,0},{20,4},{24,8},{28,12},{1,17},{... | collective-permute-start | bytes 552968 | tf_op jit(solution)/shard_map/up_proj_grad_dp/ppermute | solution.py:803
  269.2 14.3 %collective-permute-start.32 = (bf16[72,768]{1,0:T(8,128)(2,1)S(1)}, bf16[72,768]{1,0:T(8,128)(2,1)S(1)}, u32[]{:S(2)}, u32[]{:S(2)}) collective-permute-start(bf16[72,768]{1,0:T(8,128)(2,1)S(1)} %get-tuple-element.347), channel_id=1, source_target_pairs={{0,16},{4,20},{8,24},{12,28},{16,0},{20,4},{24,8},{28,12},{1,17},{... | collective-permute-start | bytes 331784 | tf_op jit(solution)/shard_map/qkv_grad_dp/ppermute | solution.py:803
  269.2 14.3 %collective-permute-start.33 = (bf16[72,768]{1,0:T(8,128)(2,1)S(1)}, bf16[72,768]{1,0:T(8,128)(2,1)S(1)}, u32[]{:S(2)}, u32[]{:S(2)}) collective-permute-start(bf16[72,768]{1,0:T(8,128)(2,1)S(1)} %get-tuple-element.348), channel_id=1, source_target_pairs={{0,8},{4,12},{8,0},{12,4},{16,24},{20,28},{24,16},{28,20},{1,9},{5... | collective-permute-start | bytes 331784 | tf_op jit(solution)/shard_map/qkv_grad_dp/ppermute | solution.py:803
  271.9 15.0 %collective-permute-start.34 = (bf16[72,768]{1,0:T(8,128)(2,1)S(1)}, bf16[72,768]{1,0:T(8,128)(2,1)S(1)}, u32[]{:S(2)}, u32[]{:S(2)}) collective-permute-start(bf16[72,768]{1,0:T(8,128)(2,1)S(1)} %get-tuple-element.349), channel_id=1, source_target_pairs={{0,24},{4,28},{8,16},{12,20},{16,8},{20,12},{24,0},{28,4},{1,25},{... | collective-permute-start | bytes 331784 | tf_op jit(solution)/shard_map/qkv_grad_dp/ppermute | solution.py:803
  287.5 10.6 %collective-permute-start.43 = (bf16[240,768]{1,0:T(8,128)(2,1)S(1)}, bf16[240,768]{1,0:T(8,128)(2,1)S(1)}, u32[]{:S(2)}, u32[]{:S(2)}) collective-permute-start(bf16[240,768]{1,0:T(8,128)(2,1)S(1)} %maximum_select_fusion.10), channel_id=1, source_target_pairs={{0,8},{4,12},{8,0},{12,4},{16,24},{20,28},{24,16},{28,20},{1,9},{5... | collective-permute-start | bytes 1105928 | tf_op jit(solution)/shard_map/up_proj_grad_dp/ppermute | solution.py:803
  287.6 2.3 collective-permute-start.37
  287.7 4.4 %collective-permute-start.38 = (f32[12,768]{1,0:T(8,128)S(1)}, f32[12,768]{1,0:T(8,128)S(1)}, u32[]{:S(2)}, u32[]{:S(2)}) collective-permute-start(f32[12,768]{1,0:T(8,128)S(1)} %pad_maximum_fusion.6), channel_id=1, source_target_pairs={{0,2},{1,3},{2,0},{3,1},{4,6},{5,7},{6,4},{7,5},{8,10},{9,11},{10,... | collective-permute-start | bytes 110600 | tf_op jit(solution)/shard_map/small_sums/ppermute | solution.py:26
  288.6 4.0 %collective-permute-start.39 = (f32[12,768]{1,0:T(8,128)S(1)}, f32[12,768]{1,0:T(8,128)S(1)}, u32[]{:S(2)}, u32[]{:S(2)}) collective-permute-start(f32[12,768]{1,0:T(8,128)S(1)} %pad_maximum_fusion.6), channel_id=1, source_target_pairs={{0,3},{1,2},{2,1},{3,0},{4,7},{5,6},{6,5},{7,4},{8,11},{9,10},{10,... | collective-permute-start | bytes 110600 | tf_op jit(solution)/shard_map/small_sums/ppermute | solution.py:930
  289.5 8.2 %collective-permute-start.42 = (bf16[72,768]{1,0:T(8,128)(2,1)S(1)}, bf16[72,768]{1,0:T(8,128)(2,1)S(1)}, u32[]{:S(2)}, u32[]{:S(2)}) collective-permute-start(bf16[72,768]{1,0:T(8,128)(2,1)S(1)} %convert_add_fusion.7), channel_id=1, source_target_pairs={{0,4},{4,0},{8,12},{12,8},{16,20},{20,16},{24,28},{28,24},{1,5},{5... | collective-permute-start | bytes 331784 | tf_op jit(solution)/shard_map/qkv_grad_dp/ppermute | solution.py:803
  292.7 4.2 %collective-permute-start.40 = (f32[12,768]{1,0:T(8,128)S(1)}, f32[12,768]{1,0:T(8,128)S(1)}, u32[]{:S(2)}, u32[]{:S(2)}) collective-permute-start(f32[12,768]{1,0:T(8,128)S(1)} %add_add_fusion), channel_id=1, source_target_pairs={{0,4},{4,0},{8,12},{12,8},{16,20},{20,16},{24,28},{28,24},{1,5},{5... | collective-permute-start | bytes 110600 | tf_op jit(solution)/shard_map/small_sums/ppermute | solution.py:803
  296.9 10.6 %collective-permute-start.41 = (bf16[256,768]{1,0:T(8,128)(2,1)S(1)}, bf16[256,768]{1,0:T(8,128)(2,1)}, u32[]{:S(2)}, u32[]{:S(2)}) collective-permute-start(bf16[256,768]{1,0:T(8,128)(2,1)S(1)} %slice.136), channel_id=1, source_target_pairs={{0,2},{1,3},{2,0},{3,1},{4,6},{5,7},{6,4},{7,5},{8,10},{9,11},{10,... | collective-permute-start | bytes 1179656 | tf_op jit(solution)/shard_map/in_grad_x/ppermute | solution.py:26
  298.4 10.2 %copy-start.22 = (bf16[256,768]{1,0:T(8,128)(2,1)S(1)}, bf16[256,768]{1,0:T(8,128)(2,1)}, u32[]{:S(2)}) copy-start(bf16[256,768]{1,0:T(8,128)(2,1)} %get-tuple-element.353) | copy-start | bytes 1179652
  298.4 17.6 %collective-permute-start.47 = (bf16[480,768]{1,0:T(8,128)(2,1)S(1)}, bf16[480,768]{1,0:T(8,128)(2,1)S(1)}, u32[]{:S(2)}, u32[]{:S(2)}) collective-permute-start(bf16[480,768]{1,0:T(8,128)(2,1)S(1)} %maximum_select_fusion.5), channel_id=1, source_target_pairs={{0,4},{4,0},{8,12},{12,8},{16,20},{20,16},{24,28},{28,24},{1,5},{5... | collective-permute-start | bytes 2211848 | tf_op jit(solution)/shard_map/up_proj_grad_dp/ppermute | solution.py:803
  298.9 20.2 %collective-permute-start.44 = (bf16[160,768]{1,0:T(8,128)(2,1)S(1)}, bf16[160,768]{1,0:T(8,128)(2,1)S(1)}, u32[]{:S(2)}, u32[]{:S(2)}) collective-permute-start(bf16[160,768]{1,0:T(8,128)(2,1)S(1)} %fusion.3), channel_id=1, source_target_pairs={{0,16},{4,20},{8,24},{12,28},{16,0},{20,4},{24,8},{28,12},{1,17},{... | collective-permute-start | bytes 737288 | tf_op jit(solution)/shard_map/qkv_grad_dp/ppermute | solution.py:803
  301.3 17.8 %collective-permute-start.45 = (bf16[160,768]{1,0:T(8,128)(2,1)S(1)}, bf16[160,768]{1,0:T(8,128)(2,1)S(1)}, u32[]{:S(2)}, u32[]{:S(2)}) collective-permute-start(bf16[160,768]{1,0:T(8,128)(2,1)S(1)} %fusion.3), channel_id=1, source_target_pairs={{0,8},{4,12},{8,0},{12,4},{16,24},{20,28},{24,16},{28,20},{1,9},{5... | collective-permute-start | bytes 737288 | tf_op jit(solution)/shard_map/qkv_grad_dp/ppermute | solution.py:803
  301.8 20.6 %collective-permute-start.46 = (bf16[160,768]{1,0:T(8,128)(2,1)S(1)}, bf16[160,768]{1,0:T(8,128)(2,1)S(1)}, u32[]{:S(2)}, u32[]{:S(2)}) collective-permute-start(bf16[160,768]{1,0:T(8,128)(2,1)S(1)} %fusion.3), channel_id=1, source_target_pairs={{0,24},{4,28},{8,16},{12,20},{16,8},{20,12},{24,0},{28,4},{1,25},{... | collective-permute-start | bytes 737288 | tf_op jit(solution)/shard_map/qkv_grad_dp/ppermute | solution.py:803
  (13 other events, 22.7 us)
